TPU v7x, 32 devices: a whole 2x2x4 slice. The times are simulated.
32 devices in a mesh: dp: 4 (over y, x), seq: 8 (over z, core).
Axes of the slice: x: 2, y: 2, z: 4, core: 2. Of those that a mesh axis runs over, the one named last changes fastest.
Arguments:
- hidden_in: bfloat16 [4, 1024, 768], P('dp', 'seq'), may hold values from -6 to 6
- query_weight: bfloat16 [768, 768], P('seq'), may hold values from -0.4375 to 0.4375
- query_bias: bfloat16 [768], P('seq'), may hold values from -2 to 2
- key_weight: bfloat16 [768, 768], P('seq'), may hold values from -0.21875 to 0.21875
- value_weight: bfloat16 [768, 768], P('seq'), may hold values from -0.21875 to 0.21875
- value_bias: bfloat16 [768], P('seq'), may hold values from -2 to 2
- output_weight: bfloat16 [768, 768], P('seq'), may hold values from -0.875 to 0.875
- output_bias: bfloat16 [768], P('seq'), may hold values from -2 to 2
- first_gain: bfloat16 [768], P('seq'), may hold values from 0.25 to 1.75
- first_shift: bfloat16 [768], P('seq'), may hold values from -2 to 2
- inner_weight: bfloat16 [768, 3072], P('seq'), may hold values from -0.21875 to 0.21875
- inner_bias: bfloat16 [3072], P('seq'), may hold values from -2 to 2
- outer_weight: bfloat16 [3072, 768], P('seq'), may hold values from -0.109375 to 0.109375
- outer_bias: bfloat16 [768], P('seq'), may hold values from -2 to 2
- second_gain: bfloat16 [768], P('seq'), may hold values from 0.25 to 1.75
- second_shift: bfloat16 [768], P('seq'), may hold values from -2 to 2
- segments: int32 [4, 1024], P('dp'), may hold values from 0 to 3, never falling along the last dimension, each value on 1 to 512 neighbouring positions
- random_blocks: int32 [4, 16, 12, 3], P('dp'), may hold values from 0 to 15, as said below
- cotangent: bfloat16 [4, 1024, 768], P('dp', 'seq'), may hold values from -6 to 6
Outputs:
- layer_out: bfloat16 [4, 1024, 768], P('dp', 'seq')
- input_grad: float32 [4, 1024, 768], P('dp', 'seq')
- query_weight_grad: float32 [768, 768], P('seq')
- query_bias_grad: float32 [768], P('seq')
- key_weight_grad: float32 [768, 768], P('seq')
- value_weight_grad: float32 [768, 768], P('seq')
- value_bias_grad: float32 [768], P('seq')
- output_weight_grad: float32 [768, 768], P('seq')
- output_bias_grad: float32 [768], P('seq')
- first_gain_grad: float32 [768], P('seq')
- first_shift_grad: float32 [768], P('seq')
- inner_weight_grad: float32 [768, 3072], P('seq')
- inner_bias_grad: float32 [3072], P('seq')
- outer_weight_grad: float32 [3072, 768], P('seq')
- outer_bias_grad: float32 [768], P('seq')
- second_gain_grad: float32 [768], P('seq')
- second_shift_grad: float32 [768], P('seq')
Inputs may be any that keep to these rules, and one draw needn't show every extreme that they name: `random_blocks`: entry [s, b, h, i] names a block of sequence s. Take one index o of seq: its query blocks o * 2 to o * 2 + 1 of the one sequence of one index of dp, over all heads and slots, make 72 entries; at most 14 of them name blocks of any one piece (blocks p * 2 to p * 2 + 1), and some piece is named exactly 14 times. An entry may repeat a sliding or global block.
All inputs are finite; a program needn't handle non-finite values.
Results may differ from a plain program's by a relative error of at most 0.017.
Values may be sent and summed in bfloat16 or wider, within the bound.
No kernel may reach another device: no remote copies, remote signals or barrier semaphores. Data moves between devices by JAX's collectives and lax.ppermute only.
A program may use at most 128 MiB of HBM per device.

v0:
```python
import jax
import jax.numpy as jnp
from jax import lax
from jax.sharding import PartitionSpec as P

HEADS = 12
BLOCK = 64


EPSILON = 1e-12
MASKED = -1000000000.0


def with_halo(block, sides, width):
    for axis, dim in sides:
        count = lax.axis_size(axis)
        forward = [(i, i + 1) for i in range(count - 1)]
        backward = [(target, source) for source, target in forward]
        low = lax.ppermute(
            lax.slice_in_dim(block, block.shape[dim] - width, None, axis=dim), axis, forward
        )
        high = lax.ppermute(lax.slice_in_dim(block, 0, width, axis=dim), axis, backward)
        block = jnp.concatenate([low, block, high], axis=dim)
    return block


def broadcast(block, axis, owner):
    block = jnp.where(lax.axis_index(axis) == owner, block, jnp.zeros_like(block))
    return lax.psum(block, axis)


def matmul(left, right):
    return jnp.dot(left, right, preferred_element_type=jnp.float32)


def left_product(left, right):
    return lax.dot_general(
        left, right, (((0,), (0,)), ((), ())), preferred_element_type=jnp.float32
    )


def right_product(left, right):
    return lax.dot_general(
        left, right, (((1,), (1,)), ((), ())), preferred_element_type=jnp.float32
    )


def layer_norm(values, gain, shift):
    center = values - jnp.mean(values, -1, keepdims=True)
    spread = jnp.mean(center * center, -1, keepdims=True)
    inverse = lax.rsqrt(spread + EPSILON)
    normed = center * inverse
    return (normed * gain + shift, normed, inverse)


def norm_back(grad, normed, inverse, gain):
    scaled = grad * gain
    return inverse * (
        scaled
        - jnp.mean(scaled, -1, keepdims=True)
        - normed * jnp.mean(scaled * normed, -1, keepdims=True)
    )


def gelu_tanh(values):
    return jax.nn.gelu(values, approximate=True)


def pick_rows(table_rows, block_ids):
    return table_rows[block_ids]


def assemble(extended, first_kv, last_kv, fetched, ext_seg, first_seg, last_seg, rand_seg):
    group_len = extended.shape[0]
    block_len = first_kv.shape[1]
    blocks_dev = fetched.shape[1]
    head_count = fetched.shape[2]
    rand_count = fetched.shape[3]
    head_size = fetched.shape[5] // 2
    fixed = jnp.stack(
        [
            jnp.concatenate(
                [extended[:, column * block_len : (column + 3) * block_len], first_kv, last_kv], 1
            )
            for column in range(blocks_dev)
        ],
        1,
    )
    fixed = fixed.reshape(group_len, blocks_dev, 5 * block_len, 2, head_count, head_size).transpose(
        3, 0, 1, 4, 2, 5
    )
    moved = fetched.reshape(
        group_len, blocks_dev, head_count, rand_count * block_len, 2, head_size
    ).transpose(4, 0, 1, 2, 3, 5)
    paired = jnp.concatenate([fixed, moved], 4)
    fixed_seg = jnp.stack(
        [
            jnp.concatenate(
                [ext_seg[:, column * block_len : (column + 3) * block_len], first_seg, last_seg], 1
            )
            for column in range(blocks_dev)
        ],
        1,
    )
    fixed_seg = jnp.broadcast_to(
        fixed_seg[:, :, None, :], (group_len, blocks_dev, head_count, 5 * block_len)
    )
    key_seg = jnp.concatenate(
        [fixed_seg, rand_seg.reshape(group_len, blocks_dev, head_count, rand_count * block_len)], 3
    )
    return (paired[0], paired[1], key_seg)


def masked_scores(query, key_all, query_seg, key_seg):
    group_len, piece_len, model_width = query.shape
    blocks_dev = key_all.shape[1]
    head_count = key_all.shape[2]
    head_size = key_all.shape[4]
    block_len = piece_len // blocks_dev
    split_query = query.reshape(group_len, blocks_dev, block_len, head_count, head_size)
    raw = jnp.einsum(
        "gjqhe,gjhke->gjhqk", split_query, key_all, preferred_element_type=jnp.float32
    ) * head_size ** (-0.5)
    key_side = key_seg[:, :, :, None, :]
    allowed = (query_seg.reshape(group_len, blocks_dev, 1, block_len, 1) == key_side) | (
        key_side == -2
    )
    return (jnp.where(allowed, raw, MASKED), split_query)


def attend_forward(inputs):
    (
        query,
        extended,
        first_kv,
        last_kv,
        fetched,
        query_seg,
        ext_seg,
        first_seg,
        last_seg,
        rand_seg,
    ) = inputs
    key_all, value_all, key_seg = assemble(
        extended, first_kv, last_kv, fetched, ext_seg, first_seg, last_seg, rand_seg
    )
    scores, split_query = masked_scores(query, key_all, query_seg, key_seg)
    row_max = jnp.max(scores, -1, keepdims=True)
    powers = jnp.exp(scores - row_max)
    row_sum = jnp.sum(powers, -1, keepdims=True)
    probs = (powers / row_sum).astype(jnp.bfloat16)
    attended = jnp.einsum(
        "gjhqk,gjhke->gjqhe", probs, value_all, preferred_element_type=jnp.float32
    )
    return (attended.reshape(query.shape).astype(jnp.bfloat16), row_max + jnp.log(row_sum))


def attend_backward(inputs):
    (
        query,
        extended,
        first_kv,
        last_kv,
        fetched,
        query_seg,
        ext_seg,
        first_seg,
        last_seg,
        rand_seg,
        log_total,
        grad_att,
    ) = inputs
    key_all, value_all, key_seg = assemble(
        extended, first_kv, last_kv, fetched, ext_seg, first_seg, last_seg, rand_seg
    )
    scores, split_query = masked_scores(query, key_all, query_seg, key_seg)
    group_len, piece_len, model_width = query.shape
    block_len = first_kv.shape[1]
    blocks_dev = fetched.shape[1]
    head_count = fetched.shape[2]
    rand_count = fetched.shape[3]
    head_size = key_all.shape[4]
    probs = jnp.exp(scores - log_total)
    grad_split = grad_att.reshape(group_len, blocks_dev, block_len, head_count, head_size)
    grad_probs = jnp.einsum(
        "gjqhe,gjhke->gjhqk", grad_split, value_all, preferred_element_type=jnp.float32
    )
    weighted = jnp.sum(probs * grad_probs, -1, keepdims=True)
    grad_scores = (probs * (grad_probs - weighted)).astype(jnp.bfloat16)
    scale = head_size ** (-0.5)
    grad_query = (
        jnp.einsum("gjhqk,gjhke->gjqhe", grad_scores, key_all, preferred_element_type=jnp.float32)
        * scale
    )
    grad_key = (
        jnp.einsum(
            "gjhqk,gjqhe->gjhke", grad_scores, split_query, preferred_element_type=jnp.float32
        )
        * scale
    )
    grad_value = jnp.einsum(
        "gjhqk,gjqhe->gjhke",
        probs.astype(jnp.bfloat16),
        grad_split,
        preferred_element_type=jnp.float32,
    )
    paired = jnp.stack([grad_key, grad_value], 0)
    fixed_len = 5 * block_len
    fixed = (
        paired[:, :, :, :, :fixed_len]
        .transpose(1, 2, 4, 0, 3, 5)
        .reshape(group_len, blocks_dev, fixed_len, 2 * model_width)
    )
    moved = (
        paired[:, :, :, :, fixed_len:]
        .transpose(1, 2, 3, 4, 0, 5)
        .reshape(group_len, blocks_dev, head_count, rand_count, block_len, 2 * head_size)
    )
    ext_grad = jnp.zeros((group_len, piece_len + 2 * block_len, 2 * model_width), jnp.float32)
    for column in range(blocks_dev):
        ext_grad = ext_grad.at[:, column * block_len : (column + 3) * block_len].add(
            fixed[:, column, : 3 * block_len]
        )
    first_grad = jnp.sum(fixed[:, :, 3 * block_len : 4 * block_len], 1)
    last_grad = jnp.sum(fixed[:, :, 4 * block_len :], 1)
    return (
        grad_query.reshape(group_len, piece_len, model_width),
        ext_grad,
        first_grad,
        last_grad,
        moved,
    )


def local(
    hidden_in,
    query_weight,
    query_bias,
    key_weight,
    value_weight,
    value_bias,
    output_weight,
    output_bias,
    first_gain,
    first_shift,
    inner_weight,
    inner_bias,
    outer_weight,
    outer_bias,
    second_gain,
    second_shift,
    segments,
    random_blocks,
    cotangent,
):
    seq_count, piece_len, model_width = hidden_in.shape
    head_count = HEADS
    head_size = model_width // head_count
    block_len = BLOCK
    blocks_dev = piece_len // block_len
    rand_count = random_blocks.shape[3]
    seq_len = segments.shape[1]
    splits = lax.axis_size("seq")
    position = lax.axis_index("seq")
    row_count = seq_count * piece_len
    req_count = seq_count * blocks_dev * head_count * rand_count
    capacity = max(2, 3 * req_count // (2 * splits) + 1)
    group_len = min(seq_count, max(1, 512 // piece_len))
    batch_count = seq_count // group_len

    def grouped(array):
        return array.reshape((batch_count, group_len) + array.shape[1:])

    def ungrouped(array):
        return array.reshape((seq_count,) + array.shape[2:])

    fwd_weights = (
        lax.all_gather(query_weight, "seq", axis=0, tiled=True),
        lax.all_gather(query_bias, "seq", axis=0, tiled=True),
        lax.all_gather(key_weight, "seq", axis=0, tiled=True),
        lax.all_gather(value_weight, "seq", axis=0, tiled=True),
        lax.all_gather(value_bias, "seq", axis=0, tiled=True),
        lax.all_gather(output_weight, "seq", axis=0, tiled=True),
        lax.all_gather(output_bias, "seq", axis=0, tiled=True),
        lax.all_gather(first_gain, "seq", axis=0, tiled=True),
        lax.all_gather(first_shift, "seq", axis=0, tiled=True),
        lax.all_gather(inner_weight, "seq", axis=0, tiled=True),
        lax.all_gather(inner_bias, "seq", axis=0, tiled=True),
        lax.all_gather(outer_weight, "seq", axis=0, tiled=True),
        lax.all_gather(outer_bias, "seq", axis=0, tiled=True),
        lax.all_gather(second_gain, "seq", axis=0, tiled=True),
        lax.all_gather(second_shift, "seq", axis=0, tiled=True),
    )
    (
        w_query,
        b_query,
        w_key,
        w_value,
        b_value,
        w_output,
        b_output,
        g_first,
        s_first,
        w_inner,
        b_inner,
        w_outer,
        b_outer,
        g_second,
        s_second,
    ) = fwd_weights
    flat = hidden_in.reshape(row_count, model_width)
    query = (matmul(flat, w_query) + b_query).astype(jnp.bfloat16)
    keys = matmul(flat, w_key).astype(jnp.bfloat16)
    values = (matmul(flat, w_value) + b_value).astype(jnp.bfloat16)
    joined = jnp.concatenate([keys, values], 1).reshape(seq_count, piece_len, 2 * model_width)
    extended = with_halo(joined, (("seq", 1),), block_len)
    first_kv = broadcast(joined[:, :block_len], "seq", 0)
    last_kv = broadcast(joined[:, piece_len - block_len :], "seq", splits - 1)
    req_index = jnp.arange(req_count, dtype=jnp.int32)
    req_seq = req_index // (blocks_dev * head_count * rand_count)
    req_head = req_index // rand_count % head_count
    asked_ids = lax.dynamic_slice_in_dim(random_blocks, position * blocks_dev, blocks_dev, 1)
    kv_tiles = (
        joined.reshape(seq_count, blocks_dev, block_len, 2, head_count, head_size)
        .transpose(0, 1, 4, 2, 3, 5)
        .reshape(seq_count * blocks_dev * head_count, block_len, 2 * head_size)
    )
    everyone = (
        random_blocks.reshape(seq_count, splits, blocks_dev, head_count, rand_count)
        .transpose(1, 0, 2, 3, 4)
        .reshape(splits, req_count)
    )
    is_mine = (everyone // blocks_dev == position).astype(jnp.int32)
    slot_place = jnp.cumsum(is_mine, axis=1) - is_mine
    slot_index = jnp.where(is_mine == 1, slot_place, capacity)
    tile_of = (req_seq[None, :] * blocks_dev + everyone % blocks_dev) * head_count + req_head[
        None, :
    ]
    sender_rows = jnp.broadcast_to(
        jnp.arange(splits, dtype=jnp.int32)[:, None], (splits, req_count)
    )
    send_index = (
        jnp.zeros((splits, capacity), jnp.int32)
        .at[sender_rows, slot_index]
        .set(tile_of, mode="drop")
    )
    outgoing = jnp.take(kv_tiles, send_index, axis=0)
    incoming = lax.all_to_all(outgoing, "seq", split_axis=0, concat_axis=0, tiled=True)
    owner_ids = asked_ids.reshape(req_count) // blocks_dev
    owner_hits = (owner_ids[:, None] == jnp.arange(splits, dtype=jnp.int32)[None, :]).astype(
        jnp.int32
    )
    earlier = jnp.sum((jnp.cumsum(owner_hits, axis=0) - owner_hits) * owner_hits, 1)
    arrival = owner_ids * capacity + earlier
    fetched = jnp.take(
        incoming.reshape(splits * capacity, block_len, 2 * head_size), arrival, axis=0
    )
    fetched = fetched.reshape(
        seq_count, blocks_dev, head_count, rand_count, block_len, 2 * head_size
    )
    edge_seg = jnp.full((seq_count, block_len), -1, jnp.int32)
    padded_seg = jnp.concatenate([edge_seg, segments, edge_seg], 1)
    query_seg = lax.dynamic_slice_in_dim(segments, position * piece_len, piece_len, 1)
    ext_seg = lax.dynamic_slice_in_dim(
        padded_seg, position * piece_len, piece_len + 2 * block_len, 1
    )
    first_seg = jnp.full((seq_count, block_len), -2, jnp.int32)
    last_seg = jnp.full((seq_count, block_len), -2, jnp.int32)
    seg_blocks = segments.reshape(seq_count, seq_len // block_len, block_len)
    rand_seg = jax.vmap(pick_rows)(seg_blocks, asked_ids)
    attn_inputs = (
        query.reshape(seq_count, piece_len, model_width),
        extended,
        first_kv,
        last_kv,
        fetched,
        query_seg,
        ext_seg,
        first_seg,
        last_seg,
        rand_seg,
    )
    grouped_inputs = tuple((grouped(item) for item in attn_inputs))
    attended, log_total = lax.map(attend_forward, grouped_inputs)
    attended = attended.reshape(row_count, model_width)
    branch = matmul(attended, w_output) + b_output
    first_norm, first_normed, first_inverse = layer_norm(flat + branch, g_first, s_first)
    first_low = first_norm.astype(jnp.bfloat16)
    inner = matmul(first_low, w_inner) + b_inner
    activated = gelu_tanh(inner).astype(jnp.bfloat16)
    mixed = matmul(activated, w_outer) + b_outer
    layer_out, second_normed, second_inverse = layer_norm(first_norm + mixed, g_second, s_second)
    back_weights = (
        lax.all_gather(query_weight, "seq", axis=0, tiled=True),
        lax.all_gather(query_bias, "seq", axis=0, tiled=True),
        lax.all_gather(key_weight, "seq", axis=0, tiled=True),
        lax.all_gather(value_weight, "seq", axis=0, tiled=True),
        lax.all_gather(value_bias, "seq", axis=0, tiled=True),
        lax.all_gather(output_weight, "seq", axis=0, tiled=True),
        lax.all_gather(output_bias, "seq", axis=0, tiled=True),
        lax.all_gather(first_gain, "seq", axis=0, tiled=True),
        lax.all_gather(first_shift, "seq", axis=0, tiled=True),
        lax.all_gather(inner_weight, "seq", axis=0, tiled=True),
        lax.all_gather(inner_bias, "seq", axis=0, tiled=True),
        lax.all_gather(outer_weight, "seq", axis=0, tiled=True),
        lax.all_gather(outer_bias, "seq", axis=0, tiled=True),
        lax.all_gather(second_gain, "seq", axis=0, tiled=True),
        lax.all_gather(second_shift, "seq", axis=0, tiled=True),
    )
    (
        w_query,
        b_query,
        w_key,
        w_value,
        b_value,
        w_output,
        b_output,
        g_first,
        s_first,
        w_inner,
        b_inner,
        w_outer,
        b_outer,
        g_second,
        s_second,
    ) = back_weights
    grad_out = cotangent.reshape(row_count, model_width).astype(jnp.float32)
    second_gain_grad = jnp.sum(grad_out * second_normed, 0)
    second_shift_grad = jnp.sum(grad_out, 0)
    grad_mix = norm_back(grad_out, second_normed, second_inverse, g_second)
    grad_mixed = grad_mix.astype(jnp.bfloat16)
    outer_bias_grad = jnp.sum(grad_mixed, 0, dtype=jnp.float32)
    outer_weight_grad = left_product(activated, grad_mixed)
    grad_act = right_product(grad_mixed, w_outer)
    grad_inner = jax.vjp(gelu_tanh, inner)[1](grad_act)[0].astype(jnp.bfloat16)
    inner_bias_grad = jnp.sum(grad_inner, 0, dtype=jnp.float32)
    inner_weight_grad = left_product(first_low, grad_inner)
    grad_first = grad_mix + right_product(grad_inner, w_inner)
    first_gain_grad = jnp.sum(grad_first * first_normed, 0)
    first_shift_grad = jnp.sum(grad_first, 0)
    grad_res = norm_back(grad_first, first_normed, first_inverse, g_first)
    grad_branch = grad_res.astype(jnp.bfloat16)
    output_bias_grad = jnp.sum(grad_branch, 0, dtype=jnp.float32)
    output_weight_grad = left_product(attended, grad_branch)
    grad_att = right_product(grad_branch, w_output).astype(jnp.bfloat16)
    back_inputs = grouped_inputs + (
        log_total,
        grouped(grad_att.reshape(seq_count, piece_len, model_width)),
    )
    grad_query, ext_grad, first_grad, last_grad, rand_grad = lax.map(attend_backward, back_inputs)
    grad_query = ungrouped(grad_query)
    ext_grad = ungrouped(ext_grad)
    first_grad = ungrouped(first_grad)
    last_grad = ungrouped(last_grad)
    rand_grad = ungrouped(rand_grad)
    rims = jnp.concatenate([ext_grad[:, :block_len], ext_grad[:, piece_len + block_len :]], 1)
    beside_all = with_halo(rims.astype(jnp.bfloat16), (("seq", 1),), block_len).astype(rims.dtype)
    kv_grad = ext_grad[:, block_len : block_len + piece_len]
    kv_grad = kv_grad.at[:, :block_len].add(beside_all[:, :block_len])
    kv_grad = kv_grad.at[:, piece_len - block_len :].add(beside_all[:, 3 * block_len :])
    global_first, global_last = lax.psum((first_grad, last_grad), "seq")
    kv_grad = kv_grad.at[:, :block_len].add(jnp.where(position == 0, global_first, 0.0))
    kv_grad = kv_grad.at[:, piece_len - block_len :].add(
        jnp.where(position == splits - 1, global_last, 0.0)
    )
    back_slots = (
        jnp.zeros((splits * capacity, block_len, 2 * head_size), jnp.float32)
        .at[arrival]
        .set(rand_grad.reshape(req_count, block_len, 2 * head_size))
    )
    returned = lax.all_to_all(
        back_slots.reshape(splits, capacity, block_len, 2 * head_size).astype(jnp.bfloat16),
        "seq",
        split_axis=0,
        concat_axis=0,
        tiled=True,
    ).astype(jnp.float32)
    tile_grad = (
        jnp.zeros((seq_count * blocks_dev * head_count, block_len, 2 * head_size), jnp.float32)
        .at[send_index.reshape(splits * capacity)]
        .add(returned.reshape(splits * capacity, block_len, 2 * head_size))
    )
    random_part = (
        tile_grad.reshape(seq_count, blocks_dev, head_count, block_len, 2, head_size)
        .transpose(0, 1, 3, 4, 2, 5)
        .reshape(seq_count, piece_len, 2 * model_width)
    )
    kv_grad = kv_grad + random_part
    grad_keys = kv_grad[:, :, :model_width].reshape(row_count, model_width).astype(jnp.bfloat16)
    grad_values = kv_grad[:, :, model_width:].reshape(row_count, model_width).astype(jnp.bfloat16)
    grad_queries = grad_query.reshape(row_count, model_width).astype(jnp.bfloat16)
    query_weight_grad = left_product(flat, grad_queries)
    query_bias_grad = jnp.sum(grad_queries, 0, dtype=jnp.float32)
    key_weight_grad = left_product(flat, grad_keys)
    value_weight_grad = left_product(flat, grad_values)
    value_bias_grad = jnp.sum(grad_values, 0, dtype=jnp.float32)
    input_grad = (
        grad_res
        + right_product(grad_queries, w_query)
        + right_product(grad_keys, w_key)
        + right_product(grad_values, w_value)
    )
    shares = (
        lax.psum_scatter(query_weight_grad, "seq", scatter_dimension=0, tiled=True),
        lax.psum_scatter(query_bias_grad, "seq", scatter_dimension=0, tiled=True),
        lax.psum_scatter(key_weight_grad, "seq", scatter_dimension=0, tiled=True),
        lax.psum_scatter(value_weight_grad, "seq", scatter_dimension=0, tiled=True),
        lax.psum_scatter(value_bias_grad, "seq", scatter_dimension=0, tiled=True),
        lax.psum_scatter(output_weight_grad, "seq", scatter_dimension=0, tiled=True),
        lax.psum_scatter(output_bias_grad, "seq", scatter_dimension=0, tiled=True),
        lax.psum_scatter(first_gain_grad, "seq", scatter_dimension=0, tiled=True),
        lax.psum_scatter(first_shift_grad, "seq", scatter_dimension=0, tiled=True),
        lax.psum_scatter(inner_weight_grad, "seq", scatter_dimension=0, tiled=True),
        lax.psum_scatter(inner_bias_grad, "seq", scatter_dimension=0, tiled=True),
        lax.psum_scatter(outer_weight_grad, "seq", scatter_dimension=0, tiled=True),
        lax.psum_scatter(outer_bias_grad, "seq", scatter_dimension=0, tiled=True),
        lax.psum_scatter(second_gain_grad, "seq", scatter_dimension=0, tiled=True),
        lax.psum_scatter(second_shift_grad, "seq", scatter_dimension=0, tiled=True),
    )
    (
        share_qw,
        share_qb,
        share_kw,
        share_vw,
        share_vb,
        share_ow,
        share_ob,
        share_fg,
        share_fs,
        share_iw,
        share_ib,
        share_uw,
        share_ub,
        share_sg,
        share_ss,
    ) = shares
    totals = (
        lax.psum(share_qw.astype(jnp.bfloat16), "dp").astype(jnp.float32),
        lax.psum(share_qb.astype(jnp.bfloat16), "dp").astype(jnp.float32),
        lax.psum(share_kw.astype(jnp.bfloat16), "dp").astype(jnp.float32),
        lax.psum(share_vw.astype(jnp.bfloat16), "dp").astype(jnp.float32),
        lax.psum(share_vb.astype(jnp.bfloat16), "dp").astype(jnp.float32),
        lax.psum(share_ow.astype(jnp.bfloat16), "dp").astype(jnp.float32),
        lax.psum(share_ob.astype(jnp.bfloat16), "dp").astype(jnp.float32),
        lax.psum(share_fg.astype(jnp.bfloat16), "dp").astype(jnp.float32),
        lax.psum(share_fs.astype(jnp.bfloat16), "dp").astype(jnp.float32),
        lax.psum(share_iw.astype(jnp.bfloat16), "dp").astype(jnp.float32),
        lax.psum(share_ib.astype(jnp.bfloat16), "dp").astype(jnp.float32),
        lax.psum(share_uw.astype(jnp.bfloat16), "dp").astype(jnp.float32),
        lax.psum(share_ub.astype(jnp.bfloat16), "dp").astype(jnp.float32),
        lax.psum(share_sg.astype(jnp.bfloat16), "dp").astype(jnp.float32),
        lax.psum(share_ss.astype(jnp.bfloat16), "dp").astype(jnp.float32),
    )
    (
        total_qw,
        total_qb,
        total_kw,
        total_vw,
        total_vb,
        total_ow,
        total_ob,
        total_fg,
        total_fs,
        total_iw,
        total_ib,
        total_uw,
        total_ub,
        total_sg,
        total_ss,
    ) = totals
    return (
        layer_out.reshape(seq_count, piece_len, model_width).astype(jnp.bfloat16),
        input_grad.reshape(seq_count, piece_len, model_width),
        total_qw,
        total_qb,
        total_kw,
        total_vw,
        total_vb,
        total_ow,
        total_ob,
        total_fg,
        total_fs,
        total_iw,
        total_ib,
        total_uw,
        total_ub,
        total_sg,
        total_ss,
    )


def solution(mesh):
    in_specs = (
        P("dp", "seq", None),
        P("seq", None),
        P("seq"),
        P("seq", None),
        P("seq", None),
        P("seq"),
        P("seq", None),
        P("seq"),
        P("seq"),
        P("seq"),
        P("seq", None),
        P("seq"),
        P("seq", None),
        P("seq"),
        P("seq"),
        P("seq"),
        P("dp", None),
        P("dp", None, None, None),
        P("dp", "seq", None),
    )
    out_specs = (
        P("dp", "seq", None),
        P("dp", "seq", None),
        P("seq", None),
        P("seq"),
        P("seq", None),
        P("seq", None),
        P("seq"),
        P("seq", None),
        P("seq"),
        P("seq"),
        P("seq"),
        P("seq", None),
        P("seq"),
        P("seq", None),
        P("seq"),
        P("seq"),
        P("seq"),
    )
    return jax.shard_map(local, mesh=mesh, in_specs=in_specs, out_specs=out_specs, check_vma=False)
```

profile of v0, /device:TPU:8, one launch (start us, length us, event | category | flops | bytes accessed | tf_op | source)
XLA Modules:
  0.0 847.6 jit_solution(10335073190083793674)
XLA Ops:
  18.2 25.3 %all-reduce.20 = (bf16[768]{0:T(1024)(128)(2,1)S(1)}, bf16[768]{0:T(1024)(128)(2,1)S(1)}, bf16[768]{0:T(1024)(128)(2,1)S(1)}, bf16[768]{0:T(1024)(128)(2,1)S(1)}...) all-reduce(bf16[768]{0:T(1024)(128)(2,1)S(1)} %dynamic-update-slice, ...), channel_id=1, replica_groups=mesh['dp'=4,'seq'=8] {'seq'}, use_global_device_ids=true, to_apply=%add.2 | all-reduce | flops 6144 | bytes 24576
  45.2 12.4 %all-gather.10.cloned.1.call-done = bf16[768,768]{1,0:T(8,128)(2,1)} async-done(((bf16[96,768]{1,0:T(8,128)(2,1)}), bf16[768,768]{1,0:T(8,128)(2,1)}) %all-gather.10.cloned.1.call-update) | async-done | bytes 1179664 | tf_op jit(solution)/shard_map/all_gather | solution.py:281
  65.5 26.8 %scatter_fusion = s32[8,14]{1,0:T(8,128)S(1)} fusion(s32[8,14]{1,0:T(8,128)S(1)} %broadcast_in_dim.148, s32[576]{0:T(1024)S(1)} %reshape.990, s32[576]{0:T(1024)S(1)} %reshape.992), kind=kCustom, calls=%fused_computation.3 | custom fusion | bytes 11520 | tf_op jit(solution)/shard_map/scatter | solution.py:345
  96.5 4.2 all-to-all-start
  101.6 53.5 %all-gather = bf16[8,1,384]{2,1,0:T(2,128)(2,1)S(1)} all-gather(bf16[1,1,384]{2,1,0:T(2,128)(2,1)S(1)} %reshape.1040), channel_id=1, replica_groups=mesh['dp'=4,'seq'=8] {'seq'}, dimensions={0}, use_global_device_ids=true | all-gather | bytes 6912 | tf_op jit(solution)/shard_map/all_gather | solution.py:288
  163.4 5.2 collective-permute-start.1
  175.2 4.4 collective-permute-done
  181.5 4.1 maximum_bitcast_fusion
  187.3 4.2 gather.15
  191.5 3.8 copy.119
  207.7 27.4 %all-gather.16.cloned.1.call-done = bf16[768,3072]{1,0:T(8,128)(2,1)} async-done(((bf16[96,3072]{1,0:T(8,128)(2,1)}), bf16[768,3072]{1,0:T(8,128)(2,1)}) %all-gather.16.cloned.1.call-update) | async-done | bytes 4718608 | tf_op jit(solution)/shard_map/all_gather | solution.py:287
  235.1 4.4 convolution_add_fusion
  239.5 47.9 %all-gather.18.cloned.1.call-done = bf16[3072,768]{1,0:T(8,128)(2,1)} async-done(((bf16[384,768]{1,0:T(8,128)(2,1)}), bf16[3072,768]{1,0:T(8,128)(2,1)}) %all-gather.18.cloned.1.call-update) | async-done | bytes 4718608 | tf_op jit(solution)/shard_map/all_gather | solution.py:289
  287.4 4.1 fusion.120
  339.0 3.9 fusion.2
  342.9 7.1 copy.135
  350.0 4.6 reshape.1000
  356.9 10.9 %scatter_fusion.1 = f32[112,64,128]{2,1,0:T(8,128)} fusion(f32[112,64,128]{2,1,0:T(8,128)} %broadcast_in_dim.162, s32[72]{0:T(128)S(1)} %copy-done.55, f32[72,64,128]{2,1,0:T(8,128)S(1)} %reshape.1000), kind=kCustom, calls=%fused_computation.4 | custom fusion | bytes 7078176 | tf_op jit(solution)/shard_map/scatter | solution.py:469
  371.6 6.3 all-to-all-start.1
  384.8 27.6 %collective-permute-done.3 = bf16[1,64,1536]{2,1,0:T(8,128)(2,1)S(1)} collective-permute-done((bf16[1,64,1536]{2,1,0:T(8,128)(2,1)S(1)}, bf16[1,64,1536]{2,1,0:T(8,128)(2,1)S(1)}, u32[]{:S(2)}, u32[]{:S(2)}) %collective-permute-start.3) | collective-permute-done | bytes 196640 | tf_op jit(solution)/shard_map/ppermute | solution.py:22
  412.5 17.6 %collective-permute-done.2 = bf16[1,64,1536]{2,1,0:T(8,128)(2,1)S(1)} collective-permute-done((bf16[1,64,1536]{2,1,0:T(8,128)(2,1)S(1)}, bf16[1,64,1536]{2,1,0:T(8,128)(2,1)S(1)}, u32[]{:S(2)}, u32[]{:S(2)}) %collective-permute-start.2) | collective-permute-done | bytes 196640 | tf_op jit(solution)/shard_map/ppermute | solution.py:19
  430.5 5.9 all-to-all-done.1
  440.1 11.9 %scatter_fusion.2 = f32[24,64,128]{2,1,0:T(8,128)S(1)} fusion(f32[24,64,128]{2,1,0:T(8,128)S(1)} %broadcast_in_dim.161, s32[112]{0:T(128)S(1)} %fusion.91, f32[112,64,128]{2,1,0:T(8,128)} %bitcast_convert_fusion), kind=kCustom, calls=%fused_computation.5 | custom fusion | flops 917504 | bytes 11010496 | tf_op jit(solution)/shard_map/scatter-add | solution.py:481
  463.8 5.2 fusion.108
  470.4 5.2 fusion.95
  481.3 36.2 %reduce-scatter.21.cloned.1.call-done = f32[96,768]{1,0:T(8,128)} async-done(((f32[768,768]{1,0:T(8,128)}), f32[96,768]{1,0:T(8,128)}) %reduce-scatter.21.cloned.1.call-update) | async-done | bytes 294928
  519.3 35.9 %reduce-scatter.23.cloned.1.call-done = f32[96,768]{1,0:T(8,128)} async-done(((f32[768,768]{1,0:T(8,128)}), f32[96,768]{1,0:T(8,128)}) %reduce-scatter.23.cloned.1.call-update) | async-done | bytes 294928
  556.9 100.1 %reduce-scatter.15.cloned.1.call-done = f32[96,3072]{1,0:T(8,128)} async-done(((f32[768,3072]{1,0:T(8,128)}), f32[96,3072]{1,0:T(8,128)}) %reduce-scatter.15.cloned.1.call-update) | async-done | bytes 1179664 | tf_op jit(solution)/shard_map/reduce_scatter | solution.py:513
  659.2 97.9 %reduce-scatter.17.cloned.1.call-done = f32[384,768]{1,0:T(8,128)} async-done(((f32[3072,768]{1,0:T(8,128)}), f32[384,768]{1,0:T(8,128)}) %reduce-scatter.17.cloned.1.call-update) | async-done | bytes 1179664 | tf_op jit(solution)/shard_map/reduce_scatter | solution.py:515
  762.8 25.8 %all-reduce.18 = (bf16[768]{0:T(1024)(128)(2,1)S(1)}, bf16[768]{0:T(1024)(128)(2,1)S(1)}, bf16[768]{0:T(1024)(128)(2,1)S(1)}, bf16[768]{0:T(1024)(128)(2,1)S(1)}...) all-reduce(f32[768]{0:T(1024)S(1)} %reduce_sum.230, ...), channel_id=3, replica_groups=mesh['dp'=4,'seq'=8] {'seq'}, use_global_device_ids=true, to_apply=%region_26.27.clone | all-reduce | flops 9216 | bytes 55296
  789.2 10.0 %all-reduce.22 = (bf16[96]{0:T(256)(128)(2,1)S(1)}, bf16[96]{0:T(256)(128)(2,1)S(1)}, bf16[96]{0:T(256)(128)(2,1)S(1)}, bf16[96]{0:T(256)(128)(2,1)S(1)}, bf16[9...) all-reduce(bf16[96]{0:T(256)(128)(2,1)S(1)} %dynamic-slice.105, ...), channel_id=1, replica_groups=mesh['dp'=4,'seq'=8] {'dp'}, use_global_device_ids=true, to_apply=%region_27.28 | all-reduce | flops 1152 | bytes 4608 | tf_op jit(solution)/shard_map/psum | solution.py:539
  807.0 24.5 %all-reduce.32.cloned.1.call-done = (bf16[96,768]{0,1:T(8,128)(2,1)}, bf16[96,768]{0,1:T(8,128)(2,1)}, bf16[96,768]{0,1:T(8,128)(2,1)}, bf16[96,768]{1,0:T(8,128...) async-done(((bf16[96,768]{0,1:T(8,128)(2,1)}, bf16[96,768]{0,1:T(8,128)(2,1)}, bf16[96,768]{0,1:T(8,128)(2,1)}, bf16[96,768]{1,0:T(8,128)(2,1)}, ...) | async-done | bytes 1769488 | tf_op jit(solution)/shard_map/psum | solution.py:538
  (368 shorter events, 166.0 us)
Async XLA Ops:
  7.2 50.4 %copy-start.8 = (bf16[1,128,768]{2,1,0:T(8,128)(2,1)S(1)}, bf16[1,128,768]{2,1,0:T(8,128)(2,1)}, u32[]{:S(2)}) copy-start(bf16[1,128,768]{2,1,0:T(8,128)(2,1)} %param.31) | copy-start | bytes 589828
  7.2 36.3 %all-gather.8.cloned.1.call-start = ((), (), s32[]{:S(2)}) async-start(), calls=%async_computation.8 | async-start | bytes 1327104 | tf_op jit(solution)/shard_map/all_gather | solution.py:280
  7.9 49.7 %all-gather.10.cloned.1.call-start = ((), (), s32[]{:S(2)}) async-start(), calls=%async_computation.9 | async-start | bytes 1327104 | tf_op jit(solution)/shard_map/all_gather | solution.py:281
  8.7 162.1 %all-gather.12.cloned.1.call-start = ((), (), s32[]{:S(2)}) async-start(), calls=%async_computation.10 | async-start | bytes 1327104 | tf_op jit(solution)/shard_map/all_gather | solution.py:278
  9.4 172.0 %all-reduce.30.cloned.1.call-start = ((), (), s32[]{:S(2)}) async-start(), calls=%async_computation.21 | async-start | bytes 1572864 | tf_op jit(solution)/shard_map/psum | solution.py:29
  62.0 142.1 %all-gather.14.cloned.1.call-start = ((), (), s32[]{:S(2)}) async-start(), calls=%async_computation.11 | async-start | bytes 1327104 | tf_op jit(solution)/shard_map/all_gather | solution.py:283
  62.6 172.6 %all-gather.16.cloned.1.call-start = ((), (), s32[]{:S(2)}) async-start(), calls=%async_computation.12 | async-start | bytes 5308416 | tf_op jit(solution)/shard_map/all_gather | solution.py:287
  63.1 224.3 %all-gather.18.cloned.1.call-start = ((), (), s32[]{:S(2)}) async-start(), calls=%async_computation.13 | async-start | bytes 5308416 | tf_op jit(solution)/shard_map/all_gather | solution.py:289
  96.5 61.2 %copy-start.48 = (s32[1,1024]{1,0:T(1,128)S(1)}, s32[1,1024]{1,0:T(1,128)}, u32[]{:S(2)}) copy-start(s32[1,1024]{1,0:T(1,128)} %param.47) | copy-start | bytes 12292
  96.5 89.0 %all-to-all-start = ((bf16[8,14,64,128]{3,2,1,0:T(8,128)(2,1)}), bf16[8,14,64,128]{3,2,1,0:T(8,128)(2,1)S(1)}, u32[]{:S(2)}, u32[]{:S(2)}) async-start(bf16[8,14,64,128]{3,2,1,0:T(8,128)(2,1)} %broadcast_select_fusion), calls=%async_computation | async-start | bytes 3670016 | tf_op jit(solution)/shard_map/all_to_all | solution.py:348
  100.8 329.4 %all-reduce.28.cloned.1.call-start = ((), (), s32[]{:S(2)}) async-start(), calls=%async_computation.20 | async-start | bytes 1572864 | tf_op jit(solution)/shard_map/psum | solution.py:461
  163.4 10.7 %collective-permute-start.1 = (bf16[1,64,1536]{2,1,0:T(8,128)(2,1)}, bf16[1,64,1536]{2,1,0:T(8,128)(2,1)}, u32[]{:S(2)}, u32[]{:S(2)}) collective-permute-start(bf16[1,64,1536]{2,1,0:T(8,128)(2,1)} %get-tuple-element.288), channel_id=1, source_target_pairs={{1,0},{2,1},{3,2},{4,3},{5,4},{6,5},{7,6},{9,8},{10,9},{11,10},{12... | collective-permute-start | bytes 589832 | tf_op jit(solution)/shard_map/ppermute | solution.py:22
  168.6 11.0 %collective-permute-start = (bf16[1,64,1536]{2,1,0:T(8,128)(2,1)}, bf16[1,64,1536]{2,1,0:T(8,128)(2,1)}, u32[]{:S(2)}, u32[]{:S(2)}) collective-permute-start(bf16[1,64,1536]{2,1,0:T(8,128)(2,1)} %get-tuple-element.285), channel_id=1, source_target_pairs={{0,1},{1,2},{2,3},{3,4},{4,5},{5,6},{6,7},{8,9},{9,10},{10,11},{11... | collective-permute-start | bytes 589832 | tf_op jit(solution)/shard_map/ppermute | solution.py:19
  173.1 23.9 %copy-start.19 = (bf16[2,64,12,64]{1,3,2,0:T(8,128)(2,1)}, bf16[2,64,12,64]{1,3,2,0:T(8,128)(2,1)S(1)}, u32[]{:S(2)}) copy-start(bf16[2,64,12,64]{1,3,2,0:T(8,128)(2,1)S(1)} %copy.128) | copy-start | bytes 589828
  287.4 6.6 copy-start.58
  320.2 155.5 %reduce-scatter.19.cloned.1.call-start = ((), (), s32[]{:S(2)}) async-start(), calls=%async_computation.17 | async-start | bytes 2654208
  326.4 153.2 %reduce-scatter.13.cloned.1.call-start = ((), (), s32[]{:S(2)}) async-start(), calls=%async_computation.14 | async-start | bytes 2654208 | tf_op jit(solution)/shard_map/reduce_scatter | solution.py:509
  371.6 64.7 %all-to-all-start.1 = ((bf16[8,14,64,128]{3,2,1,0:T(8,128)(2,1)}), bf16[8,14,64,128]{3,2,1,0:T(8,128)(2,1)}, u32[]{:S(2)}, u32[]{:S(2)}) async-start(bf16[8,14,64,128]{3,2,1,0:T(8,128)(2,1)} %bitcast.46), calls=%async_computation.1 | async-start | bytes 3670016 | tf_op jit(solution)/shard_map/all_to_all | solution.py:471
  377.9 139.6 %reduce-scatter.21.cloned.1.call-start = ((), (), s32[]{:S(2)}) async-start(), calls=%async_computation.18 | async-start | bytes 2654208
  379.4 33.1 %collective-permute-start.3 = (bf16[1,64,1536]{2,1,0:T(8,128)(2,1)S(1)}, bf16[1,64,1536]{2,1,0:T(8,128)(2,1)S(1)}, u32[]{:S(2)}, u32[]{:S(2)}) collective-permute-start(bf16[1,64,1536]{2,1,0:T(8,128)(2,1)S(1)} %slice.370), channel_id=1, source_target_pairs={{1,0},{2,1},{3,2},{4,3},{5,4},{6,5},{7,6},{9,8},{10,9},{11,10},{12... | collective-permute-start | bytes 589832 | tf_op jit(solution)/shard_map/ppermute | solution.py:22
  381.4 48.6 %collective-permute-start.2 = (bf16[1,64,1536]{2,1,0:T(8,128)(2,1)S(1)}, bf16[1,64,1536]{2,1,0:T(8,128)(2,1)S(1)}, u32[]{:S(2)}, u32[]{:S(2)}) collective-permute-start(bf16[1,64,1536]{2,1,0:T(8,128)(2,1)S(1)} %slice.371), channel_id=1, source_target_pairs={{0,1},{1,2},{2,3},{3,4},{4,5},{5,6},{6,7},{8,9},{9,10},{10,11},{11... | collective-permute-start | bytes 589832 | tf_op jit(solution)/shard_map/ppermute | solution.py:19
  459.9 95.2 %reduce-scatter.23.cloned.1.call-start = ((), (), s32[]{:S(2)}) async-start(), calls=%async_computation.19 | async-start | bytes 2654208
  462.7 194.4 %reduce-scatter.15.cloned.1.call-start = ((), (), s32[]{:S(2)}) async-start(), calls=%async_computation.15 | async-start | bytes 10616832 | tf_op jit(solution)/shard_map/reduce_scatter | solution.py:513
  469.0 288.1 %reduce-scatter.17.cloned.1.call-start = ((), (), s32[]{:S(2)}) async-start(), calls=%async_computation.16 | async-start | bytes 10616832 | tf_op jit(solution)/shard_map/reduce_scatter | solution.py:515
  475.7 355.9 %all-reduce.32.cloned.1.call-start = ((), (), s32[]{:S(2)}) async-start(), calls=%async_computation.22 | async-start | bytes 3833856 | tf_op jit(solution)/shard_map/psum | solution.py:538
  659.2 101.5 %copy-start.27 = (bf16[1,128,768]{2,1,0:T(8,128)(2,1)S(1)}, bf16[1,128,768]{2,1,0:T(8,128)(2,1)}, u32[]{:S(2)}) copy-start(bf16[1,128,768]{2,1,0:T(8,128)(2,1)} %param.49) | copy-start | bytes 589828
  659.2 101.6 %copy-start.41 = (f32[12,64]{1,0:T(8,128)S(1)}, f32[12,64]{1,0:T(8,128)}, u32[]{:S(2)}) copy-start(f32[12,64]{1,0:T(8,128)} %get-tuple-element.306) | copy-start | bytes 9220
  659.2 101.6 %copy-start.16 = (f32[128,768]{1,0:T(8,128)S(1)}, f32[128,768]{1,0:T(8,128)}, u32[]{:S(2)}) copy-start(f32[128,768]{1,0:T(8,128)} %copy-done.14) | copy-start | bytes 1179652
  659.2 101.6 %copy-start.30 = (bf16[128,768]{0,1:T(8,128)(2,1)S(1)}, bf16[128,768]{0,1:T(8,128)(2,1)}, u32[]{:S(2)}) copy-start(bf16[128,768]{0,1:T(8,128)(2,1)} %copy-done.29) | copy-start | bytes 589828
  759.3 44.6 %copy-start.17 = (bf16[768,768]{1,0:T(8,128)(2,1)S(1)}, bf16[768,768]{1,0:T(8,128)(2,1)}, u32[]{:S(2)}) copy-start(bf16[768,768]{1,0:T(8,128)(2,1)} %all-gather.8.cloned.1.call-done) | copy-start | bytes 3538948
  831.6 7.1 copy-start.32
  831.6 8.2 copy-start.31
  (50 other events, 134.1 us)
Sparse Core Ops, SparseCore 0:
  9.7 23.8 all-gather.7
  35.2 22.3 all-gather.9
  59.3 22.2 all-gather.11
  85.0 72.7 all-reduce.29
  159.4 23.3 all-gather.13
  184.4 50.6 all-gather.15
  236.8 50.5 all-gather.17
  320.3 57.0 all-reduce.27
  379.7 63.9 reduce-scatter.18
  445.9 33.7 reduce-scatter.12
  482.0 35.4 reduce-scatter.20
  519.7 35.4 reduce-scatter.22
  557.5 99.5 reduce-scatter.14
  659.2 97.8 reduce-scatter.16
  762.0 69.5 all-reduce.31
where the time goes:
time: 858 us; the launch traced here: 848 us
  waiting for transfers between devices  445 us (52%)
  local copies, waits for them, and re-layouts  135 us (16%)
  blocking collectives  115 us (13%)
  other arithmetic  61.9 us (7%)
  matrix products  50.9 us (6%)
  starting transfers between devices  23.1 us (3%)
  between operations  17.3 us (2%)
    reduce_scatter x1, waiting for transfers between devices, local(): lax.psum_scatter(inner_weight_grad, 'seq', scatter_dimension=0, tiled=True)  100 us
    reduce_scatter x1, waiting for transfers between devices, local(): lax.psum_scatter(outer_weight_grad, 'seq', scatter_dimension=0, tiled=True)  97.9 us
    unnamed x18, waiting for transfers between devices  76.1 us
    all_gather x1, blocking collectives, local(): lax.all_gather(inner_bias, 'seq', axis=0, tiled=True)  53.5 us
    unnamed x2, blocking collectives  51.1 us
    all_gather x1, waiting for transfers between devices, local(): lax.all_gather(outer_weight, 'seq', axis=0, tiled=True)  47.9 us
    unnamed x162, local copies, waits for them, and re-layouts  41.1 us
    ppermute x2, waiting for transfers between devices, with_halo(): lax.ppermute(lax.slice_in_dim(block, 0, width, axis=dim), axis, backward)  28.6 us
  transfers between devices with their start and end apart: 21, of which 14 were waited for; matrix products, arithmetic and copies ran while one was open for 23% of the time, Pallas kernels for 0%

commit v1 on v0

v1 whole, which is shorter than its diff:
```python
import functools

import jax
import jax.numpy as jnp
from jax import lax
from jax.experimental import pallas as pl
from jax.experimental.pallas import tpu as pltpu
from jax.sharding import PartitionSpec as P

HEADS = 12
BLOCK = 64
EPSILON = 1e-12
MASKED = -1000000000.0
GELU_A = 0.7978845608028654
GELU_B = 0.044715
VMEM_BYTES = 48 << 20
bf16 = jnp.bfloat16
f32 = jnp.float32


def matmul(left, right):
    return jnp.dot(left, right, preferred_element_type=f32)


def left_product(left, right):
    return lax.dot_general(left, right, (((0,), (0,)), ((), ())), preferred_element_type=f32)


def right_product(left, right):
    return lax.dot_general(left, right, (((1,), (1,)), ((), ())), preferred_element_type=f32)


def run_kernel(kernel, name, outs, args, scratch=(), scalars=0, flops=0, powers=0):
    specs = [pl.BlockSpec(memory_space=pltpu.SMEM)] * scalars
    specs += [pl.BlockSpec(memory_space=pltpu.VMEM)] * (len(args) - scalars)
    out_shape = tuple(jax.ShapeDtypeStruct(shape, dtype) for shape, dtype in outs)
    moved = sum(a.size * a.dtype.itemsize for a in args)
    moved += sum(o.size * o.dtype.itemsize for o in out_shape)
    return pl.pallas_call(
        kernel,
        name=name,
        out_shape=out_shape,
        in_specs=specs,
        out_specs=tuple(pl.BlockSpec(memory_space=pltpu.VMEM) for _ in outs),
        scratch_shapes=list(scratch),
        compiler_params=pltpu.CompilerParams(vmem_limit_bytes=VMEM_BYTES),
        cost_estimate=pl.CostEstimate(flops=flops, bytes_accessed=moved, transcendentals=powers),
    )(*args)


def normalize(values):
    center = values - jnp.mean(values, -1, keepdims=True)
    spread = jnp.mean(center * center, -1, keepdims=True)
    inverse = lax.rsqrt(spread + EPSILON)
    return center * inverse, inverse


def norm_back(grad, normed, inverse, gain):
    scaled = grad * gain
    return inverse * (
        scaled
        - jnp.mean(scaled, -1, keepdims=True)
        - normed * jnp.mean(scaled * normed, -1, keepdims=True)
    )


def bias_rows(be_ref, bn, same, head, block, blocks, block_len):
    width = same.shape[1]
    rows = [
        jnp.broadcast_to(be_ref[head * blocks + block + i : head * blocks + block + i + 1, :], (block_len, width))
        for i in range(same.shape[0] // block_len)
    ]
    return jnp.where(same, jnp.concatenate(rows, 0), bn)


def attend_kernel(ids, hid, w, qb, vb, be, bn, sk, sq, att, qo, ko, vo, lse, qs):
    pieces, piece_len, width = qs.shape
    chips = pieces // 2
    core = ids[0]
    size = 64
    heads = width // size
    blocks = be.shape[0] // heads
    per_piece = blocks // chips
    block_len = piece_len // per_piece
    model = hid.shape[2]
    tokens = hid[:, :piece_len, :].reshape(pieces * piece_len, model)
    product = matmul(tokens, w[...])
    query = (product[:, :width] + qb[...]).astype(bf16) * bf16(size**-0.5)
    qs[...] = query.reshape(pieces, piece_len, width)
    ko[...] = product[:, width : 2 * width].astype(bf16)
    vo[...] = (product[:, 2 * width :] + vb[...]).astype(bf16)
    for chip in range(chips):
        qo[chip] = qs[2 * chip + core]
    lane = lax.broadcasted_iota(jnp.int32, (piece_len, 128), 1)
    for chip in range(chips):
        same = sq[chip * piece_len : (chip + 1) * piece_len, :] == sk[...]
        logs = jnp.zeros((piece_len, 128), f32)
        outs = []
        for head in range(heads):
            cols = slice(head * size, (head + 1) * size)
            scores = right_product(qo[chip, :, cols], ko[:, cols])
            scores = scores + bias_rows(be, bn[...], same, head, chip * per_piece, blocks, block_len)
            top = jnp.max(scores, -1, keepdims=True)
            powers = jnp.exp(scores - top)
            total = jnp.sum(powers, -1, keepdims=True)
            probs = (powers * (1.0 / total)).astype(bf16)
            outs.append(matmul(probs, vo[:, cols]).astype(bf16))
            logs = jnp.where(lane == head, top + jnp.log(total), logs)
        att[chip] = jnp.concatenate(outs, 1)
        lse[chip] = logs


def attend_back_kernel(
    ids, hid, q, k, v, ga, lse, be, bn, sk, sq, dq, mine, other, dwm, dwo, ds_all, p_all, dkv, dws
):
    chips, piece_len, width = q.shape
    pieces = 2 * chips
    core = ids[0]
    chip_at = ids[1]
    size = 64
    heads = width // size
    blocks = be.shape[0] // heads
    per_piece = blocks // chips
    block_len = piece_len // per_piece
    model = hid.shape[2]
    dks = []
    dvs = []
    dqs = [[None] * heads for _ in range(chips)]
    for head in range(heads):
        cols = slice(head * size, (head + 1) * size)
        key = k[:, cols]
        value = v[:, cols]
        for chip in range(chips):
            rows = slice(chip * piece_len, (chip + 1) * piece_len)
            same = sq[rows, :] == sk[...]
            scores = right_product(q[chip, :, cols], key)
            scores = scores + bias_rows(be, bn[...], same, head, chip * per_piece, blocks, block_len)
            probs = jnp.exp(scores - lse[chip, :, head : head + 1])
            grad = right_product(ga[chip, :, cols], value)
            weighted = jnp.sum(probs * grad, -1, keepdims=True)
            ds = (probs * (grad - weighted)).astype(bf16)
            ds_all[rows, :] = ds
            p_all[rows, :] = probs.astype(bf16)
            dqs[chip][head] = (matmul(ds, key) * (size**-0.5)).astype(bf16)
        queries = q[:, :, cols].reshape(chips * piece_len, size)
        grads = ga[:, :, cols].reshape(chips * piece_len, size)
        dks.append(left_product(ds_all[...], queries).astype(bf16))
        dvs.append(left_product(p_all[...], grads).astype(bf16))
    for chip in range(chips):
        dq[chip] = jnp.concatenate(dqs[chip], 1)
    joined = jnp.concatenate(dks + dvs, 1)
    dkv[...] = joined.reshape(pieces, piece_len, 2 * width)
    for chip in range(chips):
        mine[chip] = dkv[2 * chip + core]
        other[chip] = dkv[2 * chip + 1 - core]
    tokens = hid[:, :piece_len, :].reshape(pieces * piece_len, model)
    owned = jnp.concatenate([hid[2 * chip + core, :piece_len, :] for chip in range(chips)], 0)
    grad_q = dq[...].reshape(chips * piece_len, width)
    rows = model // pieces
    weights = jnp.concatenate([left_product(owned, grad_q), left_product(tokens, joined)], 1)
    dws[:, :rows, :] = weights.reshape(pieces, rows, 3 * width)
    sums = jnp.concatenate(
        [
            jnp.sum(grad_q.astype(f32), 0, keepdims=True),
            jnp.sum(joined.astype(f32), 0, keepdims=True),
        ],
        1,
    )
    for piece in range(pieces):
        keep = (chip_at == piece // 2).astype(f32)
        dws[piece, rows:, :] = jnp.broadcast_to(sums * keep, (8, 3 * width))
    for chip in range(chips):
        dwm[chip] = dws[2 * chip + core]
        dwo[chip] = dws[2 * chip + 1 - core].astype(bf16)


def input_grad_kernel(dq, mine, recv, w, out):
    chips, piece_len, width = dq.shape
    dkv = (mine[...].astype(f32) + recv[...].astype(f32)).astype(bf16)
    grads = jnp.concatenate([dq[...], dkv], 2).reshape(chips * piece_len, 3 * width)
    out[...] = right_product(grads, w[...]).astype(bf16).reshape(out.shape)


def project_kernel(att, wo, hid, vec, low, normed, inverse):
    chips, piece_len, width = att.shape
    weight = wo[...].reshape(chips * width, -1)
    branch = vec[2:3, :] + jnp.zeros((piece_len, weight.shape[1]), f32)
    for chip in range(chips):
        branch = branch + matmul(att[chip], weight[chip * width : (chip + 1) * width])
    n1, r1 = normalize(hid[...].astype(f32) + branch)
    low[...] = (n1 * vec[3:4, :] + vec[4:5, :]).astype(bf16)
    normed[...] = n1
    inverse[...] = jnp.broadcast_to(r1, inverse.shape)


def gelu_parts(v):
    inside = GELU_A * (v + GELU_B * (v * v * v))
    return jnp.tanh(inside)


def forward_kernel(ids, *refs):
    parts = (len(refs) - 5) // 2
    x = refs[:parts]
    w1, w2, vec = refs[parts : parts + 3]
    outs = refs[parts + 3 : 2 * parts + 3]
    inner_ref, act_ref = refs[2 * parts + 3 :]
    rows = x[0].shape[0]
    weight1 = w1[...].reshape(-1, w1.shape[-1])
    weight2 = w2[...].reshape(-1, w2.shape[-1])
    tokens = jnp.concatenate([r[...] for r in x], 0)
    inner = matmul(tokens, weight1) + vec[pl.ds(8 + ids[2], 1), :]
    act = (0.5 * inner * (1.0 + gelu_parts(inner))).astype(bf16)
    inner_ref[...] = inner
    act_ref[...] = act
    mixed = matmul(act, weight2)
    for i in range(parts):
        outs[i][...] = mixed[i * rows : (i + 1) * rows].astype(outs[i].dtype)


def middle_kernel(*refs):
    recv = refs[:-7]
    normed, cot, vec, out, low, mix, sums = refs[-7:]
    first = normed[...] * vec[3:4, :] + vec[4:5, :]
    mixed = vec[5:6, :]
    for r in recv:
        mixed = mixed + r[...].astype(f32)
    n2, r2 = normalize(first + mixed)
    gain = vec[6:7, :]
    out[...] = (n2 * gain + vec[7:8, :]).astype(bf16)
    g = cot[...].astype(f32)
    grad = norm_back(g, n2, r2, gain)
    rounded = grad.astype(bf16)
    mix[...] = grad
    low[...] = rounded
    sums[0:1, :] = jnp.sum(g * n2, 0, keepdims=True)
    sums[1:2, :] = jnp.sum(g, 0, keepdims=True)
    sums[2:3, :] = jnp.sum(rounded.astype(f32), 0, keepdims=True)
    sums[3:, :] = jnp.zeros((5, sums.shape[1]), f32)


def backward_kernel(*refs):
    parts = (len(refs) - 5) // 2
    grads = refs[:parts]
    w1, w2, inner_ref = refs[parts : parts + 3]
    outs = refs[parts + 3 : 2 * parts + 3]
    gi_ref, sum_ref = refs[2 * parts + 3 :]
    rows = grads[0].shape[0]
    weight1 = w1[...].reshape(-1, w1.shape[-1])
    weight2 = w2[...].reshape(-1, w2.shape[-1])
    gm = jnp.concatenate([r[...] for r in grads], 0)
    grad_act = right_product(gm, weight2)
    v = inner_ref[...]
    t = gelu_parts(v)
    slope = 0.5 * (1.0 + t) + 0.5 * v * (1.0 - t * t) * (GELU_A * (1.0 + 3.0 * GELU_B * (v * v)))
    gi = (grad_act * slope).astype(bf16)
    gi_ref[...] = gi
    sum_ref[...] = jnp.sum(gi.astype(f32), 0, keepdims=True)
    first = right_product(gi, weight1)
    for i in range(parts):
        outs[i][...] = first[i * rows : (i + 1) * rows].astype(outs[i].dtype)


def residual_kernel(*refs):
    recv = refs[:-9]
    mix, normed, inverse, vec, wo, res, low, back, sums = refs[-9:]
    first = mix[...]
    for r in recv:
        first = first + r[...].astype(f32)
    n1 = normed[...]
    grad = norm_back(first, n1, inverse[:, 0:1], vec[3:4, :])
    rounded = grad.astype(bf16)
    res[...] = grad
    low[...] = rounded
    sums[0:1, :] = jnp.sum(first * n1, 0, keepdims=True)
    sums[1:2, :] = jnp.sum(first, 0, keepdims=True)
    sums[2:3, :] = jnp.sum(rounded.astype(f32), 0, keepdims=True)
    sums[3:, :] = jnp.zeros((5, sums.shape[1]), f32)
    weight = wo[...].reshape(-1, wo.shape[-1])
    chips, _, width = back.shape
    for chip in range(chips):
        back[chip] = right_product(rounded, weight[chip * width : (chip + 1) * width]).astype(bf16)


def weight_grad_kernel(*refs):
    parts = (len(refs) - 7) // 2
    x = refs[:parts]
    gm = refs[parts : 2 * parts]
    gi, act, att, gb, d1, d2, do = refs[2 * parts :]
    rows = x[0].shape[0]
    tokens = jnp.concatenate([r[...] for r in x], 0)
    grads = jnp.concatenate([r[...] for r in gm], 0)
    d1[...] = left_product(tokens, gi[...]).astype(bf16).reshape(d1.shape)
    d2[...] = left_product(act[...], grads).astype(bf16).reshape(d2.shape)
    chips, _, width = att.shape
    for chip in range(chips):
        do[chip * width : (chip + 1) * width, :] = left_product(att[chip], gb[...]).astype(bf16)


def finish_kernel(t0, t1, t2, t3, gq, gk, gv, bias):
    chips, _, wide = t0.shape
    width = wide // 3
    rows = gq.shape[0]
    total = t0[...].astype(f32)
    for r in (t1, t2, t3):
        total = total + r[...].astype(f32)
    for i, out in enumerate((gq, gk, gv)):
        out[...] = jnp.concatenate(
            [total[chip, :rows, i * width : (i + 1) * width] for chip in range(chips)], 1
        )
    bias[...] = total[:, rows:, :]


def log_counts(count):
    return jnp.where(count > 0, jnp.log(jnp.maximum(count, 1).astype(f32)), MASKED)


class HeadAttention:
    def __init__(self, hidden, weights, biases, segments, random_blocks, vec_local):
        self.splits = splits = lax.axis_size("seq")
        self.chips = chips = splits // 2
        self.position = position = lax.axis_index("seq")
        core = position % 2
        chip = position // 2
        self.ids = jnp.stack([core, chip, lax.axis_index("dp")]).astype(jnp.int32)
        self.hidden = hidden
        piece_len, model = hidden.shape
        rows = model // splits
        width = model // chips
        heads = HEADS // chips
        self.lines = [[2 * i + c for i in range(chips)] for c in range(2)]
        self.swap = [(i, i ^ 1) for i in range(splits)]
        extra = 8 * model - vec_local.shape[0]
        tail = jnp.concatenate([vec_local, jnp.zeros((extra,), bf16)]).reshape(8, model)
        packed = lax.all_gather(jnp.concatenate([hidden, tail], 0), "seq")
        self.packed = packed
        self.vec_all = packed[:, piece_len : piece_len + 8].reshape(splits, 8 * model)[
            :, : vec_local.shape[0]
        ]
        split = jnp.concatenate([w.reshape(rows, chips, width) for w in weights], 2)
        lined = self.line(split.transpose(1, 0, 2))
        swapped = lax.ppermute(lined, "seq", self.swap)
        even = jnp.where(core == 0, lined, swapped)
        odd = jnp.where(core == 0, swapped, lined)
        self.weight = jnp.stack([even, odd], 1).reshape(model, 3 * width)
        pair = jnp.stack(biases, 0)
        pair_other = lax.ppermute(pair, "seq", self.swap)
        bias = jnp.where(
            core == 0,
            jnp.concatenate([pair, pair_other], 1),
            jnp.concatenate([pair_other, pair], 1),
        ).astype(f32)
        self.bias_q, self.bias_v = bias[0:1], bias[1:2]
        block_count = segments.shape[1] // BLOCK
        per_piece = piece_len // BLOCK
        own = random_blocks[0].reshape(chips, 2, per_piece, HEADS, -1)
        own = lax.dynamic_index_in_dim(own, core, 1, keepdims=False)
        own = lax.dynamic_slice_in_dim(own, chip * heads, heads, 2)
        own = own.reshape(chips * per_piece, heads, -1).transpose(1, 0, 2)
        block = jnp.arange(block_count, dtype=jnp.int32)
        mine = (
            (jnp.arange(chips, dtype=jnp.int32)[:, None] * 2 + core) * per_piece
            + jnp.arange(per_piece, dtype=jnp.int32)[None, :]
        ).reshape(-1)
        ends = ((block == 0) | (block == block_count - 1)).astype(jnp.int32)
        near = (jnp.abs(block[None, :] - mine[:, None]) <= 1).astype(jnp.int32)
        listed = jnp.sum((own[..., None] == block).astype(jnp.int32), 2)
        count = listed + near[None] + ends
        self.same_bias = jnp.repeat(log_counts(count).reshape(-1, block_count), BLOCK, axis=1)
        self.other_bias = jnp.repeat(
            jnp.where(ends > 0, 0.0, MASKED).astype(f32)[None], BLOCK, axis=1
        )
        self.key_seg = segments
        self.query_seg = lax.dynamic_index_in_dim(
            segments.reshape(chips, 2, piece_len), core, 1, keepdims=False
        ).reshape(chips * piece_len, 1)
        self.piece_len, self.width, self.model = piece_len, width, model

    def line(self, array):
        return lax.all_to_all(
            array, "seq", 0, 0, tiled=True, axis_index_groups=self.lines
        )

    def masks(self):
        return (self.same_bias, self.other_bias, self.key_seg, self.query_seg)

    def forward(self):
        chips, piece_len, width = self.chips, self.piece_len, self.width
        tokens = self.splits * piece_len
        one = (chips, piece_len, width)
        att, self.q, self.k, self.v, self.lse = run_kernel(
            attend_kernel,
            "attend",
            [
                (one, bf16),
                (one, bf16),
                ((tokens, width), bf16),
                ((tokens, width), bf16),
                ((chips, piece_len, 128), f32),
            ],
            (self.ids, self.packed, self.weight, self.bias_q, self.bias_v) + self.masks(),
            scratch=[pltpu.VMEM((self.splits, piece_len, width), bf16)],
            scalars=1,
            flops=6 * tokens * self.model * width + 2 * tokens * tokens * width,
            powers=tokens * tokens * 3 // 2,
        )
        return self.line(att)

    def backward(self, grad, grad_res):
        chips, piece_len, width = self.chips, self.piece_len, self.width
        splits, model = self.splits, self.model
        tokens = splits * piece_len
        rows = model // splits
        one = (chips, piece_len, width)
        two = (chips, piece_len, 2 * width)
        out = (chips, rows + 8, 3 * width)
        grad = self.line(grad)
        dq, mine, other, dw_mine, dw_other = run_kernel(
            attend_back_kernel,
            "attend_back",
            [(one, bf16), (two, bf16), (two, bf16), (out, f32), (out, bf16)],
            (self.ids, self.packed, self.q, self.k, self.v, grad, self.lse) + self.masks(),
            scratch=[
                pltpu.VMEM((chips * piece_len, tokens), bf16),
                pltpu.VMEM((chips * piece_len, tokens), bf16),
                pltpu.VMEM((splits, piece_len, 2 * width), bf16),
                pltpu.VMEM((splits, rows + 8, 3 * width), f32),
            ],
            scalars=1,
            flops=6 * tokens * model * width + 5 * tokens * tokens * width,
            powers=tokens * tokens * 3 // 2,
        )
        dw_recv = lax.ppermute(dw_other, "seq", self.swap)
        recv = lax.ppermute(other, "seq", self.swap)
        dw = self.line((dw_mine + dw_recv.astype(f32)).astype(bf16))
        (partial,) = run_kernel(
            input_grad_kernel,
            "input_grad",
            [((chips, piece_len, model), bf16)],
            (dq, mine, recv, self.weight),
            flops=3 * tokens * model * width,
        )
        dws = [dw] + [exchange(dw, k) for k in range(1, lax.axis_size("dp"))]
        partial = self.line(partial)
        input_grad = grad_res + jnp.sum(partial.astype(f32), 0)
        grad_w = [(rows, model), f32]
        gq, gk, gv, bias = run_kernel(
            finish_kernel,
            "finish",
            [((rows, model), f32)] * 3 + [((chips, 8, 3 * width), f32)],
            tuple(dws),
        )
        core, chip = self.position % 2, self.position // 2
        row = lax.dynamic_index_in_dim(bias, chip, 0, keepdims=False)[0]
        bias_q = lax.dynamic_slice_in_dim(row, core * rows, rows)
        bias_v = lax.dynamic_slice_in_dim(row, 2 * width + core * rows, rows)
        return input_grad, gq, bias_q, gk, gv, bias_v


def exchange(array, k):
    count = lax.axis_size("dp")
    return lax.ppermute(array, "dp", [(i, i ^ k) for i in range(count)])


def one_hot(index, count):
    return (index[..., None] == jnp.arange(count, dtype=jnp.int32)).astype(bf16)


def with_halo(block, axis, dim, width):
    count = lax.axis_size(axis)
    forward = [(i, i + 1) for i in range(count - 1)]
    backward = [(target, source) for source, target in forward]
    low = lax.ppermute(
        lax.slice_in_dim(block, block.shape[dim] - width, None, axis=dim), axis, forward
    )
    high = lax.ppermute(lax.slice_in_dim(block, 0, width, axis=dim), axis, backward)
    return jnp.concatenate([low, block, high], axis=dim)


def broadcast(block, axis, owner):
    block = jnp.where(lax.axis_index(axis) == owner, block, jnp.zeros_like(block))
    return lax.psum(block, axis)


class TokenAttention:
    def __init__(self, hidden, weights, biases, segments, random_blocks, vec_local):
        self.splits = splits = lax.axis_size("seq")
        self.position = position = lax.axis_index("seq")
        self.ids = jnp.stack([position % 2, position // 2, lax.axis_index("dp")]).astype(jnp.int32)
        self.hidden = hidden
        self.segments = segments
        self.random_blocks = random_blocks
        self.weights = [lax.all_gather(w, "seq", axis=0, tiled=True) for w in weights]
        self.vec_all = lax.all_gather(vec_local, "seq")

    def forward(self):
        hidden, segments = self.hidden, self.segments
        splits, position = self.splits, self.position
        seq_count = segments.shape[0]
        row_count, model = hidden.shape
        piece_len = row_count // seq_count
        size = model // HEADS
        per = piece_len // BLOCK
        slots = self.random_blocks.shape[3]
        reqs = seq_count * per * HEADS * slots
        cap = max(2, 3 * reqs // (2 * splits) + 1)
        rows = model // splits
        vec = self.vec_all.reshape(splits, -1, rows).transpose(1, 0, 2).reshape(-1, model)
        wq, wk, wv = self.weights
        query = (matmul(hidden, wq) + vec[0:1]).astype(bf16)
        keys = matmul(hidden, wk).astype(bf16)
        values = (matmul(hidden, wv) + vec[1:2]).astype(bf16)
        joined = jnp.concatenate([keys, values], 1).reshape(seq_count, piece_len, 2 * model)
        extended = with_halo(joined, "seq", 1, BLOCK)
        first = broadcast(joined[:, :BLOCK], "seq", 0)
        last = broadcast(joined[:, piece_len - BLOCK :], "seq", splits - 1)
        tiles = seq_count * per * HEADS
        tile_size = BLOCK * 2 * size
        kv_tiles = (
            joined.reshape(seq_count, per, BLOCK, 2, HEADS, size)
            .transpose(0, 1, 4, 2, 3, 5)
            .reshape(tiles, tile_size)
        )
        req = jnp.arange(reqs, dtype=jnp.int32)
        req_seq = req // (per * HEADS * slots)
        req_head = req // slots % HEADS
        earlier = (req[:, None] > req[None, :]).astype(jnp.int32)
        everyone = (
            self.random_blocks.reshape(seq_count, splits, per, HEADS, slots)
            .transpose(1, 0, 2, 3, 4)
            .reshape(splits, reqs)
        )
        is_mine = (everyone // per == position).astype(jnp.int32)
        place = jnp.sum(is_mine[:, None, :] * earlier, 2)
        slot = jnp.where(is_mine == 1, place, cap)
        tile_of = (req_seq * per + everyone % per) * HEADS + req_head
        chosen = slot[:, :, None] == jnp.arange(cap, dtype=jnp.int32)
        send = jnp.sum(jnp.where(chosen, tile_of[:, :, None], 0), 1).reshape(splits * cap)
        self.send = one_hot(send, tiles)
        outgoing = matmul(self.send, kv_tiles).astype(bf16).reshape(splits, cap, tile_size)
        incoming = lax.all_to_all(outgoing, "seq", 0, 0, tiled=True)
        asked = lax.dynamic_slice_in_dim(self.random_blocks, position * per, per, 1)
        owner = asked.reshape(reqs) // per
        before = jnp.sum((owner[:, None] == owner[None, :]).astype(jnp.int32) * earlier, 1)
        self.arrival = one_hot(owner * cap + before, splits * cap)
        fetched = matmul(self.arrival, incoming.reshape(splits * cap, tile_size)).astype(bf16)
        moved = fetched.reshape(seq_count, per, HEADS, slots * BLOCK, 2, size)
        spans = [slice(i * BLOCK, (i + 3) * BLOCK) for i in range(per)]
        fixed = jnp.stack(
            [jnp.concatenate([extended[:, span], first, last], 1) for span in spans], 1
        )
        fixed = fixed.reshape(seq_count, per, 5 * BLOCK, 2, HEADS, size)
        paired = jnp.concatenate(
            [fixed.transpose(3, 0, 1, 4, 2, 5), moved.transpose(4, 0, 1, 2, 3, 5)], 4
        )
        self.keys, self.values = paired[0], paired[1]
        edge = jnp.full((seq_count, BLOCK), -1, jnp.int32)
        padded = jnp.concatenate([edge, segments, edge], 1)
        query_seg = lax.dynamic_slice_in_dim(segments, position * piece_len, piece_len, 1)
        ext_seg = lax.dynamic_slice_in_dim(padded, position * piece_len, piece_len + 2 * BLOCK, 1)
        always = jnp.full((seq_count, 2 * BLOCK), -2, jnp.int32)
        seg_fixed = jnp.stack(
            [jnp.concatenate([ext_seg[:, span], always], 1) for span in spans], 1
        )
        seg_fixed = jnp.broadcast_to(
            seg_fixed[:, :, None], (seq_count, per, HEADS, 5 * BLOCK)
        )
        seg_blocks = segments.reshape(seq_count, -1, BLOCK)
        asked_hot = one_hot(asked, seg_blocks.shape[1])
        seg_moved = jnp.einsum(
            "gjhrb,gbt->gjhrt", asked_hot, seg_blocks.astype(bf16), preferred_element_type=f32
        ).astype(jnp.int32)
        key_seg = jnp.concatenate(
            [seg_fixed, seg_moved.reshape(seq_count, per, HEADS, slots * BLOCK)], 3
        )[:, :, :, None, :]
        self.allowed = (
            query_seg.reshape(seq_count, per, 1, BLOCK, 1) == key_seg
        ) | (key_seg == -2)
        self.query = query.reshape(seq_count, per, BLOCK, HEADS, size)
        scores = self.scores()
        top = jnp.max(scores, -1, keepdims=True)
        powers = jnp.exp(scores - top)
        total = jnp.sum(powers, -1, keepdims=True)
        self.log_total = top + jnp.log(total)
        attended = jnp.einsum(
            "gjhqk,gjhke->gjqhe",
            (powers / total).astype(bf16),
            self.values,
            preferred_element_type=f32,
        )
        return attended.astype(bf16).reshape(1, row_count, model)

    def scores(self):
        raw = jnp.einsum("gjqhe,gjhke->gjhqk", self.query, self.keys, preferred_element_type=f32)
        return jnp.where(self.allowed, raw * self.query.shape[-1] ** -0.5, MASKED)

    def backward(self, grad, grad_res):
        hidden = self.hidden
        splits, position = self.splits, self.position
        seq_count, per, _, _, size = self.query.shape
        row_count, model = hidden.shape
        piece_len = per * BLOCK
        slots = self.random_blocks.shape[3]
        scale = size**-0.5
        probs = jnp.exp(self.scores() - self.log_total)
        grad_split = grad.reshape(seq_count, per, BLOCK, HEADS, size)
        grad_probs = jnp.einsum(
            "gjqhe,gjhke->gjhqk", grad_split, self.values, preferred_element_type=f32
        )
        weighted = jnp.sum(probs * grad_probs, -1, keepdims=True)
        grad_scores = (probs * (grad_probs - weighted)).astype(bf16)
        grad_query = (
            jnp.einsum("gjhqk,gjhke->gjqhe", grad_scores, self.keys, preferred_element_type=f32)
            * scale
        )
        grad_key = (
            jnp.einsum("gjhqk,gjqhe->gjhke", grad_scores, self.query, preferred_element_type=f32)
            * scale
        )
        grad_value = jnp.einsum(
            "gjhqk,gjqhe->gjhke", probs.astype(bf16), grad_split, preferred_element_type=f32
        )
        paired = jnp.stack([grad_key, grad_value], 0)
        fixed_len = 5 * BLOCK
        fixed = (
            paired[:, :, :, :, :fixed_len]
            .transpose(1, 2, 4, 0, 3, 5)
            .reshape(seq_count, per, fixed_len, 2 * model)
        )
        moved = (
            paired[:, :, :, :, fixed_len:]
            .transpose(1, 2, 3, 4, 0, 5)
            .reshape(seq_count * per * HEADS * slots, BLOCK * 2 * size)
        )
        ext = jnp.zeros((seq_count, piece_len + 2 * BLOCK, 2 * model), f32)
        for i in range(per):
            ext = ext.at[:, i * BLOCK : (i + 3) * BLOCK].add(fixed[:, i, : 3 * BLOCK])
        first = jnp.sum(fixed[:, :, 3 * BLOCK : 4 * BLOCK], 1)
        last = jnp.sum(fixed[:, :, 4 * BLOCK :], 1)
        rims = jnp.concatenate([ext[:, :BLOCK], ext[:, piece_len + BLOCK :]], 1)
        beside = with_halo(rims.astype(bf16), "seq", 1, BLOCK).astype(f32)
        kv_grad = ext[:, BLOCK : BLOCK + piece_len]
        kv_grad = kv_grad.at[:, :BLOCK].add(beside[:, :BLOCK])
        kv_grad = kv_grad.at[:, piece_len - BLOCK :].add(beside[:, 3 * BLOCK :])
        first, last = lax.psum((first, last), "seq")
        kv_grad = kv_grad.at[:, :BLOCK].add(jnp.where(position == 0, first, 0.0))
        kv_grad = kv_grad.at[:, piece_len - BLOCK :].add(
            jnp.where(position == splits - 1, last, 0.0)
        )
        cap = self.send.shape[0] // splits
        outgoing = left_product(self.arrival, moved.astype(bf16)).astype(bf16)
        returned = lax.all_to_all(
            outgoing.reshape(splits, cap, -1), "seq", 0, 0, tiled=True
        ).reshape(splits * cap, -1)
        kv_grad = kv_grad + (
            left_product(self.send, returned)
            .reshape(seq_count, per, HEADS, BLOCK, 2, size)
            .transpose(0, 1, 3, 4, 2, 5)
            .reshape(seq_count, piece_len, 2 * model)
        )
        kv_grad = kv_grad.reshape(row_count, 2 * model).astype(bf16)
        grad_query = grad_query.reshape(row_count, model).astype(bf16)
        grads = (grad_query, kv_grad[:, :model], kv_grad[:, model:])
        input_grad = grad_res
        shares = []
        for part, weight in zip(grads, self.weights):
            input_grad = input_grad + right_product(part, weight)
            full = left_product(hidden, part)
            share = lax.psum_scatter(full, "seq", scatter_dimension=0, tiled=True)
            shares.append(lax.psum(share.astype(bf16), "dp").astype(f32))
        biases = jnp.stack([jnp.sum(grads[i].astype(f32), 0) for i in (0, 2)], 1)
        biases = lax.psum_scatter(biases, "seq", scatter_dimension=0, tiled=True)
        biases = lax.psum(biases.astype(bf16), "dp").astype(f32)
        return input_grad, shares[0], biases[:, 0], shares[1], shares[2], biases[:, 1]


def local(
    hidden_in,
    query_weight,
    query_bias,
    key_weight,
    value_weight,
    value_bias,
    output_weight,
    output_bias,
    first_gain,
    first_shift,
    inner_weight,
    inner_bias,
    outer_weight,
    outer_bias,
    second_gain,
    second_shift,
    segments,
    random_blocks,
    cotangent,
):
    seq_count, piece_len, model = hidden_in.shape
    splits = lax.axis_size("seq")
    groups = lax.axis_size("dp")
    group = lax.axis_index("dp")
    row_count = seq_count * piece_len
    rows = model // splits
    units = outer_weight.shape[0] // groups
    hidden = hidden_in.reshape(row_count, model)
    by_heads = seq_count == 1 and 2 < splits and splits % 2 == 0 and HEADS % (splits // 2) == 0
    vec_local = jnp.concatenate(
        [
            query_bias,
            value_bias,
            output_bias,
            first_gain,
            first_shift,
            outer_bias,
            second_gain,
            second_shift,
            inner_bias,
        ]
    )
    attention = (HeadAttention if by_heads else TokenAttention)(
        hidden,
        (query_weight, key_weight, value_weight),
        (query_bias, value_bias),
        segments,
        random_blocks,
        vec_local,
    )
    inner_part = lax.dynamic_index_in_dim(
        inner_weight.reshape(rows, splits, groups, units), group, 2, keepdims=False
    ).reshape(rows, splits * units)
    outer_part = lax.dynamic_index_in_dim(
        outer_weight.reshape(groups, units, model), group, 0, keepdims=False
    )
    w_out = lax.all_gather(output_weight, "seq", axis=0, tiled=True)
    w_both = lax.all_gather(jnp.concatenate([inner_part, outer_part], 0), "seq")
    w_in = w_both[:, :rows].reshape(model, splits * units)
    w_outer = w_both[:, rows:].reshape(splits * units, model)
    attended = attention.forward()
    vec = attention.vec_all.reshape(splits, 8 + groups, rows).transpose(1, 0, 2)
    vec = vec.reshape(8 + groups, model).astype(f32)
    ids = attention.ids
    full = (row_count, model)
    low, normed, inverse = run_kernel(
        project_kernel,
        "project",
        [(full, bf16), (full, f32), ((row_count, 128), f32)],
        (attended, w_out, hidden, vec),
        flops=2 * row_count * model * model,
    )
    lows = [low] + [exchange(low, k) for k in range(1, groups)]
    work = 2 * groups * row_count * model * splits * units
    parts = run_kernel(
        forward_kernel,
        "forward",
        [(full, f32)]
        + [(full, bf16)] * (groups - 1)
        + [((groups * row_count, splits * units), f32), ((groups * row_count, splits * units), bf16)],
        (ids, *lows, w_in, w_outer, vec),
        scalars=1,
        flops=2 * work,
        powers=groups * row_count * splits * units,
    )
    inner, act = parts[groups:]
    recv = [parts[0]] + [exchange(parts[k], k) for k in range(1, groups)]
    layer_out, grad_low, grad_mix, sums2 = run_kernel(
        middle_kernel,
        "middle",
        [(full, bf16), (full, bf16), (full, f32), ((8, model), f32)],
        (*recv, normed, cotangent.reshape(row_count, model), vec),
    )
    grads = [grad_low] + [exchange(grad_low, k) for k in range(1, groups)]
    parts = run_kernel(
        backward_kernel,
        "backward",
        [(full, f32)]
        + [(full, bf16)] * (groups - 1)
        + [((groups * row_count, splits * units), bf16), ((1, splits * units), f32)],
        (*grads, w_in, w_outer, inner),
        flops=2 * work,
        powers=groups * row_count * splits * units,
    )
    grad_inner, sum_inner = parts[groups:]
    recv = [parts[0]] + [exchange(parts[k], k) for k in range(1, groups)]
    grad_res, grad_branch, grad_att, sums1 = run_kernel(
        residual_kernel,
        "residual",
        [(full, f32), (full, bf16), (attended.shape, bf16), ((8, model), f32)],
        (*recv, grad_mix, normed, inverse, vec, w_out),
        flops=2 * row_count * model * model,
    )
    d_inner, d_outer, d_output = run_kernel(
        weight_grad_kernel,
        "weight_grad",
        [((model, splits * units), bf16), ((splits * units, model), bf16), ((model, model), bf16)],
        (*lows, *grads, grad_inner, act, attended, grad_branch),
        flops=2 * work + 2 * row_count * model * model,
    )
    sums = jnp.concatenate([sums2[:3], sums1[:3], sum_inner], 0)
    sums = sums.reshape(7, splits, rows).transpose(1, 0, 2).reshape(splits, 1, 7 * rows)
    sums = jnp.pad(sums, ((0, 0), (0, 7), (0, model - 7 * rows))).astype(bf16)
    stacked = jnp.concatenate(
        [
            d_inner.reshape(splits, rows, -1),
            d_outer.reshape(splits, units, model),
            d_output.reshape(splits, rows, model),
            sums,
        ],
        1,
    )
    share = lax.psum_scatter(stacked, "seq", scatter_dimension=0, tiled=False)
    every = lax.all_gather(share, "dp")
    d_inner = (
        every[:, :rows].reshape(groups, rows, splits, units).transpose(1, 2, 0, 3)
    ).reshape(rows, -1).astype(f32)
    d_outer = every[:, rows : rows + units].reshape(groups * units, model).astype(f32)
    d_output = jnp.sum(every[:, rows + units : 2 * rows + units].astype(f32), 0)
    small = every[:, 2 * rows + units, : 7 * rows].astype(f32).reshape(groups, 7, rows)
    vectors = jnp.sum(small[:, :6], 0)
    d_inner_bias = small[:, 6].reshape(-1)
    input_grad, gq, bias_q, gk, gv, bias_v = attention.backward(grad_att, grad_res)
    return (
        layer_out.reshape(seq_count, piece_len, model),
        input_grad.reshape(seq_count, piece_len, model),
        gq,
        bias_q,
        gk,
        gv,
        bias_v,
        d_output,
        vectors[5],
        vectors[3],
        vectors[4],
        d_inner,
        d_inner_bias,
        d_outer,
        vectors[2],
        vectors[0],
        vectors[1],
    )


def solution(mesh):
    in_specs = (
        P("dp", "seq", None),
        P("seq", None),
        P("seq"),
        P("seq", None),
        P("seq", None),
        P("seq"),
        P("seq", None),
        P("seq"),
        P("seq"),
        P("seq"),
        P("seq", None),
        P("seq"),
        P("seq", None),
        P("seq"),
        P("seq"),
        P("seq"),
        P("dp", None),
        P("dp", None, None, None),
        P("dp", "seq", None),
    )
    out_specs = (
        P("dp", "seq", None),
        P("dp", "seq", None),
        P("seq", None),
        P("seq"),
        P("seq", None),
        P("seq", None),
        P("seq"),
        P("seq", None),
        P("seq"),
        P("seq"),
        P("seq"),
        P("seq", None),
        P("seq"),
        P("seq", None),
        P("seq"),
        P("seq"),
        P("seq"),
    )
    return jax.shard_map(local, mesh=mesh, in_specs=in_specs, out_specs=out_specs, check_vma=False)
```

time: 858 us -> 299 us (0.35)
  waiting for transfers between devices: 445 us -> 125 us
  blocking collectives: 115 us -> 12.2 us
  local copies, waits for them, and re-layouts: 135 us -> 48.8 us
  matrix products: 50.9 us -> 0 us
  other arithmetic: 61.9 us -> 16.2 us
  Pallas kernels: 0 us -> 32.8 us
  starting transfers between devices: 23.1 us -> 46.1 us
    reduce_scatter x3 -> x1, waiting for transfers between devices: 200 us -> 9.1 us  [local(): share = lax.psum_scatter(stacked, 'seq', scatter_dimension=0, tiled=False)]
    unnamed x18 -> x5, waiting for transfers between devices: 76.1 us -> 0.76 us
    all_gather x6 -> x4, waiting for transfers between devices: 87.7 us -> 27.9 us  [the longest x1 27.4 us: local(): w_both = lax.all_gather(jnp.concatenate([inner_part, outer_part], 0), 'seq')]
    all_gather x1 -> x0, blocking collectives: 53.5 us -> none  [local(): lax.all_gather(inner_bias, 'seq', axis=0, tiled=True)]
    unnamed x2 -> x0, blocking collectives: 51.1 us -> none
    dot_general x24 -> x0, matrix products: 50.9 us -> none  [the longest x6 15.3 us: matmul(): return jnp.dot(left, right, preferred_element_type=jnp.float32)]
    all_to_all x2 -> x4, waiting for transfers between devices: 5.88 us -> 46.7 us  [line(): lax.all_to_all(array, 'seq', 0, 0, tiled=True, axis_index_groups=self.lines)]
    scatter x2 -> x0, local copies, waits for them, and re-layouts: 37.7 us -> none  [the longest x1 26.8 us: local(): send_index = jnp.zeros((splits, capacity), jnp.int32).at[sender_rows, slo...]
  transfers between devices with their start and end apart: 21 -> 28, of which waited for: 14 -> 17; matrix products, arithmetic and copies ran while one was open for 23% -> 6% of each run, Pallas kernels for 0% -> 7%
where the time goes in v1:
time: 299 us; the launch traced here: 296 us
  waiting for transfers between devices  125 us (42%)
  local copies, waits for them, and re-layouts  48.8 us (16%)
  starting transfers between devices  46.1 us (15%)
  Pallas kernels  32.8 us (11%)
  other arithmetic  16.2 us (5%)
  between operations  14.4 us (5%)
  blocking collectives  12.2 us (4%)
    all_to_all x4, waiting for transfers between devices, line(): lax.all_to_all(array, 'seq', 0, 0, tiled=True, axis_index_groups=self.lines)  46.7 us
    ppermute x15, waiting for transfers between devices, exchange(): return lax.ppermute(array, 'dp', [(i, i ^ k) for i in range(count)])  37.7 us
    pallas_call x10, Pallas kernels, run_kernel(): pl.pallas_call(kernel, name=name, out_shape=out_shape, in_specs=specs, ou...  32.8 us
    all_to_all x4, starting transfers between devices, line(): lax.all_to_all(array, 'seq', 0, 0, tiled=True, axis_index_groups=self.lines)  28.2 us
    all_gather x1, waiting for transfers between devices, local(): w_both = lax.all_gather(jnp.concatenate([inner_part, outer_part], 0), 'seq')  27.4 us
    unnamed x103, local copies, waits for them, and re-layouts  25.4 us
    ppermute x15, starting transfers between devices, exchange(): return lax.ppermute(array, 'dp', [(i, i ^ k) for i in range(count)])  17.6 us
    all_to_all x1, blocking collectives, line(): lax.all_to_all(array, 'seq', 0, 0, tiled=True, axis_index_groups=self.lines)  12.2 us
  transfers between devices with their start and end apart: 28, of which 17 were waited for; matrix products, arithmetic and copies ran while one was open for 6% of the time, Pallas kernels for 7%

profile of v1, /device:TPU:8, one launch (start us, length us, event | category | flops | bytes accessed | tf_op | source)
XLA Modules:
  0.0 295.8 jit_solution(12811695117854861654)
XLA Ops:
  7.3 6.2 %concatenate.25 = bf16[6144]{0:T(1024)(128)(2,1)S(1)} concatenate(bf16[96]{0:T(256)(128)(2,1)} %param.21, bf16[96]{0:T(256)(128)(2,1)} %param.24, bf16[96]{0:T(256)(128)(2,1)} %param.26, bf16[96]{0:T(256)(128)(2,1)} %param.27, bf16[96]{0:T(256)(128)(2,1)} %param.28, bf16[96]{0:T(256)(128)(2,1)} %param.32, bf16[96]{0:T(256)(128)(2,1)} %param.33, bf16[96]{0:T(256)(128)(2,1)} %param.34, ...), dimensions={0} | concatenate | bytes 24576 | tf_op jit(solution)/shard_map/concatenate | solution.py:333
  16.0 2.3 reshape.208
  22.3 5.3 %all-to-all-start = ((bf16[4,96,576]{2,1,0:T(8,128)(2,1)}), bf16[4,96,576]{2,1,0:T(8,128)(2,1)S(1)}, u32[]{:S(2)}, u32[]{:S(2)}) async-start(bf16[4,96,576]{2,1,0:T(8,128)(2,1)} %maximum_bitcast_fusion), calls=%async_computation | async-start | bytes 983040 | tf_op jit(solution)/shard_map/all_to_all | solution.py:379
  28.5 20.0 %all-to-all-done = bf16[4,96,576]{2,1,0:T(8,128)(2,1)S(1)} async-done(((bf16[4,96,576]{2,1,0:T(8,128)(2,1)}), bf16[4,96,576]{2,1,0:T(8,128)(2,1)S(1)}, u32[]{:S(2)}, u32[]{:S(2)}) %all-to-all-start) | async-done | bytes 442400 | tf_op jit(solution)/shard_map/all_to_all | solution.py:379
  53.0 7.7 %attend.1 = (bf16[4,128,192]{2,1,0:T(8,128)(2,1)S(1)}, bf16[4,128,192]{2,1,0:T(8,128)(2,1)S(1)}, bf16[1024,192]{1,0:T(8,128)(2,1)S(1)}, bf16[1024,192]{1,0:T(8,128)(2,1)S(1)}, f32[4,128,128]{2,1,0:T(8,128)S(1)}) custom-call(s32[3]{0:T(128)S(1)} %pad_add_fusion.ids, bf16[8,136,768]{2,1,0:T(8,128)(2,1)S(1)} %bitcast.83, bf16[768,576]{1,0:T(8,128)(2,1)S(1)} %bitcast.74, ...), custom_call_target="tpu_custom_call" | custom-call | flops 1308622848 | bytes 4107788 | tf_op jit(solution)/shard_map/attend/pallas_call | solution.py:39
  63.8 7.0 %all-to-all-start.1 = ((bf16[4,128,192]{1,2,0:T(8,128)(2,1)}), bf16[4,128,192]{1,2,0:T(8,128)(2,1)S(1)}, u32[]{:S(2)}, u32[]{:S(2)}) async-start(bf16[4,128,192]{1,2,0:T(8,128)(2,1)} %copy.90), calls=%async_computation.1 | async-start | bytes 393216 | tf_op jit(solution)/shard_map/all_to_all | solution.py:379
  71.0 6.8 %all-to-all-done.1 = bf16[4,128,192]{1,2,0:T(8,128)(2,1)S(1)} async-done(((bf16[4,128,192]{1,2,0:T(8,128)(2,1)}), bf16[4,128,192]{1,2,0:T(8,128)(2,1)S(1)}, u32[]{:S(2)}, u32[]{:S(2)}) %all-to-all-start.1) | async-done | bytes 196640 | tf_op jit(solution)/shard_map/all_to_all | solution.py:379
  80.4 2.4 collective-permute-start.4
  83.9 27.4 %all-gather.13.cloned.1.call-done = bf16[1536,768]{1,0:T(8,128)(2,1)} async-done(((bf16[192,768]{1,0:T(8,128)(2,1)}), bf16[1536,768]{1,0:T(8,128)(2,1)}) %all-gather.13.cloned.1.call-update) | async-done | bytes 2359312 | tf_op jit(solution)/shard_map/all_gather | solution.py:734
  114.8 2.8 forward.1
  121.1 4.2 %collective-permute-done.5.refs_1_ = bf16[128,768]{1,0:T(8,128)(2,1)S(1)} collective-permute-done((bf16[128,768]{1,0:T(8,128)(2,1)S(1)}, bf16[128,768]{1,0:T(8,128)(2,1)S(1)}, u32[]{:S(2)}, u32[]{:S(2)}) %collective-permute-start.5) | collective-permute-done | bytes 196640 | tf_op jit(solution)/shard_map/ppermute | solution.py:461
  125.4 4.7 %collective-permute-done.6.refs_2_ = bf16[128,768]{1,0:T(8,128)(2,1)S(1)} collective-permute-done((bf16[128,768]{1,0:T(8,128)(2,1)S(1)}, bf16[128,768]{1,0:T(8,128)(2,1)S(1)}, u32[]{:S(2)}, u32[]{:S(2)}) %collective-permute-start.6) | collective-permute-done | bytes 196640 | tf_op jit(solution)/shard_map/ppermute | solution.py:461
  134.6 5.3 %collective-permute-done.10.refs_3_.refs_7_ = bf16[128,768]{1,0:T(8,128)(2,1)S(1)} collective-permute-done((bf16[128,768]{1,0:T(8,128)(2,1)S(1)}, bf16[128,768]{1,0:T(8,128)(2,1)S(1)}, u32[]{:S(2)}, u32[]{:S(2)}) %collective-permute-start.10) | collective-permute-done | bytes 196640 | tf_op jit(solution)/shard_map/ppermute | solution.py:461
  139.9 2.3 collective-permute-done.9.refs_2_.refs_6_
  142.3 3.6 %backward.1 = (f32[128,768]{1,0:T(8,128)S(1)}, bf16[128,768]{1,0:T(8,128)(2,1)S(1)}, bf16[128,768]{1,0:T(8,128)(2,1)S(1)}, bf16[128,768]{1,0:T(8,128)(2,1)S(1)},...) custom-call(bf16[128,768]{1,0:T(8,128)(2,1)S(1)} %get-tuple-element.65.refs_0_.refs_4_, ...), custom_call_target="tpu_custom_call" | custom-call | flops 1207959552 | bytes 6491136 | tf_op jit(solution)/shard_map/backward/pallas_call | solution.py:39
  149.5 4.3 %collective-permute-done.11.refs_1_ = bf16[128,768]{1,0:T(8,128)(2,1)S(1)} collective-permute-done((bf16[128,768]{1,0:T(8,128)(2,1)S(1)}, bf16[128,768]{1,0:T(8,128)(2,1)S(1)}, u32[]{:S(2)}, u32[]{:S(2)}) %collective-permute-start.11) | collective-permute-done | bytes 196640 | tf_op jit(solution)/shard_map/ppermute | solution.py:461
  153.8 4.4 %collective-permute-done.12.refs_2_ = bf16[128,768]{1,0:T(8,128)(2,1)S(1)} collective-permute-done((bf16[128,768]{1,0:T(8,128)(2,1)S(1)}, bf16[128,768]{1,0:T(8,128)(2,1)S(1)}, u32[]{:S(2)}, u32[]{:S(2)}) %collective-permute-start.12) | collective-permute-done | bytes 196640 | tf_op jit(solution)/shard_map/ppermute | solution.py:461
  168.4 2.7 weight_grad.1
  171.2 3.0 %fusion.1 = bf16[8,296,768]{2,1,0:T(8,128)(2,1)} fusion(bf16[8,1,672]{2,1,0:T(2,128)(2,1)S(1)} %reshape.230, bf16[8,96,768]{2,1,0:T(8,128)(2,1)} %bitcast.87, bf16[8,96,768]{2,1,0:T(8,128)(2,1)S(1)} %bitcast.77, bf16[8,96,768]{2,1,0:T(8,128)(2,1)S(1)} %bitcast.76), kind=kLoop, calls=%fused_computation.2 | loop fusion | flops 18186240 | bytes 7186944 | tf_op jit(solution)/shard_map/concatenate | solution.py:800
  174.4 12.2 %all_to_all.25 = bf16[4,128,192]{1,2,0:T(8,128)(2,1)S(1)} all-to-all(bf16[4,128,192]{1,2,0:T(8,128)(2,1)S(1)} %copy.94), channel_id=1, replica_groups={{0,2,4,6},{1,3,5,7},{8,10,12,14},{9,11,13,15},{16,18,20,22},{17,19,21,2..., dimensions={0} | all-to-all | bytes 393216 | tf_op jit(solution)/shard_map/all_to_all | solution.py:379
  193.6 10.9 %attend_back.1 = (bf16[4,128,192]{2,1,0:T(8,128)(2,1)S(1)}, bf16[4,128,384]{2,1,0:T(8,128)(2,1)S(1)}, bf16[4,128,384]{2,1,0:T(8,128)(2,1)S(1)}, f32[4,104,576]{2,1,0:T(8,128)S(1)}, bf16[4,104,576]{2,1,0:T(8,128)(2,1)}) custom-call(s32[3]{0:T(128)S(1)} %copy-done.19, bf16[8,136,768]{2,1,0:T(8,128)(2,1)} %bitcast.82, bf16[4,128,192]{2,1,0:T(8,128)(2,1)S(1)} %copy-done.41, ...), custom_call_target="tpu_custom_call" | custom-call | flops 1912602624 | bytes 5642252 | tf_op jit(solution)/shard_map/attend_back/pallas_call | solution.py:39
  206.0 9.1 %reduce-scatter.2.cloned.1.call-done = bf16[1,296,768]{2,1,0:T(8,128)(2,1)} async-done(((bf16[8,296,768]{2,1,0:T(8,128)(2,1)}), bf16[1,296,768]{2,1,0:T(8,128)(2,1)}) %reduce-scatter.2.cloned.1.call-update) | async-done | bytes 454672 | tf_op jit(solution)/shard_map/reduce_scatter | solution.py:809
  215.2 2.0 add_convert_fusion
  217.2 8.5 %all-to-all-start.4 = ((bf16[4,104,576]{2,1,0:T(8,128)(2,1)}), bf16[4,104,576]{2,1,0:T(8,128)(2,1)S(1)}, u32[]{:S(2)}, u32[]{:S(2)}) async-start(bf16[4,104,576]{2,1,0:T(8,128)(2,1)} %add_convert_fusion), calls=%async_computation.4 | async-start | bytes 1064960 | tf_op jit(solution)/shard_map/all_to_all | solution.py:379
  225.7 1.9 collective-permute-done.14.recv
  229.3 7.0 %all-to-all-done.4.t0 = bf16[4,104,576]{2,1,0:T(8,128)(2,1)S(1)} async-done(((bf16[4,104,576]{2,1,0:T(8,128)(2,1)}), bf16[4,104,576]{2,1,0:T(8,128)(2,1)S(1)}, u32[]{:S(2)}, u32[]{:S(2)}) %all-to-all-start.4) | async-done | bytes 479264 | tf_op jit(solution)/shard_map/all_to_all | solution.py:379
  236.3 7.4 %all-to-all-start.3 = ((bf16[4,128,768]{2,1,0:T(8,128)(2,1)}), bf16[4,128,768]{2,1,0:T(8,128)(2,1)}, u32[]{:S(2)}, u32[]{:S(2)}) async-start(bf16[4,128,768]{2,1,0:T(8,128)(2,1)} %input_grad.1), calls=%async_computation.3 | async-start | bytes 1572864 | tf_op jit(solution)/shard_map/all_to_all | solution.py:379
  247.2 12.9 %all-to-all-done.3 = bf16[4,128,768]{2,1,0:T(8,128)(2,1)} async-done(((bf16[4,128,768]{2,1,0:T(8,128)(2,1)}), bf16[4,128,768]{2,1,0:T(8,128)(2,1)}, u32[]{:S(2)}, u32[]{:S(2)}) %all-to-all-start.3) | async-done | bytes 786464 | tf_op jit(solution)/shard_map/all_to_all | solution.py:379
  262.2 2.6 collective-permute-done.18.t3
  264.8 9.8 %collective-permute-done.17.t2 = bf16[4,104,576]{2,1,0:T(8,128)(2,1)S(1)} collective-permute-done((bf16[4,104,576]{2,1,0:T(8,128)(2,1)S(1)}, bf16[4,104,576]{2,1,0:T(8,128)(2,1)S(1)}, u32[]{:S(2)}, u32[]{:S(2)}) %collective-permute-start.17) | collective-permute-done | bytes 479264 | tf_op jit(solution)/shard_map/ppermute | solution.py:461
  281.6 2.2 copy.100
  283.8 3.6 %reshape.223 = f32[96,3072]{1,0:T(8,128)} reshape(f32[96,8,4,96]{3,2,1,0:T(4,128)} %copy.100) | data formatting | bytes 2359296 | tf_op jit(solution)/shard_map/convert_element_type | solution.py:813
  (215 shorter events, 68.9 us)
Async XLA Ops:
  7.2 43.4 %all-gather.11.cloned.1.call-start = ((), (), s32[]{:S(2)}) async-start(), calls=%async_computation.9 | async-start | bytes 1880064 | tf_op jit(solution)/shard_map/all_gather | solution.py:334
  15.1 63.4 %all-gather.7.cloned.1.call-start = ((), (), s32[]{:S(2)}) async-start(), calls=%async_computation.6 | async-start | bytes 1327104 | tf_op jit(solution)/shard_map/all_gather | solution.py:733
  15.9 95.4 %all-gather.13.cloned.1.call-start = ((), (), s32[]{:S(2)}) async-start(), calls=%async_computation.10 | async-start | bytes 2654208 | tf_op jit(solution)/shard_map/all_gather | solution.py:734
  20.6 28.5 %collective-permute-start.1 = (bf16[2,96]{1,0:T(2,128)(2,1)S(1)}, bf16[2,96]{1,0:T(2,128)(2,1)S(1)}, u32[]{:S(2)}, u32[]{:S(2)}) collective-permute-start(bf16[2,96]{1,0:T(2,128)(2,1)S(1)} %pad_maximum_fusion.4), channel_id=1, source_target_pairs={{0,1},{1,0},{2,3},{3,2},{4,5},{5,4},{6,7},{7,6},{8,9},{9,8},{10,11... | collective-permute-start | bytes 1160 | tf_op jit(solution)/shard_map/ppermute | solution.py:346
  22.3 26.1 %all-to-all-start = ((bf16[4,96,576]{2,1,0:T(8,128)(2,1)}), bf16[4,96,576]{2,1,0:T(8,128)(2,1)S(1)}, u32[]{:S(2)}, u32[]{:S(2)}) async-start(bf16[4,96,576]{2,1,0:T(8,128)(2,1)} %maximum_bitcast_fusion), calls=%async_computation | async-start | bytes 983040 | tf_op jit(solution)/shard_map/all_to_all | solution.py:379
  48.5 1.9 collective-permute-start
  48.5 65.3 %copy-start.18 = (s32[3]{0:T(128)}, s32[3]{0:T(128)S(1)}, u32[]{:S(2)}) copy-start(s32[3]{0:T(128)S(1)} %pad_add_fusion.ids) | copy-start | bytes 40
  63.8 14.1 %all-to-all-start.1 = ((bf16[4,128,192]{1,2,0:T(8,128)(2,1)}), bf16[4,128,192]{1,2,0:T(8,128)(2,1)S(1)}, u32[]{:S(2)}, u32[]{:S(2)}) async-start(bf16[4,128,192]{1,2,0:T(8,128)(2,1)} %copy.90), calls=%async_computation.1 | async-start | bytes 393216 | tf_op jit(solution)/shard_map/all_to_all | solution.py:379
  70.7 144.4 %reduce-scatter.2.cloned.1.call-start = ((), (), s32[]{:S(2)}) async-start(), calls=%async_computation.7 | async-start | bytes 4091904 | tf_op jit(solution)/shard_map/reduce_scatter | solution.py:809
  80.3 33.5 %copy-start.23 = (bf16[128,768]{1,0:T(8,128)(2,1)}, bf16[128,768]{1,0:T(8,128)(2,1)S(1)}, u32[]{:S(2)}) copy-start(bf16[128,768]{1,0:T(8,128)(2,1)S(1)} %get-tuple-element.58.refs_0_) | copy-start | bytes 589828
  80.4 32.7 %collective-permute-start.4 = (bf16[128,768]{1,0:T(8,128)(2,1)S(1)}, bf16[128,768]{1,0:T(8,128)(2,1)S(1)}, u32[]{:S(2)}, u32[]{:S(2)}) collective-permute-start(bf16[128,768]{1,0:T(8,128)(2,1)S(1)} %get-tuple-element.58.refs_0_), channel_id=1, source_target_pairs={{0,24},{8,16},{16,8},{24,0},{1,25},{9,17},{17,9},{25,1},{2,26},{10... | collective-permute-start | bytes 589832 | tf_op jit(solution)/shard_map/ppermute | solution.py:461
  82.8 30.3 %collective-permute-start.3 = (bf16[128,768]{1,0:T(8,128)(2,1)S(1)}, bf16[128,768]{1,0:T(8,128)(2,1)S(1)}, u32[]{:S(2)}, u32[]{:S(2)}) collective-permute-start(bf16[128,768]{1,0:T(8,128)(2,1)S(1)} %get-tuple-element.58.refs_0_), channel_id=1, source_target_pairs={{0,16},{8,24},{16,0},{24,8},{1,17},{9,25},{17,1},{25,9},{2,18},{10... | collective-permute-start | bytes 589832 | tf_op jit(solution)/shard_map/ppermute | solution.py:461
  83.4 29.8 %collective-permute-start.2 = (bf16[128,768]{1,0:T(8,128)(2,1)S(1)}, bf16[128,768]{1,0:T(8,128)(2,1)S(1)}, u32[]{:S(2)}, u32[]{:S(2)}) collective-permute-start(bf16[128,768]{1,0:T(8,128)(2,1)S(1)} %get-tuple-element.58.refs_0_), channel_id=1, source_target_pairs={{0,8},{8,0},{16,24},{24,16},{1,9},{9,1},{17,25},{25,17},{2,10},{10... | collective-permute-start | bytes 589832 | tf_op jit(solution)/shard_map/ppermute | solution.py:461
  117.6 24.7 %copy-start.34 = (bf16[512,768]{1,0:T(8,128)(2,1)}, bf16[512,768]{1,0:T(8,128)(2,1)S(1)}, u32[]{:S(2)}) copy-start(bf16[512,768]{1,0:T(8,128)(2,1)S(1)} %get-tuple-element.89.refs_9_) | copy-start | bytes 2359300
  117.6 7.8 %collective-permute-start.5 = (bf16[128,768]{1,0:T(8,128)(2,1)S(1)}, bf16[128,768]{1,0:T(8,128)(2,1)S(1)}, u32[]{:S(2)}, u32[]{:S(2)}) collective-permute-start(bf16[128,768]{1,0:T(8,128)(2,1)S(1)} %get-tuple-element.60), channel_id=1, source_target_pairs={{0,8},{8,0},{16,24},{24,16},{1,9},{9,1},{17,25},{25,17},{2,10},{10... | collective-permute-start | bytes 589832 | tf_op jit(solution)/shard_map/ppermute | solution.py:461
  119.1 11.0 %collective-permute-start.6 = (bf16[128,768]{1,0:T(8,128)(2,1)S(1)}, bf16[128,768]{1,0:T(8,128)(2,1)S(1)}, u32[]{:S(2)}, u32[]{:S(2)}) collective-permute-start(bf16[128,768]{1,0:T(8,128)(2,1)S(1)} %get-tuple-element.61), channel_id=1, source_target_pairs={{0,16},{8,24},{16,0},{24,8},{1,17},{9,25},{17,1},{25,9},{2,18},{10... | collective-permute-start | bytes 589832 | tf_op jit(solution)/shard_map/ppermute | solution.py:461
  120.6 9.5 %collective-permute-start.7 = (bf16[128,768]{1,0:T(8,128)(2,1)S(1)}, bf16[128,768]{1,0:T(8,128)(2,1)S(1)}, u32[]{:S(2)}, u32[]{:S(2)}) collective-permute-start(bf16[128,768]{1,0:T(8,128)(2,1)S(1)} %get-tuple-element.62), channel_id=1, source_target_pairs={{0,24},{8,16},{16,8},{24,0},{1,25},{9,17},{17,9},{25,1},{2,26},{10... | collective-permute-start | bytes 589832 | tf_op jit(solution)/shard_map/ppermute | solution.py:461
  131.1 8.8 %collective-permute-start.10 = (bf16[128,768]{1,0:T(8,128)(2,1)S(1)}, bf16[128,768]{1,0:T(8,128)(2,1)S(1)}, u32[]{:S(2)}, u32[]{:S(2)}) collective-permute-start(bf16[128,768]{1,0:T(8,128)(2,1)S(1)} %get-tuple-element.65.refs_0_.refs_4_), channel_id=1, source_target_pairs={{0,24},{8,16},{16,8},{24,0},{1,25},{9,17},{17,9},{25,1},{2,26},{10... | collective-permute-start | bytes 589832 | tf_op jit(solution)/shard_map/ppermute | solution.py:461
  132.6 9.7 %collective-permute-start.9 = (bf16[128,768]{1,0:T(8,128)(2,1)S(1)}, bf16[128,768]{1,0:T(8,128)(2,1)S(1)}, u32[]{:S(2)}, u32[]{:S(2)}) collective-permute-start(bf16[128,768]{1,0:T(8,128)(2,1)S(1)} %get-tuple-element.65.refs_0_.refs_4_), channel_id=1, source_target_pairs={{0,16},{8,24},{16,0},{24,8},{1,17},{9,25},{17,1},{25,9},{2,18},{10... | collective-permute-start | bytes 589832 | tf_op jit(solution)/shard_map/ppermute | solution.py:461
  133.8 8.5 %collective-permute-start.8 = (bf16[128,768]{1,0:T(8,128)(2,1)S(1)}, bf16[128,768]{1,0:T(8,128)(2,1)S(1)}, u32[]{:S(2)}, u32[]{:S(2)}) collective-permute-start(bf16[128,768]{1,0:T(8,128)(2,1)S(1)} %get-tuple-element.65.refs_0_.refs_4_), channel_id=1, source_target_pairs={{0,8},{8,0},{16,24},{24,16},{1,9},{9,1},{17,25},{25,17},{2,10},{10... | collective-permute-start | bytes 589832 | tf_op jit(solution)/shard_map/ppermute | solution.py:461
  145.9 7.8 %collective-permute-start.11 = (bf16[128,768]{1,0:T(8,128)(2,1)S(1)}, bf16[128,768]{1,0:T(8,128)(2,1)S(1)}, u32[]{:S(2)}, u32[]{:S(2)}) collective-permute-start(bf16[128,768]{1,0:T(8,128)(2,1)S(1)} %get-tuple-element.68), channel_id=1, source_target_pairs={{0,8},{8,0},{16,24},{24,16},{1,9},{9,1},{17,25},{25,17},{2,10},{10... | collective-permute-start | bytes 589832 | tf_op jit(solution)/shard_map/ppermute | solution.py:461
  147.4 10.8 %collective-permute-start.12 = (bf16[128,768]{1,0:T(8,128)(2,1)S(1)}, bf16[128,768]{1,0:T(8,128)(2,1)S(1)}, u32[]{:S(2)}, u32[]{:S(2)}) collective-permute-start(bf16[128,768]{1,0:T(8,128)(2,1)S(1)} %get-tuple-element.69), channel_id=1, source_target_pairs={{0,16},{8,24},{16,0},{24,8},{1,17},{9,25},{17,1},{25,9},{2,18},{10... | collective-permute-start | bytes 589832 | tf_op jit(solution)/shard_map/ppermute | solution.py:461
  148.0 10.2 %collective-permute-start.13 = (bf16[128,768]{1,0:T(8,128)(2,1)S(1)}, bf16[128,768]{1,0:T(8,128)(2,1)S(1)}, u32[]{:S(2)}, u32[]{:S(2)}) collective-permute-start(bf16[128,768]{1,0:T(8,128)(2,1)S(1)} %get-tuple-element.70), channel_id=1, source_target_pairs={{0,24},{8,16},{16,8},{24,0},{1,25},{9,17},{17,9},{25,1},{2,26},{10... | collective-permute-start | bytes 589832 | tf_op jit(solution)/shard_map/ppermute | solution.py:461
  174.2 102.1 %all-gather.9.cloned.1.call-start = ((), (), s32[]{:S(2)}) async-start(), calls=%async_computation.8 | async-start | bytes 2273280 | tf_op jit(solution)/shard_map/all_gather | solution.py:810
  206.0 9.1 %collective-permute-start.15 = (bf16[4,104,576]{2,1,0:T(8,128)(2,1)}, bf16[4,104,576]{2,1,0:T(8,128)(2,1)}, u32[]{:S(2)}, u32[]{:S(2)}) collective-permute-start(bf16[4,104,576]{2,1,0:T(8,128)(2,1)} %get-tuple-element.83), channel_id=1, source_target_pairs={{0,1},{1,0},{2,3},{3,2},{4,5},{5,4},{6,7},{7,6},{8,9},{9,8},{10,11... | collective-permute-start | bytes 1437704 | tf_op jit(solution)/shard_map/ppermute | solution.py:432
  217.2 19.1 %all-to-all-start.4 = ((bf16[4,104,576]{2,1,0:T(8,128)(2,1)}), bf16[4,104,576]{2,1,0:T(8,128)(2,1)S(1)}, u32[]{:S(2)}, u32[]{:S(2)}) async-start(bf16[4,104,576]{2,1,0:T(8,128)(2,1)} %add_convert_fusion), calls=%async_computation.4 | async-start | bytes 1064960 | tf_op jit(solution)/shard_map/all_to_all | solution.py:379
  225.7 1.9 collective-permute-start.14
  229.3 32.1 %copy-start.5 = (f32[128,768]{1,0:T(8,128)S(1)}, f32[128,768]{1,0:T(8,128)}, u32[]{:S(2)}) copy-start(f32[128,768]{1,0:T(8,128)} %copy-done.4) | copy-start | bytes 1179652
  236.3 23.8 %all-to-all-start.3 = ((bf16[4,128,768]{2,1,0:T(8,128)(2,1)}), bf16[4,128,768]{2,1,0:T(8,128)(2,1)}, u32[]{:S(2)}, u32[]{:S(2)}) async-start(bf16[4,128,768]{2,1,0:T(8,128)(2,1)} %input_grad.1), calls=%async_computation.3 | async-start | bytes 1572864 | tf_op jit(solution)/shard_map/all_to_all | solution.py:379
  243.7 21.1 %collective-permute-start.18 = (bf16[4,104,576]{2,1,0:T(8,128)(2,1)S(1)}, bf16[4,104,576]{2,1,0:T(8,128)(2,1)S(1)}, u32[]{:S(2)}, u32[]{:S(2)}) collective-permute-start(bf16[4,104,576]{2,1,0:T(8,128)(2,1)S(1)} %all-to-all-done.4.t0), channel_id=1, source_target_pairs={{0,24},{8,16},{16,8},{24,0},{1,25},{9,17},{17,9},{25,1},{2,26},{10... | collective-permute-start | bytes 1437704 | tf_op jit(solution)/shard_map/ppermute | solution.py:461
  245.4 29.2 %collective-permute-start.17 = (bf16[4,104,576]{2,1,0:T(8,128)(2,1)S(1)}, bf16[4,104,576]{2,1,0:T(8,128)(2,1)S(1)}, u32[]{:S(2)}, u32[]{:S(2)}) collective-permute-start(bf16[4,104,576]{2,1,0:T(8,128)(2,1)S(1)} %all-to-all-done.4.t0), channel_id=1, source_target_pairs={{0,16},{8,24},{16,0},{24,8},{1,17},{9,25},{17,1},{25,9},{2,18},{10... | collective-permute-start | bytes 1437704 | tf_op jit(solution)/shard_map/ppermute | solution.py:461
  246.0 28.6 %collective-permute-start.16 = (bf16[4,104,576]{2,1,0:T(8,128)(2,1)S(1)}, bf16[4,104,576]{2,1,0:T(8,128)(2,1)S(1)}, u32[]{:S(2)}, u32[]{:S(2)}) collective-permute-start(bf16[4,104,576]{2,1,0:T(8,128)(2,1)S(1)} %all-to-all-done.4.t0), channel_id=1, source_target_pairs={{0,8},{8,0},{16,24},{24,16},{1,9},{9,1},{17,25},{25,17},{2,10},{10... | collective-permute-start | bytes 1437704 | tf_op jit(solution)/shard_map/ppermute | solution.py:461
  (46 other events, 170.0 us)
Sparse Core Ops, SparseCore 0:
  15.2 35.0 all-gather.10
  51.9 26.5 all-gather.6
  80.7 30.5 all-gather.12
  174.3 40.7 reduce-scatter.1
  216.8 51.8 all-gather.8

commit v2 on v1

v2 whole, which is shorter than its diff:
```python
import functools

import jax
import jax.numpy as jnp
from jax import lax
from jax.experimental import pallas as pl
from jax.experimental.pallas import tpu as pltpu
from jax.sharding import PartitionSpec as P

HEADS = 12
BLOCK = 64
EPSILON = 1e-12
MASKED = -1000000000.0
GELU_A = 0.7978845608028654
GELU_B = 0.044715
VMEM_BYTES = 6 << 20
bf16 = jnp.bfloat16
f32 = jnp.float32


def matmul(left, right):
    return jnp.dot(left, right, preferred_element_type=f32)


def left_product(left, right):
    return lax.dot_general(left, right, (((0,), (0,)), ((), ())), preferred_element_type=f32)


def right_product(left, right):
    return lax.dot_general(left, right, (((1,), (1,)), ((), ())), preferred_element_type=f32)


def run_kernel(kernel, name, outs, args, scratch=(), scalars=0, flops=0, powers=0, grant=VMEM_BYTES):
    specs = [pl.BlockSpec(memory_space=pltpu.SMEM)] * scalars
    specs += [pl.BlockSpec(memory_space=pltpu.VMEM)] * (len(args) - scalars)
    out_shape = tuple(jax.ShapeDtypeStruct(shape, dtype) for shape, dtype in outs)
    moved = sum(a.size * a.dtype.itemsize for a in args)
    moved += sum(o.size * o.dtype.itemsize for o in out_shape)
    return pl.pallas_call(
        kernel,
        name=name,
        out_shape=out_shape,
        in_specs=specs,
        out_specs=tuple(pl.BlockSpec(memory_space=pltpu.VMEM) for _ in outs),
        scratch_shapes=list(scratch),
        compiler_params=pltpu.CompilerParams(vmem_limit_bytes=grant),
        cost_estimate=pl.CostEstimate(flops=flops, bytes_accessed=moved, transcendentals=powers),
    )(*args)


def normalize(values):
    center = values - jnp.mean(values, -1, keepdims=True)
    spread = jnp.mean(center * center, -1, keepdims=True)
    inverse = lax.rsqrt(spread + EPSILON)
    return center * inverse, inverse


def norm_back(grad, normed, inverse, gain):
    scaled = grad * gain
    return inverse * (
        scaled
        - jnp.mean(scaled, -1, keepdims=True)
        - normed * jnp.mean(scaled * normed, -1, keepdims=True)
    )


def bias_rows(be_ref, bn, same, head, block, blocks, block_len):
    width = same.shape[1]
    rows = [
        jnp.broadcast_to(be_ref[head * blocks + block + i : head * blocks + block + i + 1, :], (block_len, width))
        for i in range(same.shape[0] // block_len)
    ]
    return jnp.where(same, jnp.concatenate(rows, 0), bn)


def bias_rows(lines, bn, same):
    count, width = lines.shape
    length = same.shape[0] // count
    rows = [jnp.broadcast_to(lines[i : i + 1, :], (length, width)) for i in range(count)]
    return jnp.where(same, jnp.concatenate(rows, 0), bn)


def assemble_kernel(ids, mine, mine_next, other, other_next, out, *, bit, relative):
    core = ids[0]
    half = lax.rem(ids[2] // bit, 2)
    for k in range(mine.shape[0]):
        chip = ids[1] ^ k if relative else k
        out[2 * chip + core, half] = mine[k]
        out[2 * chip + core, 1 - half] = mine_next[k]
        out[2 * chip + 1 - core, half] = other[k]
        out[2 * chip + 1 - core, 1 - half] = other_next[k]


def attend_kernel(ids, hid, w, qb, vb, be, bn, sk, sq, *refs):
    outs = refs[:-5]
    qo, ko, vo, lse, qs = refs[-5:]
    pieces, piece_len, width = qs.shape
    chips = pieces // 2
    core = ids[0]
    size = 64
    heads = width // size
    model = hid.shape[2]
    tokens = hid[...].reshape(pieces * piece_len, model)
    product = matmul(tokens, w[...])
    query = (product[:, :width] + qb[...]).astype(bf16) * bf16(size**-0.5)
    qs[...] = query.reshape(pieces, piece_len, width)
    ko[...] = product[:, width : 2 * width].astype(bf16)
    vo[...] = (product[:, 2 * width :] + vb[...]).astype(bf16)
    lane = lax.broadcasted_iota(jnp.int32, (piece_len, 128), 1)
    for k in range(chips):
        chip = ids[1] ^ k
        qo[k] = qs[2 * chip + core]
        same = sq[chip] == sk[...]
        logs = jnp.zeros((piece_len, 128), f32)
        parts = []
        for head in range(heads):
            cols = slice(head * size, (head + 1) * size)
            scores = right_product(qo[k, :, cols], ko[:, cols])
            scores = scores + bias_rows(be[head * chips + chip], bn[...], same)
            top = jnp.max(scores, -1, keepdims=True)
            powers = jnp.exp(scores - top)
            total = jnp.sum(powers, -1, keepdims=True)
            probs = (powers * (1.0 / total)).astype(bf16)
            parts.append(matmul(probs, vo[:, cols]))
            logs = jnp.where(lane == head, top + jnp.log(total), logs)
        outs[k][...] = jnp.concatenate(parts, 1).T.astype(bf16)
        lse[k] = logs


def attend_back_kernel(ids, q, k, v, lse, be, bn, sk, sq, *refs):
    chips, piece_len, width = q.shape
    ga = refs[:chips]
    dq, own, mine, other, ds_all, p_all, dkv = refs[chips:]
    pieces = 2 * chips
    core = ids[0]
    size = 64
    heads = width // size
    dks = []
    dvs = []
    dqs = [[None] * heads for _ in range(chips)]
    gas = [g[...].astype(f32).T.astype(bf16) for g in ga]
    for head in range(heads):
        cols = slice(head * size, (head + 1) * size)
        key = k[:, cols]
        value = v[:, cols]
        for i in range(chips):
            chip = ids[1] ^ i
            rows = slice(i * piece_len, (i + 1) * piece_len)
            same = sq[chip] == sk[...]
            scores = right_product(q[i, :, cols], key)
            scores = scores + bias_rows(be[head * chips + chip], bn[...], same)
            probs = jnp.exp(scores - lse[i, :, head : head + 1])
            grad = right_product(gas[i][:, cols], value)
            weighted = jnp.sum(probs * grad, -1, keepdims=True)
            ds = (probs * (grad - weighted)).astype(bf16)
            ds_all[rows, :] = ds
            p_all[rows, :] = probs.astype(bf16)
            dqs[i][head] = (matmul(ds, key) * (size**-0.5)).astype(bf16)
        queries = q[:, :, cols].reshape(chips * piece_len, size)
        grads = jnp.concatenate([g[:, cols] for g in gas], 0)
        dks.append(left_product(ds_all[...], queries).astype(bf16))
        dvs.append(left_product(p_all[...], grads).astype(bf16))
    for i in range(chips):
        dq[i] = jnp.concatenate(dqs[i], 1)
    joined = jnp.concatenate(dks + dvs, 1)
    own[...] = joined
    dkv[...] = joined.reshape(pieces, piece_len, 2 * width)
    for i in range(chips):
        chip = ids[1] ^ i
        mine[i] = dkv[2 * chip + core]
        other[i] = dkv[2 * chip + 1 - core]


def attend_weight_kernel(ids, hid, dq, dkv, mine, other, sums, dws):
    pieces, piece_len, model = hid.shape
    chips, _, width = dq.shape
    core = ids[0]
    tokens = hid[...].reshape(pieces * piece_len, model)
    owned = jnp.concatenate([hid[2 * (ids[1] ^ k) + core] for k in range(chips)], 0)
    grad_q = dq[...].reshape(chips * piece_len, width)
    grad_kv = dkv[...]
    weights = jnp.concatenate([left_product(owned, grad_q), left_product(tokens, grad_kv)], 1)
    quarters, _, rows, _ = mine.shape
    dws[...] = weights.reshape(dws.shape)
    for k in range(chips):
        chip = ids[1] ^ k
        for j in range(quarters):
            mine[j, k] = dws[2 * chip + core, ids[2] ^ j]
            other[j, k] = dws[2 * chip + 1 - core, ids[2] ^ j].astype(bf16)
    total = jnp.concatenate(
        [
            jnp.sum(grad_q.astype(f32), 0, keepdims=True),
            jnp.sum(grad_kv.astype(f32), 0, keepdims=True),
        ],
        1,
    )
    sums[...] = jnp.broadcast_to(total, sums.shape)


def input_grad_kernel(dq, mine, recv, w, *outs):
    chips, piece_len, width = dq.shape
    dkv = (mine[...].astype(f32) + recv[...].astype(f32)).astype(bf16)
    grads = jnp.concatenate([dq[...], dkv], 2).reshape(chips * piece_len, 3 * width)
    total = right_product(grads, w[...])
    for k, out in enumerate(outs):
        out[...] = total[k * piece_len : (k + 1) * piece_len].astype(out.dtype)


def add_split_kernel(left, right, *outs):
    for k, out in enumerate(outs):
        out[...] = (left[k].astype(f32) + right[k].astype(f32)).astype(out.dtype)


def sum_split_kernel(*refs, parts):
    total = refs[0][...].astype(f32)
    for r in refs[1:parts]:
        total = total + r[...].astype(f32)
    outs = refs[parts:]
    if len(outs) == 1:
        outs[0][...] = total.astype(outs[0].dtype)
    else:
        for k, out in enumerate(outs):
            out[...] = total[k].astype(out.dtype)


def stack_kernel(*refs):
    for k, r in enumerate(refs[:-1]):
        refs[-1][k] = r[...]


def project_kernel(ids, wo, hid, vec, *refs):
    att = refs[:-3]
    low, normed, inverse = refs[-3:]
    branch = vec[2:3, :] + jnp.zeros(hid.shape, f32)
    for k, r in enumerate(att):
        branch = branch + left_product(r[...], wo[ids[1] ^ k])
    n1, r1 = normalize(hid[...].astype(f32) + branch)
    low[...] = (n1 * vec[3:4, :] + vec[4:5, :]).astype(bf16)
    normed[...] = n1
    inverse[...] = jnp.broadcast_to(r1, inverse.shape)


def gelu_parts(v):
    return jnp.tanh(GELU_A * (v + GELU_B * (v * v * v)))


def two_weights(both):
    pieces, rows, model = both.shape
    half = rows // 2
    first = both[:, :half, :].reshape(pieces * half, model)
    return first, both[:, half:, :].reshape(pieces * half, model)


def forward_kernel(ids, *refs):
    parts = (len(refs) - 4) // 2
    x = refs[:parts]
    both, vec = refs[parts : parts + 2]
    outs = refs[parts + 2 : 2 * parts + 2]
    inner_ref, act_ref = refs[2 * parts + 2 :]
    rows = x[0].shape[0]
    weight1, weight2 = two_weights(both)
    tokens = jnp.concatenate([r[...] for r in x], 0)
    inner = matmul(tokens, weight1) + vec[pl.ds(8 + ids[2], 1), :]
    act = (0.5 * inner * (1.0 + gelu_parts(inner))).astype(bf16)
    inner_ref[...] = inner
    act_ref[...] = act
    mixed = matmul(act, weight2)
    for i in range(parts):
        outs[i][...] = mixed[i * rows : (i + 1) * rows].astype(outs[i].dtype)


def middle_kernel(*refs):
    recv = refs[:-7]
    normed, cot, vec, out, low, mix, sums = refs[-7:]
    first = normed[...] * vec[3:4, :] + vec[4:5, :]
    mixed = vec[5:6, :]
    for r in recv:
        mixed = mixed + r[...].astype(f32)
    n2, r2 = normalize(first + mixed)
    gain = vec[6:7, :]
    out[...] = (n2 * gain + vec[7:8, :]).astype(bf16)
    g = cot[...].astype(f32)
    grad = norm_back(g, n2, r2, gain)
    rounded = grad.astype(bf16)
    mix[...] = grad
    low[...] = rounded
    sums[0:1, :] = jnp.sum(g * n2, 0, keepdims=True)
    sums[1:2, :] = jnp.sum(g, 0, keepdims=True)
    sums[2:3, :] = jnp.sum(rounded.astype(f32), 0, keepdims=True)
    sums[3:, :] = jnp.zeros((5, sums.shape[1]), f32)


def backward_kernel(*refs):
    parts = (len(refs) - 4) // 2
    grads = refs[:parts]
    both, inner_ref = refs[parts : parts + 2]
    outs = refs[parts + 2 : 2 * parts + 2]
    gi_ref, sum_ref = refs[2 * parts + 2 :]
    rows = grads[0].shape[0]
    weight1, weight2 = two_weights(both)
    gm = jnp.concatenate([r[...] for r in grads], 0)
    grad_act = right_product(gm, weight2)
    v = inner_ref[...]
    t = gelu_parts(v)
    slope = 0.5 * (1.0 + t) + 0.5 * v * (1.0 - t * t) * (GELU_A * (1.0 + 3.0 * GELU_B * (v * v)))
    gi = (grad_act * slope).astype(bf16)
    gi_ref[...] = gi
    sum_ref[...] = jnp.sum(gi.astype(f32), 0, keepdims=True)
    first = right_product(gi, weight1)
    for i in range(parts):
        outs[i][...] = first[i * rows : (i + 1) * rows].astype(outs[i].dtype)


def residual_kernel(ids, mix, normed, inverse, vec, wo, *refs, parts):
    first = mix[...]
    for r in refs[:parts]:
        first = first + r[...].astype(f32)
    res, low, sums = refs[parts : parts + 3]
    n1 = normed[...]
    grad = norm_back(first, n1, inverse[:, 0:1], vec[3:4, :])
    rounded = grad.astype(bf16)
    for k, back in enumerate(refs[parts + 3 :]):
        back[...] = right_product(wo[ids[1] ^ k], rounded).astype(bf16)
    res[...] = grad
    low[...] = rounded
    sums[0:1, :] = jnp.sum(first * n1, 0, keepdims=True)
    sums[1:2, :] = jnp.sum(first, 0, keepdims=True)
    sums[2:3, :] = jnp.sum(rounded.astype(f32), 0, keepdims=True)
    sums[3:, :] = jnp.zeros((5, sums.shape[1]), f32)


def put_vectors(out, piece, row, vectors, rows):
    parts = [v[:, piece * rows : (piece + 1) * rows] for v in vectors]
    fill = out.shape[2] - rows * len(parts)
    line = jnp.concatenate(parts + [jnp.zeros((1, fill), f32)], 1)
    out[piece, row : row + 8, :] = jnp.broadcast_to(line, (8, out.shape[2])).astype(bf16)


def inner_outer_kernel(*refs):
    parts = (len(refs) - 5) // 2
    x = refs[:parts]
    gm = refs[parts : 2 * parts]
    gi, act, sums, sum_inner, out = refs[2 * parts :]
    pieces, tall, model = out.shape
    rows = (tall - 8) // 2
    tokens = jnp.concatenate([r[...] for r in x], 0)
    grads = jnp.concatenate([r[...] for r in gm], 0)
    out[:, :rows, :] = left_product(tokens, gi[...]).astype(bf16).reshape(pieces, rows, model)
    out[:, rows : 2 * rows, :] = (
        left_product(act[...], grads).astype(bf16).reshape(pieces, rows, model)
    )
    vectors = [sums[i : i + 1, :] for i in range(3)] + [sum_inner[...]]
    for piece in range(pieces):
        put_vectors(out, piece, 2 * rows, vectors, rows)


def output_grad_kernel(ids, gb, sums, *refs):
    mine, other, dws = refs[-3:]
    core = ids[0]
    chips, tall, model = mine.shape
    rows = tall - 8
    grad = gb[...]
    vectors = [sums[i : i + 1, :] for i in range(3)]
    for piece in range(2 * chips):
        put_vectors(dws, piece, rows, vectors, rows)
    for k in range(chips):
        chip = ids[1] ^ k
        part = matmul(refs[k][...], grad).astype(bf16)
        for i in range(2):
            dws[2 * chip + i, :rows, :] = part[i * rows : (i + 1) * rows]
        mine[k] = dws[2 * chip + core]
        other[k] = dws[2 * chip + 1 - core]


def ordered(ids, refs, scratch):
    for k, r in enumerate(refs):
        scratch[ids[2] ^ k] = r[...]


def finish_inner_kernel(ids, *refs):
    parts = len(refs) - 4
    inner, outer, vectors, scratch = refs[parts:]
    ordered(ids, refs[:parts], scratch)
    rows = inner.shape[0]
    units = outer.shape[0] // parts
    pieces = scratch.shape[2] // units
    for piece in range(pieces):
        inner[:, piece * parts * units : (piece + 1) * parts * units] = jnp.concatenate(
            [
                scratch[g, :rows, piece * units : (piece + 1) * units].astype(f32)
                for g in range(parts)
            ],
            1,
        )
    total = jnp.zeros((1, scratch.shape[2]), f32)
    for g in range(parts):
        outer[g * units : (g + 1) * units, :] = scratch[g, rows : rows + units, :].astype(f32)
        line = scratch[g, rows + units : rows + units + 8, :].astype(f32)[0:1]
        vectors[g : g + 1, :] = line
        total = total + line
    vectors[parts : parts + 1, :] = total


def finish_output_kernel(p0, p1, p2, p3, out, vectors):
    rows = out.shape[0]
    total = p0[...].astype(f32)
    for r in (p1, p2, p3):
        total = total + r[...].astype(f32)
    out[...] = total[:rows]
    vectors[...] = total[rows:]


def finish_kernel(ids, *refs):
    parts = len(refs) - 4
    gq, gk, gv, scratch = refs[parts:]
    quarters, chips, rows, wide = scratch.shape
    for j, r in enumerate(refs[:parts]):
        for k in range(chips):
            scratch[ids[2] ^ j, ids[1] ^ k] = r[k]
    width = wide // 3
    for part in range(quarters):
        block = [scratch[part, chip].astype(f32) for chip in range(chips)]
        for i, out in enumerate((gq, gk, gv)):
            out[part * rows : (part + 1) * rows, :] = jnp.concatenate(
                [b[:, i * width : (i + 1) * width] for b in block], 1
            )


def log_counts(count):
    return jnp.where(count > 0, jnp.log(jnp.maximum(count, 1).astype(f32)), MASKED)


def exchange(array, k):
    count = lax.axis_size("dp")
    return lax.ppermute(array, "dp", [(i, i ^ k) for i in range(count)])


def exchange_all(array):
    return [array] + [exchange(array, k) for k in range(1, lax.axis_size("dp"))]


def exchange_parts(parts):
    return [parts[0]] + [exchange(parts[k], k) for k in range(1, lax.axis_size("dp"))]


def swap_cores(array):
    count = lax.axis_size("seq")
    return lax.ppermute(array, "seq", [(i, i ^ 1) for i in range(count)])


def line_exchange(array, k):
    count = lax.axis_size("seq")
    return lax.ppermute(array, "seq", [(i, i ^ (2 * k)) for i in range(count)])


def line_parts(parts):
    return [parts[0]] + [line_exchange(parts[k], k) for k in range(1, len(parts))]


def tied(value, *others):
    return lax.optimization_barrier((value,) + others)[0]


def add_split(left, right, outs):
    return run_kernel(add_split_kernel, "add", outs, (left, right))


def sum_split(arrays, outs):
    return run_kernel(
        functools.partial(sum_split_kernel, parts=len(arrays)), "sum", outs, tuple(arrays)
    )


def along_line(array):
    count = lax.axis_size("seq")
    lines = [[2 * i + c for i in range(count // 2)] for c in range(2)]
    return lax.all_to_all(array, "seq", 0, 0, tiled=True, axis_index_groups=lines)


def device_ids():
    position = lax.axis_index("seq")
    return jnp.stack([position % 2, position // 2, lax.axis_index("dp")]).astype(jnp.int32)


def assemble(ids, mine, bit, relative):
    mine_next = exchange(mine, bit)
    other = swap_cores(mine)
    other_next = swap_cores(mine_next)
    chips, half, width = mine.shape
    (out,) = run_kernel(
        functools.partial(assemble_kernel, bit=bit, relative=relative),
        "assemble",
        [((2 * chips, 2, half, width), bf16)],
        (ids, mine, mine_next, other, other_next),
        scalars=1,
    )
    return out.reshape(4 * chips * half, width)


class HeadAttention:
    def __init__(self, hidden, weights, biases, segments, random_blocks, output_weight, vec_local):
        self.splits = splits = lax.axis_size("seq")
        self.chips = chips = splits // 2
        self.position = position = lax.axis_index("seq")
        core = position % 2
        chip = position // 2
        group = lax.axis_index("dp")
        self.ids = device_ids()
        piece_len, model = hidden.shape
        rows = model // splits
        width = model // chips
        heads = HEADS // chips
        self.packed = lax.all_gather(hidden, "seq")
        half = rows // 2
        start = group % 2 * half
        split = jnp.concatenate(
            [
                lax.dynamic_slice_in_dim(w, start, half, 0).reshape(half, chips, width)
                for w in weights
            ],
            2,
        )
        self.weight = assemble(self.ids, along_line(split.transpose(1, 0, 2)), 1, False)
        out_half = lax.dynamic_slice_in_dim(output_weight, group // 2 % 2 * half, half, 0)
        self.out_parts = [out_half] + [line_exchange(out_half, k) for k in range(1, chips)]
        tall = -(-vec_local.shape[0] // 16) * 16
        vec = jnp.pad(vec_local, ((0, tall - vec_local.shape[0]), (0, 128 - rows)))
        vec = lax.all_to_all(
            jnp.broadcast_to(vec[None], (splits,) + vec.shape), "seq", 0, 0, tiled=True
        )
        self.vec = (
            vec[:, : vec_local.shape[0], :rows].transpose(1, 0, 2).reshape(-1, model).astype(f32)
        )
        pair = jnp.stack(biases, 0)
        pair_other = swap_cores(pair)
        bias = jnp.where(
            core == 0,
            jnp.concatenate([pair, pair_other], 1),
            jnp.concatenate([pair_other, pair], 1),
        ).astype(f32)
        self.bias_q, self.bias_v = bias[0:1], bias[1:2]
        block_count = segments.shape[1] // BLOCK
        per_piece = piece_len // BLOCK
        own = random_blocks[0].reshape(chips, 2, per_piece, HEADS, -1)
        own = lax.dynamic_index_in_dim(own, core, 1, keepdims=False)
        own = lax.dynamic_slice_in_dim(own, chip * heads, heads, 2)
        own = own.reshape(chips * per_piece, heads, -1).transpose(1, 0, 2)
        block = jnp.arange(block_count, dtype=jnp.int32)
        mine = (
            (jnp.arange(chips, dtype=jnp.int32)[:, None] * 2 + core) * per_piece
            + jnp.arange(per_piece, dtype=jnp.int32)[None, :]
        ).reshape(-1)
        ends = ((block == 0) | (block == block_count - 1)).astype(jnp.int32)
        near = (jnp.abs(block[None, :] - mine[:, None]) <= 1).astype(jnp.int32)
        listed = jnp.sum((own[..., None] == block).astype(jnp.int32), 2)
        count = listed + near[None] + ends
        self.same_bias = jnp.repeat(log_counts(count), BLOCK, axis=2).reshape(
            heads * chips, per_piece, -1
        )
        self.other_bias = jnp.repeat(
            jnp.where(ends > 0, 0.0, MASKED).astype(f32)[None], BLOCK, axis=1
        )
        self.key_seg = segments
        self.query_seg = lax.dynamic_index_in_dim(
            segments.reshape(chips, 2, piece_len), core, 1, keepdims=False
        ).reshape(chips, piece_len, 1)
        self.piece_len, self.width, self.model = piece_len, width, model

    def masks(self):
        return (self.same_bias, self.other_bias, self.key_seg, self.query_seg)

    def forward(self):
        chips, piece_len, width, model = self.chips, self.piece_len, self.width, self.model
        tokens = self.splits * piece_len
        one = (chips, piece_len, width)
        *att, self.q, self.k, self.v, self.lse = run_kernel(
            attend_kernel,
            "attend",
            [((width, piece_len), bf16)] * chips
            + [
                (one, bf16),
                ((tokens, width), bf16),
                ((tokens, width), bf16),
                ((chips, piece_len, 128), f32),
            ],
            (self.ids, self.packed, self.weight, self.bias_q, self.bias_v) + self.masks(),
            scratch=[pltpu.VMEM((self.splits, piece_len, width), bf16)],
            scalars=1,
            flops=6 * tokens * model * width + 2 * tokens * tokens * width,
            powers=tokens * tokens * 3 // 2,
        )
        parts = lax.optimization_barrier((tuple(self.out_parts), att[0]))[0]
        rows = parts[0].shape
        (mine,) = run_kernel(stack_kernel, "stack", [((chips,) + rows, bf16)], parts)
        weight = assemble(self.ids, mine, 2, True)
        self.output_weight = weight.reshape(chips, width, model)
        return line_parts(att)

    def output_grad(self, attended, grad_branch, sums):
        chips, model = self.chips, self.model
        rows = model // self.splits
        one = (rows + 8, model)
        mine, other = run_kernel(
            output_grad_kernel,
            "output_grad",
            [((chips,) + one, bf16)] * 2,
            (self.ids, grad_branch, sums, *attended),
            scratch=[pltpu.VMEM((self.splits,) + one, bf16)],
            scalars=1,
            flops=2 * self.piece_len * model * model,
        )
        parts = add_split(mine, swap_cores(other), [(one, bf16)] * chips)
        (share,) = sum_split(line_parts(parts), [(one, bf16)])
        out, vectors = run_kernel(
            finish_output_kernel,
            "finish_output",
            [((rows, model), f32), ((8, model), f32)],
            tuple(exchange_all(share)),
        )
        return out, vectors[0]

    def backward(self, grads, grad_res, share):
        chips, piece_len, width = self.chips, self.piece_len, self.width
        splits, model = self.splits, self.model
        groups = lax.axis_size("dp")
        tokens = splits * piece_len
        rows = model // splits
        one = (chips, piece_len, width)
        two = (chips, piece_len, 2 * width)
        dq, dkv, mine, other = run_kernel(
            attend_back_kernel,
            "attend_back",
            [(one, bf16), ((tokens, 2 * width), bf16), (two, bf16), (two, bf16)],
            (self.ids, self.q, self.k, self.v, self.lse) + self.masks() + tuple(grads),
            scratch=[
                pltpu.VMEM((chips * piece_len, tokens), bf16),
                pltpu.VMEM((chips * piece_len, tokens), bf16),
                pltpu.VMEM((splits, piece_len, 2 * width), bf16),
            ],
            scalars=1,
            flops=5 * tokens * tokens * width,
            powers=tokens * tokens * 3 // 2,
            grant=10 << 20,
        )
        recv = swap_cores(other)
        quarter = (rows // groups, 3 * width)
        part = (groups, chips) + quarter
        dw_mine, dw_other, sums = run_kernel(
            attend_weight_kernel,
            "attend_weight",
            [(part, f32), (part, bf16), ((8, 3 * width), f32)],
            (self.ids, self.packed, dq, dkv),
            scratch=[pltpu.VMEM((splits, groups) + quarter, f32)],
            scalars=1,
            flops=6 * tokens * model * width,
        )
        dws = add_split(dw_mine, swap_cores(dw_other), [(part[1:], bf16)] * groups)
        dws = exchange_parts(dws)
        full = (piece_len, model)
        partial = run_kernel(
            input_grad_kernel,
            "input_grad",
            [(full, f32)] + [(full, bf16)] * (chips - 1),
            (dq, mine, recv, self.weight),
            flops=3 * tokens * model * width,
        )
        partial = line_parts(partial)
        dws = sum_split(dws, [(quarter, bf16)] * chips)
        share = tied(share, dws[0])
        dws = line_parts(dws)
        shares = exchange_all(share)
        (dw,) = run_kernel(stack_kernel, "stack", [(part[1:], bf16)], tuple(dws))
        gq, gk, gv = run_kernel(
            finish_kernel,
            "finish",
            [((rows, model), f32)] * 3,
            (self.ids, *exchange_all(dw)),
            scratch=[pltpu.VMEM(part, bf16)],
            scalars=1,
        )
        (input_grad,) = sum_split([grad_res] + partial, [(full, f32)])
        sums = sum(exchange_all(sums + swap_cores(sums)))
        core = self.position % 2
        bias_q = lax.dynamic_slice_in_dim(sums[0], core * rows, rows)
        bias_v = lax.dynamic_slice_in_dim(sums[0], 2 * width + core * rows, rows)
        return input_grad, gq, bias_q, gk, gv, bias_v, shares


def one_hot(index, count):
    return (index[..., None] == jnp.arange(count, dtype=jnp.int32)).astype(bf16)


def with_halo(block, axis, dim, width):
    count = lax.axis_size(axis)
    forward = [(i, i + 1) for i in range(count - 1)]
    backward = [(target, source) for source, target in forward]
    low = lax.ppermute(
        lax.slice_in_dim(block, block.shape[dim] - width, None, axis=dim), axis, forward
    )
    high = lax.ppermute(lax.slice_in_dim(block, 0, width, axis=dim), axis, backward)
    return jnp.concatenate([low, block, high], axis=dim)


def broadcast(block, axis, owner):
    block = jnp.where(lax.axis_index(axis) == owner, block, jnp.zeros_like(block))
    return lax.psum(block, axis)


class TokenAttention:
    def __init__(self, hidden, weights, biases, segments, random_blocks, output_weight, vec_local):
        self.splits = splits = lax.axis_size("seq")
        self.position = position = lax.axis_index("seq")
        self.ids = device_ids() * jnp.array([1, 0, 1], jnp.int32)
        self.hidden = hidden
        self.segments = segments
        self.random_blocks = random_blocks
        self.weights = [lax.all_gather(w, "seq", axis=0, tiled=True) for w in weights]
        self.output_weight = lax.all_gather(output_weight, "seq", axis=0, tiled=True)[None]
        vec = lax.all_gather(vec_local, "seq")
        self.vec = vec.transpose(1, 0, 2).reshape(vec_local.shape[0], -1).astype(f32)

    def forward(self):
        hidden, segments = self.hidden, self.segments
        splits, position = self.splits, self.position
        seq_count = segments.shape[0]
        row_count, model = hidden.shape
        piece_len = row_count // seq_count
        size = model // HEADS
        per = piece_len // BLOCK
        slots = self.random_blocks.shape[3]
        reqs = seq_count * per * HEADS * slots
        cap = max(2, 3 * reqs // (2 * splits) + 1)
        vec = self.vec
        wq, wk, wv = self.weights
        query = (matmul(hidden, wq) + vec[0:1]).astype(bf16)
        keys = matmul(hidden, wk).astype(bf16)
        values = (matmul(hidden, wv) + vec[1:2]).astype(bf16)
        joined = jnp.concatenate([keys, values], 1).reshape(seq_count, piece_len, 2 * model)
        extended = with_halo(joined, "seq", 1, BLOCK)
        first = broadcast(joined[:, :BLOCK], "seq", 0)
        last = broadcast(joined[:, piece_len - BLOCK :], "seq", splits - 1)
        tiles = seq_count * per * HEADS
        tile_size = BLOCK * 2 * size
        kv_tiles = (
            joined.reshape(seq_count, per, BLOCK, 2, HEADS, size)
            .transpose(0, 1, 4, 2, 3, 5)
            .reshape(tiles, tile_size)
        )
        req = jnp.arange(reqs, dtype=jnp.int32)
        req_seq = req // (per * HEADS * slots)
        req_head = req // slots % HEADS
        earlier = (req[:, None] > req[None, :]).astype(jnp.int32)
        everyone = (
            self.random_blocks.reshape(seq_count, splits, per, HEADS, slots)
            .transpose(1, 0, 2, 3, 4)
            .reshape(splits, reqs)
        )
        is_mine = (everyone // per == position).astype(jnp.int32)
        place = jnp.sum(is_mine[:, None, :] * earlier, 2)
        slot = jnp.where(is_mine == 1, place, cap)
        tile_of = (req_seq * per + everyone % per) * HEADS + req_head
        chosen = slot[:, :, None] == jnp.arange(cap, dtype=jnp.int32)
        send = jnp.sum(jnp.where(chosen, tile_of[:, :, None], 0), 1).reshape(splits * cap)
        self.send = one_hot(send, tiles)
        outgoing = matmul(self.send, kv_tiles).astype(bf16).reshape(splits, cap, tile_size)
        incoming = lax.all_to_all(outgoing, "seq", 0, 0, tiled=True)
        asked = lax.dynamic_slice_in_dim(self.random_blocks, position * per, per, 1)
        owner = asked.reshape(reqs) // per
        before = jnp.sum((owner[:, None] == owner[None, :]).astype(jnp.int32) * earlier, 1)
        self.arrival = one_hot(owner * cap + before, splits * cap)
        fetched = matmul(self.arrival, incoming.reshape(splits * cap, tile_size)).astype(bf16)
        moved = fetched.reshape(seq_count, per, HEADS, slots * BLOCK, 2, size)
        spans = [slice(i * BLOCK, (i + 3) * BLOCK) for i in range(per)]
        fixed = jnp.stack(
            [jnp.concatenate([extended[:, span], first, last], 1) for span in spans], 1
        )
        fixed = fixed.reshape(seq_count, per, 5 * BLOCK, 2, HEADS, size)
        paired = jnp.concatenate(
            [fixed.transpose(3, 0, 1, 4, 2, 5), moved.transpose(4, 0, 1, 2, 3, 5)], 4
        )
        self.keys, self.values = paired[0], paired[1]
        edge = jnp.full((seq_count, BLOCK), -1, jnp.int32)
        padded = jnp.concatenate([edge, segments, edge], 1)
        query_seg = lax.dynamic_slice_in_dim(segments, position * piece_len, piece_len, 1)
        ext_seg = lax.dynamic_slice_in_dim(padded, position * piece_len, piece_len + 2 * BLOCK, 1)
        always = jnp.full((seq_count, 2 * BLOCK), -2, jnp.int32)
        seg_fixed = jnp.stack(
            [jnp.concatenate([ext_seg[:, span], always], 1) for span in spans], 1
        )
        seg_fixed = jnp.broadcast_to(
            seg_fixed[:, :, None], (seq_count, per, HEADS, 5 * BLOCK)
        )
        seg_blocks = segments.reshape(seq_count, -1, BLOCK)
        asked_hot = one_hot(asked, seg_blocks.shape[1])
        seg_moved = jnp.einsum(
            "gjhrb,gbt->gjhrt", asked_hot, seg_blocks.astype(bf16), preferred_element_type=f32
        ).astype(jnp.int32)
        key_seg = jnp.concatenate(
            [seg_fixed, seg_moved.reshape(seq_count, per, HEADS, slots * BLOCK)], 3
        )[:, :, :, None, :]
        self.allowed = (
            query_seg.reshape(seq_count, per, 1, BLOCK, 1) == key_seg
        ) | (key_seg == -2)
        self.query = query.reshape(seq_count, per, BLOCK, HEADS, size)
        scores = self.scores()
        top = jnp.max(scores, -1, keepdims=True)
        powers = jnp.exp(scores - top)
        total = jnp.sum(powers, -1, keepdims=True)
        self.log_total = top + jnp.log(total)
        attended = jnp.einsum(
            "gjhqk,gjhke->gjqhe",
            (powers / total).astype(bf16),
            self.values,
            preferred_element_type=f32,
        )
        return [attended.astype(bf16).reshape(row_count, model).T]

    def scores(self):
        raw = jnp.einsum("gjqhe,gjhke->gjhqk", self.query, self.keys, preferred_element_type=f32)
        return jnp.where(self.allowed, raw * self.query.shape[-1] ** -0.5, MASKED)

    def output_grad(self, attended, grad_branch, sums):
        splits = self.splits
        full = matmul(attended[0], grad_branch)
        share = lax.psum_scatter(full, "seq", scatter_dimension=0, tiled=True)
        total = lax.psum(share.astype(bf16), "dp").astype(f32)
        lines = lax.psum(sums[:3], ("dp", "seq")).reshape(3, splits, -1)
        lines = lax.dynamic_index_in_dim(lines, self.position, 1, keepdims=False)
        return total, lines.reshape(-1)

    def backward(self, grads, grad_res, inner_share):
        hidden = self.hidden
        grad = grads[0].T
        splits, position = self.splits, self.position
        seq_count, per, _, _, size = self.query.shape
        row_count, model = hidden.shape
        piece_len = per * BLOCK
        slots = self.random_blocks.shape[3]
        scale = size**-0.5
        probs = jnp.exp(self.scores() - self.log_total)
        grad_split = grad.reshape(seq_count, per, BLOCK, HEADS, size)
        grad_probs = jnp.einsum(
            "gjqhe,gjhke->gjhqk", grad_split, self.values, preferred_element_type=f32
        )
        weighted = jnp.sum(probs * grad_probs, -1, keepdims=True)
        grad_scores = (probs * (grad_probs - weighted)).astype(bf16)
        grad_query = (
            jnp.einsum("gjhqk,gjhke->gjqhe", grad_scores, self.keys, preferred_element_type=f32)
            * scale
        )
        grad_key = (
            jnp.einsum("gjhqk,gjqhe->gjhke", grad_scores, self.query, preferred_element_type=f32)
            * scale
        )
        grad_value = jnp.einsum(
            "gjhqk,gjqhe->gjhke", probs.astype(bf16), grad_split, preferred_element_type=f32
        )
        paired = jnp.stack([grad_key, grad_value], 0)
        fixed_len = 5 * BLOCK
        fixed = (
            paired[:, :, :, :, :fixed_len]
            .transpose(1, 2, 4, 0, 3, 5)
            .reshape(seq_count, per, fixed_len, 2 * model)
        )
        moved = (
            paired[:, :, :, :, fixed_len:]
            .transpose(1, 2, 3, 4, 0, 5)
            .reshape(seq_count * per * HEADS * slots, BLOCK * 2 * size)
        )
        ext = jnp.zeros((seq_count, piece_len + 2 * BLOCK, 2 * model), f32)
        for i in range(per):
            ext = ext.at[:, i * BLOCK : (i + 3) * BLOCK].add(fixed[:, i, : 3 * BLOCK])
        first = jnp.sum(fixed[:, :, 3 * BLOCK : 4 * BLOCK], 1)
        last = jnp.sum(fixed[:, :, 4 * BLOCK :], 1)
        rims = jnp.concatenate([ext[:, :BLOCK], ext[:, piece_len + BLOCK :]], 1)
        beside = with_halo(rims.astype(bf16), "seq", 1, BLOCK).astype(f32)
        kv_grad = ext[:, BLOCK : BLOCK + piece_len]
        kv_grad = kv_grad.at[:, :BLOCK].add(beside[:, :BLOCK])
        kv_grad = kv_grad.at[:, piece_len - BLOCK :].add(beside[:, 3 * BLOCK :])
        first, last = lax.psum((first, last), "seq")
        kv_grad = kv_grad.at[:, :BLOCK].add(jnp.where(position == 0, first, 0.0))
        kv_grad = kv_grad.at[:, piece_len - BLOCK :].add(
            jnp.where(position == splits - 1, last, 0.0)
        )
        cap = self.send.shape[0] // splits
        outgoing = left_product(self.arrival, moved.astype(bf16)).astype(bf16)
        returned = lax.all_to_all(
            outgoing.reshape(splits, cap, -1), "seq", 0, 0, tiled=True
        ).reshape(splits * cap, -1)
        kv_grad = kv_grad + (
            left_product(self.send, returned)
            .reshape(seq_count, per, HEADS, BLOCK, 2, size)
            .transpose(0, 1, 3, 4, 2, 5)
            .reshape(seq_count, piece_len, 2 * model)
        )
        kv_grad = kv_grad.reshape(row_count, 2 * model).astype(bf16)
        grad_query = grad_query.reshape(row_count, model).astype(bf16)
        grads = (grad_query, kv_grad[:, :model], kv_grad[:, model:])
        input_grad = grad_res
        shares = []
        for part, weight in zip(grads, self.weights):
            input_grad = input_grad + right_product(part, weight)
            full = left_product(hidden, part)
            share = lax.psum_scatter(full, "seq", scatter_dimension=0, tiled=True)
            shares.append(lax.psum(share.astype(bf16), "dp").astype(f32))
        biases = jnp.stack([jnp.sum(grads[i].astype(f32), 0) for i in (0, 2)], 1)
        biases = lax.psum_scatter(biases, "seq", scatter_dimension=0, tiled=True)
        biases = lax.psum(biases.astype(bf16), "dp").astype(f32)
        parts = exchange_all(inner_share)
        return input_grad, shares[0], biases[:, 0], shares[1], shares[2], biases[:, 1], parts


def local(
    hidden_in,
    query_weight,
    query_bias,
    key_weight,
    value_weight,
    value_bias,
    output_weight,
    output_bias,
    first_gain,
    first_shift,
    inner_weight,
    inner_bias,
    outer_weight,
    outer_bias,
    second_gain,
    second_shift,
    segments,
    random_blocks,
    cotangent,
):
    seq_count, piece_len, model = hidden_in.shape
    splits = lax.axis_size("seq")
    groups = lax.axis_size("dp")
    group = lax.axis_index("dp")
    row_count = seq_count * piece_len
    rows = model // splits
    units = outer_weight.shape[0] // groups
    hidden = hidden_in.reshape(row_count, model)
    by_heads = (
        seq_count == 1 and groups == 4 and 2 < splits and HEADS % max(1, splits // 2) == 0
    )
    vec_local = jnp.concatenate(
        [
            v.reshape(-1, rows)
            for v in (
                query_bias,
                value_bias,
                output_bias,
                first_gain,
                first_shift,
                outer_bias,
                second_gain,
                second_shift,
                inner_bias,
            )
        ]
    )
    attention = (HeadAttention if by_heads else TokenAttention)(
        hidden,
        (query_weight, key_weight, value_weight),
        (query_bias, value_bias),
        segments,
        random_blocks,
        output_weight,
        vec_local,
    )
    inner_part = lax.dynamic_index_in_dim(
        inner_weight.reshape(rows, splits, groups, units), group, 2, keepdims=False
    ).reshape(rows, splits * units)
    outer_part = lax.dynamic_index_in_dim(
        outer_weight.reshape(groups, units, model), group, 0, keepdims=False
    )
    both = jnp.concatenate([inner_part, outer_part], 0)
    if by_heads:
        both = tied(both, attention.packed, attention.weight)
    both = lax.all_gather(both, "seq")
    if not by_heads:
        both = both.reshape(splits, 2, rows, model).transpose(1, 0, 2, 3)
        both = both.reshape(1, 2 * model, model)
    attended = attention.forward()
    vec = attention.vec
    ids = attention.ids
    w_out = attention.output_weight
    full = (row_count, model)
    wide = (groups * row_count, splits * units)
    low, normed, inverse = run_kernel(
        project_kernel,
        "project",
        [(full, bf16), (full, f32), ((row_count, 128), f32)],
        (ids, w_out, hidden, vec, *attended),
        scalars=1,
        flops=2 * row_count * model * model,
    )
    lows = exchange_all(low)
    work = 2 * wide[0] * wide[1] * model
    parts = run_kernel(
        forward_kernel,
        "forward",
        [(full, f32)] + [(full, bf16)] * (groups - 1) + [(wide, f32), (wide, bf16)],
        (ids, *lows, both, vec),
        scalars=1,
        flops=2 * work,
        powers=wide[0] * wide[1],
    )
    inner, act = parts[groups:]
    layer_out, grad_low, grad_mix, sums2 = run_kernel(
        middle_kernel,
        "middle",
        [(full, bf16), (full, bf16), (full, f32), ((8, model), f32)],
        (*exchange_parts(parts), normed, cotangent.reshape(row_count, model), vec),
    )
    grads = exchange_all(grad_low)
    parts = run_kernel(
        backward_kernel,
        "backward",
        [(full, f32)] + [(full, bf16)] * (groups - 1) + [(wide, bf16), ((1, wide[1]), f32)],
        (*grads, both, inner),
        flops=2 * work,
        powers=wide[0] * wide[1],
    )
    grad_inner, sum_inner = parts[groups:]
    recv = exchange_parts(parts)
    (stacked,) = run_kernel(
        inner_outer_kernel,
        "inner_outer",
        [((splits, 2 * rows + 8, model), bf16)],
        (*lows, *grads, tied(grad_inner, recv[1]), act, sums2, sum_inner),
        flops=2 * work,
    )
    grad_res, grad_branch, sums1, *grad_att = run_kernel(
        functools.partial(residual_kernel, parts=groups),
        "residual",
        [(full, f32), (full, bf16), ((8, model), f32)] + [(a.shape, bf16) for a in attended],
        (ids, grad_mix, normed, inverse, vec, w_out, *recv),
        scalars=1,
        flops=2 * row_count * model * model,
    )
    share = lax.psum_scatter(stacked, "seq", scatter_dimension=0, tiled=False)
    if by_heads:
        grad_att = line_parts(grad_att)
    input_grad, gq, bias_q, gk, gv, bias_v, shares = attention.backward(
        grad_att, grad_res, share
    )
    d_output, first_sums = attention.output_grad(attended, grad_branch, sums1)
    d_inner, d_outer, vectors = run_kernel(
        finish_inner_kernel,
        "finish_inner",
        [((rows, groups * splits * units), f32), ((groups * units, model), f32), ((8, model), f32)],
        (ids, *shares),
        scratch=[pltpu.VMEM((groups,) + share.shape, bf16)],
        scalars=1,
    )
    second_sums = vectors[groups]

    def cut(line, i):
        return line[i * rows : (i + 1) * rows]

    return (
        layer_out.reshape(seq_count, piece_len, model),
        input_grad.reshape(seq_count, piece_len, model),
        gq,
        bias_q,
        gk,
        gv,
        bias_v,
        d_output,
        cut(first_sums, 2),
        cut(first_sums, 0),
        cut(first_sums, 1),
        d_inner,
        vectors[:groups, 3 * rows : 3 * rows + units].reshape(-1),
        d_outer,
        cut(second_sums, 2),
        cut(second_sums, 0),
        cut(second_sums, 1),
    )


def solution(mesh):
    in_specs = (
        P("dp", "seq", None),
        P("seq", None),
        P("seq"),
        P("seq", None),
        P("seq", None),
        P("seq"),
        P("seq", None),
        P("seq"),
        P("seq"),
        P("seq"),
        P("seq", None),
        P("seq"),
        P("seq", None),
        P("seq"),
        P("seq"),
        P("seq"),
        P("dp", None),
        P("dp", None, None, None),
        P("dp", "seq", None),
    )
    out_specs = (
        P("dp", "seq", None),
        P("dp", "seq", None),
        P("seq", None),
        P("seq"),
        P("seq", None),
        P("seq", None),
        P("seq"),
        P("seq", None),
        P("seq"),
        P("seq"),
        P("seq"),
        P("seq", None),
        P("seq"),
        P("seq", None),
        P("seq"),
        P("seq"),
        P("seq"),
    )
    return jax.shard_map(local, mesh=mesh, in_specs=in_specs, out_specs=out_specs, check_vma=False)
```

time: 299 us -> 258 us (0.86)
  waiting for transfers between devices: 125 us -> 91.5 us
  starting transfers between devices: 46.1 us -> 60.9 us
  local copies, waits for them, and re-layouts: 48.8 us -> 34.6 us
  other arithmetic: 16.2 us -> 2.67 us
  Pallas kernels: 32.8 us -> 37.5 us
    all_to_all x4 -> x1, waiting for transfers between devices: 46.7 us -> 1.17 us  [__init__(): lax.all_to_all(jnp.broadcast_to(vec[None], (splits,) + vec.shape), 'seq',...]
    all_gather x4 -> x2, waiting for transfers between devices: 27.9 us -> 2.84 us  [the longest x1 2.84 us: __init__(): self.packed = lax.all_gather(hidden, 'seq')]
    ppermute x4 -> x27, waiting for transfers between devices: 3.07 us -> 28.2 us  [the longest x18 25.1 us: line_exchange(): return lax.ppermute(array, 'seq', [(i, i ^ 2 * k) for i in range(count)])]
    all_to_all x4 -> x1, starting transfers between devices: 28.2 us -> 5.7 us  [__init__(): lax.all_to_all(jnp.broadcast_to(vec[None], (splits,) + vec.shape), 'seq',...]
    ppermute x15 -> x29, waiting for transfers between devices: 37.7 us -> 58.6 us  [exchange(): return lax.ppermute(array, 'dp', [(i, i ^ k) for i in range(count)])]
    ppermute x4 -> x27, starting transfers between devices: 0.08 us -> 20.3 us  [the longest x18 19.2 us: line_exchange(): return lax.ppermute(array, 'seq', [(i, i ^ 2 * k) for i in range(count)])]
    ppermute x15 -> x29, starting transfers between devices: 17.6 us -> 34.8 us  [exchange(): return lax.ppermute(array, 'dp', [(i, i ^ k) for i in range(count)])]
    reduce_scatter x1, waiting for transfers between devices: 9.1 us -> 0.01 us  [local(): share = lax.psum_scatter(stacked, 'seq', scatter_dimension=0, tiled=False)]
  transfers between devices with their start and end apart: 28 -> 60, of which waited for: 17 -> 28; matrix products, arithmetic and copies ran while one was open for 6% -> 4% of each run, Pallas kernels for 7% -> 11%
where the time goes in v2:
time: 258 us; the launch traced here: 257 us
  waiting for transfers between devices  91.5 us (35%)
  starting transfers between devices  60.9 us (24%)
  Pallas kernels  37.5 us (15%)
  local copies, waits for them, and re-layouts  34.6 us (13%)
  blocking collectives  15.1 us (6%)
  between operations  14.7 us (6%)
  other arithmetic  2.67 us (1%)
    ppermute x29, waiting for transfers between devices, exchange(): return lax.ppermute(array, 'dp', [(i, i ^ k) for i in range(count)])  58.6 us
    pallas_call x23, Pallas kernels, run_kernel(): pl.pallas_call(kernel, name=name, out_shape=out_shape, in_specs=specs, ou...  37.5 us
    ppermute x29, starting transfers between devices, exchange(): return lax.ppermute(array, 'dp', [(i, i ^ k) for i in range(count)])  34.8 us
    unnamed x159, local copies, waits for them, and re-layouts  25.7 us
    ppermute x18, waiting for transfers between devices, line_exchange(): return lax.ppermute(array, 'seq', [(i, i ^ 2 * k) for i in range(count)])  25.1 us
    ppermute x18, starting transfers between devices, line_exchange(): return lax.ppermute(array, 'seq', [(i, i ^ 2 * k) for i in range(count)])  19.2 us
    all_to_all x1, blocking collectives, along_line(): lax.all_to_all(array, 'seq', 0, 0, tiled=True, axis_index_groups=lines)  15.1 us
    all_to_all x1, starting transfers between devices, __init__(): lax.all_to_all(jnp.broadcast_to(vec[None], (splits,) + vec.shape), 'seq',...  5.7 us
  transfers between devices with their start and end apart: 60, of which 28 were waited for; matrix products, arithmetic and copies ran while one was open for 4% of the time, Pallas kernels for 11%

profile of v2, /device:TPU:8, one launch (start us, length us, event | category | flops | bytes accessed | tf_op | source)
XLA Modules:
  0.0 256.8 jit_solution(10089733345483556474)
XLA Ops:
  10.5 15.1 %all_to_all.10.mine = bf16[4,48,576]{2,1,0:T(8,128)(2,1)S(1)} all-to-all(bf16[4,48,576]{2,1,0:T(8,128)(2,1)S(1)} %maximum_bitcast_fusion), channel_id=1, replica_groups={{0,2,4,6},{1,3,5,7},{8,10,12,14},{9,11,13,15},{16,18,20,22},{17,19,21,2..., dimensions={0} | all-to-all | bytes 442368 | tf_op jit(solution)/shard_map/all_to_all | solution.py:477
  29.4 2.3 collective-permute-done.3.mine_next
  33.9 2.8 %all-gather.4.cloned.1.call-done.hid = bf16[8,128,768]{2,1,0:T(8,128)(2,1)} async-done(((bf16[1,128,768]{2,1,0:T(8,128)(2,1)}), bf16[8,128,768]{2,1,0:T(8,128)(2,1)}) %all-gather.4.cloned.1.call-update) | async-done | bytes 1572880 | tf_op jit(solution)/shard_map/all_gather | solution.py:513
  43.4 8.3 %attend.1 = (bf16[192,128]{1,0:T(8,128)(2,1)S(1)}, bf16[192,128]{1,0:T(8,128)(2,1)}, bf16[192,128]{1,0:T(8,128)(2,1)}, bf16[192,128]{1,0:T(8,128)(2,1)}, bf16[4,...) custom-call(s32[3]{0:T(128)S(1)} %pad_add_fusion.ids, ...), custom_call_target="tpu_custom_call" | custom-call | flops 1308622848 | bytes 4009484 | tf_op jit(solution)/shard_map/attend/pallas_call | solution.py:39
  55.8 7.7 %collective-permute-done.7.mine_next = bf16[4,48,768]{2,1,0:T(8,128)(2,1)S(1)} collective-permute-done((bf16[4,48,768]{2,1,0:T(8,128)(2,1)S(1)}, bf16[4,48,768]{2,1,0:T(8,128)(2,1)S(1)}, u32[]{:S(2)}, u32[]{:S(2)}) %collective-permute-start.7) | collective-permute-done | bytes 294944 | tf_op jit(solution)/shard_map/ppermute | solution.py:435
  64.4 5.7 %all-to-all-start.1 = ((bf16[8,16,128]{2,1,0:T(8,128)(2,1)}), bf16[8,16,128]{2,1,0:T(8,128)(2,1)S(1)}, u32[]{:S(2)}, u32[]{:S(2)}) async-start(bf16[8,16,128]{2,1,0:T(8,128)(2,1)} %broadcast_in_dim.44), calls=%async_computation.1 | async-start | bytes 65536 | tf_op jit(solution)/shard_map/all_to_all | solution.py:528
  70.5 2.5 collective-permute-start.11
  90.1 3.6 %collective-permute-done.13.refs_1_ = bf16[128,768]{1,0:T(8,128)(2,1)S(1)} collective-permute-done((bf16[128,768]{1,0:T(8,128)(2,1)S(1)}, bf16[128,768]{1,0:T(8,128)(2,1)S(1)}, u32[]{:S(2)}, u32[]{:S(2)}) %collective-permute-start.13) | collective-permute-done | bytes 196640 | tf_op jit(solution)/shard_map/ppermute | solution.py:435
  93.8 4.1 %collective-permute-done.14.refs_2_ = bf16[128,768]{1,0:T(8,128)(2,1)S(1)} collective-permute-done((bf16[128,768]{1,0:T(8,128)(2,1)S(1)}, bf16[128,768]{1,0:T(8,128)(2,1)S(1)}, u32[]{:S(2)}, u32[]{:S(2)}) %collective-permute-start.14) | collective-permute-done | bytes 196640 | tf_op jit(solution)/shard_map/ppermute | solution.py:435
  104.4 2.1 forward.1
  110.1 3.6 %collective-permute-done.16.refs_1_ = bf16[128,768]{1,0:T(8,128)(2,1)S(1)} collective-permute-done((bf16[128,768]{1,0:T(8,128)(2,1)S(1)}, bf16[128,768]{1,0:T(8,128)(2,1)S(1)}, u32[]{:S(2)}, u32[]{:S(2)}) %collective-permute-start.16) | collective-permute-done | bytes 196640 | tf_op jit(solution)/shard_map/ppermute | solution.py:435
  113.7 3.0 %collective-permute-done.17.refs_2_ = bf16[128,768]{1,0:T(8,128)(2,1)S(1)} collective-permute-done((bf16[128,768]{1,0:T(8,128)(2,1)S(1)}, bf16[128,768]{1,0:T(8,128)(2,1)S(1)}, u32[]{:S(2)}, u32[]{:S(2)}) %collective-permute-start.17) | collective-permute-done | bytes 196640 | tf_op jit(solution)/shard_map/ppermute | solution.py:435
  118.4 1.9 collective-permute-start.20
  121.3 2.2 collective-permute-done.19.refs_1_.refs_5_
  123.5 2.1 collective-permute-done.20.refs_2_.refs_6_
  126.8 2.1 backward.1
  130.5 4.9 %collective-permute-done.22.refs_1_ = bf16[128,768]{1,0:T(8,128)(2,1)S(1)} collective-permute-done((bf16[128,768]{1,0:T(8,128)(2,1)S(1)}, bf16[128,768]{1,0:T(8,128)(2,1)S(1)}, u32[]{:S(2)}, u32[]{:S(2)}) %collective-permute-start.22) | collective-permute-done | bytes 196640 | tf_op jit(solution)/shard_map/ppermute | solution.py:435
  141.3 4.6 %collective-permute-done.23.refs_2_ = bf16[128,768]{1,0:T(8,128)(2,1)S(1)} collective-permute-done((bf16[128,768]{1,0:T(8,128)(2,1)}, bf16[128,768]{1,0:T(8,128)(2,1)S(1)}, u32[]{:S(2)}, u32[]{:S(2)}) %collective-permute-start.23) | collective-permute-done | bytes 196640 | tf_op jit(solution)/shard_map/ppermute | solution.py:435
  152.8 1.9 collective-permute-start.27
  156.0 2.5 collective-permute-done.26.refs_2_
  158.4 2.6 %collective-permute-done.27.refs_3_ = bf16[192,128]{1,0:T(8,128)(2,1)S(1)} collective-permute-done((bf16[192,128]{1,0:T(8,128)(2,1)S(1)}, bf16[192,128]{1,0:T(8,128)(2,1)S(1)}, u32[]{:S(2)}, u32[]{:S(2)}) %collective-permute-start.27) | collective-permute-done | bytes 49184 | tf_op jit(solution)/shard_map/ppermute | solution.py:453
  161.1 8.1 %attend_back.1 = (bf16[4,128,192]{2,1,0:T(8,128)(2,1)S(1)}, bf16[1024,384]{1,0:T(8,128)(2,1)S(1)}, bf16[4,128,384]{2,1,0:T(8,128)(2,1)S(1)}, bf16[4,128,384]{2,1,0:T(8,128)(2,1)S(1)}) custom-call(s32[3]{0:T(128)S(1)} %copy-done.46, bf16[4,128,192]{2,1,0:T(8,128)(2,1)S(1)} %copy-done.61, bf16[1024,192]{1,0:T(8,128)(2,1)S(1)} %copy-done.57, ...), custom_call_target="tpu_custom_call" | custom-call | flops 1006632960 | bytes 3319820 | tf_op jit(solution)/shard_map/attend_back/pallas_call | solution.py:39
  169.2 2.1 attend_weight.1
  175.0 1.9 collective-permute-start.35
  181.5 2.6 %collective-permute-start.45 = (f32[8,576]{1,0:T(8,128)}, f32[8,576]{1,0:T(8,128)S(1)}, u32[]{:S(2)}, u32[]{:S(2)}) collective-permute-start(f32[8,576]{1,0:T(8,128)} %add.133), channel_id=1, source_target_pairs={{0,24},{8,16},{16,8},{24,0},{1,25},{9,17},{17,9},{25,1},{2,26},{10... | collective-permute-start | bytes 55304 | tf_op jit(solution)/shard_map/ppermute | solution.py:435
  191.4 2.6 %collective-permute-start.29 = (bf16[128,768]{1,0:T(8,128)(2,1)}, bf16[128,768]{1,0:T(8,128)(2,1)S(1)}, u32[]{:S(2)}, u32[]{:S(2)}) collective-permute-start(bf16[128,768]{1,0:T(8,128)(2,1)} %get-tuple-element.128), channel_id=1, source_target_pairs={{0,2},{1,3},{2,0},{3,1},{4,6},{5,7},{6,4},{7,5},{8,10},{9,11},{10,... | collective-permute-start | bytes 589832 | tf_op jit(solution)/shard_map/ppermute | solution.py:453
  197.5 19.8 %collective-permute-done.49.refs_3_ = bf16[104,768]{1,0:T(8,128)(2,1)S(1)} collective-permute-done((bf16[104,768]{1,0:T(8,128)(2,1)S(1)}, bf16[104,768]{1,0:T(8,128)(2,1)S(1)}, u32[]{:S(2)}, u32[]{:S(2)}) %collective-permute-start.49) | collective-permute-done | bytes 159776 | tf_op jit(solution)/shard_map/ppermute | solution.py:453
  218.2 3.1 %collective-permute-done.43 = f32[8,576]{1,0:T(8,128)S(1)} collective-permute-done((f32[8,576]{1,0:T(8,128)}, f32[8,576]{1,0:T(8,128)S(1)}, u32[]{:S(2)}, u32[]{:S(2)}) %collective-permute-start.43) | collective-permute-done | bytes 18464 | tf_op jit(solution)/shard_map/ppermute | solution.py:435
  227.9 2.7 %collective-permute-done.40.refs_2_ = bf16[4,24,576]{2,1,0:T(8,128)(2,1)S(1)} collective-permute-done((bf16[4,24,576]{2,1,0:T(8,128)(2,1)S(1)}, bf16[4,24,576]{2,1,0:T(8,128)(2,1)S(1)}, u32[]{:S(2)}, u32[]{:S(2)}) %collective-permute-start.40) | collective-permute-done | bytes 110624 | tf_op jit(solution)/shard_map/ppermute | solution.py:435
  238.5 3.0 %collective-permute-done.53.refs_1_ = bf16[200,768]{1,0:T(8,128)(2,1)S(1)} collective-permute-done((bf16[200,768]{1,0:T(8,128)(2,1)}, bf16[200,768]{1,0:T(8,128)(2,1)S(1)}, u32[]{:S(2)}, u32[]{:S(2)}) %collective-permute-start.53) | collective-permute-done | bytes 307232 | tf_op jit(solution)/shard_map/ppermute | solution.py:435
  241.6 5.1 %collective-permute-done.54.refs_2_ = bf16[200,768]{1,0:T(8,128)(2,1)S(1)} collective-permute-done((bf16[200,768]{1,0:T(8,128)(2,1)}, bf16[200,768]{1,0:T(8,128)(2,1)S(1)}, u32[]{:S(2)}, u32[]{:S(2)}) %collective-permute-start.54) | collective-permute-done | bytes 307232 | tf_op jit(solution)/shard_map/ppermute | solution.py:435
  246.6 2.4 finish_inner.1
  (324 shorter events, 103.0 us)
Async XLA Ops:
  7.2 29.5 %all-gather.4.cloned.1.call-start = ((), (), s32[]{:S(2)}) async-start(), calls=%async_computation.3 | async-start | bytes 1769472 | tf_op jit(solution)/shard_map/all_gather | solution.py:513
  7.9 91.3 %all-gather.6.cloned.1.call-start = ((), (), s32[]{:S(2)}) async-start(), calls=%async_computation.5 | async-start | bytes 2654208 | tf_op jit(solution)/shard_map/all_gather | solution.py:979
  36.8 17.1 %collective-permute-start = (bf16[48,768]{1,0:T(8,128)(2,1)S(1)}, bf16[48,768]{1,0:T(8,128)(2,1)S(1)}, u32[]{:S(2)}, u32[]{:S(2)}) collective-permute-start(bf16[48,768]{1,0:T(8,128)(2,1)S(1)} %constant_dynamic-slice_fusion.7.refs_0_), channel_id=1, source_target_pairs={{0,2},{1,3},{2,0},{3,1},{4,6},{5,7},{6,4},{7,5},{8,10},{9,11},{10,... | collective-permute-start | bytes 221192 | tf_op jit(solution)/shard_map/ppermute | solution.py:453
  38.4 15.5 %collective-permute-start.1 = (bf16[48,768]{1,0:T(8,128)(2,1)S(1)}, bf16[48,768]{1,0:T(8,128)(2,1)S(1)}, u32[]{:S(2)}, u32[]{:S(2)}) collective-permute-start(bf16[48,768]{1,0:T(8,128)(2,1)S(1)} %constant_dynamic-slice_fusion.7.refs_0_), channel_id=1, source_target_pairs={{0,4},{1,5},{2,6},{3,7},{4,0},{5,1},{6,2},{7,3},{8,12},{9,13},{10,... | collective-permute-start | bytes 221192 | tf_op jit(solution)/shard_map/ppermute | solution.py:453
  39.6 14.3 %collective-permute-start.2 = (bf16[48,768]{1,0:T(8,128)(2,1)S(1)}, bf16[48,768]{1,0:T(8,128)(2,1)S(1)}, u32[]{:S(2)}, u32[]{:S(2)}) collective-permute-start(bf16[48,768]{1,0:T(8,128)(2,1)S(1)} %constant_dynamic-slice_fusion.7.refs_0_), channel_id=1, source_target_pairs={{0,6},{1,7},{2,4},{3,5},{4,2},{5,3},{6,0},{7,1},{8,14},{9,15},{10,... | collective-permute-start | bytes 221192 | tf_op jit(solution)/shard_map/ppermute | solution.py:453
  54.0 9.5 %collective-permute-start.7 = (bf16[4,48,768]{2,1,0:T(8,128)(2,1)S(1)}, bf16[4,48,768]{2,1,0:T(8,128)(2,1)S(1)}, u32[]{:S(2)}, u32[]{:S(2)}) collective-permute-start(bf16[4,48,768]{2,1,0:T(8,128)(2,1)S(1)} %stack.30.mine), channel_id=1, source_target_pairs={{0,16},{8,24},{16,0},{24,8},{1,17},{9,25},{17,1},{25,9},{2,18},{10... | collective-permute-start | bytes 884744 | tf_op jit(solution)/shard_map/ppermute | solution.py:435
  55.6 19.3 %collective-permute-start.8 = (bf16[4,48,768]{2,1,0:T(8,128)(2,1)S(1)}, bf16[4,48,768]{2,1,0:T(8,128)(2,1)S(1)}, u32[]{:S(2)}, u32[]{:S(2)}) collective-permute-start(bf16[4,48,768]{2,1,0:T(8,128)(2,1)S(1)} %stack.30.mine), channel_id=1, source_target_pairs={{0,1},{1,0},{2,3},{3,2},{4,5},{5,4},{6,7},{7,6},{8,9},{9,8},{10,11... | collective-permute-start | bytes 884744 | tf_op jit(solution)/shard_map/ppermute | solution.py:448
  63.5 12.1 %collective-permute-start.9 = (bf16[4,48,768]{2,1,0:T(8,128)(2,1)S(1)}, bf16[4,48,768]{2,1,0:T(8,128)(2,1)S(1)}, u32[]{:S(2)}, u32[]{:S(2)}) collective-permute-start(bf16[4,48,768]{2,1,0:T(8,128)(2,1)S(1)} %collective-permute-done.7.mine_next), channel_id=1, source_target_pairs={{0,1},{1,0},{2,3},{3,2},{4,5},{5,4},{6,7},{7,6},{8,9},{9,8},{10,11... | collective-permute-start | bytes 884744 | tf_op jit(solution)/shard_map/ppermute | solution.py:448
  64.4 10.4 %all-to-all-start.1 = ((bf16[8,16,128]{2,1,0:T(8,128)(2,1)}), bf16[8,16,128]{2,1,0:T(8,128)(2,1)S(1)}, u32[]{:S(2)}, u32[]{:S(2)}) async-start(bf16[8,16,128]{2,1,0:T(8,128)(2,1)} %broadcast_in_dim.44), calls=%async_computation.1 | async-start | bytes 65536 | tf_op jit(solution)/shard_map/all_to_all | solution.py:528
  70.1 157.8 %reduce-scatter.2.cloned.1.call-start = ((), (), s32[]{:S(2)}) async-start(), calls=%async_computation.4 | async-start | bytes 2764800 | tf_op jit(solution)/shard_map/reduce_scatter | solution.py:1041
  70.1 9.8 %collective-permute-start.10 = (bf16[192,128]{1,0:T(8,128)(2,1)}, bf16[192,128]{1,0:T(8,128)(2,1)S(1)}, u32[]{:S(2)}, u32[]{:S(2)}) collective-permute-start(bf16[192,128]{1,0:T(8,128)(2,1)} %get-tuple-element.96), channel_id=1, source_target_pairs={{0,2},{1,3},{2,0},{3,1},{4,6},{5,7},{6,4},{7,5},{8,10},{9,11},{10,... | collective-permute-start | bytes 147464 | tf_op jit(solution)/shard_map/ppermute | solution.py:453
  70.5 10.0 %collective-permute-start.11 = (bf16[192,128]{1,0:T(8,128)(2,1)}, bf16[192,128]{1,0:T(8,128)(2,1)S(1)}, u32[]{:S(2)}, u32[]{:S(2)}) collective-permute-start(bf16[192,128]{1,0:T(8,128)(2,1)} %get-tuple-element.97), channel_id=1, source_target_pairs={{0,4},{1,5},{2,6},{3,7},{4,0},{5,1},{6,2},{7,3},{8,12},{9,13},{10,... | collective-permute-start | bytes 147464 | tf_op jit(solution)/shard_map/ppermute | solution.py:453
  87.4 10.5 %collective-permute-start.14 = (bf16[128,768]{1,0:T(8,128)(2,1)S(1)}, bf16[128,768]{1,0:T(8,128)(2,1)S(1)}, u32[]{:S(2)}, u32[]{:S(2)}) collective-permute-start(bf16[128,768]{1,0:T(8,128)(2,1)S(1)} %get-tuple-element.99.refs_0_), channel_id=1, source_target_pairs={{0,16},{8,24},{16,0},{24,8},{1,17},{9,25},{17,1},{25,9},{2,18},{10... | collective-permute-start | bytes 589832 | tf_op jit(solution)/shard_map/ppermute | solution.py:435
  89.0 9.6 %collective-permute-start.15 = (bf16[128,768]{1,0:T(8,128)(2,1)S(1)}, bf16[128,768]{1,0:T(8,128)(2,1)S(1)}, u32[]{:S(2)}, u32[]{:S(2)}) collective-permute-start(bf16[128,768]{1,0:T(8,128)(2,1)S(1)} %get-tuple-element.99.refs_0_), channel_id=1, source_target_pairs={{0,24},{8,16},{16,8},{24,0},{1,25},{9,17},{17,9},{25,1},{2,26},{10... | collective-permute-start | bytes 589832 | tf_op jit(solution)/shard_map/ppermute | solution.py:435
  107.2 9.6 %collective-permute-start.17 = (bf16[128,768]{1,0:T(8,128)(2,1)S(1)}, bf16[128,768]{1,0:T(8,128)(2,1)S(1)}, u32[]{:S(2)}, u32[]{:S(2)}) collective-permute-start(bf16[128,768]{1,0:T(8,128)(2,1)S(1)} %get-tuple-element.103), channel_id=1, source_target_pairs={{0,16},{8,24},{16,0},{24,8},{1,17},{9,25},{17,1},{25,9},{2,18},{10... | collective-permute-start | bytes 589832 | tf_op jit(solution)/shard_map/ppermute | solution.py:435
  155.8 21.1 %collective-permute-start.46 = (bf16[4,104,768]{2,1,0:T(8,128)(2,1)S(1)}, bf16[4,104,768]{2,1,0:T(8,128)(2,1)S(1)}, u32[]{:S(2)}, u32[]{:S(2)}) collective-permute-start(bf16[4,104,768]{2,1,0:T(8,128)(2,1)S(1)} %get-tuple-element.149), channel_id=1, source_target_pairs={{0,1},{1,0},{2,3},{3,2},{4,5},{5,4},{6,7},{7,6},{8,9},{9,8},{10,11... | collective-permute-start | bytes 1916936 | tf_op jit(solution)/shard_map/ppermute | solution.py:448
  171.4 17.7 %collective-permute-start.28 = (bf16[4,128,384]{2,1,0:T(8,128)(2,1)S(1)}, bf16[4,128,384]{2,1,0:T(8,128)(2,1)S(1)}, u32[]{:S(2)}, u32[]{:S(2)}) collective-permute-start(bf16[4,128,384]{2,1,0:T(8,128)(2,1)S(1)} %get-tuple-element.126), channel_id=1, source_target_pairs={{0,1},{1,0},{2,3},{3,2},{4,5},{5,4},{6,7},{7,6},{8,9},{9,8},{10,11... | collective-permute-start | bytes 1179656 | tf_op jit(solution)/shard_map/ppermute | solution.py:448
  175.0 9.1 %collective-permute-start.35 = (bf16[4,24,576]{2,1,0:T(8,128)(2,1)S(1)}, bf16[4,24,576]{2,1,0:T(8,128)(2,1)S(1)}, u32[]{:S(2)}, u32[]{:S(2)}) collective-permute-start(bf16[4,24,576]{2,1,0:T(8,128)(2,1)S(1)} %get-tuple-element.137), channel_id=1, source_target_pairs={{0,24},{8,16},{16,8},{24,0},{1,25},{9,17},{17,9},{25,1},{2,26},{10... | collective-permute-start | bytes 331784 | tf_op jit(solution)/shard_map/ppermute | solution.py:435
  178.1 17.5 %collective-permute-start.47 = (bf16[104,768]{1,0:T(8,128)(2,1)S(1)}, bf16[104,768]{1,0:T(8,128)(2,1)S(1)}, u32[]{:S(2)}, u32[]{:S(2)}) collective-permute-start(bf16[104,768]{1,0:T(8,128)(2,1)S(1)} %get-tuple-element.151), channel_id=1, source_target_pairs={{0,2},{1,3},{2,0},{3,1},{4,6},{5,7},{6,4},{7,5},{8,10},{9,11},{10,... | collective-permute-start | bytes 479240 | tf_op jit(solution)/shard_map/ppermute | solution.py:453
  179.6 16.6 %collective-permute-start.48 = (bf16[104,768]{1,0:T(8,128)(2,1)S(1)}, bf16[104,768]{1,0:T(8,128)(2,1)S(1)}, u32[]{:S(2)}, u32[]{:S(2)}) collective-permute-start(bf16[104,768]{1,0:T(8,128)(2,1)S(1)} %get-tuple-element.152), channel_id=1, source_target_pairs={{0,4},{1,5},{2,6},{3,7},{4,0},{5,1},{6,2},{7,3},{8,12},{9,13},{10,... | collective-permute-start | bytes 479240 | tf_op jit(solution)/shard_map/ppermute | solution.py:453
  191.4 31.0 %collective-permute-start.29 = (bf16[128,768]{1,0:T(8,128)(2,1)}, bf16[128,768]{1,0:T(8,128)(2,1)S(1)}, u32[]{:S(2)}, u32[]{:S(2)}) collective-permute-start(bf16[128,768]{1,0:T(8,128)(2,1)} %get-tuple-element.128), channel_id=1, source_target_pairs={{0,2},{1,3},{2,0},{3,1},{4,6},{5,7},{6,4},{7,5},{8,10},{9,11},{10,... | collective-permute-start | bytes 589832 | tf_op jit(solution)/shard_map/ppermute | solution.py:453
  194.0 29.6 %collective-permute-start.30 = (bf16[128,768]{1,0:T(8,128)(2,1)}, bf16[128,768]{1,0:T(8,128)(2,1)S(1)}, u32[]{:S(2)}, u32[]{:S(2)}) collective-permute-start(bf16[128,768]{1,0:T(8,128)(2,1)} %get-tuple-element.129), channel_id=1, source_target_pairs={{0,4},{1,5},{2,6},{3,7},{4,0},{5,1},{6,2},{7,3},{8,12},{9,13},{10,... | collective-permute-start | bytes 589832 | tf_op jit(solution)/shard_map/ppermute | solution.py:453
  194.1 30.7 %collective-permute-start.31 = (bf16[128,768]{1,0:T(8,128)(2,1)S(1)}, bf16[128,768]{1,0:T(8,128)(2,1)S(1)}, u32[]{:S(2)}, u32[]{:S(2)}) collective-permute-start(bf16[128,768]{1,0:T(8,128)(2,1)S(1)} %get-tuple-element.130), channel_id=1, source_target_pairs={{0,6},{1,7},{2,4},{3,5},{4,2},{5,3},{6,0},{7,1},{8,14},{9,15},{10,... | collective-permute-start | bytes 589832 | tf_op jit(solution)/shard_map/ppermute | solution.py:453
  195.6 21.7 %collective-permute-start.49 = (bf16[104,768]{1,0:T(8,128)(2,1)S(1)}, bf16[104,768]{1,0:T(8,128)(2,1)S(1)}, u32[]{:S(2)}, u32[]{:S(2)}) collective-permute-start(bf16[104,768]{1,0:T(8,128)(2,1)S(1)} %get-tuple-element.153), channel_id=1, source_target_pairs={{0,6},{1,7},{2,4},{3,5},{4,2},{5,3},{6,0},{7,1},{8,14},{9,15},{10,... | collective-permute-start | bytes 479240 | tf_op jit(solution)/shard_map/ppermute | solution.py:453
  196.2 29.7 %collective-permute-start.39 = (bf16[4,24,576]{2,1,0:T(8,128)(2,1)S(1)}, bf16[4,24,576]{2,1,0:T(8,128)(2,1)S(1)}, u32[]{:S(2)}, u32[]{:S(2)}) collective-permute-start(bf16[4,24,576]{2,1,0:T(8,128)(2,1)S(1)} %stack.31.refs_0_), channel_id=1, source_target_pairs={{0,8},{8,0},{16,24},{24,16},{1,9},{9,1},{17,25},{25,17},{2,10},{10... | collective-permute-start | bytes 331784 | tf_op jit(solution)/shard_map/ppermute | solution.py:435
  221.3 9.3 %collective-permute-start.40 = (bf16[4,24,576]{2,1,0:T(8,128)(2,1)S(1)}, bf16[4,24,576]{2,1,0:T(8,128)(2,1)S(1)}, u32[]{:S(2)}, u32[]{:S(2)}) collective-permute-start(bf16[4,24,576]{2,1,0:T(8,128)(2,1)S(1)} %stack.31.refs_0_), channel_id=1, source_target_pairs={{0,16},{8,24},{16,0},{24,8},{1,17},{9,25},{17,1},{25,9},{2,18},{10... | collective-permute-start | bytes 331784 | tf_op jit(solution)/shard_map/ppermute | solution.py:435
  223.6 9.1 %collective-permute-start.50 = (bf16[104,768]{1,0:T(8,128)(2,1)S(1)}, bf16[104,768]{1,0:T(8,128)(2,1)S(1)}, u32[]{:S(2)}, u32[]{:S(2)}) collective-permute-start(bf16[104,768]{1,0:T(8,128)(2,1)S(1)} %sum.5.p0), channel_id=1, source_target_pairs={{0,8},{8,0},{16,24},{24,16},{1,9},{9,1},{17,25},{25,17},{2,10},{10... | collective-permute-start | bytes 479240 | tf_op jit(solution)/shard_map/ppermute | solution.py:435
  224.8 12.3 %collective-permute-start.51 = (bf16[104,768]{1,0:T(8,128)(2,1)S(1)}, bf16[104,768]{1,0:T(8,128)(2,1)S(1)}, u32[]{:S(2)}, u32[]{:S(2)}) collective-permute-start(bf16[104,768]{1,0:T(8,128)(2,1)S(1)} %sum.5.p0), channel_id=1, source_target_pairs={{0,16},{8,24},{16,0},{24,8},{1,17},{9,25},{17,1},{25,9},{2,18},{10... | collective-permute-start | bytes 479240 | tf_op jit(solution)/shard_map/ppermute | solution.py:435
  225.9 11.3 %collective-permute-start.52 = (bf16[104,768]{1,0:T(8,128)(2,1)S(1)}, bf16[104,768]{1,0:T(8,128)(2,1)S(1)}, u32[]{:S(2)}, u32[]{:S(2)}) collective-permute-start(bf16[104,768]{1,0:T(8,128)(2,1)S(1)} %sum.5.p0), channel_id=1, source_target_pairs={{0,24},{8,16},{16,8},{24,0},{1,25},{9,17},{17,9},{25,1},{2,26},{10... | collective-permute-start | bytes 479240 | tf_op jit(solution)/shard_map/ppermute | solution.py:435
  230.6 11.0 %collective-permute-start.53 = (bf16[200,768]{1,0:T(8,128)(2,1)}, bf16[200,768]{1,0:T(8,128)(2,1)S(1)}, u32[]{:S(2)}, u32[]{:S(2)}) collective-permute-start(bf16[200,768]{1,0:T(8,128)(2,1)} %bitcast.60), channel_id=1, source_target_pairs={{0,8},{8,0},{16,24},{24,16},{1,9},{9,1},{17,25},{25,17},{2,10},{10... | collective-permute-start | bytes 921608 | tf_op jit(solution)/shard_map/ppermute | solution.py:435
  231.4 15.2 %collective-permute-start.54 = (bf16[200,768]{1,0:T(8,128)(2,1)}, bf16[200,768]{1,0:T(8,128)(2,1)S(1)}, u32[]{:S(2)}, u32[]{:S(2)}) collective-permute-start(bf16[200,768]{1,0:T(8,128)(2,1)} %bitcast.61), channel_id=1, source_target_pairs={{0,16},{8,24},{16,0},{24,8},{1,17},{9,25},{17,1},{25,9},{2,18},{10... | collective-permute-start | bytes 921608 | tf_op jit(solution)/shard_map/ppermute | solution.py:435
  232.7 14.0 %collective-permute-start.55 = (bf16[200,768]{1,0:T(8,128)(2,1)}, bf16[200,768]{1,0:T(8,128)(2,1)S(1)}, u32[]{:S(2)}, u32[]{:S(2)}) collective-permute-start(bf16[200,768]{1,0:T(8,128)(2,1)} %bitcast.62), channel_id=1, source_target_pairs={{0,24},{8,16},{16,8},{24,0},{1,25},{9,17},{17,9},{25,1},{2,26},{10... | collective-permute-start | bytes 921608 | tf_op jit(solution)/shard_map/ppermute | solution.py:435
  (107 other events, 887.8 us)
Sparse Core Ops, SparseCore 0:
  9.7 27.0 all-gather.3
  39.0 31.1 all-gather.5
  139.1 33.2 reduce-scatter.1

commit v3 on v2

--- a/solution.py
+++ b/solution.py
@@ -30,18 +30,27 @@
     return lax.dot_general(left, right, (((1,), (1,)), ((), ())), preferred_element_type=f32)
 
 
-def run_kernel(kernel, name, outs, args, scratch=(), scalars=0, flops=0, powers=0, grant=VMEM_BYTES):
+def run_kernel(
+    kernel, name, outs, args, scratch=(), scalars=0, raw=(), raw_outs=(), flops=0, powers=0, grant=VMEM_BYTES
+):
+    def spec(i, held):
+        return pl.BlockSpec(memory_space=pltpu.MemorySpace.HBM if i in held else pltpu.VMEM)
+
     specs = [pl.BlockSpec(memory_space=pltpu.SMEM)] * scalars
-    specs += [pl.BlockSpec(memory_space=pltpu.VMEM)] * (len(args) - scalars)
-    out_shape = tuple(jax.ShapeDtypeStruct(shape, dtype) for shape, dtype in outs)
-    moved = sum(a.size * a.dtype.itemsize for a in args)
-    moved += sum(o.size * o.dtype.itemsize for o in out_shape)
+    specs += [spec(i, raw) for i in range(scalars, len(args))]
+    shapes = [jax.ShapeDtypeStruct(shape, dtype) for shape, dtype in outs]
+    moved = sum(a.size * a.dtype.itemsize for a in (*args, *shapes))
+    out_shape = tuple(pltpu.HBM(o.shape, o.dtype) if i in raw_outs else o for i, o in enumerate(shapes))
+    args = [
+        pltpu.with_memory_space_constraint(a, pltpu.HBM) if i in raw else a
+        for i, a in enumerate(args)
+    ]
     return pl.pallas_call(
         kernel,
         name=name,
         out_shape=out_shape,
         in_specs=specs,
-        out_specs=tuple(pl.BlockSpec(memory_space=pltpu.VMEM) for _ in outs),
+        out_specs=tuple(spec(i, raw_outs) for i in range(len(outs))),
         scratch_shapes=list(scratch),
         compiler_params=pltpu.CompilerParams(vmem_limit_bytes=grant),
         cost_estimate=pl.CostEstimate(flops=flops, bytes_accessed=moved, transcendentals=powers),
@@ -80,36 +89,137 @@
     return jnp.where(same, jnp.concatenate(rows, 0), bn)
 
 
-def assemble_kernel(ids, mine, mine_next, other, other_next, out, *, bit, relative):
+def place(ids, mine, other, out):
+    for k in range(out.shape[0] // 2):
+        chip = ids[1] ^ k
+        out[2 * chip + ids[0]] = mine[k]
+        out[2 * chip + 1 - ids[0]] = other[k]
+
+
+def concat_kernel(*refs):
+    out = refs[-1]
+    at = 0
+    for r in refs[:-1]:
+        rows = r.shape[0]
+        out[at : at + rows] = r[...]
+        at += rows
+
+
+def stack_kernel(*refs):
+    for k, r in enumerate(refs[:-1]):
+        refs[-1][k] = r[...]
+
+
+def cut_kernel(ids, wq, wk, wv, *refs):
+    outs = refs[:-3]
+    raw, scratch, sems = refs[-3:]
+    _, half, _ = raw.shape
+    start = pl.multiple_of(lax.rem(ids[2], 2) * half, half)
+    copies = [
+        pltpu.make_async_copy(w.at[pl.ds(start, half), :], raw.at[i], sems.at[i])
+        for i, w in enumerate((wq, wk, wv))
+    ]
+    for copy in copies:
+        copy.start()
+    for copy in copies:
+        copy.wait()
+    chips, _, wide = scratch.shape
+    width = wide // 3
+    for chip in range(chips):
+        scratch[chip] = jnp.concatenate(
+            [raw[i, :, chip * width : (chip + 1) * width] for i in range(3)], 1
+        )
+    for k, out in enumerate(outs):
+        out[...] = scratch[ids[1] ^ k]
+
+
+def assemble_kernel(ids, mine, other, out):
     core = ids[0]
-    half = lax.rem(ids[2] // bit, 2)
-    for k in range(mine.shape[0]):
-        chip = ids[1] ^ k if relative else k
-        out[2 * chip + core, half] = mine[k]
-        out[2 * chip + core, 1 - half] = mine_next[k]
-        out[2 * chip + 1 - core, half] = other[k]
-        out[2 * chip + 1 - core, 1 - half] = other_next[k]
-
-
-def attend_kernel(ids, hid, w, qb, vb, be, bn, sk, sq, *refs):
-    outs = refs[:-5]
-    qo, ko, vo, lse, qs = refs[-5:]
+    own = lax.rem(ids[2], 2)
+    _, chips, _, _ = mine.shape
+    for h in range(2):
+        for k in range(chips):
+            chip = ids[1] ^ k
+            out[2 * chip + core, own ^ h] = mine[h, k]
+            out[2 * chip + 1 - core, own ^ h] = other[h, k]
+
+
+def cut_output_kernel(ids, wo, vec, out):
+    half = wo.shape[0] // 2
+    count, rows = vec.shape
+    start = pl.multiple_of(lax.rem(ids[2] // 2, 2) * half, half)
+    tall, model = out.shape
+    out[:half, :] = wo[pl.ds(start, half), :]
+    line = jnp.concatenate([vec[...], jnp.zeros((count, model - rows), bf16)], 1)
+    out[half:, :] = jnp.concatenate([line, jnp.zeros((tall - half - count, model), bf16)], 0)
+
+
+def cut_inner_kernel(ids, w1, w2, out, scratch):
+    groups, rows, model = scratch.shape
+    units = w2.shape[0] // groups
+    pieces = model // units
+    for g in range(groups):
+        scratch[g] = jnp.concatenate(
+            [
+                w1[:, (s * groups + g) * units : (s * groups + g + 1) * units]
+                for s in range(pieces)
+            ],
+            1,
+        )
+    out[:rows, :] = scratch[ids[2]]
+    out[rows:, :] = w2[pl.ds(pl.multiple_of(ids[2] * units, units), units), :]
+
+
+def assemble_output_kernel(ids, mine, other, out, vec, scratch):
+    core = ids[0]
+    pieces, _, half, _ = out.shape
+    chips = pieces // 2
+    own = lax.rem(ids[2] // 2, 2)
+    for k in range(chips):
+        chip = ids[1] ^ k
+        scratch[2 * chip + core] = mine[0, k, half:, :]
+        scratch[2 * chip + 1 - core] = other[0, k, half:, :]
+        for h in range(2):
+            out[2 * chip + core, own ^ h] = mine[h, k, :half, :]
+            out[2 * chip + 1 - core, own ^ h] = other[h, k, :half, :]
+    rows = 2 * half
+    vec[...] = jnp.concatenate(
+        [scratch[piece].astype(f32)[:, :rows] for piece in range(pieces)], 1
+    )
+
+
+def attend_kernel(ids, w, be, bn, sk, sq, hid, ours, theirs, *refs):
+    att = refs[0]
+    kept = refs[1:5]
+    qo, ko, vo, lse, qs, sems = refs[5:]
+    copies = [
+        pltpu.make_async_copy(here, there, sems.at[i])
+        for i, (here, there) in enumerate(zip((qo, ko, vo, lse), kept))
+    ]
     pieces, piece_len, width = qs.shape
     chips = pieces // 2
     core = ids[0]
     size = 64
     heads = width // size
     model = hid.shape[2]
+    ours, theirs = ours[...].astype(f32), theirs[...].astype(f32)
+    first = jnp.where(core == 0, ours, theirs)
+    second = jnp.where(core == 0, theirs, ours)
+    biases = jnp.concatenate([first, second], 1)
+    qb, vb = biases[0:1, :], biases[1:2, :]
     tokens = hid[...].reshape(pieces * piece_len, model)
     product = matmul(tokens, w[...])
-    query = (product[:, :width] + qb[...]).astype(bf16) * bf16(size**-0.5)
+    query = (product[:, :width] + qb).astype(bf16) * bf16(size**-0.5)
     qs[...] = query.reshape(pieces, piece_len, width)
     ko[...] = product[:, width : 2 * width].astype(bf16)
-    vo[...] = (product[:, 2 * width :] + vb[...]).astype(bf16)
+    vo[...] = (product[:, 2 * width :] + vb).astype(bf16)
     lane = lax.broadcasted_iota(jnp.int32, (piece_len, 128), 1)
     for k in range(chips):
+        qo[k] = qs[2 * (ids[1] ^ k) + core]
+    for copy in copies[:3]:
+        copy.start()
+    for k in range(chips):
         chip = ids[1] ^ k
-        qo[k] = qs[2 * chip + core]
         same = sq[chip] == sk[...]
         logs = jnp.zeros((piece_len, 128), f32)
         parts = []
@@ -123,14 +233,26 @@
             probs = (powers * (1.0 / total)).astype(bf16)
             parts.append(matmul(probs, vo[:, cols]))
             logs = jnp.where(lane == head, top + jnp.log(total), logs)
-        outs[k][...] = jnp.concatenate(parts, 1).T.astype(bf16)
+        att[chip] = jnp.concatenate(parts, 1).T.astype(bf16)
         lse[k] = logs
-
-
-def attend_back_kernel(ids, q, k, v, lse, be, bn, sk, sq, *refs):
-    chips, piece_len, width = q.shape
+    copies[3].start()
+    for copy in copies:
+        copy.wait()
+
+
+def attend_back_kernel(ids, hid_raw, q_raw, k_raw, v_raw, lse_raw, be, bn, sk, sq, *refs):
+    chips, piece_len, width = q_raw.shape
     ga = refs[:chips]
-    dq, own, mine, other, ds_all, p_all, dkv = refs[chips:]
+    dq, mine, other, dw_mine, dw_other = refs[chips : chips + 5]
+    hid, q, k, v, lse, ds_all, p_all, dkv, dws, sems = refs[chips + 5 :]
+    copies = [
+        pltpu.make_async_copy(there, here, sems.at[i])
+        for i, (there, here) in enumerate(
+            zip((q_raw, k_raw, v_raw, lse_raw, hid_raw), (q, k, v, lse, hid))
+        )
+    ]
+    for copy in copies:
+        copy.start()
     pieces = 2 * chips
     core = ids[0]
     size = 64
@@ -138,6 +260,8 @@
     dks = []
     dvs = []
     dqs = [[None] * heads for _ in range(chips)]
+    for copy in copies[:4]:
+        copy.wait()
     gas = [g[...].astype(f32).T.astype(bf16) for g in ga]
     for head in range(heads):
         cols = slice(head * size, (head + 1) * size)
@@ -163,47 +287,58 @@
     for i in range(chips):
         dq[i] = jnp.concatenate(dqs[i], 1)
     joined = jnp.concatenate(dks + dvs, 1)
-    own[...] = joined
     dkv[...] = joined.reshape(pieces, piece_len, 2 * width)
     for i in range(chips):
         chip = ids[1] ^ i
         mine[i] = dkv[2 * chip + core]
         other[i] = dkv[2 * chip + 1 - core]
-
-
-def attend_weight_kernel(ids, hid, dq, dkv, mine, other, sums, dws):
-    pieces, piece_len, model = hid.shape
-    chips, _, width = dq.shape
-    core = ids[0]
+    copies[4].wait()
+    _, _, model = hid.shape
     tokens = hid[...].reshape(pieces * piece_len, model)
-    owned = jnp.concatenate([hid[2 * (ids[1] ^ k) + core] for k in range(chips)], 0)
+    owned = jnp.concatenate([hid[2 * (ids[1] ^ i) + core] for i in range(chips)], 0)
     grad_q = dq[...].reshape(chips * piece_len, width)
-    grad_kv = dkv[...]
-    weights = jnp.concatenate([left_product(owned, grad_q), left_product(tokens, grad_kv)], 1)
-    quarters, _, rows, _ = mine.shape
+    weights = jnp.concatenate([left_product(owned, grad_q), left_product(tokens, joined)], 1)
+    groups = dw_mine.shape[0]
+    rows = dws.shape[2]
     dws[...] = weights.reshape(dws.shape)
-    for k in range(chips):
-        chip = ids[1] ^ k
-        for j in range(quarters):
-            mine[j, k] = dws[2 * chip + core, ids[2] ^ j]
-            other[j, k] = dws[2 * chip + 1 - core, ids[2] ^ j].astype(bf16)
+    for i in range(chips):
+        chip = ids[1] ^ i
+        for j in range(groups):
+            span = slice(i * rows, (i + 1) * rows)
+            dw_mine[j, span] = dws[2 * chip + core, ids[2] ^ j]
+            dw_other[j, span] = dws[2 * chip + 1 - core, ids[2] ^ j].astype(bf16)
     total = jnp.concatenate(
         [
             jnp.sum(grad_q.astype(f32), 0, keepdims=True),
-            jnp.sum(grad_kv.astype(f32), 0, keepdims=True),
+            jnp.sum(joined.astype(f32), 0, keepdims=True),
         ],
         1,
     )
-    sums[...] = jnp.broadcast_to(total, sums.shape)
-
-
-def input_grad_kernel(dq, mine, recv, w, *outs):
+    total = jnp.broadcast_to(total, (8, 3 * width))
+    for j in range(groups):
+        dw_mine[j, chips * rows :] = total
+        dw_other[j, chips * rows :] = total.astype(bf16)
+
+
+def input_grad_kernel(ids, dq, mine, recv, w, out, scratch):
     chips, piece_len, width = dq.shape
     dkv = (mine[...].astype(f32) + recv[...].astype(f32)).astype(bf16)
     grads = jnp.concatenate([dq[...], dkv], 2).reshape(chips * piece_len, 3 * width)
     total = right_product(grads, w[...])
-    for k, out in enumerate(outs):
-        out[...] = total[k * piece_len : (k + 1) * piece_len].astype(out.dtype)
+    scratch[...] = total.astype(bf16).reshape(scratch.shape)
+    for chip in range(chips):
+        out[chip] = scratch[ids[1] ^ chip]
+
+
+def add_kernel(left, right, out):
+    out[...] = (left[...].astype(f32) + right[...].astype(f32)).astype(out.dtype)
+
+
+def sum_rows_kernel(first, parts, out):
+    total = first[...]
+    for i in range(parts.shape[0]):
+        total = total + parts[i].astype(f32)
+    out[...] = total
 
 
 def add_split_kernel(left, right, *outs):
@@ -211,29 +346,26 @@
         out[...] = (left[k].astype(f32) + right[k].astype(f32)).astype(out.dtype)
 
 
-def sum_split_kernel(*refs, parts):
+def sum_split_kernel(*refs, parts, rows):
     total = refs[0][...].astype(f32)
     for r in refs[1:parts]:
         total = total + r[...].astype(f32)
-    outs = refs[parts:]
-    if len(outs) == 1:
-        outs[0][...] = total.astype(outs[0].dtype)
-    else:
-        for k, out in enumerate(outs):
-            out[...] = total[k].astype(out.dtype)
-
-
-def stack_kernel(*refs):
-    for k, r in enumerate(refs[:-1]):
-        refs[-1][k] = r[...]
-
-
-def project_kernel(ids, wo, hid, vec, *refs):
-    att = refs[:-3]
-    low, normed, inverse = refs[-3:]
+    for k, out in enumerate(refs[parts:]):
+        out[...] = total[k * rows : k * rows + out.shape[0]].astype(out.dtype)
+
+
+def sum_lead_kernel(parts, *outs, rows):
+    total = parts[0].astype(f32)
+    for i in range(1, parts.shape[0]):
+        total = total + parts[i].astype(f32)
+    for k, out in enumerate(outs):
+        out[...] = total[k * rows : k * rows + out.shape[0]].astype(out.dtype)
+
+
+def project_kernel(wo, hid, vec, att, low, normed, inverse):
     branch = vec[2:3, :] + jnp.zeros(hid.shape, f32)
-    for k, r in enumerate(att):
-        branch = branch + left_product(r[...], wo[ids[1] ^ k])
+    for chip in range(att.shape[0]):
+        branch = branch + left_product(att[chip], wo[chip])
     n1, r1 = normalize(hid[...].astype(f32) + branch)
     low[...] = (n1 * vec[3:4, :] + vec[4:5, :]).astype(bf16)
     normed[...] = n1
@@ -251,16 +383,19 @@
     return first, both[:, half:, :].reshape(pieces * half, model)
 
 
-def forward_kernel(ids, *refs):
-    parts = (len(refs) - 4) // 2
-    x = refs[:parts]
-    both, vec = refs[parts : parts + 2]
-    outs = refs[parts + 2 : 2 * parts + 2]
-    inner_ref, act_ref = refs[2 * parts + 2 :]
-    rows = x[0].shape[0]
+def forward_kernel(ids, vec, both_raw, *refs, parts):
+    raw = refs[:parts]
+    outs = refs[parts : 2 * parts]
+    inner_ref, act_ref, both, x, sems = refs[2 * parts :]
+    copies = [pltpu.make_async_copy(r, x.at[i], sems.at[i]) for i, r in enumerate(raw)]
+    copies.append(pltpu.make_async_copy(both_raw, both, sems.at[parts]))
+    for copy in copies:
+        copy.start()
+    for copy in copies:
+        copy.wait()
+    _, rows, model = x.shape
     weight1, weight2 = two_weights(both)
-    tokens = jnp.concatenate([r[...] for r in x], 0)
-    inner = matmul(tokens, weight1) + vec[pl.ds(8 + ids[2], 1), :]
+    inner = matmul(x[...].reshape(parts * rows, model), weight1) + vec[pl.ds(8 + ids[2], 1), :]
     act = (0.5 * inner * (1.0 + gelu_parts(inner))).astype(bf16)
     inner_ref[...] = inner
     act_ref[...] = act
@@ -290,12 +425,11 @@
     sums[3:, :] = jnp.zeros((5, sums.shape[1]), f32)
 
 
-def backward_kernel(*refs):
-    parts = (len(refs) - 4) // 2
-    grads = refs[:parts]
-    both, inner_ref = refs[parts : parts + 2]
-    outs = refs[parts + 2 : 2 * parts + 2]
-    gi_ref, sum_ref = refs[2 * parts + 2 :]
+def backward_kernel(ids, both, inner_ref, act, sums, *refs, parts):
+    x = refs[:parts]
+    grads = refs[parts : 2 * parts]
+    outs = refs[2 * parts : 3 * parts]
+    rest = refs[3 * parts :]
     rows = grads[0].shape[0]
     weight1, weight2 = two_weights(both)
     gm = jnp.concatenate([r[...] for r in grads], 0)
@@ -304,11 +438,25 @@
     t = gelu_parts(v)
     slope = 0.5 * (1.0 + t) + 0.5 * v * (1.0 - t * t) * (GELU_A * (1.0 + 3.0 * GELU_B * (v * v)))
     gi = (grad_act * slope).astype(bf16)
-    gi_ref[...] = gi
-    sum_ref[...] = jnp.sum(gi.astype(f32), 0, keepdims=True)
     first = right_product(gi, weight1)
     for i in range(parts):
         outs[i][...] = first[i * rows : (i + 1) * rows].astype(outs[i].dtype)
+    tokens = jnp.concatenate([r[...] for r in x], 0)
+    inner = left_product(tokens, gi).astype(bf16)
+    outer = left_product(act[...], gm).astype(bf16)
+    total = jnp.sum(gi.astype(f32), 0, keepdims=True)
+    vectors = [sums[i : i + 1, :] for i in range(3)] + [total]
+
+    def write(place_of):
+        for piece in range(inner.shape[0] // units):
+            out, at = place_of(piece)
+            span = slice(piece * units, (piece + 1) * units)
+            out[at, :units, :] = inner[span]
+            out[at, units : 2 * units, :] = outer[span]
+            put_vectors(out, piece, at, 2 * units, vectors, units)
+
+    units = (rest[0].shape[1] - 8) // 2
+    write(lambda piece: (rest[0], piece))
 
 
 def residual_kernel(ids, mix, normed, inverse, vec, wo, *refs, parts):
@@ -329,47 +477,23 @@
     sums[3:, :] = jnp.zeros((5, sums.shape[1]), f32)
 
 
-def put_vectors(out, piece, row, vectors, rows):
+def put_vectors(out, piece, at, row, vectors, rows):
     parts = [v[:, piece * rows : (piece + 1) * rows] for v in vectors]
     fill = out.shape[2] - rows * len(parts)
     line = jnp.concatenate(parts + [jnp.zeros((1, fill), f32)], 1)
-    out[piece, row : row + 8, :] = jnp.broadcast_to(line, (8, out.shape[2])).astype(bf16)
-
-
-def inner_outer_kernel(*refs):
-    parts = (len(refs) - 5) // 2
-    x = refs[:parts]
-    gm = refs[parts : 2 * parts]
-    gi, act, sums, sum_inner, out = refs[2 * parts :]
-    pieces, tall, model = out.shape
-    rows = (tall - 8) // 2
-    tokens = jnp.concatenate([r[...] for r in x], 0)
-    grads = jnp.concatenate([r[...] for r in gm], 0)
-    out[:, :rows, :] = left_product(tokens, gi[...]).astype(bf16).reshape(pieces, rows, model)
-    out[:, rows : 2 * rows, :] = (
-        left_product(act[...], grads).astype(bf16).reshape(pieces, rows, model)
-    )
-    vectors = [sums[i : i + 1, :] for i in range(3)] + [sum_inner[...]]
-    for piece in range(pieces):
-        put_vectors(out, piece, 2 * rows, vectors, rows)
-
-
-def output_grad_kernel(ids, gb, sums, *refs):
-    mine, other, dws = refs[-3:]
-    core = ids[0]
-    chips, tall, model = mine.shape
-    rows = tall - 8
+    out[at, row : row + 8, :] = jnp.broadcast_to(line, (8, out.shape[2])).astype(bf16)
+
+
+def output_grad_kernel(gb, sums, att, out):
+    rows = out.shape[1] - 8
     grad = gb[...]
     vectors = [sums[i : i + 1, :] for i in range(3)]
-    for piece in range(2 * chips):
-        put_vectors(dws, piece, rows, vectors, rows)
-    for k in range(chips):
-        chip = ids[1] ^ k
-        part = matmul(refs[k][...], grad).astype(bf16)
+    for chip in range(att.shape[0]):
+        part = matmul(att[chip], grad).astype(bf16)
         for i in range(2):
-            dws[2 * chip + i, :rows, :] = part[i * rows : (i + 1) * rows]
-        mine[k] = dws[2 * chip + core]
-        other[k] = dws[2 * chip + 1 - core]
+            piece = 2 * chip + i
+            out[piece, :rows] = part[i * rows : (i + 1) * rows]
+            put_vectors(out, piece, piece, rows, vectors, rows)
 
 
 def ordered(ids, refs, scratch):
@@ -377,8 +501,7 @@
         scratch[ids[2] ^ k] = r[...]
 
 
-def finish_inner_kernel(ids, *refs):
-    parts = len(refs) - 4
+def finish_inner_kernel(ids, *refs, parts):
     inner, outer, vectors, scratch = refs[parts:]
     ordered(ids, refs[:parts], scratch)
     rows = inner.shape[0]
@@ -393,9 +516,10 @@
             1,
         )
     total = jnp.zeros((1, scratch.shape[2]), f32)
+    at = rows + units
     for g in range(parts):
-        outer[g * units : (g + 1) * units, :] = scratch[g, rows : rows + units, :].astype(f32)
-        line = scratch[g, rows + units : rows + units + 8, :].astype(f32)[0:1]
+        outer[g * units : (g + 1) * units, :] = scratch[g, rows:at, :].astype(f32)
+        line = scratch[g, at : at + 8, :].astype(f32)[0:1]
         vectors[g : g + 1, :] = line
         total = total + line
     vectors[parts : parts + 1, :] = total
@@ -467,8 +591,15 @@
 
 def sum_split(arrays, outs):
     return run_kernel(
-        functools.partial(sum_split_kernel, parts=len(arrays)), "sum", outs, tuple(arrays)
-    )
+        functools.partial(sum_split_kernel, parts=len(arrays), rows=outs[0][0][0]),
+        "sum",
+        outs,
+        tuple(arrays),
+    )
+
+
+def line_all(array):
+    return [array] + [line_exchange(array, k) for k in range(1, lax.axis_size("seq") // 2)]
 
 
 def along_line(array):
@@ -477,24 +608,33 @@
     return lax.all_to_all(array, "seq", 0, 0, tiled=True, axis_index_groups=lines)
 
 
+def stack(*arrays):
+    shape = (len(arrays),) + arrays[0].shape
+    return run_kernel(stack_kernel, "stack", [(shape, bf16)], arrays)[0]
+
+
+def concat(*arrays):
+    shape = (sum(a.shape[0] for a in arrays),) + arrays[0].shape[1:]
+    return run_kernel(concat_kernel, "concat", [(shape, bf16)], arrays)[0]
+
+
 def device_ids():
     position = lax.axis_index("seq")
     return jnp.stack([position % 2, position // 2, lax.axis_index("dp")]).astype(jnp.int32)
 
 
-def assemble(ids, mine, bit, relative):
-    mine_next = exchange(mine, bit)
-    other = swap_cores(mine)
-    other_next = swap_cores(mine_next)
-    chips, half, width = mine.shape
-    (out,) = run_kernel(
-        functools.partial(assemble_kernel, bit=bit, relative=relative),
-        "assemble",
-        [((2 * chips, 2, half, width), bf16)],
-        (ids, mine, mine_next, other, other_next),
+def finish_inner(ids, shares, rows):
+    groups = len(shares)
+    share = shares[0]
+    model = share.shape[1]
+    return run_kernel(
+        functools.partial(finish_inner_kernel, parts=groups),
+        "finish_inner",
+        [((rows, groups * model), f32), ((groups * rows, model), f32), ((8, model), f32)],
+        (ids, *shares),
+        scratch=[pltpu.VMEM((groups,) + share.shape, bf16)],
         scalars=1,
     )
-    return out.reshape(4 * chips * half, width)
 
 
 class HeadAttention:
@@ -506,39 +646,47 @@
         chip = position // 2
         group = lax.axis_index("dp")
         self.ids = device_ids()
+        self.packed = lax.all_gather(hidden, "seq")
         piece_len, model = hidden.shape
         rows = model // splits
         width = model // chips
         heads = HEADS // chips
-        self.packed = lax.all_gather(hidden, "seq")
         half = rows // 2
-        start = group % 2 * half
-        split = jnp.concatenate(
-            [
-                lax.dynamic_slice_in_dim(w, start, half, 0).reshape(half, chips, width)
-                for w in weights
+        cut = run_kernel(
+            cut_kernel,
+            "cut",
+            [((half, 3 * width), bf16)] * chips,
+            (self.ids, *weights),
+            scratch=[
+                pltpu.VMEM((3, half, model), bf16),
+                pltpu.VMEM((chips, half, 3 * width), bf16),
+                pltpu.SemaphoreType.DMA((3,)),
             ],
-            2,
-        )
-        self.weight = assemble(self.ids, along_line(split.transpose(1, 0, 2)), 1, False)
-        out_half = lax.dynamic_slice_in_dim(output_weight, group // 2 % 2 * half, half, 0)
-        self.out_parts = [out_half] + [line_exchange(out_half, k) for k in range(1, chips)]
-        tall = -(-vec_local.shape[0] // 16) * 16
-        vec = jnp.pad(vec_local, ((0, tall - vec_local.shape[0]), (0, 128 - rows)))
-        vec = lax.all_to_all(
-            jnp.broadcast_to(vec[None], (splits,) + vec.shape), "seq", 0, 0, tiled=True
-        )
-        self.vec = (
-            vec[:, : vec_local.shape[0], :rows].transpose(1, 0, 2).reshape(-1, model).astype(f32)
-        )
-        pair = jnp.stack(biases, 0)
-        pair_other = swap_cores(pair)
-        bias = jnp.where(
-            core == 0,
-            jnp.concatenate([pair, pair_other], 1),
-            jnp.concatenate([pair_other, pair], 1),
-        ).astype(f32)
-        self.bias_q, self.bias_v = bias[0:1], bias[1:2]
+            scalars=1,
+            raw=range(1, 4),
+        )
+        cut = stack(*line_parts(cut))
+        cut_next = exchange(cut, 1)
+        (out_half,) = run_kernel(
+            cut_output_kernel,
+            "cut_output",
+            [((half + 16, model), bf16)],
+            (self.ids, output_weight, vec_local),
+            scalars=1,
+        )
+        cut = stack(cut, cut_next)
+        (weight,) = run_kernel(
+            assemble_kernel,
+            "assemble",
+            [((splits, 2, half, 3 * width), bf16)],
+            (self.ids, cut, swap_cores(cut)),
+            scalars=1,
+        )
+        self.out_half = stack(*line_all(tied(out_half, cut_next)))
+        self.out_next = exchange(self.out_half, 2)
+        self.weight = weight.reshape(model, 3 * width)
+        self.biases = biases
+        self.hidden = hidden
         block_count = segments.shape[1] // BLOCK
         per_piece = piece_len // BLOCK
         own = random_blocks[0].reshape(chips, 2, per_piece, HEADS, -1)
@@ -569,57 +717,94 @@
     def masks(self):
         return (self.same_bias, self.other_bias, self.key_seg, self.query_seg)
 
+    def inner_weights(self, inner_weight, outer_weight):
+        groups = lax.axis_size("dp")
+        rows = inner_weight.shape[0]
+        units = outer_weight.shape[0] // groups
+        (both,) = run_kernel(
+            cut_inner_kernel,
+            "cut_inner",
+            [((rows + units, self.model), bf16)],
+            (self.ids, inner_weight, outer_weight),
+            scratch=[pltpu.VMEM((groups, rows, self.model), bf16)],
+            scalars=1,
+        )
+        self.pair = jnp.stack(self.biases, 0)
+        self.pair_other = swap_cores(self.pair)
+        self.both = lax.all_gather(tied(both, self.packed, self.weight, self.out_half), "seq")
+
     def forward(self):
         chips, piece_len, width, model = self.chips, self.piece_len, self.width, self.model
         tokens = self.splits * piece_len
         one = (chips, piece_len, width)
-        *att, self.q, self.k, self.v, self.lse = run_kernel(
+        kept = [
+            (one, bf16),
+            ((tokens, width), bf16),
+            ((tokens, width), bf16),
+            ((chips, piece_len, 128), f32),
+        ]
+        att, self.q, self.k, self.v, self.lse = run_kernel(
             attend_kernel,
             "attend",
-            [((width, piece_len), bf16)] * chips
+            [((chips, width, piece_len), bf16)] + kept,
+            (self.ids, self.weight, *self.masks(), self.packed, self.pair, self.pair_other),
+            scratch=[pltpu.VMEM(*spec) for spec in kept]
             + [
-                (one, bf16),
-                ((tokens, width), bf16),
-                ((tokens, width), bf16),
-                ((chips, piece_len, 128), f32),
+                pltpu.VMEM((self.splits, piece_len, width), bf16),
+                pltpu.SemaphoreType.DMA((len(kept),)),
             ],
-            (self.ids, self.packed, self.weight, self.bias_q, self.bias_v) + self.masks(),
-            scratch=[pltpu.VMEM((self.splits, piece_len, width), bf16)],
             scalars=1,
+            raw_outs=range(1, 1 + len(kept)),
             flops=6 * tokens * model * width + 2 * tokens * tokens * width,
             powers=tokens * tokens * 3 // 2,
-        )
-        parts = lax.optimization_barrier((tuple(self.out_parts), att[0]))[0]
-        rows = parts[0].shape
-        (mine,) = run_kernel(stack_kernel, "stack", [((chips,) + rows, bf16)], parts)
-        weight = assemble(self.ids, mine, 2, True)
+            grant=12 << 20,
+        )
+        out_half = stack(tied(self.out_half, att), self.out_next)
+        half = model // self.splits // 2
+        weight, self.vec = run_kernel(
+            assemble_output_kernel,
+            "assemble_output",
+            [((self.splits, 2, half, model), bf16), ((16, model), f32)],
+            (self.ids, out_half, swap_cores(out_half)),
+            scratch=[pltpu.VMEM((self.splits, 16, model), bf16)],
+            scalars=1,
+        )
         self.output_weight = weight.reshape(chips, width, model)
-        return line_parts(att)
+        att = along_line(att)
+        return att
+
+    def inner_shapes(self, tall):
+        return [((self.splits, tall, self.model), bf16)]
+
+    def inner_grads(self, stacked):
+        self.share = lax.psum_scatter(stacked, "seq", scatter_dimension=0, tiled=False)
 
     def output_grad(self, attended, grad_branch, sums):
         chips, model = self.chips, self.model
-        rows = model // self.splits
-        one = (rows + 8, model)
-        mine, other = run_kernel(
+        (stacked,) = run_kernel(
             output_grad_kernel,
             "output_grad",
-            [((chips,) + one, bf16)] * 2,
-            (self.ids, grad_branch, sums, *attended),
-            scratch=[pltpu.VMEM((self.splits,) + one, bf16)],
-            scalars=1,
+            [((self.splits, model // self.splits + 8, model), bf16)],
+            (grad_branch, sums, attended),
             flops=2 * self.piece_len * model * model,
         )
-        parts = add_split(mine, swap_cores(other), [(one, bf16)] * chips)
-        (share,) = sum_split(line_parts(parts), [(one, bf16)])
-        out, vectors = run_kernel(
+        stacked = tied(stacked, self.share)
+        self.output_share = lax.psum_scatter(stacked, "seq", scatter_dimension=0, tiled=False)
+
+    def finish_grads(self, after):
+        model = self.model
+        groups = lax.axis_size("dp")
+        rows = model // self.splits
+        d_inner, d_outer, vectors = finish_inner(self.ids, self.shares, rows)
+        d_output, lines = run_kernel(
             finish_output_kernel,
             "finish_output",
             [((rows, model), f32), ((8, model), f32)],
-            tuple(exchange_all(share)),
-        )
-        return out, vectors[0]
-
-    def backward(self, grads, grad_res, share):
+            tuple(exchange_all(self.output_share)),
+        )
+        return d_inner, d_outer, d_output, lines[0], vectors
+
+    def backward(self, grads, grad_res):
         chips, piece_len, width = self.chips, self.piece_len, self.width
         splits, model = self.splits, self.model
         groups = lax.axis_size("dp")
@@ -627,63 +812,65 @@
         rows = model // splits
         one = (chips, piece_len, width)
         two = (chips, piece_len, 2 * width)
-        dq, dkv, mine, other = run_kernel(
+        quarter = (rows // groups, 3 * width)
+        group = (chips * quarter[0] + 8, 3 * width)
+        wide = ((groups,) + group, bf16)
+        keep = (self.packed, self.q, self.k, self.v, self.lse)
+        dq, mine, other, dw_mine, dw_other = run_kernel(
             attend_back_kernel,
             "attend_back",
-            [(one, bf16), ((tokens, 2 * width), bf16), (two, bf16), (two, bf16)],
-            (self.ids, self.q, self.k, self.v, self.lse) + self.masks() + tuple(grads),
-            scratch=[
+            [(one, bf16), (two, bf16), (two, bf16), (wide[0], f32), wide],
+            (self.ids,) + keep + self.masks() + tuple(grads),
+            scratch=[pltpu.VMEM(a.shape, a.dtype) for a in keep]
+            + [
                 pltpu.VMEM((chips * piece_len, tokens), bf16),
                 pltpu.VMEM((chips * piece_len, tokens), bf16),
                 pltpu.VMEM((splits, piece_len, 2 * width), bf16),
+                pltpu.VMEM((splits, groups) + quarter, f32),
+                pltpu.SemaphoreType.DMA((len(keep),)),
             ],
             scalars=1,
-            flops=5 * tokens * tokens * width,
+            raw=range(1, 6),
+            flops=5 * tokens * tokens * width + 6 * tokens * model * width,
             powers=tokens * tokens * 3 // 2,
-            grant=10 << 20,
+            grant=18 << 20,
         )
         recv = swap_cores(other)
-        quarter = (rows // groups, 3 * width)
-        part = (groups, chips) + quarter
-        dw_mine, dw_other, sums = run_kernel(
-            attend_weight_kernel,
-            "attend_weight",
-            [(part, f32), (part, bf16), ((8, 3 * width), f32)],
-            (self.ids, self.packed, dq, dkv),
-            scratch=[pltpu.VMEM((splits, groups) + quarter, f32)],
-            scalars=1,
-            flops=6 * tokens * model * width,
-        )
-        dws = add_split(dw_mine, swap_cores(dw_other), [(part[1:], bf16)] * groups)
+        dws = add_split(dw_mine, swap_cores(dw_other), [(group, bf16)] * groups)
+        dq = tied(dq, dws[0])
+        self.last = dws[0]
         dws = exchange_parts(dws)
         full = (piece_len, model)
-        partial = run_kernel(
+        (partial,) = run_kernel(
             input_grad_kernel,
             "input_grad",
-            [(full, f32)] + [(full, bf16)] * (chips - 1),
-            (dq, mine, recv, self.weight),
+            [((chips,) + full, bf16)],
+            (self.ids, dq, mine, recv, self.weight),
+            scratch=[pltpu.VMEM((chips,) + full, bf16)],
+            scalars=1,
             flops=3 * tokens * model * width,
         )
-        partial = line_parts(partial)
-        dws = sum_split(dws, [(quarter, bf16)] * chips)
-        share = tied(share, dws[0])
+        *dws, sums = sum_split(dws, [(quarter, bf16)] * chips + [((8, 3 * width), f32)])
         dws = line_parts(dws)
-        shares = exchange_all(share)
-        (dw,) = run_kernel(stack_kernel, "stack", [(part[1:], bf16)], tuple(dws))
+        self.shares = exchange_all(tied(self.share, dws[0]))
+        partial = along_line(tied(partial, *dws[1:], self.shares[1]))
+        part = (chips,) + quarter
+        dw = stack(*dws)
         gq, gk, gv = run_kernel(
             finish_kernel,
             "finish",
             [((rows, model), f32)] * 3,
             (self.ids, *exchange_all(dw)),
-            scratch=[pltpu.VMEM(part, bf16)],
+            scratch=[pltpu.VMEM((groups,) + part, bf16)],
             scalars=1,
         )
-        (input_grad,) = sum_split([grad_res] + partial, [(full, f32)])
-        sums = sum(exchange_all(sums + swap_cores(sums)))
+        (input_grad,) = run_kernel(
+            sum_rows_kernel, "sum_rows", [(full, f32)], (grad_res, partial)
+        )
         core = self.position % 2
         bias_q = lax.dynamic_slice_in_dim(sums[0], core * rows, rows)
         bias_v = lax.dynamic_slice_in_dim(sums[0], 2 * width + core * rows, rows)
-        return input_grad, gq, bias_q, gk, gv, bias_v, shares
+        return input_grad, gq, bias_q, gk, gv, bias_v, dws[0]
 
 
 def one_hot(index, count):
@@ -813,22 +1000,47 @@
             self.values,
             preferred_element_type=f32,
         )
-        return [attended.astype(bf16).reshape(row_count, model).T]
+        return attended.astype(bf16).reshape(row_count, model).T[None]
 
     def scores(self):
         raw = jnp.einsum("gjqhe,gjhke->gjhqk", self.query, self.keys, preferred_element_type=f32)
         return jnp.where(self.allowed, raw * self.query.shape[-1] ** -0.5, MASKED)
+
+    def inner_weights(self, inner_weight, outer_weight):
+        splits = self.splits
+        groups, group = lax.axis_size("dp"), lax.axis_index("dp")
+        rows = inner_weight.shape[0]
+        units, model = outer_weight.shape[0] // groups, outer_weight.shape[1]
+        inner = inner_weight.reshape(rows, splits, groups, units)
+        outer = outer_weight.reshape(groups, units, model)
+        inner = lax.dynamic_index_in_dim(inner, group, 2, keepdims=False).reshape(rows, model)
+        outer = lax.dynamic_index_in_dim(outer, group, 0, keepdims=False)
+        both = lax.all_gather(jnp.concatenate([inner, outer], 0), "seq")
+        both = both.reshape(splits, 2, rows, model).transpose(1, 0, 2, 3)
+        self.both = both.reshape(1, 2 * model, model)
+
+    def inner_shapes(self, tall):
+        return [((self.splits, tall, self.hidden.shape[1]), bf16)]
+
+    def inner_grads(self, stacked):
+        self.share = lax.psum_scatter(stacked, "seq", scatter_dimension=0, tiled=False)
 
     def output_grad(self, attended, grad_branch, sums):
         splits = self.splits
         full = matmul(attended[0], grad_branch)
         share = lax.psum_scatter(full, "seq", scatter_dimension=0, tiled=True)
-        total = lax.psum(share.astype(bf16), "dp").astype(f32)
+        self.total = lax.psum(share.astype(bf16), "dp").astype(f32)
         lines = lax.psum(sums[:3], ("dp", "seq")).reshape(3, splits, -1)
-        lines = lax.dynamic_index_in_dim(lines, self.position, 1, keepdims=False)
-        return total, lines.reshape(-1)
-
-    def backward(self, grads, grad_res, inner_share):
+        self.lines = lax.dynamic_index_in_dim(lines, self.position, 1, keepdims=False)
+
+    def finish_grads(self, after):
+        model = self.hidden.shape[1]
+        groups = lax.axis_size("dp")
+        rows = model // self.splits
+        d_inner, d_outer, vectors = finish_inner(self.ids, exchange_all(self.share), rows)
+        return d_inner, d_outer, self.total, self.lines.reshape(-1), vectors
+
+    def backward(self, grads, grad_res):
         hidden = self.hidden
         grad = grads[0].T
         splits, position = self.splits, self.position
@@ -906,8 +1118,8 @@
         biases = jnp.stack([jnp.sum(grads[i].astype(f32), 0) for i in (0, 2)], 1)
         biases = lax.psum_scatter(biases, "seq", scatter_dimension=0, tiled=True)
         biases = lax.psum(biases.astype(bf16), "dp").astype(f32)
-        parts = exchange_all(inner_share)
-        return input_grad, shares[0], biases[:, 0], shares[1], shares[2], biases[:, 1], parts
+        self.last = input_grad
+        return input_grad, shares[0], biases[:, 0], shares[1], shares[2], biases[:, 1], biases
 
 
 def local(
@@ -934,7 +1146,6 @@
     seq_count, piece_len, model = hidden_in.shape
     splits = lax.axis_size("seq")
     groups = lax.axis_size("dp")
-    group = lax.axis_index("dp")
     row_count = seq_count * piece_len
     rows = model // splits
     units = outer_weight.shape[0] // groups
@@ -967,19 +1178,7 @@
         output_weight,
         vec_local,
     )
-    inner_part = lax.dynamic_index_in_dim(
-        inner_weight.reshape(rows, splits, groups, units), group, 2, keepdims=False
-    ).reshape(rows, splits * units)
-    outer_part = lax.dynamic_index_in_dim(
-        outer_weight.reshape(groups, units, model), group, 0, keepdims=False
-    )
-    both = jnp.concatenate([inner_part, outer_part], 0)
-    if by_heads:
-        both = tied(both, attention.packed, attention.weight)
-    both = lax.all_gather(both, "seq")
-    if not by_heads:
-        both = both.reshape(splits, 2, rows, model).transpose(1, 0, 2, 3)
-        both = both.reshape(1, 2 * model, model)
+    attention.inner_weights(inner_weight, outer_weight)
     attended = attention.forward()
     vec = attention.vec
     ids = attention.ids
@@ -990,20 +1189,27 @@
         project_kernel,
         "project",
         [(full, bf16), (full, f32), ((row_count, 128), f32)],
-        (ids, w_out, hidden, vec, *attended),
-        scalars=1,
+        (w_out, hidden, vec, attended),
         flops=2 * row_count * model * model,
     )
     lows = exchange_all(low)
     work = 2 * wide[0] * wide[1] * model
+    both = attention.both
     parts = run_kernel(
-        forward_kernel,
+        functools.partial(forward_kernel, parts=groups),
         "forward",
         [(full, f32)] + [(full, bf16)] * (groups - 1) + [(wide, f32), (wide, bf16)],
-        (ids, *lows, both, vec),
+        (ids, vec, both, *lows),
+        scratch=[
+            pltpu.VMEM(both.shape, bf16),
+            pltpu.VMEM((groups,) + full, bf16),
+            pltpu.SemaphoreType.DMA((groups + 1,)),
+        ],
         scalars=1,
+        raw=range(2, 3 + groups),
         flops=2 * work,
         powers=wide[0] * wide[1],
+        grant=10 << 20,
     )
     inner, act = parts[groups:]
     layer_out, grad_low, grad_mix, sums2 = run_kernel(
@@ -1014,45 +1220,31 @@
     )
     grads = exchange_all(grad_low)
     parts = run_kernel(
-        backward_kernel,
+        functools.partial(backward_kernel, parts=groups),
         "backward",
-        [(full, f32)] + [(full, bf16)] * (groups - 1) + [(wide, bf16), ((1, wide[1]), f32)],
-        (*grads, both, inner),
-        flops=2 * work,
+        [(full, f32)] + [(full, bf16)] * (groups - 1) + attention.inner_shapes(2 * rows + 8),
+        (ids, both, inner, act, sums2, *lows, *grads),
+        scalars=1,
+        flops=4 * work,
         powers=wide[0] * wide[1],
-    )
-    grad_inner, sum_inner = parts[groups:]
-    recv = exchange_parts(parts)
-    (stacked,) = run_kernel(
-        inner_outer_kernel,
-        "inner_outer",
-        [((splits, 2 * rows + 8, model), bf16)],
-        (*lows, *grads, tied(grad_inner, recv[1]), act, sums2, sum_inner),
-        flops=2 * work,
-    )
+        grant=VMEM_BYTES if by_heads else 4 * VMEM_BYTES,
+    )
+    recv = exchange_parts(parts[:groups])
+    attention.inner_grads(*parts[groups:])
     grad_res, grad_branch, sums1, *grad_att = run_kernel(
         functools.partial(residual_kernel, parts=groups),
         "residual",
-        [(full, f32), (full, bf16), ((8, model), f32)] + [(a.shape, bf16) for a in attended],
+        [(full, f32), (full, bf16), ((8, model), f32)]
+        + [(attended.shape[1:], bf16)] * attended.shape[0],
         (ids, grad_mix, normed, inverse, vec, w_out, *recv),
         scalars=1,
         flops=2 * row_count * model * model,
     )
-    share = lax.psum_scatter(stacked, "seq", scatter_dimension=0, tiled=False)
     if by_heads:
         grad_att = line_parts(grad_att)
-    input_grad, gq, bias_q, gk, gv, bias_v, shares = attention.backward(
-        grad_att, grad_res, share
-    )
-    d_output, first_sums = attention.output_grad(attended, grad_branch, sums1)
-    d_inner, d_outer, vectors = run_kernel(
-        finish_inner_kernel,
-        "finish_inner",
-        [((rows, groups * splits * units), f32), ((groups * units, model), f32), ((8, model), f32)],
-        (ids, *shares),
-        scratch=[pltpu.VMEM((groups,) + share.shape, bf16)],
-        scalars=1,
-    )
+    input_grad, gq, bias_q, gk, gv, bias_v, after = attention.backward(grad_att, grad_res)
+    attention.output_grad(attended, tied(grad_branch, attention.last), sums1)
+    d_inner, d_outer, d_output, first_sums, vectors = attention.finish_grads(after)
     second_sums = vectors[groups]
 
     def cut(line, i):

time: 258 us -> 225 us (0.87)
  local copies, waits for them, and re-layouts: 34.6 us -> 15.8 us
  blocking collectives: 15.1 us -> 0 us
  Pallas kernels: 37.5 us -> 46.4 us
  waiting for transfers between devices: 91.5 us -> 86.9 us
    all_to_all x1 -> x0, blocking collectives: 15.1 us -> none  [along_line(): lax.all_to_all(array, 'seq', 0, 0, tiled=True, axis_index_groups=lines)]
    unnamed x159 -> x97, local copies, waits for them, and re-layouts: 25.7 us -> 12.2 us
    pallas_call x23 -> x25, Pallas kernels: 37.5 us -> 46.4 us  [run_kernel(): pl.pallas_call(kernel, name=name, out_shape=out_shape, in_specs=specs, ou...]
    all_to_all x1 -> x2, waiting for transfers between devices: 1.17 us -> 7.5 us  [along_line(): lax.all_to_all(array, 'seq', 0, 0, tiled=True, axis_index_groups=lines)]
    ppermute x29 -> x26, waiting for transfers between devices: 58.6 us -> 52.4 us  [exchange(): return lax.ppermute(array, 'dp', [(i, i ^ k) for i in range(count)])]
    ppermute x29 -> x26, starting transfers between devices: 34.8 us -> 31.1 us  [exchange(): return lax.ppermute(array, 'dp', [(i, i ^ k) for i in range(count)])]
    dynamic_slice x4 -> x0, local copies, waits for them, and re-layouts: 3.09 us -> none  [the longest x2 1.83 us: __init__(): lax.dynamic_slice_in_dim(w, start, half, 0).reshape(half, chips, width)]
    all_gather x1, waiting for transfers between devices: 2.84 us -> 0.02 us  [__init__(): self.packed = lax.all_gather(hidden, 'seq')]
  transfers between devices with their start and end apart: 60 -> 49, of which waited for: 28 -> 29; matrix products, arithmetic and copies ran while one was open for 4% -> 2% of each run, Pallas kernels for 11% -> 16%
where the time goes in v3:
time: 225 us; the launch traced here: 223 us
  waiting for transfers between devices  86.9 us (39%)
  starting transfers between devices  59.2 us (26%)
  Pallas kernels  46.4 us (21%)
  local copies, waits for them, and re-layouts  15.8 us (7%)
  between operations  14.5 us (6%)
    ppermute x26, waiting for transfers between devices, exchange(): return lax.ppermute(array, 'dp', [(i, i ^ k) for i in range(count)])  52.4 us
    pallas_call x25, Pallas kernels, run_kernel(): pl.pallas_call(kernel, name=name, out_shape=out_shape, in_specs=specs, ou...  46.4 us
    ppermute x26, starting transfers between devices, exchange(): return lax.ppermute(array, 'dp', [(i, i ^ k) for i in range(count)])  31.1 us
    ppermute x12, waiting for transfers between devices, line_exchange(): return lax.ppermute(array, 'seq', [(i, i ^ 2 * k) for i in range(count)])  24.3 us
    ppermute x12, starting transfers between devices, line_exchange(): return lax.ppermute(array, 'seq', [(i, i ^ 2 * k) for i in range(count)])  18.5 us
    unnamed x97, local copies, waits for them, and re-layouts  12.2 us
    all_to_all x2, starting transfers between devices, along_line(): lax.all_to_all(array, 'seq', 0, 0, tiled=True, axis_index_groups=lines)  8.48 us
    all_to_all x2, waiting for transfers between devices, along_line(): lax.all_to_all(array, 'seq', 0, 0, tiled=True, axis_index_groups=lines)  7.5 us
  transfers between devices with their start and end apart: 49, of which 29 were waited for; matrix products, arithmetic and copies ran while one was open for 2% of the time, Pallas kernels for 16%

profile of v3, /device:TPU:8, one launch (start us, length us, event | category | flops | bytes accessed | tf_op | source)
XLA Modules:
  0.0 223.1 jit_solution(9230848892291835900)
XLA Ops:
  9.9 3.0 %collective-permute-start.1 = (bf16[48,576]{1,0:T(8,128)(2,1)S(1)}, bf16[48,576]{1,0:T(8,128)(2,1)S(1)}, u32[]{:S(2)}, u32[]{:S(2)}) collective-permute-start(bf16[48,576]{1,0:T(8,128)(2,1)S(1)} %get-tuple-element.85), channel_id=1, source_target_pairs={{0,4},{1,5},{2,6},{3,7},{4,0},{5,1},{6,2},{7,3},{8,12},{9,13},{10,... | collective-permute-start | bytes 165896 | tf_op jit(solution)/shard_map/ppermute | solution.py:577
  14.1 3.1 %collective-permute-done.1.refs_2_ = bf16[48,576]{1,0:T(8,128)(2,1)S(1)} collective-permute-done((bf16[48,576]{1,0:T(8,128)(2,1)S(1)}, bf16[48,576]{1,0:T(8,128)(2,1)S(1)}, u32[]{:S(2)}, u32[]{:S(2)}) %collective-permute-start.1) | collective-permute-done | bytes 55328 | tf_op jit(solution)/shard_map/ppermute | solution.py:577
  19.7 4.7 %collective-permute-done.3.refs_1_ = bf16[4,48,576]{2,1,0:T(8,128)(2,1)S(1)} collective-permute-done((bf16[4,48,576]{2,1,0:T(8,128)(2,1)S(1)}, bf16[4,48,576]{2,1,0:T(8,128)(2,1)S(1)}, u32[]{:S(2)}, u32[]{:S(2)}) %collective-permute-start.3) | collective-permute-done | bytes 221216 | tf_op jit(solution)/shard_map/ppermute | solution.py:559
  25.4 2.5 %collective-permute-start.4 = (bf16[64,768]{1,0:T(8,128)(2,1)S(1)}, bf16[64,768]{1,0:T(8,128)(2,1)S(1)}, u32[]{:S(2)}, u32[]{:S(2)}) collective-permute-start(bf16[64,768]{1,0:T(8,128)(2,1)S(1)} %cut_output.1.refs_0_), channel_id=1, source_target_pairs={{0,2},{1,3},{2,0},{3,1},{4,6},{5,7},{6,4},{7,5},{8,10},{9,11},{10,... | collective-permute-start | bytes 294920 | tf_op jit(solution)/shard_map/ppermute | solution.py:577
  31.0 5.6 %collective-permute-done.4.refs_1_ = bf16[64,768]{1,0:T(8,128)(2,1)S(1)} collective-permute-done((bf16[64,768]{1,0:T(8,128)(2,1)S(1)}, bf16[64,768]{1,0:T(8,128)(2,1)S(1)}, u32[]{:S(2)}, u32[]{:S(2)}) %collective-permute-start.4) | collective-permute-done | bytes 98336 | tf_op jit(solution)/shard_map/ppermute | solution.py:577
  36.6 2.5 %collective-permute-done.5.refs_2_ = bf16[64,768]{1,0:T(8,128)(2,1)S(1)} collective-permute-done((bf16[64,768]{1,0:T(8,128)(2,1)S(1)}, bf16[64,768]{1,0:T(8,128)(2,1)S(1)}, u32[]{:S(2)}, u32[]{:S(2)}) %collective-permute-start.5) | collective-permute-done | bytes 98336 | tf_op jit(solution)/shard_map/ppermute | solution.py:577
  39.1 3.4 %collective-permute-done.6.refs_3_ = bf16[64,768]{1,0:T(8,128)(2,1)S(1)} collective-permute-done((bf16[64,768]{1,0:T(8,128)(2,1)S(1)}, bf16[64,768]{1,0:T(8,128)(2,1)S(1)}, u32[]{:S(2)}, u32[]{:S(2)}) %collective-permute-start.6) | collective-permute-done | bytes 98336 | tf_op jit(solution)/shard_map/ppermute | solution.py:577
  47.7 8.9 %attend.1 = (bf16[4,192,128]{2,1,0:T(8,128)(2,1)}, bf16[4,128,192]{2,1,0:T(8,128)(2,1)}, bf16[1024,192]{1,0:T(8,128)(2,1)}, bf16[1024,192]{1,0:T(8,128)(2,1)}, f32[4,128,128]{2,1,0:T(8,128)}) custom-call(s32[3]{0:T(128)S(1)} %pad_add_fusion.ids, bf16[768,576]{1,0:T(8,128)(2,1)S(1)} %bitcast.48, f32[12,2,1024]{2,1,0:T(2,128)S(1)} %reshape_reshape.3.be, ...), custom_call_target="tpu_custom_call" | custom-call | flops 1308622848 | bytes 4008716 | tf_op jit(solution)/shard_map/attend/pallas_call | solution.py:48
  57.0 3.4 %all-to-all-start = ((bf16[4,192,128]{2,1,0:T(8,128)(2,1)}), bf16[4,192,128]{2,1,0:T(8,128)(2,1)S(1)}, u32[]{:S(2)}, u32[]{:S(2)}) async-start(bf16[4,192,128]{2,1,0:T(8,128)(2,1)} %get-tuple-element.88), calls=%async_computation | async-start | bytes 393216 | tf_op jit(solution)/shard_map/all_to_all | solution.py:608
  63.3 7.5 %all-to-all-done.att = bf16[4,192,128]{2,1,0:T(8,128)(2,1)S(1)} async-done(((bf16[4,192,128]{2,1,0:T(8,128)(2,1)}), bf16[4,192,128]{2,1,0:T(8,128)(2,1)S(1)}, u32[]{:S(2)}, u32[]{:S(2)}) %all-to-all-start) | async-done | bytes 196640 | tf_op jit(solution)/shard_map/all_to_all | solution.py:608
  75.0 4.4 %collective-permute-done.11.refs_1_ = bf16[128,768]{1,0:T(8,128)(2,1)S(1)} collective-permute-done((bf16[128,768]{1,0:T(8,128)(2,1)S(1)}, bf16[128,768]{1,0:T(8,128)(2,1)S(1)}, u32[]{:S(2)}, u32[]{:S(2)}) %collective-permute-start.11) | collective-permute-done | bytes 196640 | tf_op jit(solution)/shard_map/ppermute | solution.py:559
  79.3 3.7 %collective-permute-done.12.refs_2_ = bf16[128,768]{1,0:T(8,128)(2,1)S(1)} collective-permute-done((bf16[128,768]{1,0:T(8,128)(2,1)S(1)}, bf16[128,768]{1,0:T(8,128)(2,1)S(1)}, u32[]{:S(2)}, u32[]{:S(2)}) %collective-permute-start.12) | collective-permute-done | bytes 196640 | tf_op jit(solution)/shard_map/ppermute | solution.py:559
  83.8 4.4 %forward.1 = (f32[128,768]{1,0:T(8,128)S(1)}, bf16[128,768]{1,0:T(8,128)(2,1)S(1)}, bf16[128,768]{1,0:T(8,128)(2,1)S(1)}, bf16[128,768]{1,0:T(8,128)(2,1)S(1)}, ...) custom-call(s32[3]{0:T(128)S(1)} %copy-done.17, f32[16,768]{1,0:T(8,128)S(1)} %get-tuple-element.90.vec.refs_6_, ...), custom_call_target="tpu_custom_call" | custom-call | flops 1207959552 | bytes 6537228 | tf_op jit(solution)/shard_map/forward/pallas_call | solution.py:48
  89.5 2.3 %collective-permute-start.16 = (bf16[128,768]{1,0:T(8,128)(2,1)S(1)}, bf16[128,768]{1,0:T(8,128)(2,1)S(1)}, u32[]{:S(2)}, u32[]{:S(2)}) collective-permute-start(bf16[128,768]{1,0:T(8,128)(2,1)S(1)} %get-tuple-element.97), channel_id=1, source_target_pairs={{0,24},{8,16},{16,8},{24,0},{1,25},{9,17},{17,9},{25,1},{2,26},{10... | collective-permute-start | bytes 589832 | tf_op jit(solution)/shard_map/ppermute | solution.py:559
  91.8 2.2 %collective-permute-done.14.refs_1_ = bf16[128,768]{1,0:T(8,128)(2,1)S(1)} collective-permute-done((bf16[128,768]{1,0:T(8,128)(2,1)S(1)}, bf16[128,768]{1,0:T(8,128)(2,1)S(1)}, u32[]{:S(2)}, u32[]{:S(2)}) %collective-permute-start.14) | collective-permute-done | bytes 196640 | tf_op jit(solution)/shard_map/ppermute | solution.py:559
  94.1 3.5 %collective-permute-done.15.refs_2_ = bf16[128,768]{1,0:T(8,128)(2,1)S(1)} collective-permute-done((bf16[128,768]{1,0:T(8,128)(2,1)S(1)}, bf16[128,768]{1,0:T(8,128)(2,1)S(1)}, u32[]{:S(2)}, u32[]{:S(2)}) %collective-permute-start.15) | collective-permute-done | bytes 196640 | tf_op jit(solution)/shard_map/ppermute | solution.py:559
  102.1 2.3 %collective-permute-done.17.refs_5_ = bf16[128,768]{1,0:T(8,128)(2,1)S(1)} collective-permute-done((bf16[128,768]{1,0:T(8,128)(2,1)S(1)}, bf16[128,768]{1,0:T(8,128)(2,1)S(1)}, u32[]{:S(2)}, u32[]{:S(2)}) %collective-permute-start.17) | collective-permute-done | bytes 196640 | tf_op jit(solution)/shard_map/ppermute | solution.py:559
  104.4 3.5 %collective-permute-done.18.refs_6_ = bf16[128,768]{1,0:T(8,128)(2,1)S(1)} collective-permute-done((bf16[128,768]{1,0:T(8,128)(2,1)S(1)}, bf16[128,768]{1,0:T(8,128)(2,1)S(1)}, u32[]{:S(2)}, u32[]{:S(2)}) %collective-permute-start.18) | collective-permute-done | bytes 196640 | tf_op jit(solution)/shard_map/ppermute | solution.py:559
  107.9 4.3 %backward.1 = (f32[128,768]{1,0:T(8,128)S(1)}, bf16[128,768]{1,0:T(8,128)(2,1)S(1)}, bf16[128,768]{1,0:T(8,128)(2,1)S(1)}, bf16[128,768]{1,0:T(8,128)(2,1)S(1)}, bf16[8,200,768]{2,1,0:T(8,128)(2,1)S(1)}) custom-call(s32[3]{0:T(128)S(1)} %copy-done.18, bf16[8,192,768]{2,1,0:T(8,128)(2,1)S(1)} %bitcast.62, f32[512,768]{1,0:T(8,128)S(1)} %get-tuple-element.102.inner_ref, ...), custom_call_target="tpu_custom_call" | custom-call | flops 2415919104 | bytes 9756684 | tf_op jit(solution)/shard_map/backward/pallas_call | solution.py:48
  119.7 2.4 %collective-permute-done.20.refs_1_ = bf16[128,768]{1,0:T(8,128)(2,1)S(1)} collective-permute-done((bf16[128,768]{1,0:T(8,128)(2,1)}, bf16[128,768]{1,0:T(8,128)(2,1)S(1)}, u32[]{:S(2)}, u32[]{:S(2)}) %collective-permute-start.20) | collective-permute-done | bytes 196640 | tf_op jit(solution)/shard_map/ppermute | solution.py:559
  122.1 2.6 %collective-permute-done.21.refs_2_ = bf16[128,768]{1,0:T(8,128)(2,1)S(1)} collective-permute-done((bf16[128,768]{1,0:T(8,128)(2,1)}, bf16[128,768]{1,0:T(8,128)(2,1)S(1)}, u32[]{:S(2)}, u32[]{:S(2)}) %collective-permute-start.21) | collective-permute-done | bytes 196640 | tf_op jit(solution)/shard_map/ppermute | solution.py:559
  128.4 6.0 %collective-permute-start.23 = (bf16[192,128]{1,0:T(8,128)(2,1)S(1)}, bf16[192,128]{1,0:T(8,128)(2,1)S(1)}, u32[]{:S(2)}, u32[]{:S(2)}) collective-permute-start(bf16[192,128]{1,0:T(8,128)(2,1)S(1)} %get-tuple-element.116), channel_id=1, source_target_pairs={{0,2},{1,3},{2,0},{3,1},{4,6},{5,7},{6,4},{7,5},{8,10},{9,11},{10,... | collective-permute-start | bytes 147464 | tf_op jit(solution)/shard_map/ppermute | solution.py:577
  137.6 2.9 %collective-permute-done.24.refs_2_ = bf16[192,128]{1,0:T(8,128)(2,1)S(1)} collective-permute-done((bf16[192,128]{1,0:T(8,128)(2,1)S(1)}, bf16[192,128]{1,0:T(8,128)(2,1)S(1)}, u32[]{:S(2)}, u32[]{:S(2)}) %collective-permute-start.24) | collective-permute-done | bytes 49184 | tf_op jit(solution)/shard_map/ppermute | solution.py:577
  140.5 2.2 collective-permute-done.25.refs_3_
  142.8 11.0 %attend_back.1 = (bf16[4,128,192]{2,1,0:T(8,128)(2,1)S(1)}, bf16[4,128,384]{2,1,0:T(8,128)(2,1)S(1)}, bf16[4,128,384]{2,1,0:T(8,128)(2,1)S(1)}, f32[4,104,576]{2,1,0:T(8,128)S(1)}, bf16[4,104,576]{2,1,0:T(8,128)(2,1)S(1)}) custom-call(s32[3]{0:T(128)S(1)} %copy-done.20, bf16[8,128,768]{2,1,0:T(8,128)(2,1)} %all-gather.4.cloned.1.call-done.hid.hid_raw, ...), custom_call_target="tpu_custom_call" | custom-call | flops 1912602624 | bytes 5543948 | tf_op jit(solution)/shard_map/attend_back/pallas_call | solution.py:48
  162.7 2.9 %collective-permute-done.28.refs_1_ = bf16[104,576]{1,0:T(8,128)(2,1)S(1)} collective-permute-done((bf16[104,576]{1,0:T(8,128)(2,1)S(1)}, bf16[104,576]{1,0:T(8,128)(2,1)S(1)}, u32[]{:S(2)}, u32[]{:S(2)}) %collective-permute-start.28) | collective-permute-done | bytes 119840 | tf_op jit(solution)/shard_map/ppermute | solution.py:559
  165.6 3.3 %collective-permute-done.29.refs_2_ = bf16[104,576]{1,0:T(8,128)(2,1)S(1)} collective-permute-done((bf16[104,576]{1,0:T(8,128)(2,1)S(1)}, bf16[104,576]{1,0:T(8,128)(2,1)S(1)}, u32[]{:S(2)}, u32[]{:S(2)}) %collective-permute-start.29) | collective-permute-done | bytes 119840 | tf_op jit(solution)/shard_map/ppermute | solution.py:559
  173.3 2.3 %input_grad.1 = bf16[4,128,768]{2,1,0:T(8,128)(2,1)} custom-call(s32[3]{0:T(128)S(1)} %copy-done.21, bf16[4,128,192]{2,1,0:T(8,128)(2,1)S(1)} %get-tuple-element.123.dq, bf16[4,128,384]{2,1,0:T(8,128)(2,1)S(1)} %get-tuple-element.124.mine, bf16[4,128,384]{2,1,0:T(8,128)(2,1)S(1)} %collective-permute-done.27.recv, bf16[768,576]{1,0:T(8,128)(2,1)S(1)} %bitcast.49), custom_call_target="tpu_custom_call" | custom-call | flops 452984832 | bytes 2654220 | tf_op jit(solution)/shard_map/input_grad/pallas_call | solution.py:48
  177.4 5.1 %all-to-all-start.1 = ((bf16[4,128,768]{2,1,0:T(8,128)(2,1)}), bf16[4,128,768]{2,1,0:T(8,128)(2,1)S(1)}, u32[]{:S(2)}, u32[]{:S(2)}) async-start(bf16[4,128,768]{2,1,0:T(8,128)(2,1)} %input_grad.1), calls=%async_computation.2 | async-start | bytes 1572864 | tf_op jit(solution)/shard_map/all_to_all | solution.py:608
  189.2 4.8 %collective-permute-done.35.refs_1_ = bf16[4,24,576]{2,1,0:T(8,128)(2,1)S(1)} collective-permute-done((bf16[4,24,576]{2,1,0:T(8,128)(2,1)S(1)}, bf16[4,24,576]{2,1,0:T(8,128)(2,1)S(1)}, u32[]{:S(2)}, u32[]{:S(2)}) %collective-permute-start.35) | collective-permute-done | bytes 110624 | tf_op jit(solution)/shard_map/ppermute | solution.py:559
  194.0 6.6 %collective-permute-done.36.refs_2_ = bf16[4,24,576]{2,1,0:T(8,128)(2,1)S(1)} collective-permute-done((bf16[4,24,576]{2,1,0:T(8,128)(2,1)S(1)}, bf16[4,24,576]{2,1,0:T(8,128)(2,1)S(1)}, u32[]{:S(2)}, u32[]{:S(2)}) %collective-permute-start.36) | collective-permute-done | bytes 110624 | tf_op jit(solution)/shard_map/ppermute | solution.py:559
  202.3 2.4 %finish_inner.1 = (f32[96,3072]{1,0:T(8,128)}, f32[384,768]{1,0:T(8,128)}, f32[8,768]{1,0:T(8,128)S(1)}) custom-call(s32[3]{0:T(128)S(1)} %copy-done.21, bf16[200,768]{1,0:T(8,128)(2,1)S(1)} %bitcast.54, bf16[200,768]{1,0:T(8,128)(2,1)S(1)} %collective-permute-done.34.refs_1_, bf16[200,768]{1,0:T(8,128)(2,1)S(1)} %collective-permute-done.41.refs_2_, ...), custom_call_target="tpu_custom_call" | custom-call | bytes 3612684 | tf_op jit(solution)/shard_map/finish_inner/pallas_call | solution.py:48
  (219 shorter events, 78.9 us)
Async XLA Ops:
  7.3 35.9 %all-gather.4.cloned.1.call-start = ((), (), s32[]{:S(2)}) async-start(), calls=%async_computation.4 | async-start | bytes 1769472 | tf_op jit(solution)/shard_map/all_gather | solution.py:649
  8.0 75.7 %all-gather.6.cloned.1.call-start = ((), (), s32[]{:S(2)}) async-start(), calls=%async_computation.7 | async-start | bytes 2654208 | tf_op jit(solution)/shard_map/all_gather | solution.py:734
  9.9 7.3 %collective-permute-start.1 = (bf16[48,576]{1,0:T(8,128)(2,1)S(1)}, bf16[48,576]{1,0:T(8,128)(2,1)S(1)}, u32[]{:S(2)}, u32[]{:S(2)}) collective-permute-start(bf16[48,576]{1,0:T(8,128)(2,1)S(1)} %get-tuple-element.85), channel_id=1, source_target_pairs={{0,4},{1,5},{2,6},{3,7},{4,0},{5,1},{6,2},{7,3},{8,12},{9,13},{10,... | collective-permute-start | bytes 165896 | tf_op jit(solution)/shard_map/ppermute | solution.py:577
  24.5 18.0 %collective-permute-start.7 = (bf16[2,4,48,576]{3,2,1,0:T(8,128)(2,1)S(1)}, bf16[2,4,48,576]{3,2,1,0:T(8,128)(2,1)S(1)}, u32[]{:S(2)}, u32[]{:S(2)}) collective-permute-start(bf16[2,4,48,576]{3,2,1,0:T(8,128)(2,1)S(1)} %stack.29.mine), channel_id=1, source_target_pairs={{0,1},{1,0},{2,3},{3,2},{4,5},{5,4},{6,7},{7,6},{8,9},{9,8},{10,11... | collective-permute-start | bytes 1327112 | tf_op jit(solution)/shard_map/ppermute | solution.py:572
  25.4 11.2 %collective-permute-start.4 = (bf16[64,768]{1,0:T(8,128)(2,1)S(1)}, bf16[64,768]{1,0:T(8,128)(2,1)S(1)}, u32[]{:S(2)}, u32[]{:S(2)}) collective-permute-start(bf16[64,768]{1,0:T(8,128)(2,1)S(1)} %cut_output.1.refs_0_), channel_id=1, source_target_pairs={{0,2},{1,3},{2,0},{3,1},{4,6},{5,7},{6,4},{7,5},{8,10},{9,11},{10,... | collective-permute-start | bytes 294920 | tf_op jit(solution)/shard_map/ppermute | solution.py:577
  27.8 11.2 %collective-permute-start.5 = (bf16[64,768]{1,0:T(8,128)(2,1)S(1)}, bf16[64,768]{1,0:T(8,128)(2,1)S(1)}, u32[]{:S(2)}, u32[]{:S(2)}) collective-permute-start(bf16[64,768]{1,0:T(8,128)(2,1)S(1)} %cut_output.1.refs_0_), channel_id=1, source_target_pairs={{0,4},{1,5},{2,6},{3,7},{4,0},{5,1},{6,2},{7,3},{8,12},{9,13},{10,... | collective-permute-start | bytes 294920 | tf_op jit(solution)/shard_map/ppermute | solution.py:577
  29.4 13.0 %collective-permute-start.6 = (bf16[64,768]{1,0:T(8,128)(2,1)S(1)}, bf16[64,768]{1,0:T(8,128)(2,1)S(1)}, u32[]{:S(2)}, u32[]{:S(2)}) collective-permute-start(bf16[64,768]{1,0:T(8,128)(2,1)S(1)} %cut_output.1.refs_0_), channel_id=1, source_target_pairs={{0,6},{1,7},{2,4},{3,5},{4,2},{5,3},{6,0},{7,1},{8,14},{9,15},{10,... | collective-permute-start | bytes 294920 | tf_op jit(solution)/shard_map/ppermute | solution.py:577
  44.1 12.5 %collective-permute-start.9 = (bf16[4,64,768]{2,1,0:T(8,128)(2,1)S(1)}, bf16[4,64,768]{2,1,0:T(8,128)(2,1)S(1)}, u32[]{:S(2)}, u32[]{:S(2)}) collective-permute-start(bf16[4,64,768]{2,1,0:T(8,128)(2,1)S(1)} %stack.28.refs_0_), channel_id=1, source_target_pairs={{0,16},{8,24},{16,0},{24,8},{1,17},{9,25},{17,1},{25,9},{2,18},{10... | collective-permute-start | bytes 1179656 | tf_op jit(solution)/shard_map/ppermute | solution.py:559
  57.0 13.8 %all-to-all-start = ((bf16[4,192,128]{2,1,0:T(8,128)(2,1)}), bf16[4,192,128]{2,1,0:T(8,128)(2,1)S(1)}, u32[]{:S(2)}, u32[]{:S(2)}) async-start(bf16[4,192,128]{2,1,0:T(8,128)(2,1)} %get-tuple-element.88), calls=%async_computation | async-start | bytes 393216 | tf_op jit(solution)/shard_map/all_to_all | solution.py:608
  60.4 97.6 %reduce-scatter.3.cloned.1.call-start = ((), (), s32[]{:S(2)}) async-start(), calls=%async_computation.5 | async-start | bytes 2764800 | tf_op jit(solution)/shard_map/reduce_scatter | solution.py:780
  71.4 7.9 %collective-permute-start.11 = (bf16[128,768]{1,0:T(8,128)(2,1)S(1)}, bf16[128,768]{1,0:T(8,128)(2,1)S(1)}, u32[]{:S(2)}, u32[]{:S(2)}) collective-permute-start(bf16[128,768]{1,0:T(8,128)(2,1)S(1)} %get-tuple-element.93.refs_0_), channel_id=1, source_target_pairs={{0,8},{8,0},{16,24},{24,16},{1,9},{9,1},{17,25},{25,17},{2,10},{10... | collective-permute-start | bytes 589832 | tf_op jit(solution)/shard_map/ppermute | solution.py:559
  72.9 10.1 %collective-permute-start.12 = (bf16[128,768]{1,0:T(8,128)(2,1)S(1)}, bf16[128,768]{1,0:T(8,128)(2,1)S(1)}, u32[]{:S(2)}, u32[]{:S(2)}) collective-permute-start(bf16[128,768]{1,0:T(8,128)(2,1)S(1)} %get-tuple-element.93.refs_0_), channel_id=1, source_target_pairs={{0,16},{8,24},{16,0},{24,8},{1,17},{9,25},{17,1},{25,9},{2,18},{10... | collective-permute-start | bytes 589832 | tf_op jit(solution)/shard_map/ppermute | solution.py:559
  73.4 10.3 %collective-permute-start.13 = (bf16[128,768]{1,0:T(8,128)(2,1)S(1)}, bf16[128,768]{1,0:T(8,128)(2,1)}, u32[]{:S(2)}, u32[]{:S(2)}) collective-permute-start(bf16[128,768]{1,0:T(8,128)(2,1)S(1)} %get-tuple-element.93.refs_0_), channel_id=1, source_target_pairs={{0,24},{8,16},{16,8},{24,0},{1,25},{9,17},{17,9},{25,1},{2,26},{10... | collective-permute-start | bytes 589832 | tf_op jit(solution)/shard_map/ppermute | solution.py:559
  88.9 8.7 %collective-permute-start.15 = (bf16[128,768]{1,0:T(8,128)(2,1)S(1)}, bf16[128,768]{1,0:T(8,128)(2,1)S(1)}, u32[]{:S(2)}, u32[]{:S(2)}) collective-permute-start(bf16[128,768]{1,0:T(8,128)(2,1)S(1)} %get-tuple-element.96), channel_id=1, source_target_pairs={{0,16},{8,24},{16,0},{24,8},{1,17},{9,25},{17,1},{25,9},{2,18},{10... | collective-permute-start | bytes 589832 | tf_op jit(solution)/shard_map/ppermute | solution.py:559
  89.5 8.1 %collective-permute-start.16 = (bf16[128,768]{1,0:T(8,128)(2,1)S(1)}, bf16[128,768]{1,0:T(8,128)(2,1)S(1)}, u32[]{:S(2)}, u32[]{:S(2)}) collective-permute-start(bf16[128,768]{1,0:T(8,128)(2,1)S(1)} %get-tuple-element.97), channel_id=1, source_target_pairs={{0,24},{8,16},{16,8},{24,0},{1,25},{9,17},{17,9},{25,1},{2,26},{10... | collective-permute-start | bytes 589832 | tf_op jit(solution)/shard_map/ppermute | solution.py:559
  100.1 7.8 %collective-permute-start.18 = (bf16[128,768]{1,0:T(8,128)(2,1)S(1)}, bf16[128,768]{1,0:T(8,128)(2,1)S(1)}, u32[]{:S(2)}, u32[]{:S(2)}) collective-permute-start(bf16[128,768]{1,0:T(8,128)(2,1)S(1)} %get-tuple-element.105.refs_4_), channel_id=1, source_target_pairs={{0,16},{8,24},{16,0},{24,8},{1,17},{9,25},{17,1},{25,9},{2,18},{10... | collective-permute-start | bytes 589832 | tf_op jit(solution)/shard_map/ppermute | solution.py:559
  100.2 7.7 %collective-permute-start.19 = (bf16[128,768]{1,0:T(8,128)(2,1)S(1)}, bf16[128,768]{1,0:T(8,128)(2,1)S(1)}, u32[]{:S(2)}, u32[]{:S(2)}) collective-permute-start(bf16[128,768]{1,0:T(8,128)(2,1)S(1)} %get-tuple-element.105.refs_4_), channel_id=1, source_target_pairs={{0,24},{8,16},{16,8},{24,0},{1,25},{9,17},{17,9},{25,1},{2,26},{10... | collective-permute-start | bytes 589832 | tf_op jit(solution)/shard_map/ppermute | solution.py:559
  115.8 89.6 %reduce-scatter.5.cloned.1.call-start = ((), (), s32[]{:S(2)}) async-start(), calls=%async_computation.6 | async-start | bytes 1437696 | tf_op jit(solution)/shard_map/reduce_scatter | solution.py:792
  116.7 8.0 %collective-permute-start.21 = (bf16[128,768]{1,0:T(8,128)(2,1)}, bf16[128,768]{1,0:T(8,128)(2,1)S(1)}, u32[]{:S(2)}, u32[]{:S(2)}) collective-permute-start(bf16[128,768]{1,0:T(8,128)(2,1)} %copy-done.36), channel_id=1, source_target_pairs={{0,16},{8,24},{16,0},{24,8},{1,17},{9,25},{17,1},{25,9},{2,18},{10... | collective-permute-start | bytes 589832 | tf_op jit(solution)/shard_map/ppermute | solution.py:559
  128.4 9.2 %collective-permute-start.23 = (bf16[192,128]{1,0:T(8,128)(2,1)S(1)}, bf16[192,128]{1,0:T(8,128)(2,1)S(1)}, u32[]{:S(2)}, u32[]{:S(2)}) collective-permute-start(bf16[192,128]{1,0:T(8,128)(2,1)S(1)} %get-tuple-element.116), channel_id=1, source_target_pairs={{0,2},{1,3},{2,0},{3,1},{4,6},{5,7},{6,4},{7,5},{8,10},{9,11},{10,... | collective-permute-start | bytes 147464 | tf_op jit(solution)/shard_map/ppermute | solution.py:577
  134.4 8.4 %collective-permute-start.25 = (bf16[192,128]{1,0:T(8,128)(2,1)S(1)}, bf16[192,128]{1,0:T(8,128)(2,1)S(1)}, u32[]{:S(2)}, u32[]{:S(2)}) collective-permute-start(bf16[192,128]{1,0:T(8,128)(2,1)S(1)} %get-tuple-element.118), channel_id=1, source_target_pairs={{0,6},{1,7},{2,4},{3,5},{4,2},{5,3},{6,0},{7,1},{8,14},{9,15},{10,... | collective-permute-start | bytes 147464 | tf_op jit(solution)/shard_map/ppermute | solution.py:577
  159.1 14.2 %collective-permute-start.27 = (bf16[4,128,384]{2,1,0:T(8,128)(2,1)S(1)}, bf16[4,128,384]{2,1,0:T(8,128)(2,1)S(1)}, u32[]{:S(2)}, u32[]{:S(2)}) collective-permute-start(bf16[4,128,384]{2,1,0:T(8,128)(2,1)S(1)} %copy-done.29), channel_id=1, source_target_pairs={{0,1},{1,0},{2,3},{3,2},{4,5},{5,4},{6,7},{7,6},{8,9},{9,8},{10,11... | collective-permute-start | bytes 1179656 | tf_op jit(solution)/shard_map/ppermute | solution.py:572
  160.6 8.4 %collective-permute-start.29 = (bf16[104,576]{1,0:T(8,128)(2,1)S(1)}, bf16[104,576]{1,0:T(8,128)(2,1)S(1)}, u32[]{:S(2)}, u32[]{:S(2)}) collective-permute-start(bf16[104,576]{1,0:T(8,128)(2,1)S(1)} %get-tuple-element.127), channel_id=1, source_target_pairs={{0,16},{8,24},{16,0},{24,8},{1,17},{9,25},{17,1},{25,9},{2,18},{10... | collective-permute-start | bytes 359432 | tf_op jit(solution)/shard_map/ppermute | solution.py:559
  161.2 7.8 %collective-permute-start.30 = (bf16[104,576]{1,0:T(8,128)(2,1)S(1)}, bf16[104,576]{1,0:T(8,128)(2,1)S(1)}, u32[]{:S(2)}, u32[]{:S(2)}) collective-permute-start(bf16[104,576]{1,0:T(8,128)(2,1)S(1)} %get-tuple-element.128), channel_id=1, source_target_pairs={{0,24},{8,16},{16,8},{24,0},{1,25},{9,17},{17,9},{25,1},{2,26},{10... | collective-permute-start | bytes 359432 | tf_op jit(solution)/shard_map/ppermute | solution.py:559
  169.0 8.3 %collective-permute-start.34 = (bf16[200,768]{1,0:T(8,128)(2,1)S(1)}, bf16[200,768]{1,0:T(8,128)(2,1)S(1)}, u32[]{:S(2)}, u32[]{:S(2)}) collective-permute-start(bf16[200,768]{1,0:T(8,128)(2,1)S(1)} %bitcast.51), channel_id=1, source_target_pairs={{0,8},{8,0},{16,24},{24,16},{1,9},{9,1},{17,25},{25,17},{2,10},{10... | collective-permute-start | bytes 921608 | tf_op jit(solution)/shard_map/ppermute | solution.py:559
  177.4 32.1 %all-to-all-start.1 = ((bf16[4,128,768]{2,1,0:T(8,128)(2,1)}), bf16[4,128,768]{2,1,0:T(8,128)(2,1)S(1)}, u32[]{:S(2)}, u32[]{:S(2)}) async-start(bf16[4,128,768]{2,1,0:T(8,128)(2,1)} %input_grad.1), calls=%async_computation.2 | async-start | bytes 1572864 | tf_op jit(solution)/shard_map/all_to_all | solution.py:608
  182.5 19.8 %collective-permute-start.41 = (bf16[200,768]{1,0:T(8,128)(2,1)S(1)}, bf16[200,768]{1,0:T(8,128)(2,1)S(1)}, u32[]{:S(2)}, u32[]{:S(2)}) collective-permute-start(bf16[200,768]{1,0:T(8,128)(2,1)S(1)} %bitcast.52), channel_id=1, source_target_pairs={{0,16},{8,24},{16,0},{24,8},{1,17},{9,25},{17,1},{25,9},{2,18},{10... | collective-permute-start | bytes 921608 | tf_op jit(solution)/shard_map/ppermute | solution.py:559
  184.0 18.3 %collective-permute-start.42 = (bf16[200,768]{1,0:T(8,128)(2,1)S(1)}, bf16[200,768]{1,0:T(8,128)(2,1)S(1)}, u32[]{:S(2)}, u32[]{:S(2)}) collective-permute-start(bf16[200,768]{1,0:T(8,128)(2,1)S(1)} %bitcast.53), channel_id=1, source_target_pairs={{0,24},{8,16},{16,8},{24,0},{1,25},{9,17},{17,9},{25,1},{2,26},{10... | collective-permute-start | bytes 921608 | tf_op jit(solution)/shard_map/ppermute | solution.py:559
  185.1 9.0 %collective-permute-start.35 = (bf16[4,24,576]{2,1,0:T(8,128)(2,1)S(1)}, bf16[4,24,576]{2,1,0:T(8,128)(2,1)S(1)}, u32[]{:S(2)}, u32[]{:S(2)}) collective-permute-start(bf16[4,24,576]{2,1,0:T(8,128)(2,1)S(1)} %stack.31.refs_0_), channel_id=1, source_target_pairs={{0,8},{8,0},{16,24},{24,16},{1,9},{9,1},{17,25},{25,17},{2,10},{10... | collective-permute-start | bytes 331784 | tf_op jit(solution)/shard_map/ppermute | solution.py:559
  186.0 14.6 %collective-permute-start.36 = (bf16[4,24,576]{2,1,0:T(8,128)(2,1)S(1)}, bf16[4,24,576]{2,1,0:T(8,128)(2,1)S(1)}, u32[]{:S(2)}, u32[]{:S(2)}) collective-permute-start(bf16[4,24,576]{2,1,0:T(8,128)(2,1)S(1)} %stack.31.refs_0_), channel_id=1, source_target_pairs={{0,16},{8,24},{16,0},{24,8},{1,17},{9,25},{17,1},{25,9},{2,18},{10... | collective-permute-start | bytes 331784 | tf_op jit(solution)/shard_map/ppermute | solution.py:559
  187.6 13.1 %collective-permute-start.37 = (bf16[4,24,576]{2,1,0:T(8,128)(2,1)S(1)}, bf16[4,24,576]{2,1,0:T(8,128)(2,1)S(1)}, u32[]{:S(2)}, u32[]{:S(2)}) collective-permute-start(bf16[4,24,576]{2,1,0:T(8,128)(2,1)S(1)} %stack.31.refs_0_), channel_id=1, source_target_pairs={{0,24},{8,16},{16,8},{24,0},{1,25},{9,17},{17,9},{25,1},{2,26},{10... | collective-permute-start | bytes 331784 | tf_op jit(solution)/shard_map/ppermute | solution.py:559
  206.3 7.8 %collective-permute-start.39 = (bf16[104,768]{1,0:T(8,128)(2,1)}, bf16[104,768]{1,0:T(8,128)(2,1)S(1)}, u32[]{:S(2)}, u32[]{:S(2)}) collective-permute-start(bf16[104,768]{1,0:T(8,128)(2,1)} %bitcast.57), channel_id=1, source_target_pairs={{0,16},{8,24},{16,0},{24,8},{1,17},{9,25},{17,1},{25,9},{2,18},{10... | collective-permute-start | bytes 479240 | tf_op jit(solution)/shard_map/ppermute | solution.py:559
  (65 other events, 697.1 us)
Sparse Core Ops, SparseCore 0:
  9.8 29.9 all-gather.3
  43.3 33.4 all-gather.5
  116.0 37.2 reduce-scatter.2
  158.2 34.4 reduce-scatter.4

commit v4 on v3

--- a/solution.py
+++ b/solution.py
@@ -191,7 +191,7 @@
 def attend_kernel(ids, w, be, bn, sk, sq, hid, ours, theirs, *refs):
     att = refs[0]
     kept = refs[1:5]
-    qo, ko, vo, lse, qs, sems = refs[5:]
+    qo, ko, vo, lse, qs, s_all, p_all, sems = refs[5:]
     copies = [
         pltpu.make_async_copy(here, there, sems.at[i])
         for i, (here, there) in enumerate(zip((qo, ko, vo, lse), kept))
@@ -218,23 +218,30 @@
         qo[k] = qs[2 * (ids[1] ^ k) + core]
     for copy in copies[:3]:
         copy.start()
-    for k in range(chips):
-        chip = ids[1] ^ k
-        same = sq[chip] == sk[...]
-        logs = jnp.zeros((piece_len, 128), f32)
-        parts = []
-        for head in range(heads):
-            cols = slice(head * size, (head + 1) * size)
-            scores = right_product(qo[k, :, cols], ko[:, cols])
-            scores = scores + bias_rows(be[head * chips + chip], bn[...], same)
+    logs = [jnp.zeros((piece_len, 128), f32)] * chips
+    parts = [[] for _ in range(chips)]
+    for head in range(heads):
+        cols = slice(head * size, (head + 1) * size)
+        queries = qo[:, :, cols].reshape(chips * piece_len, size)
+        s_all[...] = right_product(queries, ko[:, cols])
+        shares = []
+        for k in range(chips):
+            chip = ids[1] ^ k
+            rows = slice(k * piece_len, (k + 1) * piece_len)
+            same = sq[chip] == sk[...]
+            scores = s_all[rows, :] + bias_rows(be[head * chips + chip], bn[...], same)
             top = jnp.max(scores, -1, keepdims=True)
             powers = jnp.exp(scores - top)
             total = jnp.sum(powers, -1, keepdims=True)
-            probs = (powers * (1.0 / total)).astype(bf16)
-            parts.append(matmul(probs, vo[:, cols]))
-            logs = jnp.where(lane == head, top + jnp.log(total), logs)
-        att[chip] = jnp.concatenate(parts, 1).T.astype(bf16)
-        lse[k] = logs
+            p_all[rows, :] = powers.astype(bf16)
+            shares.append(1.0 / total)
+            logs[k] = jnp.where(lane == head, top + jnp.log(total), logs[k])
+        out = matmul(p_all[...], vo[:, cols])
+        for k in range(chips):
+            parts[k].append(out[k * piece_len : (k + 1) * piece_len] * shares[k])
+    for k in range(chips):
+        att[ids[1] ^ k] = jnp.concatenate(parts[k], 1).T.astype(bf16)
+        lse[k] = logs[k]
     copies[3].start()
     for copy in copies:
         copy.wait()
@@ -242,14 +249,17 @@
 
 def attend_back_kernel(ids, hid_raw, q_raw, k_raw, v_raw, lse_raw, be, bn, sk, sq, *refs):
     chips, piece_len, width = q_raw.shape
-    ga = refs[:chips]
+    ga_raw = refs[:chips]
     dq, mine, other, dw_mine, dw_other = refs[chips : chips + 5]
-    hid, q, k, v, lse, ds_all, p_all, dkv, dws, sems = refs[chips + 5 :]
+    hid, q, k, v, lse, ga, s_all, g_all, ds_all, p_all, dkv, dws, sems = refs[chips + 5 :]
     copies = [
         pltpu.make_async_copy(there, here, sems.at[i])
         for i, (there, here) in enumerate(
             zip((q_raw, k_raw, v_raw, lse_raw, hid_raw), (q, k, v, lse, hid))
         )
+    ]
+    copies[4:4] = [
+        pltpu.make_async_copy(there, ga.at[i], sems.at[5 + i]) for i, there in enumerate(ga_raw)
     ]
     for copy in copies:
         copy.start()
@@ -260,28 +270,30 @@
     dks = []
     dvs = []
     dqs = [[None] * heads for _ in range(chips)]
-    for copy in copies[:4]:
+    for copy in copies[:-1]:
         copy.wait()
-    gas = [g[...].astype(f32).T.astype(bf16) for g in ga]
+    gas = jnp.concatenate([ga[i].astype(f32).T.astype(bf16) for i in range(chips)], 0)
     for head in range(heads):
         cols = slice(head * size, (head + 1) * size)
         key = k[:, cols]
         value = v[:, cols]
+        queries = q[:, :, cols].reshape(chips * piece_len, size)
+        grads = gas[:, cols]
+        s_all[...] = right_product(queries, key)
+        g_all[...] = right_product(grads, value)
         for i in range(chips):
             chip = ids[1] ^ i
             rows = slice(i * piece_len, (i + 1) * piece_len)
             same = sq[chip] == sk[...]
-            scores = right_product(q[i, :, cols], key)
-            scores = scores + bias_rows(be[head * chips + chip], bn[...], same)
+            scores = s_all[rows, :] + bias_rows(be[head * chips + chip], bn[...], same)
             probs = jnp.exp(scores - lse[i, :, head : head + 1])
-            grad = right_product(gas[i][:, cols], value)
+            grad = g_all[rows, :]
             weighted = jnp.sum(probs * grad, -1, keepdims=True)
-            ds = (probs * (grad - weighted)).astype(bf16)
-            ds_all[rows, :] = ds
+            ds_all[rows, :] = (probs * (grad - weighted)).astype(bf16)
             p_all[rows, :] = probs.astype(bf16)
-            dqs[i][head] = (matmul(ds, key) * (size**-0.5)).astype(bf16)
-        queries = q[:, :, cols].reshape(chips * piece_len, size)
-        grads = jnp.concatenate([g[:, cols] for g in gas], 0)
+        grad_q = (matmul(ds_all[...], key) * (size**-0.5)).astype(bf16)
+        for i in range(chips):
+            dqs[i][head] = grad_q[i * piece_len : (i + 1) * piece_len]
         dks.append(left_product(ds_all[...], queries).astype(bf16))
         dvs.append(left_product(p_all[...], grads).astype(bf16))
     for i in range(chips):
@@ -292,7 +304,7 @@
         chip = ids[1] ^ i
         mine[i] = dkv[2 * chip + core]
         other[i] = dkv[2 * chip + 1 - core]
-    copies[4].wait()
+    copies[-1].wait()
     _, _, model = hid.shape
     tokens = hid[...].reshape(pieces * piece_len, model)
     owned = jnp.concatenate([hid[2 * (ids[1] ^ i) + core] for i in range(chips)], 0)
@@ -429,8 +441,10 @@
     x = refs[:parts]
     grads = refs[parts : 2 * parts]
     outs = refs[2 * parts : 3 * parts]
-    rest = refs[3 * parts :]
+    out = refs[3 * parts]
     rows = grads[0].shape[0]
+    pieces, tall, model = out.shape
+    units = (tall - 8) // 2
     weight1, weight2 = two_weights(both)
     gm = jnp.concatenate([r[...] for r in grads], 0)
     grad_act = right_product(gm, weight2)
@@ -442,39 +456,42 @@
     for i in range(parts):
         outs[i][...] = first[i * rows : (i + 1) * rows].astype(outs[i].dtype)
     tokens = jnp.concatenate([r[...] for r in x], 0)
-    inner = left_product(tokens, gi).astype(bf16)
-    outer = left_product(act[...], gm).astype(bf16)
+    out[:, :units, :] = left_product(tokens, gi).astype(bf16).reshape(pieces, units, model)
+    out[:, units : 2 * units, :] = (
+        left_product(act[...], gm).astype(bf16).reshape(pieces, units, model)
+    )
     total = jnp.sum(gi.astype(f32), 0, keepdims=True)
     vectors = [sums[i : i + 1, :] for i in range(3)] + [total]
-
-    def write(place_of):
-        for piece in range(inner.shape[0] // units):
-            out, at = place_of(piece)
-            span = slice(piece * units, (piece + 1) * units)
-            out[at, :units, :] = inner[span]
-            out[at, units : 2 * units, :] = outer[span]
-            put_vectors(out, piece, at, 2 * units, vectors, units)
-
-    units = (rest[0].shape[1] - 8) // 2
-    write(lambda piece: (rest[0], piece))
+    for piece in range(pieces):
+        put_vectors(out, piece, piece, 2 * units, vectors, units)
 
 
 def residual_kernel(ids, mix, normed, inverse, vec, wo, *refs, parts):
+    recv = refs[:parts]
+    low, sums, res_raw = refs[parts : parts + 3]
+    back_raw = refs[parts + 3 : -3]
+    res, back, sems = refs[-3:]
     first = mix[...]
-    for r in refs[:parts]:
+    for r in recv:
         first = first + r[...].astype(f32)
-    res, low, sums = refs[parts : parts + 3]
     n1 = normed[...]
     grad = norm_back(first, n1, inverse[:, 0:1], vec[3:4, :])
     rounded = grad.astype(bf16)
-    for k, back in enumerate(refs[parts + 3 :]):
-        back[...] = right_product(wo[ids[1] ^ k], rounded).astype(bf16)
+    copies = []
+    for k, out in enumerate(back_raw):
+        back[k] = right_product(wo[ids[1] ^ k], rounded).astype(bf16)
+        copies.append(pltpu.make_async_copy(back.at[k], out, sems.at[k]))
+        copies[-1].start()
     res[...] = grad
+    copies.append(pltpu.make_async_copy(res, res_raw, sems.at[len(back_raw)]))
+    copies[-1].start()
     low[...] = rounded
     sums[0:1, :] = jnp.sum(first * n1, 0, keepdims=True)
     sums[1:2, :] = jnp.sum(first, 0, keepdims=True)
     sums[2:3, :] = jnp.sum(rounded.astype(f32), 0, keepdims=True)
     sums[3:, :] = jnp.zeros((5, sums.shape[1]), f32)
+    for copy in copies:
+        copy.wait()
 
 
 def put_vectors(out, piece, at, row, vectors, rows):
@@ -484,7 +501,10 @@
     out[at, row : row + 8, :] = jnp.broadcast_to(line, (8, out.shape[2])).astype(bf16)
 
 
-def output_grad_kernel(gb, sums, att, out):
+def output_grad_kernel(gb, sums, att, above, stacked, out, sems):
+    tall = above.shape[1]
+    first = pltpu.make_async_copy(above, stacked.at[:, pl.ds(0, tall), :], sems.at[0])
+    first.start()
     rows = out.shape[1] - 8
     grad = gb[...]
     vectors = [sums[i : i + 1, :] for i in range(3)]
@@ -494,6 +514,10 @@
             piece = 2 * chip + i
             out[piece, :rows] = part[i * rows : (i + 1) * rows]
             put_vectors(out, piece, piece, rows, vectors, rows)
+    second = pltpu.make_async_copy(out, stacked.at[:, pl.ds(tall, rows + 8), :], sems.at[1])
+    second.start()
+    first.wait()
+    second.wait()
 
 
 def ordered(ids, refs, scratch):
@@ -502,7 +526,7 @@
 
 
 def finish_inner_kernel(ids, *refs, parts):
-    inner, outer, vectors, scratch = refs[parts:]
+    inner, outer, output, vectors, scratch = refs[parts:]
     ordered(ids, refs[:parts], scratch)
     rows = inner.shape[0]
     units = outer.shape[0] // parts
@@ -523,15 +547,12 @@
         vectors[g : g + 1, :] = line
         total = total + line
     vectors[parts : parts + 1, :] = total
-
-
-def finish_output_kernel(p0, p1, p2, p3, out, vectors):
-    rows = out.shape[0]
-    total = p0[...].astype(f32)
-    for r in (p1, p2, p3):
-        total = total + r[...].astype(f32)
-    out[...] = total[:rows]
-    vectors[...] = total[rows:]
+    if scratch.shape[1] > at + 8:
+        last = scratch[0, at + 8 :, :].astype(f32)
+        for g in range(1, parts):
+            last = last + scratch[g, at + 8 :, :].astype(f32)
+        output[...] = last[:rows]
+        vectors[parts + 1 : parts + 2, :] = last[rows : rows + 1]
 
 
 def finish_kernel(ids, *refs):
@@ -630,7 +651,12 @@
     return run_kernel(
         functools.partial(finish_inner_kernel, parts=groups),
         "finish_inner",
-        [((rows, groups * model), f32), ((groups * rows, model), f32), ((8, model), f32)],
+        [
+            ((rows, groups * model), f32),
+            ((groups * rows, model), f32),
+            ((rows, model), f32),
+            ((8, model), f32),
+        ],
         (ids, *shares),
         scratch=[pltpu.VMEM((groups,) + share.shape, bf16)],
         scalars=1,
@@ -751,13 +777,15 @@
             scratch=[pltpu.VMEM(*spec) for spec in kept]
             + [
                 pltpu.VMEM((self.splits, piece_len, width), bf16),
+                pltpu.VMEM((chips * piece_len, tokens), f32),
+                pltpu.VMEM((chips * piece_len, tokens), bf16),
                 pltpu.SemaphoreType.DMA((len(kept),)),
             ],
             scalars=1,
             raw_outs=range(1, 1 + len(kept)),
             flops=6 * tokens * model * width + 2 * tokens * tokens * width,
             powers=tokens * tokens * 3 // 2,
-            grant=12 << 20,
+            grant=16 << 20,
         )
         out_half = stack(tied(self.out_half, att), self.out_next)
         half = model // self.splits // 2
@@ -773,36 +801,31 @@
         att = along_line(att)
         return att
 
-    def inner_shapes(self, tall):
-        return [((self.splits, tall, self.model), bf16)]
-
     def inner_grads(self, stacked):
-        self.share = lax.psum_scatter(stacked, "seq", scatter_dimension=0, tiled=False)
+        self.stacked = stacked
 
     def output_grad(self, attended, grad_branch, sums):
         chips, model = self.chips, self.model
+        rows = model // self.splits + 8
+        below = self.stacked.shape[1]
         (stacked,) = run_kernel(
             output_grad_kernel,
             "output_grad",
-            [((self.splits, model // self.splits + 8, model), bf16)],
-            (grad_branch, sums, attended),
+            [((self.splits, below + rows, model), bf16)],
+            (grad_branch, sums, attended, self.stacked),
+            scratch=[
+                pltpu.VMEM((self.splits, rows, model), bf16),
+                pltpu.SemaphoreType.DMA((2,)),
+            ],
+            raw_outs=(0,),
             flops=2 * self.piece_len * model * model,
         )
-        stacked = tied(stacked, self.share)
-        self.output_share = lax.psum_scatter(stacked, "seq", scatter_dimension=0, tiled=False)
+        self.share = lax.psum_scatter(stacked, "seq", scatter_dimension=0, tiled=False)
 
     def finish_grads(self, after):
-        model = self.model
-        groups = lax.axis_size("dp")
-        rows = model // self.splits
-        d_inner, d_outer, vectors = finish_inner(self.ids, self.shares, rows)
-        d_output, lines = run_kernel(
-            finish_output_kernel,
-            "finish_output",
-            [((rows, model), f32), ((8, model), f32)],
-            tuple(exchange_all(self.output_share)),
-        )
-        return d_inner, d_outer, d_output, lines[0], vectors
+        rows = self.model // self.splits
+        d_inner, d_outer, d_output, vectors = finish_inner(self.ids, self.shares, rows)
+        return d_inner, d_outer, d_output, vectors[len(self.shares) + 1], vectors
 
     def backward(self, grads, grad_res):
         chips, piece_len, width = self.chips, self.piece_len, self.width
@@ -823,22 +846,24 @@
             (self.ids,) + keep + self.masks() + tuple(grads),
             scratch=[pltpu.VMEM(a.shape, a.dtype) for a in keep]
             + [
+                pltpu.VMEM((chips,) + grads[0].shape, bf16),
+                pltpu.VMEM((chips * piece_len, tokens), f32),
+                pltpu.VMEM((chips * piece_len, tokens), f32),
                 pltpu.VMEM((chips * piece_len, tokens), bf16),
                 pltpu.VMEM((chips * piece_len, tokens), bf16),
                 pltpu.VMEM((splits, piece_len, 2 * width), bf16),
                 pltpu.VMEM((splits, groups) + quarter, f32),
-                pltpu.SemaphoreType.DMA((len(keep),)),
+                pltpu.SemaphoreType.DMA((len(keep) + chips,)),
             ],
             scalars=1,
-            raw=range(1, 6),
+            raw=(*range(1, 6), *range(10, 10 + chips)),
             flops=5 * tokens * tokens * width + 6 * tokens * model * width,
             powers=tokens * tokens * 3 // 2,
-            grant=18 << 20,
+            grant=24 << 20,
         )
         recv = swap_cores(other)
         dws = add_split(dw_mine, swap_cores(dw_other), [(group, bf16)] * groups)
         dq = tied(dq, dws[0])
-        self.last = dws[0]
         dws = exchange_parts(dws)
         full = (piece_len, model)
         (partial,) = run_kernel(
@@ -852,15 +877,20 @@
         )
         *dws, sums = sum_split(dws, [(quarter, bf16)] * chips + [((8, 3 * width), f32)])
         dws = line_parts(dws)
-        self.shares = exchange_all(tied(self.share, dws[0]))
-        partial = along_line(tied(partial, *dws[1:], self.shares[1]))
         part = (chips,) + quarter
         dw = stack(*dws)
+        every = exchange_all(dw)
+        self.shares = exchange_all(tied(self.share, *every[1:]))
+        count = splits
+        lines = [[2 * i + c for i in range(count // 2)] for c in range(2)]
+        partial = lax.psum_scatter(
+            partial, "seq", scatter_dimension=0, axis_index_groups=lines, tiled=False
+        )[None]
         gq, gk, gv = run_kernel(
             finish_kernel,
             "finish",
             [((rows, model), f32)] * 3,
-            (self.ids, *exchange_all(dw)),
+            (self.ids, *every),
             scratch=[pltpu.VMEM((groups,) + part, bf16)],
             scalars=1,
         )
@@ -1019,9 +1049,6 @@
         both = both.reshape(splits, 2, rows, model).transpose(1, 0, 2, 3)
         self.both = both.reshape(1, 2 * model, model)
 
-    def inner_shapes(self, tall):
-        return [((self.splits, tall, self.hidden.shape[1]), bf16)]
-
     def inner_grads(self, stacked):
         self.share = lax.psum_scatter(stacked, "seq", scatter_dimension=0, tiled=False)
 
@@ -1037,7 +1064,7 @@
         model = self.hidden.shape[1]
         groups = lax.axis_size("dp")
         rows = model // self.splits
-        d_inner, d_outer, vectors = finish_inner(self.ids, exchange_all(self.share), rows)
+        d_inner, d_outer, _, vectors = finish_inner(self.ids, exchange_all(self.share), rows)
         return d_inner, d_outer, self.total, self.lines.reshape(-1), vectors
 
     def backward(self, grads, grad_res):
@@ -1118,7 +1145,6 @@
         biases = jnp.stack([jnp.sum(grads[i].astype(f32), 0) for i in (0, 2)], 1)
         biases = lax.psum_scatter(biases, "seq", scatter_dimension=0, tiled=True)
         biases = lax.psum(biases.astype(bf16), "dp").astype(f32)
-        self.last = input_grad
         return input_grad, shares[0], biases[:, 0], shares[1], shares[2], biases[:, 1], biases
 
 
@@ -1219,31 +1245,38 @@
         (*exchange_parts(parts), normed, cotangent.reshape(row_count, model), vec),
     )
     grads = exchange_all(grad_low)
+    stacked = ((splits, 2 * rows + 8, model), bf16)
     parts = run_kernel(
         functools.partial(backward_kernel, parts=groups),
         "backward",
-        [(full, f32)] + [(full, bf16)] * (groups - 1) + attention.inner_shapes(2 * rows + 8),
+        [(full, f32)] + [(full, bf16)] * (groups - 1) + [stacked],
         (ids, both, inner, act, sums2, *lows, *grads),
         scalars=1,
         flops=4 * work,
         powers=wide[0] * wide[1],
-        grant=VMEM_BYTES if by_heads else 4 * VMEM_BYTES,
+        grant=(2 if by_heads else 5) * VMEM_BYTES,
     )
     recv = exchange_parts(parts[:groups])
     attention.inner_grads(*parts[groups:])
-    grad_res, grad_branch, sums1, *grad_att = run_kernel(
+    slots = attended.shape[0]
+    grad_branch, sums1, grad_res, *grad_att = run_kernel(
         functools.partial(residual_kernel, parts=groups),
         "residual",
-        [(full, f32), (full, bf16), ((8, model), f32)]
-        + [(attended.shape[1:], bf16)] * attended.shape[0],
+        [(full, bf16), ((8, model), f32), (full, f32)] + [(attended.shape[1:], bf16)] * slots,
         (ids, grad_mix, normed, inverse, vec, w_out, *recv),
+        scratch=[
+            pltpu.VMEM(full, f32),
+            pltpu.VMEM(attended.shape, bf16),
+            pltpu.SemaphoreType.DMA((slots + 1,)),
+        ],
         scalars=1,
+        raw_outs=range(2, 3 + slots),
         flops=2 * row_count * model * model,
     )
     if by_heads:
         grad_att = line_parts(grad_att)
+    attention.output_grad(attended, grad_branch, sums1)
     input_grad, gq, bias_q, gk, gv, bias_v, after = attention.backward(grad_att, grad_res)
-    attention.output_grad(attended, tied(grad_branch, attention.last), sums1)
     d_inner, d_outer, d_output, first_sums, vectors = attention.finish_grads(after)
     second_sums = vectors[groups]
 

time: 225 us -> 213 us (0.947)
  starting transfers between devices: 59.2 us -> 50.8 us
  local copies, waits for them, and re-layouts: 15.8 us -> 9.42 us
  waiting for transfers between devices: 86.9 us -> 91.4 us
  Pallas kernels: 46.4 us -> 42.9 us
    reduce_scatter x1, waiting for transfers between devices: 0.01 us -> 14.8 us  [backward(): lax.psum_scatter(partial, 'seq', scatter_dimension=0, axis_index_groups=l...]
    ppermute x26 -> x23, waiting for transfers between devices: 52.4 us -> 41.6 us  [exchange(): return lax.ppermute(array, 'dp', [(i, i ^ k) for i in range(count)])]
    unnamed x97 -> x89, local copies, waits for them, and re-layouts: 12.2 us -> 6.42 us
    all_to_all x2 -> x1, starting transfers between devices: 8.48 us -> 3.42 us  [along_line(): lax.all_to_all(array, 'seq', 0, 0, tiled=True, axis_index_groups=lines)]
    pallas_call x25 -> x24, Pallas kernels: 46.4 us -> 42.9 us  [run_kernel(): pl.pallas_call(kernel, name=name, out_shape=out_shape, in_specs=specs, ou...]
    ppermute x26 -> x23, starting transfers between devices: 31.1 us -> 27.8 us  [exchange(): return lax.ppermute(array, 'dp', [(i, i ^ k) for i in range(count)])]
    all_to_all x2 -> x1, waiting for transfers between devices: 7.5 us -> 7.7 us  [along_line(): lax.all_to_all(array, 'seq', 0, 0, tiled=True, axis_index_groups=lines)]
  transfers between devices with their start and end apart: 49 -> 45, of which waited for: 29 -> 31; matrix products, arithmetic and copies ran while one was open for 2% -> 1% of each run, Pallas kernels for 16% -> 13%
where the time goes in v4:
time: 213 us; the launch traced here: 209 us
  waiting for transfers between devices  91.4 us (43%)
  starting transfers between devices  50.8 us (24%)
  Pallas kernels  42.9 us (20%)
  between operations  14.5 us (7%)
  local copies, waits for them, and re-layouts  9.42 us (4%)
    pallas_call x24, Pallas kernels, run_kernel(): pl.pallas_call(kernel, name=name, out_shape=out_shape, in_specs=specs, ou...  42.9 us
    ppermute x23, waiting for transfers between devices, exchange(): return lax.ppermute(array, 'dp', [(i, i ^ k) for i in range(count)])  41.6 us
    ppermute x23, starting transfers between devices, exchange(): return lax.ppermute(array, 'dp', [(i, i ^ k) for i in range(count)])  27.8 us
    ppermute x12, waiting for transfers between devices, line_exchange(): return lax.ppermute(array, 'seq', [(i, i ^ 2 * k) for i in range(count)])  24.6 us
    ppermute x12, starting transfers between devices, line_exchange(): return lax.ppermute(array, 'seq', [(i, i ^ 2 * k) for i in range(count)])  18.2 us
    reduce_scatter x1, waiting for transfers between devices, backward(): lax.psum_scatter(partial, 'seq', scatter_dimension=0, axis_index_groups=l...  14.8 us
    all_to_all x1, waiting for transfers between devices, along_line(): lax.all_to_all(array, 'seq', 0, 0, tiled=True, axis_index_groups=lines)  7.7 us
    unnamed x89, local copies, waits for them, and re-layouts  6.42 us
  transfers between devices with their start and end apart: 45, of which 31 were waited for; matrix products, arithmetic and copies ran while one was open for 1% of the time, Pallas kernels for 13%

profile of v4, /device:TPU:8, one launch (start us, length us, event | category | flops | bytes accessed | tf_op | source)
XLA Modules:
  0.0 209.3 jit_solution(17941344435268149265)
XLA Ops:
  9.9 3.0 %collective-permute-start.1 = (bf16[48,576]{1,0:T(8,128)(2,1)S(1)}, bf16[48,576]{1,0:T(8,128)(2,1)S(1)}, u32[]{:S(2)}, u32[]{:S(2)}) collective-permute-start(bf16[48,576]{1,0:T(8,128)(2,1)S(1)} %get-tuple-element.81), channel_id=1, source_target_pairs={{0,4},{1,5},{2,6},{3,7},{4,0},{5,1},{6,2},{7,3},{8,12},{9,13},{10,... | collective-permute-start | bytes 165896 | tf_op jit(solution)/shard_map/ppermute | solution.py:598
  14.1 3.1 %collective-permute-done.1.refs_2_ = bf16[48,576]{1,0:T(8,128)(2,1)S(1)} collective-permute-done((bf16[48,576]{1,0:T(8,128)(2,1)S(1)}, bf16[48,576]{1,0:T(8,128)(2,1)S(1)}, u32[]{:S(2)}, u32[]{:S(2)}) %collective-permute-start.1) | collective-permute-done | bytes 55328 | tf_op jit(solution)/shard_map/ppermute | solution.py:598
  19.7 4.7 %collective-permute-done.3.refs_1_ = bf16[4,48,576]{2,1,0:T(8,128)(2,1)S(1)} collective-permute-done((bf16[4,48,576]{2,1,0:T(8,128)(2,1)S(1)}, bf16[4,48,576]{2,1,0:T(8,128)(2,1)S(1)}, u32[]{:S(2)}, u32[]{:S(2)}) %collective-permute-start.3) | collective-permute-done | bytes 221216 | tf_op jit(solution)/shard_map/ppermute | solution.py:580
  25.4 2.5 %collective-permute-start.4 = (bf16[64,768]{1,0:T(8,128)(2,1)S(1)}, bf16[64,768]{1,0:T(8,128)(2,1)S(1)}, u32[]{:S(2)}, u32[]{:S(2)}) collective-permute-start(bf16[64,768]{1,0:T(8,128)(2,1)S(1)} %cut_output.1.refs_0_), channel_id=1, source_target_pairs={{0,2},{1,3},{2,0},{3,1},{4,6},{5,7},{6,4},{7,5},{8,10},{9,11},{10,... | collective-permute-start | bytes 294920 | tf_op jit(solution)/shard_map/ppermute | solution.py:598
  31.0 5.6 %collective-permute-done.4.refs_1_ = bf16[64,768]{1,0:T(8,128)(2,1)S(1)} collective-permute-done((bf16[64,768]{1,0:T(8,128)(2,1)S(1)}, bf16[64,768]{1,0:T(8,128)(2,1)S(1)}, u32[]{:S(2)}, u32[]{:S(2)}) %collective-permute-start.4) | collective-permute-done | bytes 98336 | tf_op jit(solution)/shard_map/ppermute | solution.py:598
  36.6 2.5 %collective-permute-done.5.refs_2_ = bf16[64,768]{1,0:T(8,128)(2,1)S(1)} collective-permute-done((bf16[64,768]{1,0:T(8,128)(2,1)S(1)}, bf16[64,768]{1,0:T(8,128)(2,1)S(1)}, u32[]{:S(2)}, u32[]{:S(2)}) %collective-permute-start.5) | collective-permute-done | bytes 98336 | tf_op jit(solution)/shard_map/ppermute | solution.py:598
  39.1 3.4 %collective-permute-done.6.refs_3_ = bf16[64,768]{1,0:T(8,128)(2,1)S(1)} collective-permute-done((bf16[64,768]{1,0:T(8,128)(2,1)S(1)}, bf16[64,768]{1,0:T(8,128)(2,1)S(1)}, u32[]{:S(2)}, u32[]{:S(2)}) %collective-permute-start.6) | collective-permute-done | bytes 98336 | tf_op jit(solution)/shard_map/ppermute | solution.py:598
  47.7 6.2 %attend.1 = (bf16[4,192,128]{2,1,0:T(8,128)(2,1)}, bf16[4,128,192]{2,1,0:T(8,128)(2,1)}, bf16[1024,192]{1,0:T(8,128)(2,1)}, bf16[1024,192]{1,0:T(8,128)(2,1)}, f32[4,128,128]{2,1,0:T(8,128)}) custom-call(s32[3]{0:T(128)S(1)} %pad_add_fusion.ids, bf16[768,576]{1,0:T(8,128)(2,1)S(1)} %bitcast.47, f32[12,2,1024]{2,1,0:T(2,128)S(1)} %reshape_reshape.3.be, ...), custom_call_target="tpu_custom_call" | custom-call | flops 1308622848 | bytes 4008716 | tf_op jit(solution)/shard_map/attend/pallas_call | solution.py:48
  55.7 3.4 %all-to-all-start = ((bf16[4,192,128]{2,1,0:T(8,128)(2,1)}), bf16[4,192,128]{2,1,0:T(8,128)(2,1)S(1)}, u32[]{:S(2)}, u32[]{:S(2)}) async-start(bf16[4,192,128]{2,1,0:T(8,128)(2,1)} %get-tuple-element.84), calls=%async_computation | async-start | bytes 393216 | tf_op jit(solution)/shard_map/all_to_all | solution.py:629
  62.0 7.7 %all-to-all-done.att = bf16[4,192,128]{2,1,0:T(8,128)(2,1)S(1)} async-done(((bf16[4,192,128]{2,1,0:T(8,128)(2,1)}), bf16[4,192,128]{2,1,0:T(8,128)(2,1)S(1)}, u32[]{:S(2)}, u32[]{:S(2)}) %all-to-all-start) | async-done | bytes 196640 | tf_op jit(solution)/shard_map/all_to_all | solution.py:629
  73.9 4.3 %collective-permute-done.11.refs_1_ = bf16[128,768]{1,0:T(8,128)(2,1)S(1)} collective-permute-done((bf16[128,768]{1,0:T(8,128)(2,1)S(1)}, bf16[128,768]{1,0:T(8,128)(2,1)S(1)}, u32[]{:S(2)}, u32[]{:S(2)}) %collective-permute-start.11) | collective-permute-done | bytes 196640 | tf_op jit(solution)/shard_map/ppermute | solution.py:580
  78.2 3.7 %collective-permute-done.12.refs_2_ = bf16[128,768]{1,0:T(8,128)(2,1)S(1)} collective-permute-done((bf16[128,768]{1,0:T(8,128)(2,1)S(1)}, bf16[128,768]{1,0:T(8,128)(2,1)S(1)}, u32[]{:S(2)}, u32[]{:S(2)}) %collective-permute-start.12) | collective-permute-done | bytes 196640 | tf_op jit(solution)/shard_map/ppermute | solution.py:580
  82.6 4.4 %forward.1 = (f32[128,768]{1,0:T(8,128)S(1)}, bf16[128,768]{1,0:T(8,128)(2,1)S(1)}, bf16[128,768]{1,0:T(8,128)(2,1)S(1)}, bf16[128,768]{1,0:T(8,128)(2,1)S(1)}, ...) custom-call(s32[3]{0:T(128)S(1)} %copy-done.13, f32[16,768]{1,0:T(8,128)S(1)} %get-tuple-element.86.vec.refs_6_, ...), custom_call_target="tpu_custom_call" | custom-call | flops 1207959552 | bytes 6537228 | tf_op jit(solution)/shard_map/forward/pallas_call | solution.py:48
  90.7 3.3 %collective-permute-done.14.refs_1_ = bf16[128,768]{1,0:T(8,128)(2,1)S(1)} collective-permute-done((bf16[128,768]{1,0:T(8,128)(2,1)S(1)}, bf16[128,768]{1,0:T(8,128)(2,1)S(1)}, u32[]{:S(2)}, u32[]{:S(2)}) %collective-permute-start.14) | collective-permute-done | bytes 196640 | tf_op jit(solution)/shard_map/ppermute | solution.py:580
  93.9 3.0 %collective-permute-done.15.refs_2_ = bf16[128,768]{1,0:T(8,128)(2,1)S(1)} collective-permute-done((bf16[128,768]{1,0:T(8,128)(2,1)S(1)}, bf16[128,768]{1,0:T(8,128)(2,1)S(1)}, u32[]{:S(2)}, u32[]{:S(2)}) %collective-permute-start.15) | collective-permute-done | bytes 196640 | tf_op jit(solution)/shard_map/ppermute | solution.py:580
  101.5 2.2 %collective-permute-done.17.refs_5_ = bf16[128,768]{1,0:T(8,128)(2,1)S(1)} collective-permute-done((bf16[128,768]{1,0:T(8,128)(2,1)S(1)}, bf16[128,768]{1,0:T(8,128)(2,1)S(1)}, u32[]{:S(2)}, u32[]{:S(2)}) %collective-permute-start.17) | collective-permute-done | bytes 196640 | tf_op jit(solution)/shard_map/ppermute | solution.py:580
  103.7 2.0 collective-permute-done.18.refs_6_
  107.0 4.3 %backward.1 = (f32[128,768]{1,0:T(8,128)S(1)}, bf16[128,768]{1,0:T(8,128)(2,1)S(1)}, bf16[128,768]{1,0:T(8,128)(2,1)S(1)}, bf16[128,768]{1,0:T(8,128)(2,1)S(1)}, bf16[8,200,768]{2,1,0:T(8,128)(2,1)S(1)}) custom-call(s32[3]{0:T(128)S(1)} %copy-done.14, bf16[8,192,768]{2,1,0:T(8,128)(2,1)S(1)} %bitcast.57, f32[512,768]{1,0:T(8,128)S(1)} %get-tuple-element.98.inner_ref, ...), custom_call_target="tpu_custom_call" | custom-call | flops 2415919104 | bytes 9756684 | tf_op jit(solution)/shard_map/backward/pallas_call | solution.py:48
  114.9 2.2 %collective-permute-done.20.refs_1_ = bf16[128,768]{1,0:T(8,128)(2,1)S(1)} collective-permute-done((bf16[128,768]{1,0:T(8,128)(2,1)S(1)}, bf16[128,768]{1,0:T(8,128)(2,1)S(1)}, u32[]{:S(2)}, u32[]{:S(2)}) %collective-permute-start.20) | collective-permute-done | bytes 196640 | tf_op jit(solution)/shard_map/ppermute | solution.py:580
  117.1 2.9 %collective-permute-done.21.refs_2_ = bf16[128,768]{1,0:T(8,128)(2,1)S(1)} collective-permute-done((bf16[128,768]{1,0:T(8,128)(2,1)S(1)}, bf16[128,768]{1,0:T(8,128)(2,1)S(1)}, u32[]{:S(2)}, u32[]{:S(2)}) %collective-permute-start.21) | collective-permute-done | bytes 196640 | tf_op jit(solution)/shard_map/ppermute | solution.py:580
  120.0 2.2 %residual.1 = (bf16[128,768]{1,0:T(8,128)(2,1)S(1)}, f32[8,768]{1,0:T(8,128)S(1)}, f32[128,768]{1,0:T(8,128)}, bf16[192,128]{1,0:T(8,128)(2,1)}, bf16[192,128]{1...) custom-call(s32[3]{0:T(128)S(1)} %copy-done.14, f32[128,768]{1,0:T(8,128)S(1)} %get-tuple-element.96.mix, ...), custom_call_target="tpu_custom_call" | custom-call | flops 150994944 | bytes 3874828 | tf_op jit(solution)/shard_map/residual/pallas_call | solution.py:48
  124.9 4.0 %collective-permute-start.23 = (bf16[192,128]{1,0:T(8,128)(2,1)S(1)}, bf16[192,128]{1,0:T(8,128)(2,1)S(1)}, u32[]{:S(2)}, u32[]{:S(2)}) collective-permute-start(bf16[192,128]{1,0:T(8,128)(2,1)S(1)} %copy-done.40), channel_id=1, source_target_pairs={{0,2},{1,3},{2,0},{3,1},{4,6},{5,7},{6,4},{7,5},{8,10},{9,11},{10,... | collective-permute-start | bytes 147464 | tf_op jit(solution)/shard_map/ppermute | solution.py:598
  131.0 2.9 %collective-permute-done.24.refs_2_ = bf16[192,128]{1,0:T(8,128)(2,1)S(1)} collective-permute-done((bf16[192,128]{1,0:T(8,128)(2,1)S(1)}, bf16[192,128]{1,0:T(8,128)(2,1)S(1)}, u32[]{:S(2)}, u32[]{:S(2)}) %collective-permute-start.24) | collective-permute-done | bytes 49184 | tf_op jit(solution)/shard_map/ppermute | solution.py:598
  134.6 9.5 %attend_back.1 = (bf16[4,128,192]{2,1,0:T(8,128)(2,1)S(1)}, bf16[4,128,384]{2,1,0:T(8,128)(2,1)S(1)}, bf16[4,128,384]{2,1,0:T(8,128)(2,1)S(1)}, f32[4,104,576]{2,1,0:T(8,128)S(1)}, bf16[4,104,576]{2,1,0:T(8,128)(2,1)S(1)}) custom-call(s32[3]{0:T(128)S(1)} %copy-done.15, bf16[8,128,768]{2,1,0:T(8,128)(2,1)} %all-gather.4.cloned.1.call-done.hid.hid_raw, ...), custom_call_target="tpu_custom_call" | custom-call | flops 1912602624 | bytes 5543948 | tf_op jit(solution)/shard_map/attend_back/pallas_call | solution.py:48
  146.8 2.3 %input_grad.1 = bf16[4,128,768]{2,1,0:T(8,128)(2,1)} custom-call(s32[3]{0:T(128)S(1)} %copy-done.15, bf16[4,128,192]{2,1,0:T(8,128)(2,1)S(1)} %get-tuple-element.119.dq, bf16[4,128,384]{2,1,0:T(8,128)(2,1)S(1)} %get-tuple-element.120.mine, bf16[4,128,384]{2,1,0:T(8,128)(2,1)S(1)} %collective-permute-done.27.recv, bf16[768,576]{1,0:T(8,128)(2,1)S(1)} %bitcast.48), custom_call_target="tpu_custom_call" | custom-call | flops 452984832 | bytes 2654220 | tf_op jit(solution)/shard_map/input_grad/pallas_call | solution.py:48
  152.6 2.8 %collective-permute-done.28.refs_1_ = bf16[104,576]{1,0:T(8,128)(2,1)S(1)} collective-permute-done((bf16[104,576]{1,0:T(8,128)(2,1)S(1)}, bf16[104,576]{1,0:T(8,128)(2,1)S(1)}, u32[]{:S(2)}, u32[]{:S(2)}) %collective-permute-start.28) | collective-permute-done | bytes 119840 | tf_op jit(solution)/shard_map/ppermute | solution.py:580
  155.5 3.1 %collective-permute-done.29.refs_2_ = bf16[104,576]{1,0:T(8,128)(2,1)S(1)} collective-permute-done((bf16[104,576]{1,0:T(8,128)(2,1)S(1)}, bf16[104,576]{1,0:T(8,128)(2,1)S(1)}, u32[]{:S(2)}, u32[]{:S(2)}) %collective-permute-start.29) | collective-permute-done | bytes 119840 | tf_op jit(solution)/shard_map/ppermute | solution.py:580
  158.6 3.4 %collective-permute-start.31 = (bf16[24,576]{1,0:T(8,128)(2,1)S(1)}, bf16[24,576]{1,0:T(8,128)(2,1)S(1)}, u32[]{:S(2)}, u32[]{:S(2)}) collective-permute-start(bf16[24,576]{1,0:T(8,128)(2,1)S(1)} %get-tuple-element.126), channel_id=1, source_target_pairs={{0,2},{1,3},{2,0},{3,1},{4,6},{5,7},{6,4},{7,5},{8,10},{9,11},{10,... | collective-permute-start | bytes 82952 | tf_op jit(solution)/shard_map/ppermute | solution.py:598
  164.9 2.8 %collective-permute-done.32.refs_2_ = bf16[24,576]{1,0:T(8,128)(2,1)S(1)} collective-permute-done((bf16[24,576]{1,0:T(8,128)(2,1)S(1)}, bf16[24,576]{1,0:T(8,128)(2,1)S(1)}, u32[]{:S(2)}, u32[]{:S(2)}) %collective-permute-start.32) | collective-permute-done | bytes 27680 | tf_op jit(solution)/shard_map/ppermute | solution.py:598
  172.2 2.0 collective-permute-done.34.refs_1_
  182.4 14.8 %reduce-scatter.3.cloned.1.call-done.parts = bf16[1,128,768]{2,1,0:T(8,128)(2,1)} async-done(((bf16[4,128,768]{2,1,0:T(8,128)(2,1)}), bf16[1,128,768]{2,1,0:T(8,128)(2,1)}) %reduce-scatter.3.cloned.1.call-update) | async-done | bytes 196624 | tf_op jit(solution)/shard_map/reduce_scatter | solution.py:886
  198.9 2.5 %finish_inner.1 = (f32[96,3072]{1,0:T(8,128)}, f32[384,768]{1,0:T(8,128)}, f32[96,768]{1,0:T(8,128)}, f32[8,768]{1,0:T(8,128)S(1)}) custom-call(s32[3]{0:T(128)S(1)} %copy-done.15, bf16[304,768]{1,0:T(8,128)(2,1)S(1)} %bitcast.53, bf16[304,768]{1,0:T(8,128)(2,1)S(1)} %collective-permute-done.37.refs_1_, ...), custom_call_target="tpu_custom_call" | custom-call | bytes 4546572 | tf_op jit(solution)/shard_map/finish_inner/pallas_call | solution.py:48
  (201 shorter events, 67.9 us)
Async XLA Ops:
  7.3 35.8 %all-gather.4.cloned.1.call-start = ((), (), s32[]{:S(2)}) async-start(), calls=%async_computation.3 | async-start | bytes 1769472 | tf_op jit(solution)/shard_map/all_gather | solution.py:675
  8.0 74.5 %all-gather.6.cloned.1.call-start = ((), (), s32[]{:S(2)}) async-start(), calls=%async_computation.6 | async-start | bytes 2654208 | tf_op jit(solution)/shard_map/all_gather | solution.py:760
  9.9 7.3 %collective-permute-start.1 = (bf16[48,576]{1,0:T(8,128)(2,1)S(1)}, bf16[48,576]{1,0:T(8,128)(2,1)S(1)}, u32[]{:S(2)}, u32[]{:S(2)}) collective-permute-start(bf16[48,576]{1,0:T(8,128)(2,1)S(1)} %get-tuple-element.81), channel_id=1, source_target_pairs={{0,4},{1,5},{2,6},{3,7},{4,0},{5,1},{6,2},{7,3},{8,12},{9,13},{10,... | collective-permute-start | bytes 165896 | tf_op jit(solution)/shard_map/ppermute | solution.py:598
  18.2 6.3 %collective-permute-start.3 = (bf16[4,48,576]{2,1,0:T(8,128)(2,1)S(1)}, bf16[4,48,576]{2,1,0:T(8,128)(2,1)S(1)}, u32[]{:S(2)}, u32[]{:S(2)}) collective-permute-start(bf16[4,48,576]{2,1,0:T(8,128)(2,1)S(1)} %stack.27.refs_0_), channel_id=1, source_target_pairs={{0,8},{8,0},{16,24},{24,16},{1,9},{9,1},{17,25},{25,17},{2,10},{10... | collective-permute-start | bytes 663560 | tf_op jit(solution)/shard_map/ppermute | solution.py:580
  24.5 18.0 %collective-permute-start.7 = (bf16[2,4,48,576]{3,2,1,0:T(8,128)(2,1)S(1)}, bf16[2,4,48,576]{3,2,1,0:T(8,128)(2,1)S(1)}, u32[]{:S(2)}, u32[]{:S(2)}) collective-permute-start(bf16[2,4,48,576]{3,2,1,0:T(8,128)(2,1)S(1)} %stack.29.mine), channel_id=1, source_target_pairs={{0,1},{1,0},{2,3},{3,2},{4,5},{5,4},{6,7},{7,6},{8,9},{9,8},{10,11... | collective-permute-start | bytes 1327112 | tf_op jit(solution)/shard_map/ppermute | solution.py:593
  25.4 11.2 %collective-permute-start.4 = (bf16[64,768]{1,0:T(8,128)(2,1)S(1)}, bf16[64,768]{1,0:T(8,128)(2,1)S(1)}, u32[]{:S(2)}, u32[]{:S(2)}) collective-permute-start(bf16[64,768]{1,0:T(8,128)(2,1)S(1)} %cut_output.1.refs_0_), channel_id=1, source_target_pairs={{0,2},{1,3},{2,0},{3,1},{4,6},{5,7},{6,4},{7,5},{8,10},{9,11},{10,... | collective-permute-start | bytes 294920 | tf_op jit(solution)/shard_map/ppermute | solution.py:598
  27.8 11.2 %collective-permute-start.5 = (bf16[64,768]{1,0:T(8,128)(2,1)S(1)}, bf16[64,768]{1,0:T(8,128)(2,1)S(1)}, u32[]{:S(2)}, u32[]{:S(2)}) collective-permute-start(bf16[64,768]{1,0:T(8,128)(2,1)S(1)} %cut_output.1.refs_0_), channel_id=1, source_target_pairs={{0,4},{1,5},{2,6},{3,7},{4,0},{5,1},{6,2},{7,3},{8,12},{9,13},{10,... | collective-permute-start | bytes 294920 | tf_op jit(solution)/shard_map/ppermute | solution.py:598
  29.4 13.0 %collective-permute-start.6 = (bf16[64,768]{1,0:T(8,128)(2,1)S(1)}, bf16[64,768]{1,0:T(8,128)(2,1)S(1)}, u32[]{:S(2)}, u32[]{:S(2)}) collective-permute-start(bf16[64,768]{1,0:T(8,128)(2,1)S(1)} %cut_output.1.refs_0_), channel_id=1, source_target_pairs={{0,6},{1,7},{2,4},{3,5},{4,2},{5,3},{6,0},{7,1},{8,14},{9,15},{10,... | collective-permute-start | bytes 294920 | tf_op jit(solution)/shard_map/ppermute | solution.py:598
  44.1 11.5 %collective-permute-start.9 = (bf16[4,64,768]{2,1,0:T(8,128)(2,1)S(1)}, bf16[4,64,768]{2,1,0:T(8,128)(2,1)S(1)}, u32[]{:S(2)}, u32[]{:S(2)}) collective-permute-start(bf16[4,64,768]{2,1,0:T(8,128)(2,1)S(1)} %stack.28.refs_0_), channel_id=1, source_target_pairs={{0,16},{8,24},{16,0},{24,8},{1,17},{9,25},{17,1},{25,9},{2,18},{10... | collective-permute-start | bytes 1179656 | tf_op jit(solution)/shard_map/ppermute | solution.py:580
  55.7 14.0 %all-to-all-start = ((bf16[4,192,128]{2,1,0:T(8,128)(2,1)}), bf16[4,192,128]{2,1,0:T(8,128)(2,1)S(1)}, u32[]{:S(2)}, u32[]{:S(2)}) async-start(bf16[4,192,128]{2,1,0:T(8,128)(2,1)} %get-tuple-element.84), calls=%async_computation | async-start | bytes 393216 | tf_op jit(solution)/shard_map/all_to_all | solution.py:629
  59.1 117.6 %reduce-scatter.5.cloned.1.call-start = ((), (), s32[]{:S(2)}) async-start(), calls=%async_computation.5 | async-start | bytes 4202496 | tf_op jit(solution)/shard_map/reduce_scatter | solution.py:823
  70.3 7.9 %collective-permute-start.11 = (bf16[128,768]{1,0:T(8,128)(2,1)S(1)}, bf16[128,768]{1,0:T(8,128)(2,1)S(1)}, u32[]{:S(2)}, u32[]{:S(2)}) collective-permute-start(bf16[128,768]{1,0:T(8,128)(2,1)S(1)} %get-tuple-element.89.refs_0_), channel_id=1, source_target_pairs={{0,8},{8,0},{16,24},{24,16},{1,9},{9,1},{17,25},{25,17},{2,10},{10... | collective-permute-start | bytes 589832 | tf_op jit(solution)/shard_map/ppermute | solution.py:580
  71.8 10.1 %collective-permute-start.12 = (bf16[128,768]{1,0:T(8,128)(2,1)S(1)}, bf16[128,768]{1,0:T(8,128)(2,1)S(1)}, u32[]{:S(2)}, u32[]{:S(2)}) collective-permute-start(bf16[128,768]{1,0:T(8,128)(2,1)S(1)} %get-tuple-element.89.refs_0_), channel_id=1, source_target_pairs={{0,16},{8,24},{16,0},{24,8},{1,17},{9,25},{17,1},{25,9},{2,18},{10... | collective-permute-start | bytes 589832 | tf_op jit(solution)/shard_map/ppermute | solution.py:580
  73.3 9.3 %collective-permute-start.13 = (bf16[128,768]{1,0:T(8,128)(2,1)S(1)}, bf16[128,768]{1,0:T(8,128)(2,1)}, u32[]{:S(2)}, u32[]{:S(2)}) collective-permute-start(bf16[128,768]{1,0:T(8,128)(2,1)S(1)} %get-tuple-element.89.refs_0_), channel_id=1, source_target_pairs={{0,24},{8,16},{16,8},{24,0},{1,25},{9,17},{17,9},{25,1},{2,26},{10... | collective-permute-start | bytes 589832 | tf_op jit(solution)/shard_map/ppermute | solution.py:580
  87.1 6.8 %collective-permute-start.14 = (bf16[128,768]{1,0:T(8,128)(2,1)S(1)}, bf16[128,768]{1,0:T(8,128)(2,1)S(1)}, u32[]{:S(2)}, u32[]{:S(2)}) collective-permute-start(bf16[128,768]{1,0:T(8,128)(2,1)S(1)} %get-tuple-element.91), channel_id=1, source_target_pairs={{0,8},{8,0},{16,24},{24,16},{1,9},{9,1},{17,25},{25,17},{2,10},{10... | collective-permute-start | bytes 589832 | tf_op jit(solution)/shard_map/ppermute | solution.py:580
  87.8 9.2 %collective-permute-start.15 = (bf16[128,768]{1,0:T(8,128)(2,1)S(1)}, bf16[128,768]{1,0:T(8,128)(2,1)S(1)}, u32[]{:S(2)}, u32[]{:S(2)}) collective-permute-start(bf16[128,768]{1,0:T(8,128)(2,1)S(1)} %get-tuple-element.92), channel_id=1, source_target_pairs={{0,16},{8,24},{16,0},{24,8},{1,17},{9,25},{17,1},{25,9},{2,18},{10... | collective-permute-start | bytes 589832 | tf_op jit(solution)/shard_map/ppermute | solution.py:580
  89.2 7.8 %collective-permute-start.16 = (bf16[128,768]{1,0:T(8,128)(2,1)S(1)}, bf16[128,768]{1,0:T(8,128)(2,1)S(1)}, u32[]{:S(2)}, u32[]{:S(2)}) collective-permute-start(bf16[128,768]{1,0:T(8,128)(2,1)S(1)} %get-tuple-element.93), channel_id=1, source_target_pairs={{0,24},{8,16},{16,8},{24,0},{1,25},{9,17},{17,9},{25,1},{2,26},{10... | collective-permute-start | bytes 589832 | tf_op jit(solution)/shard_map/ppermute | solution.py:580
  98.6 7.1 %collective-permute-start.18 = (bf16[128,768]{1,0:T(8,128)(2,1)S(1)}, bf16[128,768]{1,0:T(8,128)(2,1)S(1)}, u32[]{:S(2)}, u32[]{:S(2)}) collective-permute-start(bf16[128,768]{1,0:T(8,128)(2,1)S(1)} %get-tuple-element.101.refs_4_), channel_id=1, source_target_pairs={{0,16},{8,24},{16,0},{24,8},{1,17},{9,25},{17,1},{25,9},{2,18},{10... | collective-permute-start | bytes 589832 | tf_op jit(solution)/shard_map/ppermute | solution.py:580
  100.4 6.6 %collective-permute-start.19 = (bf16[128,768]{1,0:T(8,128)(2,1)S(1)}, bf16[128,768]{1,0:T(8,128)(2,1)S(1)}, u32[]{:S(2)}, u32[]{:S(2)}) collective-permute-start(bf16[128,768]{1,0:T(8,128)(2,1)S(1)} %get-tuple-element.101.refs_4_), channel_id=1, source_target_pairs={{0,24},{8,16},{16,8},{24,0},{1,25},{9,17},{17,9},{25,1},{2,26},{10... | collective-permute-start | bytes 589832 | tf_op jit(solution)/shard_map/ppermute | solution.py:580
  111.3 5.7 %collective-permute-start.20 = (bf16[128,768]{1,0:T(8,128)(2,1)S(1)}, bf16[128,768]{1,0:T(8,128)(2,1)S(1)}, u32[]{:S(2)}, u32[]{:S(2)}) collective-permute-start(bf16[128,768]{1,0:T(8,128)(2,1)S(1)} %get-tuple-element.103), channel_id=1, source_target_pairs={{0,8},{8,0},{16,24},{24,16},{1,9},{9,1},{17,25},{25,17},{2,10},{10... | collective-permute-start | bytes 589832 | tf_op jit(solution)/shard_map/ppermute | solution.py:580
  112.2 7.8 %collective-permute-start.21 = (bf16[128,768]{1,0:T(8,128)(2,1)S(1)}, bf16[128,768]{1,0:T(8,128)(2,1)S(1)}, u32[]{:S(2)}, u32[]{:S(2)}) collective-permute-start(bf16[128,768]{1,0:T(8,128)(2,1)S(1)} %get-tuple-element.104), channel_id=1, source_target_pairs={{0,16},{8,24},{16,0},{24,8},{1,17},{9,25},{17,1},{25,9},{2,18},{10... | collective-permute-start | bytes 589832 | tf_op jit(solution)/shard_map/ppermute | solution.py:580
  113.0 7.0 %collective-permute-start.22 = (bf16[128,768]{1,0:T(8,128)(2,1)S(1)}, bf16[128,768]{1,0:T(8,128)(2,1)S(1)}, u32[]{:S(2)}, u32[]{:S(2)}) collective-permute-start(bf16[128,768]{1,0:T(8,128)(2,1)S(1)} %get-tuple-element.105), channel_id=1, source_target_pairs={{0,24},{8,16},{16,8},{24,0},{1,25},{9,17},{17,9},{25,1},{2,26},{10... | collective-permute-start | bytes 589832 | tf_op jit(solution)/shard_map/ppermute | solution.py:580
  124.2 73.0 %reduce-scatter.3.cloned.1.call-start = ((), (), s32[]{:S(2)}) async-start(), calls=%async_computation.4 | async-start | bytes 983040 | tf_op jit(solution)/shard_map/reduce_scatter | solution.py:886
  124.9 6.1 %collective-permute-start.23 = (bf16[192,128]{1,0:T(8,128)(2,1)S(1)}, bf16[192,128]{1,0:T(8,128)(2,1)S(1)}, u32[]{:S(2)}, u32[]{:S(2)}) collective-permute-start(bf16[192,128]{1,0:T(8,128)(2,1)S(1)} %copy-done.40), channel_id=1, source_target_pairs={{0,2},{1,3},{2,0},{3,1},{4,6},{5,7},{6,4},{7,5},{8,10},{9,11},{10,... | collective-permute-start | bytes 147464 | tf_op jit(solution)/shard_map/ppermute | solution.py:598
  149.1 6.4 %collective-permute-start.28 = (bf16[104,576]{1,0:T(8,128)(2,1)S(1)}, bf16[104,576]{1,0:T(8,128)(2,1)S(1)}, u32[]{:S(2)}, u32[]{:S(2)}) collective-permute-start(bf16[104,576]{1,0:T(8,128)(2,1)S(1)} %get-tuple-element.122), channel_id=1, source_target_pairs={{0,8},{8,0},{16,24},{24,16},{1,9},{9,1},{17,25},{25,17},{2,10},{10... | collective-permute-start | bytes 359432 | tf_op jit(solution)/shard_map/ppermute | solution.py:580
  150.4 8.2 %collective-permute-start.29 = (bf16[104,576]{1,0:T(8,128)(2,1)S(1)}, bf16[104,576]{1,0:T(8,128)(2,1)S(1)}, u32[]{:S(2)}, u32[]{:S(2)}) collective-permute-start(bf16[104,576]{1,0:T(8,128)(2,1)S(1)} %get-tuple-element.123), channel_id=1, source_target_pairs={{0,16},{8,24},{16,0},{24,8},{1,17},{9,25},{17,1},{25,9},{2,18},{10... | collective-permute-start | bytes 359432 | tf_op jit(solution)/shard_map/ppermute | solution.py:580
  151.6 7.0 %collective-permute-start.30 = (bf16[104,576]{1,0:T(8,128)(2,1)S(1)}, bf16[104,576]{1,0:T(8,128)(2,1)S(1)}, u32[]{:S(2)}, u32[]{:S(2)}) collective-permute-start(bf16[104,576]{1,0:T(8,128)(2,1)S(1)} %get-tuple-element.124), channel_id=1, source_target_pairs={{0,24},{8,16},{16,8},{24,0},{1,25},{9,17},{17,9},{25,1},{2,26},{10... | collective-permute-start | bytes 359432 | tf_op jit(solution)/shard_map/ppermute | solution.py:580
  158.6 6.3 %collective-permute-start.31 = (bf16[24,576]{1,0:T(8,128)(2,1)S(1)}, bf16[24,576]{1,0:T(8,128)(2,1)S(1)}, u32[]{:S(2)}, u32[]{:S(2)}) collective-permute-start(bf16[24,576]{1,0:T(8,128)(2,1)S(1)} %get-tuple-element.126), channel_id=1, source_target_pairs={{0,2},{1,3},{2,0},{3,1},{4,6},{5,7},{6,4},{7,5},{8,10},{9,11},{10,... | collective-permute-start | bytes 82952 | tf_op jit(solution)/shard_map/ppermute | solution.py:598
  170.9 5.8 %collective-permute-start.36 = (bf16[4,24,576]{2,1,0:T(8,128)(2,1)S(1)}, bf16[4,24,576]{2,1,0:T(8,128)(2,1)S(1)}, u32[]{:S(2)}, u32[]{:S(2)}) collective-permute-start(bf16[4,24,576]{2,1,0:T(8,128)(2,1)S(1)} %stack.31.refs_0_), channel_id=1, source_target_pairs={{0,24},{8,16},{16,8},{24,0},{1,25},{9,17},{17,9},{25,1},{2,26},{10... | collective-permute-start | bytes 331784 | tf_op jit(solution)/shard_map/ppermute | solution.py:580
  176.7 22.2 %collective-permute-start.37 = (bf16[304,768]{1,0:T(8,128)(2,1)}, bf16[304,768]{1,0:T(8,128)(2,1)S(1)}, u32[]{:S(2)}, u32[]{:S(2)}) collective-permute-start(bf16[304,768]{1,0:T(8,128)(2,1)} %bitcast.50), channel_id=1, source_target_pairs={{0,8},{8,0},{16,24},{24,16},{1,9},{9,1},{17,25},{25,17},{2,10},{10... | collective-permute-start | bytes 1400840 | tf_op jit(solution)/shard_map/ppermute | solution.py:580
  177.9 21.0 %collective-permute-start.38 = (bf16[304,768]{1,0:T(8,128)(2,1)}, bf16[304,768]{1,0:T(8,128)(2,1)S(1)}, u32[]{:S(2)}, u32[]{:S(2)}) collective-permute-start(bf16[304,768]{1,0:T(8,128)(2,1)} %bitcast.51), channel_id=1, source_target_pairs={{0,16},{8,24},{16,0},{24,8},{1,17},{9,25},{17,1},{25,9},{2,18},{10... | collective-permute-start | bytes 1400840 | tf_op jit(solution)/shard_map/ppermute | solution.py:580
  178.5 20.3 %collective-permute-start.39 = (bf16[304,768]{1,0:T(8,128)(2,1)}, bf16[304,768]{1,0:T(8,128)(2,1)S(1)}, u32[]{:S(2)}, u32[]{:S(2)}) collective-permute-start(bf16[304,768]{1,0:T(8,128)(2,1)} %bitcast.52), channel_id=1, source_target_pairs={{0,24},{8,16},{16,8},{24,0},{1,25},{9,17},{17,9},{25,1},{2,26},{10... | collective-permute-start | bytes 1400840 | tf_op jit(solution)/shard_map/ppermute | solution.py:580
  (57 other events, 673.6 us)
Sparse Core Ops, SparseCore 0:
  9.8 29.9 all-gather.3
  43.3 33.4 all-gather.5
  124.3 46.5 reduce-scatter.4
  173.6 23.4 reduce-scatter.2

commit v5 on v4

--- a/solution.py
+++ b/solution.py
@@ -149,9 +149,15 @@
     count, rows = vec.shape
     start = pl.multiple_of(lax.rem(ids[2] // 2, 2) * half, half)
     tall, model = out.shape
+    each = model // rows
     out[:half, :] = wo[pl.ds(start, half), :]
-    line = jnp.concatenate([vec[...], jnp.zeros((count, model - rows), bf16)], 1)
-    out[half:, :] = jnp.concatenate([line, jnp.zeros((tall - half - count, model), bf16)], 0)
+    lines = []
+    for first in range(0, count, each):
+        parts = [vec[i : i + 1, :] for i in range(first, min(count, first + each))]
+        parts += [jnp.zeros((1, rows), bf16)] * (each - len(parts))
+        lines.append(jnp.concatenate(parts, 1))
+    fill = jnp.zeros((tall - half - len(lines), model), bf16)
+    out[half:, :] = jnp.concatenate(lines + [fill], 0)
 
 
 def cut_inner_kernel(ids, w1, w2, out, scratch):
@@ -183,15 +189,29 @@
             out[2 * chip + core, own ^ h] = mine[h, k, :half, :]
             out[2 * chip + 1 - core, own ^ h] = other[h, k, :half, :]
     rows = 2 * half
-    vec[...] = jnp.concatenate(
-        [scratch[piece].astype(f32)[:, :rows] for piece in range(pieces)], 1
-    )
-
-
-def attend_kernel(ids, w, be, bn, sk, sq, hid, ours, theirs, *refs):
+    each = vec.shape[1] // rows
+    lines = [scratch[piece].astype(f32) for piece in range(pieces)]
+    for i in range(vec.shape[0]):
+        at, first = i // each, i % each * rows
+        vec[i : i + 1, :] = jnp.concatenate(
+            [line[at : at + 1, first : first + rows] for line in lines], 1
+        )
+
+
+def attend_kernel(ids, w, be, bn, sk, sq, ours, theirs, hid_raw, *refs):
     att = refs[0]
     kept = refs[1:5]
-    qo, ko, vo, lse, qs, s_all, p_all, sems = refs[5:]
+    hid, qo, ko, vo, lse, qs, s_all, p_all, sems = refs[5:]
+    count = 2
+    step = hid_raw.shape[0] // count
+    loads = [
+        pltpu.make_async_copy(
+            hid_raw.at[pl.ds(i * step, step)], hid.at[pl.ds(i * step, step)], sems.at[4 + i]
+        )
+        for i in range(count)
+    ]
+    for load in loads:
+        load.start()
     copies = [
         pltpu.make_async_copy(here, there, sems.at[i])
         for i, (here, there) in enumerate(zip((qo, ko, vo, lse), kept))
@@ -207,12 +227,15 @@
     second = jnp.where(core == 0, theirs, ours)
     biases = jnp.concatenate([first, second], 1)
     qb, vb = biases[0:1, :], biases[1:2, :]
-    tokens = hid[...].reshape(pieces * piece_len, model)
-    product = matmul(tokens, w[...])
-    query = (product[:, :width] + qb).astype(bf16) * bf16(size**-0.5)
-    qs[...] = query.reshape(pieces, piece_len, width)
-    ko[...] = product[:, width : 2 * width].astype(bf16)
-    vo[...] = (product[:, 2 * width :] + vb).astype(bf16)
+    for i, load in enumerate(loads):
+        load.wait()
+        some = slice(i * step, (i + 1) * step)
+        span = slice(i * step * piece_len, (i + 1) * step * piece_len)
+        product = matmul(hid[some].reshape(step * piece_len, model), w[...])
+        query = (product[:, :width] + qb).astype(bf16) * bf16(size**-0.5)
+        qs[some] = query.reshape(step, piece_len, width)
+        ko[span] = product[:, width : 2 * width].astype(bf16)
+        vo[span] = (product[:, 2 * width :] + vb).astype(bf16)
     lane = lax.broadcasted_iota(jnp.int32, (piece_len, 128), 1)
     for k in range(chips):
         qo[k] = qs[2 * (ids[1] ^ k) + core]
@@ -399,19 +422,23 @@
     raw = refs[:parts]
     outs = refs[parts : 2 * parts]
     inner_ref, act_ref, both, x, sems = refs[2 * parts :]
+    half = both.shape[1] // 2
     copies = [pltpu.make_async_copy(r, x.at[i], sems.at[i]) for i, r in enumerate(raw)]
-    copies.append(pltpu.make_async_copy(both_raw, both, sems.at[parts]))
+    for i in range(2):
+        span = (slice(None), pl.ds(i * half, half), slice(None))
+        copies.append(pltpu.make_async_copy(both_raw.at[span], both.at[span], sems.at[parts + i]))
     for copy in copies:
         copy.start()
-    for copy in copies:
+    for copy in copies[:-1]:
         copy.wait()
     _, rows, model = x.shape
-    weight1, weight2 = two_weights(both)
+    weight1 = both[:, :half, :].reshape(-1, model)
     inner = matmul(x[...].reshape(parts * rows, model), weight1) + vec[pl.ds(8 + ids[2], 1), :]
     act = (0.5 * inner * (1.0 + gelu_parts(inner))).astype(bf16)
     inner_ref[...] = inner
     act_ref[...] = act
-    mixed = matmul(act, weight2)
+    copies[-1].wait()
+    mixed = matmul(act, both[:, half:, :].reshape(-1, model))
     for i in range(parts):
         outs[i][...] = mixed[i * rows : (i + 1) * rows].astype(outs[i].dtype)
 
@@ -437,14 +464,11 @@
     sums[3:, :] = jnp.zeros((5, sums.shape[1]), f32)
 
 
-def backward_kernel(ids, both, inner_ref, act, sums, *refs, parts):
-    x = refs[:parts]
-    grads = refs[parts : 2 * parts]
-    outs = refs[2 * parts : 3 * parts]
-    out = refs[3 * parts]
+def backward_kernel(both, inner_ref, *refs, parts):
+    grads = refs[:parts]
+    outs = refs[parts : 2 * parts]
+    gi_ref, total = refs[2 * parts :]
     rows = grads[0].shape[0]
-    pieces, tall, model = out.shape
-    units = (tall - 8) // 2
     weight1, weight2 = two_weights(both)
     gm = jnp.concatenate([r[...] for r in grads], 0)
     grad_act = right_product(gm, weight2)
@@ -452,44 +476,68 @@
     t = gelu_parts(v)
     slope = 0.5 * (1.0 + t) + 0.5 * v * (1.0 - t * t) * (GELU_A * (1.0 + 3.0 * GELU_B * (v * v)))
     gi = (grad_act * slope).astype(bf16)
+    gi_ref[...] = gi
     first = right_product(gi, weight1)
     for i in range(parts):
         outs[i][...] = first[i * rows : (i + 1) * rows].astype(outs[i].dtype)
+    total[...] = jnp.sum(gi.astype(f32), 0, keepdims=True)
+
+
+def inner_outer_kernel(gi, act, sums, total, *refs, parts):
+    x = refs[:parts]
+    grads = refs[parts : 2 * parts]
+    out = refs[2 * parts]
+    pieces, tall, model = out.shape
+    units = (tall - 8) // 2
+    gm = jnp.concatenate([r[...] for r in grads], 0)
     tokens = jnp.concatenate([r[...] for r in x], 0)
-    out[:, :units, :] = left_product(tokens, gi).astype(bf16).reshape(pieces, units, model)
+    out[:, :units, :] = left_product(tokens, gi[...]).astype(bf16).reshape(pieces, units, model)
     out[:, units : 2 * units, :] = (
         left_product(act[...], gm).astype(bf16).reshape(pieces, units, model)
     )
-    total = jnp.sum(gi.astype(f32), 0, keepdims=True)
-    vectors = [sums[i : i + 1, :] for i in range(3)] + [total]
+    vectors = [sums[i : i + 1, :] for i in range(3)] + [total[...]]
     for piece in range(pieces):
         put_vectors(out, piece, piece, 2 * units, vectors, units)
 
 
-def residual_kernel(ids, mix, normed, inverse, vec, wo, *refs, parts):
+def residual_kernel(ids, mix, normed, inverse, vec, wo, att, above, *refs, parts):
     recv = refs[:parts]
-    low, sums, res_raw = refs[parts : parts + 3]
-    back_raw = refs[parts + 3 : -3]
-    res, back, sems = refs[-3:]
+    res_raw, stacked = refs[parts : parts + 2]
+    back_raw = refs[parts + 2 : -4]
+    res, back, out, sems = refs[-4:]
+    copies = []
+
+    def send(here, there):
+        copies.append(pltpu.make_async_copy(here, there, sems.at[len(copies)]))
+        copies[-1].start()
+
+    tall = above.shape[1]
+    send(above, stacked.at[:, pl.ds(0, tall), :])
     first = mix[...]
     for r in recv:
         first = first + r[...].astype(f32)
     n1 = normed[...]
     grad = norm_back(first, n1, inverse[:, 0:1], vec[3:4, :])
     rounded = grad.astype(bf16)
-    copies = []
-    for k, out in enumerate(back_raw):
+    for k, raw in enumerate(back_raw):
         back[k] = right_product(wo[ids[1] ^ k], rounded).astype(bf16)
-        copies.append(pltpu.make_async_copy(back.at[k], out, sems.at[k]))
-        copies[-1].start()
+        send(back.at[k], raw)
     res[...] = grad
-    copies.append(pltpu.make_async_copy(res, res_raw, sems.at[len(back_raw)]))
-    copies[-1].start()
-    low[...] = rounded
-    sums[0:1, :] = jnp.sum(first * n1, 0, keepdims=True)
-    sums[1:2, :] = jnp.sum(first, 0, keepdims=True)
-    sums[2:3, :] = jnp.sum(rounded.astype(f32), 0, keepdims=True)
-    sums[3:, :] = jnp.zeros((5, sums.shape[1]), f32)
+    send(res, res_raw)
+    vectors = [
+        jnp.sum(first * n1, 0, keepdims=True),
+        jnp.sum(first, 0, keepdims=True),
+        jnp.sum(rounded.astype(f32), 0, keepdims=True),
+    ]
+    rows = out.shape[1] - 8
+    each = out.shape[0] // att.shape[0]
+    for chip in range(att.shape[0]):
+        part = matmul(att[chip], rounded).astype(bf16)
+        for i in range(each):
+            piece = each * chip + i
+            out[piece, :rows] = part[i * rows : (i + 1) * rows]
+            put_vectors(out, piece, piece, rows, vectors, rows)
+    send(out, stacked.at[:, pl.ds(tall, rows + 8), :])
     for copy in copies:
         copy.wait()
 
@@ -499,25 +547,6 @@
     fill = out.shape[2] - rows * len(parts)
     line = jnp.concatenate(parts + [jnp.zeros((1, fill), f32)], 1)
     out[at, row : row + 8, :] = jnp.broadcast_to(line, (8, out.shape[2])).astype(bf16)
-
-
-def output_grad_kernel(gb, sums, att, above, stacked, out, sems):
-    tall = above.shape[1]
-    first = pltpu.make_async_copy(above, stacked.at[:, pl.ds(0, tall), :], sems.at[0])
-    first.start()
-    rows = out.shape[1] - 8
-    grad = gb[...]
-    vectors = [sums[i : i + 1, :] for i in range(3)]
-    for chip in range(att.shape[0]):
-        part = matmul(att[chip], grad).astype(bf16)
-        for i in range(2):
-            piece = 2 * chip + i
-            out[piece, :rows] = part[i * rows : (i + 1) * rows]
-            put_vectors(out, piece, piece, rows, vectors, rows)
-    second = pltpu.make_async_copy(out, stacked.at[:, pl.ds(tall, rows + 8), :], sems.at[1])
-    second.start()
-    first.wait()
-    second.wait()
 
 
 def ordered(ids, refs, scratch):
@@ -696,7 +725,7 @@
         (out_half,) = run_kernel(
             cut_output_kernel,
             "cut_output",
-            [((half + 16, model), bf16)],
+            [((half + 8, model), bf16)],
             (self.ids, output_weight, vec_local),
             scalars=1,
         )
@@ -773,15 +802,17 @@
             attend_kernel,
             "attend",
             [((chips, width, piece_len), bf16)] + kept,
-            (self.ids, self.weight, *self.masks(), self.packed, self.pair, self.pair_other),
-            scratch=[pltpu.VMEM(*spec) for spec in kept]
+            (self.ids, self.weight, *self.masks(), self.pair, self.pair_other, self.packed),
+            scratch=[pltpu.VMEM(self.packed.shape, bf16)]
+            + [pltpu.VMEM(*spec) for spec in kept]
             + [
                 pltpu.VMEM((self.splits, piece_len, width), bf16),
                 pltpu.VMEM((chips * piece_len, tokens), f32),
                 pltpu.VMEM((chips * piece_len, tokens), bf16),
-                pltpu.SemaphoreType.DMA((len(kept),)),
+                pltpu.SemaphoreType.DMA((len(kept) + 2,)),
             ],
             scalars=1,
+            raw=(8,),
             raw_outs=range(1, 1 + len(kept)),
             flops=6 * tokens * model * width + 2 * tokens * tokens * width,
             powers=tokens * tokens * 3 // 2,
@@ -794,40 +825,14 @@
             "assemble_output",
             [((self.splits, 2, half, model), bf16), ((16, model), f32)],
             (self.ids, out_half, swap_cores(out_half)),
-            scratch=[pltpu.VMEM((self.splits, 16, model), bf16)],
+            scratch=[pltpu.VMEM((self.splits, 8, model), bf16)],
             scalars=1,
         )
         self.output_weight = weight.reshape(chips, width, model)
         att = along_line(att)
         return att
 
-    def inner_grads(self, stacked):
-        self.stacked = stacked
-
-    def output_grad(self, attended, grad_branch, sums):
-        chips, model = self.chips, self.model
-        rows = model // self.splits + 8
-        below = self.stacked.shape[1]
-        (stacked,) = run_kernel(
-            output_grad_kernel,
-            "output_grad",
-            [((self.splits, below + rows, model), bf16)],
-            (grad_branch, sums, attended, self.stacked),
-            scratch=[
-                pltpu.VMEM((self.splits, rows, model), bf16),
-                pltpu.SemaphoreType.DMA((2,)),
-            ],
-            raw_outs=(0,),
-            flops=2 * self.piece_len * model * model,
-        )
-        self.share = lax.psum_scatter(stacked, "seq", scatter_dimension=0, tiled=False)
-
-    def finish_grads(self, after):
-        rows = self.model // self.splits
-        d_inner, d_outer, d_output, vectors = finish_inner(self.ids, self.shares, rows)
-        return d_inner, d_outer, d_output, vectors[len(self.shares) + 1], vectors
-
-    def backward(self, grads, grad_res):
+    def backward(self, grads, grad_res, share):
         chips, piece_len, width = self.chips, self.piece_len, self.width
         splits, model = self.splits, self.model
         groups = lax.axis_size("dp")
@@ -863,9 +868,10 @@
         )
         recv = swap_cores(other)
         dws = add_split(dw_mine, swap_cores(dw_other), [(group, bf16)] * groups)
-        dq = tied(dq, dws[0])
         dws = exchange_parts(dws)
         full = (piece_len, model)
+        *dws, sums = sum_split(dws, [(quarter, bf16)] * chips + [((8, 3 * width), f32)])
+        dq = tied(dq, dws[0])
         (partial,) = run_kernel(
             input_grad_kernel,
             "input_grad",
@@ -875,12 +881,11 @@
             scalars=1,
             flops=3 * tokens * model * width,
         )
-        *dws, sums = sum_split(dws, [(quarter, bf16)] * chips + [((8, 3 * width), f32)])
         dws = line_parts(dws)
         part = (chips,) + quarter
         dw = stack(*dws)
         every = exchange_all(dw)
-        self.shares = exchange_all(tied(self.share, *every[1:]))
+        self.shares = exchange_all(tied(share, *every[1:]))
         count = splits
         lines = [[2 * i + c for i in range(count // 2)] for c in range(2)]
         partial = lax.psum_scatter(
@@ -900,7 +905,7 @@
         core = self.position % 2
         bias_q = lax.dynamic_slice_in_dim(sums[0], core * rows, rows)
         bias_v = lax.dynamic_slice_in_dim(sums[0], 2 * width + core * rows, rows)
-        return input_grad, gq, bias_q, gk, gv, bias_v, dws[0]
+        return input_grad, gq, bias_q, gk, gv, bias_v
 
 
 def one_hot(index, count):
@@ -1049,27 +1054,10 @@
         both = both.reshape(splits, 2, rows, model).transpose(1, 0, 2, 3)
         self.both = both.reshape(1, 2 * model, model)
 
-    def inner_grads(self, stacked):
-        self.share = lax.psum_scatter(stacked, "seq", scatter_dimension=0, tiled=False)
-
-    def output_grad(self, attended, grad_branch, sums):
-        splits = self.splits
-        full = matmul(attended[0], grad_branch)
-        share = lax.psum_scatter(full, "seq", scatter_dimension=0, tiled=True)
-        self.total = lax.psum(share.astype(bf16), "dp").astype(f32)
-        lines = lax.psum(sums[:3], ("dp", "seq")).reshape(3, splits, -1)
-        self.lines = lax.dynamic_index_in_dim(lines, self.position, 1, keepdims=False)
-
-    def finish_grads(self, after):
-        model = self.hidden.shape[1]
-        groups = lax.axis_size("dp")
-        rows = model // self.splits
-        d_inner, d_outer, _, vectors = finish_inner(self.ids, exchange_all(self.share), rows)
-        return d_inner, d_outer, self.total, self.lines.reshape(-1), vectors
-
-    def backward(self, grads, grad_res):
+    def backward(self, grads, grad_res, share):
         hidden = self.hidden
         grad = grads[0].T
+        self.shares = exchange_all(share)
         splits, position = self.splits, self.position
         seq_count, per, _, _, size = self.query.shape
         row_count, model = hidden.shape
@@ -1145,7 +1133,7 @@
         biases = jnp.stack([jnp.sum(grads[i].astype(f32), 0) for i in (0, 2)], 1)
         biases = lax.psum_scatter(biases, "seq", scatter_dimension=0, tiled=True)
         biases = lax.psum(biases.astype(bf16), "dp").astype(f32)
-        return input_grad, shares[0], biases[:, 0], shares[1], shares[2], biases[:, 1], biases
+        return input_grad, shares[0], biases[:, 0], shares[1], shares[2], biases[:, 1]
 
 
 def local(
@@ -1229,7 +1217,7 @@
         scratch=[
             pltpu.VMEM(both.shape, bf16),
             pltpu.VMEM((groups,) + full, bf16),
-            pltpu.SemaphoreType.DMA((groups + 1,)),
+            pltpu.SemaphoreType.DMA((groups + 2,)),
         ],
         scalars=1,
         raw=range(2, 3 + groups),
@@ -1245,39 +1233,48 @@
         (*exchange_parts(parts), normed, cotangent.reshape(row_count, model), vec),
     )
     grads = exchange_all(grad_low)
-    stacked = ((splits, 2 * rows + 8, model), bf16)
     parts = run_kernel(
         functools.partial(backward_kernel, parts=groups),
         "backward",
-        [(full, f32)] + [(full, bf16)] * (groups - 1) + [stacked],
-        (ids, both, inner, act, sums2, *lows, *grads),
-        scalars=1,
-        flops=4 * work,
+        [(full, f32)] + [(full, bf16)] * (groups - 1) + [(wide, bf16), ((1, wide[1]), f32)],
+        (both, inner, *grads),
+        flops=2 * work,
         powers=wide[0] * wide[1],
-        grant=(2 if by_heads else 5) * VMEM_BYTES,
     )
     recv = exchange_parts(parts[:groups])
-    attention.inner_grads(*parts[groups:])
+    (above,) = run_kernel(
+        functools.partial(inner_outer_kernel, parts=groups),
+        "inner_outer",
+        [((splits, 2 * rows + 8, model), bf16)],
+        (parts[groups], act, sums2, parts[groups + 1], *lows, *grads),
+        flops=2 * work,
+        grant=(1 if by_heads else 4) * VMEM_BYTES,
+    )
     slots = attended.shape[0]
-    grad_branch, sums1, grad_res, *grad_att = run_kernel(
+    below = rows + 8
+    grad_res, stacked, *grad_att = run_kernel(
         functools.partial(residual_kernel, parts=groups),
         "residual",
-        [(full, bf16), ((8, model), f32), (full, f32)] + [(attended.shape[1:], bf16)] * slots,
-        (ids, grad_mix, normed, inverse, vec, w_out, *recv),
+        [(full, f32), ((splits, 3 * rows + 16, model), bf16)]
+        + [(attended.shape[1:], bf16)] * slots,
+        (ids, grad_mix, normed, inverse, vec, w_out, attended, above, *recv),
         scratch=[
             pltpu.VMEM(full, f32),
             pltpu.VMEM(attended.shape, bf16),
-            pltpu.SemaphoreType.DMA((slots + 1,)),
+            pltpu.VMEM((splits, below, model), bf16),
+            pltpu.SemaphoreType.DMA((slots + 3,)),
         ],
         scalars=1,
-        raw_outs=range(2, 3 + slots),
-        flops=2 * row_count * model * model,
-    )
+        raw_outs=range(2 + slots),
+        flops=4 * row_count * model * model,
+        grant=2 * VMEM_BYTES,
+    )
+    share = lax.psum_scatter(stacked, "seq", scatter_dimension=0, tiled=False)
     if by_heads:
         grad_att = line_parts(grad_att)
-    attention.output_grad(attended, grad_branch, sums1)
-    input_grad, gq, bias_q, gk, gv, bias_v, after = attention.backward(grad_att, grad_res)
-    d_inner, d_outer, d_output, first_sums, vectors = attention.finish_grads(after)
+    input_grad, gq, bias_q, gk, gv, bias_v = attention.backward(grad_att, grad_res, share)
+    d_inner, d_outer, d_output, vectors = finish_inner(ids, attention.shares, rows)
+    first_sums = vectors[groups + 1]
     second_sums = vectors[groups]
 
     def cut(line, i):

time: 213 us -> 208 us (0.977)
  waiting for transfers between devices: 91.4 us -> 87.7 us
  transfers between devices with their start and end apart: 45 -> 45, of which waited for: 31 -> 30; matrix products, arithmetic and copies ran while one was open for 1% -> 1% of each run, Pallas kernels for 13% -> 15%
where the time goes in v5:
time: 208 us; the launch traced here: 204 us
  waiting for transfers between devices  87.7 us (42%)
  starting transfers between devices  49.7 us (24%)
  Pallas kernels  43.2 us (21%)
  between operations  14.4 us (7%)
  local copies, waits for them, and re-layouts  9.17 us (4%)
    pallas_call x24, Pallas kernels, run_kernel(): pl.pallas_call(kernel, name=name, out_shape=out_shape, in_specs=specs, ou...  43.2 us
    ppermute x23, waiting for transfers between devices, exchange(): return lax.ppermute(array, 'dp', [(i, i ^ k) for i in range(count)])  39.5 us
    ppermute x23, starting transfers between devices, exchange(): return lax.ppermute(array, 'dp', [(i, i ^ k) for i in range(count)])  27.8 us
    ppermute x12, waiting for transfers between devices, line_exchange(): return lax.ppermute(array, 'seq', [(i, i ^ 2 * k) for i in range(count)])  23.7 us
    ppermute x12, starting transfers between devices, line_exchange(): return lax.ppermute(array, 'seq', [(i, i ^ 2 * k) for i in range(count)])  17 us
    reduce_scatter x1, waiting for transfers between devices, backward(): lax.psum_scatter(partial, 'seq', scatter_dimension=0, axis_index_groups=l...  15.3 us
    all_to_all x1, waiting for transfers between devices, along_line(): lax.all_to_all(array, 'seq', 0, 0, tiled=True, axis_index_groups=lines)  6.87 us
    unnamed x89, local copies, waits for them, and re-layouts  6.16 us
  transfers between devices with their start and end apart: 45, of which 30 were waited for; matrix products, arithmetic and copies ran while one was open for 1% of the time, Pallas kernels for 15%

profile of v5, /device:TPU:8, one launch (start us, length us, event | category | flops | bytes accessed | tf_op | source)
XLA Modules:
  0.0 204.5 jit_solution(9340082588196056962)
XLA Ops:
  9.9 3.0 %collective-permute-start.1 = (bf16[48,576]{1,0:T(8,128)(2,1)S(1)}, bf16[48,576]{1,0:T(8,128)(2,1)S(1)}, u32[]{:S(2)}, u32[]{:S(2)}) collective-permute-start(bf16[48,576]{1,0:T(8,128)(2,1)S(1)} %get-tuple-element.81), channel_id=1, source_target_pairs={{0,4},{1,5},{2,6},{3,7},{4,0},{5,1},{6,2},{7,3},{8,12},{9,13},{10,... | collective-permute-start | bytes 165896 | tf_op jit(solution)/shard_map/ppermute | solution.py:627
  14.1 3.1 %collective-permute-done.1.refs_2_ = bf16[48,576]{1,0:T(8,128)(2,1)S(1)} collective-permute-done((bf16[48,576]{1,0:T(8,128)(2,1)S(1)}, bf16[48,576]{1,0:T(8,128)(2,1)S(1)}, u32[]{:S(2)}, u32[]{:S(2)}) %collective-permute-start.1) | collective-permute-done | bytes 55328 | tf_op jit(solution)/shard_map/ppermute | solution.py:627
  19.7 4.7 %collective-permute-done.3.refs_1_ = bf16[4,48,576]{2,1,0:T(8,128)(2,1)S(1)} collective-permute-done((bf16[4,48,576]{2,1,0:T(8,128)(2,1)S(1)}, bf16[4,48,576]{2,1,0:T(8,128)(2,1)S(1)}, u32[]{:S(2)}, u32[]{:S(2)}) %collective-permute-start.3) | collective-permute-done | bytes 221216 | tf_op jit(solution)/shard_map/ppermute | solution.py:609
  25.4 2.5 %collective-permute-start.4 = (bf16[56,768]{1,0:T(8,128)(2,1)S(1)}, bf16[56,768]{1,0:T(8,128)(2,1)S(1)}, u32[]{:S(2)}, u32[]{:S(2)}) collective-permute-start(bf16[56,768]{1,0:T(8,128)(2,1)S(1)} %cut_output.1.refs_0_), channel_id=1, source_target_pairs={{0,2},{1,3},{2,0},{3,1},{4,6},{5,7},{6,4},{7,5},{8,10},{9,11},{10,... | collective-permute-start | bytes 258056 | tf_op jit(solution)/shard_map/ppermute | solution.py:627
  31.0 4.7 %collective-permute-done.4.refs_1_ = bf16[56,768]{1,0:T(8,128)(2,1)S(1)} collective-permute-done((bf16[56,768]{1,0:T(8,128)(2,1)S(1)}, bf16[56,768]{1,0:T(8,128)(2,1)S(1)}, u32[]{:S(2)}, u32[]{:S(2)}) %collective-permute-start.4) | collective-permute-done | bytes 86048 | tf_op jit(solution)/shard_map/ppermute | solution.py:627
  35.7 2.6 %collective-permute-done.5.refs_2_ = bf16[56,768]{1,0:T(8,128)(2,1)S(1)} collective-permute-done((bf16[56,768]{1,0:T(8,128)(2,1)S(1)}, bf16[56,768]{1,0:T(8,128)(2,1)S(1)}, u32[]{:S(2)}, u32[]{:S(2)}) %collective-permute-start.5) | collective-permute-done | bytes 86048 | tf_op jit(solution)/shard_map/ppermute | solution.py:627
  38.3 3.1 %collective-permute-done.6.refs_3_ = bf16[56,768]{1,0:T(8,128)(2,1)S(1)} collective-permute-done((bf16[56,768]{1,0:T(8,128)(2,1)S(1)}, bf16[56,768]{1,0:T(8,128)(2,1)S(1)}, u32[]{:S(2)}, u32[]{:S(2)}) %collective-permute-start.6) | collective-permute-done | bytes 86048 | tf_op jit(solution)/shard_map/ppermute | solution.py:627
  45.2 7.1 %attend.1 = (bf16[4,192,128]{2,1,0:T(8,128)(2,1)S(1)}, bf16[4,128,192]{2,1,0:T(8,128)(2,1)}, bf16[1024,192]{1,0:T(8,128)(2,1)}, bf16[1024,192]{1,0:T(8,128)(2,1)}, f32[4,128,128]{2,1,0:T(8,128)}) custom-call(s32[3]{0:T(128)S(1)} %pad_add_fusion.ids, bf16[768,576]{1,0:T(8,128)(2,1)S(1)} %bitcast.47, f32[12,2,1024]{2,1,0:T(2,128)S(1)} %reshape_reshape.3.be, ...), custom_call_target="tpu_custom_call" | custom-call | flops 1308622848 | bytes 4008716 | tf_op jit(solution)/shard_map/attend/pallas_call | solution.py:48
  53.7 3.7 %all-to-all-start = ((bf16[4,192,128]{2,1,0:T(8,128)(2,1)}), bf16[4,192,128]{2,1,0:T(8,128)(2,1)S(1)}, u32[]{:S(2)}, u32[]{:S(2)}) async-start(bf16[4,192,128]{2,1,0:T(8,128)(2,1)} %copy-done.15), calls=%async_computation | async-start | bytes 393216 | tf_op jit(solution)/shard_map/all_to_all | solution.py:658
  60.7 6.9 %all-to-all-done.att = bf16[4,192,128]{2,1,0:T(8,128)(2,1)S(1)} async-done(((bf16[4,192,128]{2,1,0:T(8,128)(2,1)}), bf16[4,192,128]{2,1,0:T(8,128)(2,1)S(1)}, u32[]{:S(2)}, u32[]{:S(2)}) %all-to-all-start) | async-done | bytes 196640 | tf_op jit(solution)/shard_map/all_to_all | solution.py:658
  71.8 4.3 %collective-permute-done.11.refs_1_ = bf16[128,768]{1,0:T(8,128)(2,1)S(1)} collective-permute-done((bf16[128,768]{1,0:T(8,128)(2,1)S(1)}, bf16[128,768]{1,0:T(8,128)(2,1)S(1)}, u32[]{:S(2)}, u32[]{:S(2)}) %collective-permute-start.11) | collective-permute-done | bytes 196640 | tf_op jit(solution)/shard_map/ppermute | solution.py:609
  76.1 4.0 %collective-permute-done.12.refs_2_ = bf16[128,768]{1,0:T(8,128)(2,1)S(1)} collective-permute-done((bf16[128,768]{1,0:T(8,128)(2,1)S(1)}, bf16[128,768]{1,0:T(8,128)(2,1)S(1)}, u32[]{:S(2)}, u32[]{:S(2)}) %collective-permute-start.12) | collective-permute-done | bytes 196640 | tf_op jit(solution)/shard_map/ppermute | solution.py:609
  81.5 4.5 %forward.1 = (f32[128,768]{1,0:T(8,128)S(1)}, bf16[128,768]{1,0:T(8,128)(2,1)S(1)}, bf16[128,768]{1,0:T(8,128)(2,1)S(1)}, bf16[128,768]{1,0:T(8,128)(2,1)S(1)}, ...) custom-call(s32[3]{0:T(128)S(1)} %copy-done.22, f32[16,768]{1,0:T(8,128)S(1)} %get-tuple-element.86.vec.refs_6_, ...), custom_call_target="tpu_custom_call" | custom-call | flops 1207959552 | bytes 6537228 | tf_op jit(solution)/shard_map/forward/pallas_call | solution.py:48
  89.5 3.6 %collective-permute-done.14.refs_1_ = bf16[128,768]{1,0:T(8,128)(2,1)S(1)} collective-permute-done((bf16[128,768]{1,0:T(8,128)(2,1)S(1)}, bf16[128,768]{1,0:T(8,128)(2,1)S(1)}, u32[]{:S(2)}, u32[]{:S(2)}) %collective-permute-start.14) | collective-permute-done | bytes 196640 | tf_op jit(solution)/shard_map/ppermute | solution.py:609
  93.1 3.0 %collective-permute-done.15.refs_2_ = bf16[128,768]{1,0:T(8,128)(2,1)S(1)} collective-permute-done((bf16[128,768]{1,0:T(8,128)(2,1)S(1)}, bf16[128,768]{1,0:T(8,128)(2,1)S(1)}, u32[]{:S(2)}, u32[]{:S(2)}) %collective-permute-start.15) | collective-permute-done | bytes 196640 | tf_op jit(solution)/shard_map/ppermute | solution.py:609
  97.8 1.8 collective-permute-start.18
  100.7 2.2 %collective-permute-done.17.refs_1_.refs_5_ = bf16[128,768]{1,0:T(8,128)(2,1)S(1)} collective-permute-done((bf16[128,768]{1,0:T(8,128)(2,1)S(1)}, bf16[128,768]{1,0:T(8,128)(2,1)S(1)}, u32[]{:S(2)}, u32[]{:S(2)}) %collective-permute-start.17) | collective-permute-done | bytes 196640 | tf_op jit(solution)/shard_map/ppermute | solution.py:609
  102.9 2.0 %collective-permute-done.18.refs_2_.refs_6_ = bf16[128,768]{1,0:T(8,128)(2,1)S(1)} collective-permute-done((bf16[128,768]{1,0:T(8,128)(2,1)S(1)}, bf16[128,768]{1,0:T(8,128)(2,1)S(1)}, u32[]{:S(2)}, u32[]{:S(2)}) %collective-permute-start.18) | collective-permute-done | bytes 196640 | tf_op jit(solution)/shard_map/ppermute | solution.py:609
  106.2 2.1 %backward.1 = (f32[128,768]{1,0:T(8,128)S(1)}, bf16[128,768]{1,0:T(8,128)(2,1)S(1)}, bf16[128,768]{1,0:T(8,128)(2,1)S(1)}, bf16[128,768]{1,0:T(8,128)(2,1)S(1)},...) custom-call(bf16[8,192,768]{2,1,0:T(8,128)(2,1)S(1)} %bitcast.50, f32[512,768]{1,0:T(8,128)S(1)} %get-tuple-element.98.inner_ref, ...), custom_call_target="tpu_custom_call" | custom-call | flops 1207959552 | bytes 6491136 | tf_op jit(solution)/shard_map/backward/pallas_call | solution.py:48
  111.9 2.4 %inner_outer.1.above = bf16[8,200,768]{2,1,0:T(8,128)(2,1)S(1)} custom-call(bf16[512,768]{1,0:T(8,128)(2,1)S(1)} %get-tuple-element.100.gi, bf16[512,768]{1,0:T(8,128)(2,1)S(1)} %get-tuple-element.101.act, f32[8,768]{1,0:T(8,128)S(1)} %get-tuple-element.102.sums, f32[1,768]{1,0:T(1,128)S(1)} %get-tuple-element.103.total, bf16[128,768]{1,0:T(8,128)(2,1)S(1)} %copy-done.9, ...), custom_call_target="tpu_custom_call" | custom-call | flops 1207959552 | bytes 5630976 | tf_op jit(solution)/shard_map/inner_outer/pallas_call | solution.py:48
  114.3 2.7 %collective-permute-done.21.refs_2_ = bf16[128,768]{1,0:T(8,128)(2,1)S(1)} collective-permute-done((bf16[128,768]{1,0:T(8,128)(2,1)S(1)}, bf16[128,768]{1,0:T(8,128)(2,1)S(1)}, u32[]{:S(2)}, u32[]{:S(2)}) %collective-permute-start.21) | collective-permute-done | bytes 196640 | tf_op jit(solution)/shard_map/ppermute | solution.py:609
  117.0 3.1 %residual.1 = (f32[128,768]{1,0:T(8,128)}, bf16[8,304,768]{2,1,0:T(8,128)(2,1)}, bf16[192,128]{1,0:T(8,128)(2,1)}, bf16[192,128]{1,0:T(8,128)(2,1)}, bf16[192,128]{1,0:T(8,128)(2,1)}, /*index=5*/bf16[192,128]{1,0:T(8,128)(2,1)}) custom-call(s32[3]{0:T(128)S(1)} %copy-done.23, f32[128,768]{1,0:T(8,128)S(1)} %get-tuple-element.96.mix, ...), custom_call_target="tpu_custom_call" | custom-call | flops 301989888 | bytes 10043404 | tf_op jit(solution)/shard_map/residual/pallas_call | solution.py:48
  121.0 2.9 %collective-permute-start.23 = (bf16[192,128]{1,0:T(8,128)(2,1)S(1)}, bf16[192,128]{1,0:T(8,128)(2,1)S(1)}, u32[]{:S(2)}, u32[]{:S(2)}) collective-permute-start(bf16[192,128]{1,0:T(8,128)(2,1)S(1)} %copy-done.40), channel_id=1, source_target_pairs={{0,2},{1,3},{2,0},{3,1},{4,6},{5,7},{6,4},{7,5},{8,10},{9,11},{10,... | collective-permute-start | bytes 147464 | tf_op jit(solution)/shard_map/ppermute | solution.py:627
  125.9 3.0 %collective-permute-done.24.refs_2_ = bf16[192,128]{1,0:T(8,128)(2,1)S(1)} collective-permute-done((bf16[192,128]{1,0:T(8,128)(2,1)S(1)}, bf16[192,128]{1,0:T(8,128)(2,1)S(1)}, u32[]{:S(2)}, u32[]{:S(2)}) %collective-permute-start.24) | collective-permute-done | bytes 49184 | tf_op jit(solution)/shard_map/ppermute | solution.py:627
  129.7 9.6 %attend_back.1 = (bf16[4,128,192]{2,1,0:T(8,128)(2,1)S(1)}, bf16[4,128,384]{2,1,0:T(8,128)(2,1)S(1)}, bf16[4,128,384]{2,1,0:T(8,128)(2,1)S(1)}, f32[4,104,576]{2,1,0:T(8,128)S(1)}, bf16[4,104,576]{2,1,0:T(8,128)(2,1)S(1)}) custom-call(s32[3]{0:T(128)S(1)} %copy-done.23, bf16[8,128,768]{2,1,0:T(8,128)(2,1)} %all-gather.4.cloned.1.call-done.hid_raw, ...), custom_call_target="tpu_custom_call" | custom-call | flops 1912602624 | bytes 5543948 | tf_op jit(solution)/shard_map/attend_back/pallas_call | solution.py:48
  145.1 2.9 %collective-permute-done.27.refs_1_ = bf16[104,576]{1,0:T(8,128)(2,1)S(1)} collective-permute-done((bf16[104,576]{1,0:T(8,128)(2,1)S(1)}, bf16[104,576]{1,0:T(8,128)(2,1)S(1)}, u32[]{:S(2)}, u32[]{:S(2)}) %collective-permute-start.27) | collective-permute-done | bytes 119840 | tf_op jit(solution)/shard_map/ppermute | solution.py:609
  148.0 2.9 %collective-permute-done.28.refs_2_ = bf16[104,576]{1,0:T(8,128)(2,1)S(1)} collective-permute-done((bf16[104,576]{1,0:T(8,128)(2,1)S(1)}, bf16[104,576]{1,0:T(8,128)(2,1)S(1)}, u32[]{:S(2)}, u32[]{:S(2)}) %collective-permute-start.28) | collective-permute-done | bytes 119840 | tf_op jit(solution)/shard_map/ppermute | solution.py:609
  150.9 2.3 %input_grad.1 = bf16[4,128,768]{2,1,0:T(8,128)(2,1)} custom-call(s32[3]{0:T(128)S(1)} %copy-done.23, bf16[4,128,192]{2,1,0:T(8,128)(2,1)S(1)} %get-tuple-element.125.dq, bf16[4,128,384]{2,1,0:T(8,128)(2,1)S(1)} %get-tuple-element.126.mine, bf16[4,128,384]{2,1,0:T(8,128)(2,1)S(1)} %collective-permute-done.30.recv, bf16[768,576]{1,0:T(8,128)(2,1)S(1)} %bitcast.48), custom_call_target="tpu_custom_call" | custom-call | flops 452984832 | bytes 2654220 | tf_op jit(solution)/shard_map/input_grad/pallas_call | solution.py:48
  153.3 3.5 %collective-permute-start.31 = (bf16[24,576]{1,0:T(8,128)(2,1)S(1)}, bf16[24,576]{1,0:T(8,128)(2,1)S(1)}, u32[]{:S(2)}, u32[]{:S(2)}) collective-permute-start(bf16[24,576]{1,0:T(8,128)(2,1)S(1)} %get-tuple-element.128), channel_id=1, source_target_pairs={{0,2},{1,3},{2,0},{3,1},{4,6},{5,7},{6,4},{7,5},{8,10},{9,11},{10,... | collective-permute-start | bytes 82952 | tf_op jit(solution)/shard_map/ppermute | solution.py:627
  159.8 2.6 %collective-permute-done.32.refs_2_ = bf16[24,576]{1,0:T(8,128)(2,1)S(1)} collective-permute-done((bf16[24,576]{1,0:T(8,128)(2,1)S(1)}, bf16[24,576]{1,0:T(8,128)(2,1)S(1)}, u32[]{:S(2)}, u32[]{:S(2)}) %collective-permute-start.32) | collective-permute-done | bytes 27680 | tf_op jit(solution)/shard_map/ppermute | solution.py:627
  177.1 15.3 %reduce-scatter.3.cloned.1.call-done.parts = bf16[1,128,768]{2,1,0:T(8,128)(2,1)} async-done(((bf16[4,128,768]{2,1,0:T(8,128)(2,1)}), bf16[1,128,768]{2,1,0:T(8,128)(2,1)}) %reduce-scatter.3.cloned.1.call-update) | async-done | bytes 196624 | tf_op jit(solution)/shard_map/reduce_scatter | solution.py:891
  194.1 2.5 %finish_inner.1 = (f32[96,3072]{1,0:T(8,128)}, f32[384,768]{1,0:T(8,128)}, f32[96,768]{1,0:T(8,128)}, f32[8,768]{1,0:T(8,128)S(1)}) custom-call(s32[3]{0:T(128)S(1)} %copy-done.23, bf16[304,768]{1,0:T(8,128)(2,1)S(1)} %bitcast.55, bf16[304,768]{1,0:T(8,128)(2,1)S(1)} %collective-permute-done.37.refs_1_, ...), custom_call_target="tpu_custom_call" | custom-call | bytes 4546572 | tf_op jit(solution)/shard_map/finish_inner/pallas_call | solution.py:48
  (201 shorter events, 65.4 us)
Async XLA Ops:
  7.3 34.8 %all-gather.4.cloned.1.call-start = ((), (), s32[]{:S(2)}) async-start(), calls=%async_computation.3 | async-start | bytes 1769472 | tf_op jit(solution)/shard_map/all_gather | solution.py:704
  8.0 72.8 %all-gather.6.cloned.1.call-start = ((), (), s32[]{:S(2)}) async-start(), calls=%async_computation.6 | async-start | bytes 2654208 | tf_op jit(solution)/shard_map/all_gather | solution.py:789
  9.9 7.3 %collective-permute-start.1 = (bf16[48,576]{1,0:T(8,128)(2,1)S(1)}, bf16[48,576]{1,0:T(8,128)(2,1)S(1)}, u32[]{:S(2)}, u32[]{:S(2)}) collective-permute-start(bf16[48,576]{1,0:T(8,128)(2,1)S(1)} %get-tuple-element.81), channel_id=1, source_target_pairs={{0,4},{1,5},{2,6},{3,7},{4,0},{5,1},{6,2},{7,3},{8,12},{9,13},{10,... | collective-permute-start | bytes 165896 | tf_op jit(solution)/shard_map/ppermute | solution.py:627
  18.2 6.3 %collective-permute-start.3 = (bf16[4,48,576]{2,1,0:T(8,128)(2,1)S(1)}, bf16[4,48,576]{2,1,0:T(8,128)(2,1)S(1)}, u32[]{:S(2)}, u32[]{:S(2)}) collective-permute-start(bf16[4,48,576]{2,1,0:T(8,128)(2,1)S(1)} %stack.27.refs_0_), channel_id=1, source_target_pairs={{0,8},{8,0},{16,24},{24,16},{1,9},{9,1},{17,25},{25,17},{2,10},{10... | collective-permute-start | bytes 663560 | tf_op jit(solution)/shard_map/ppermute | solution.py:609
  24.5 16.9 %collective-permute-start.7 = (bf16[2,4,48,576]{3,2,1,0:T(8,128)(2,1)S(1)}, bf16[2,4,48,576]{3,2,1,0:T(8,128)(2,1)S(1)}, u32[]{:S(2)}, u32[]{:S(2)}) collective-permute-start(bf16[2,4,48,576]{3,2,1,0:T(8,128)(2,1)S(1)} %stack.29.mine), channel_id=1, source_target_pairs={{0,1},{1,0},{2,3},{3,2},{4,5},{5,4},{6,7},{7,6},{8,9},{9,8},{10,11... | collective-permute-start | bytes 1327112 | tf_op jit(solution)/shard_map/ppermute | solution.py:622
  25.4 10.3 %collective-permute-start.4 = (bf16[56,768]{1,0:T(8,128)(2,1)S(1)}, bf16[56,768]{1,0:T(8,128)(2,1)S(1)}, u32[]{:S(2)}, u32[]{:S(2)}) collective-permute-start(bf16[56,768]{1,0:T(8,128)(2,1)S(1)} %cut_output.1.refs_0_), channel_id=1, source_target_pairs={{0,2},{1,3},{2,0},{3,1},{4,6},{5,7},{6,4},{7,5},{8,10},{9,11},{10,... | collective-permute-start | bytes 258056 | tf_op jit(solution)/shard_map/ppermute | solution.py:627
  27.9 10.4 %collective-permute-start.5 = (bf16[56,768]{1,0:T(8,128)(2,1)S(1)}, bf16[56,768]{1,0:T(8,128)(2,1)S(1)}, u32[]{:S(2)}, u32[]{:S(2)}) collective-permute-start(bf16[56,768]{1,0:T(8,128)(2,1)S(1)} %cut_output.1.refs_0_), channel_id=1, source_target_pairs={{0,4},{1,5},{2,6},{3,7},{4,0},{5,1},{6,2},{7,3},{8,12},{9,13},{10,... | collective-permute-start | bytes 258056 | tf_op jit(solution)/shard_map/ppermute | solution.py:627
  29.5 11.9 %collective-permute-start.6 = (bf16[56,768]{1,0:T(8,128)(2,1)S(1)}, bf16[56,768]{1,0:T(8,128)(2,1)S(1)}, u32[]{:S(2)}, u32[]{:S(2)}) collective-permute-start(bf16[56,768]{1,0:T(8,128)(2,1)S(1)} %cut_output.1.refs_0_), channel_id=1, source_target_pairs={{0,6},{1,7},{2,4},{3,5},{4,2},{5,3},{6,0},{7,1},{8,14},{9,15},{10,... | collective-permute-start | bytes 258056 | tf_op jit(solution)/shard_map/ppermute | solution.py:627
  43.0 10.5 %collective-permute-start.9 = (bf16[4,56,768]{2,1,0:T(8,128)(2,1)S(1)}, bf16[4,56,768]{2,1,0:T(8,128)(2,1)S(1)}, u32[]{:S(2)}, u32[]{:S(2)}) collective-permute-start(bf16[4,56,768]{2,1,0:T(8,128)(2,1)S(1)} %stack.28.refs_0_), channel_id=1, source_target_pairs={{0,16},{8,24},{16,0},{24,8},{1,17},{9,25},{17,1},{25,9},{2,18},{10... | collective-permute-start | bytes 1032200 | tf_op jit(solution)/shard_map/ppermute | solution.py:609
  53.7 13.9 %all-to-all-start = ((bf16[4,192,128]{2,1,0:T(8,128)(2,1)}), bf16[4,192,128]{2,1,0:T(8,128)(2,1)S(1)}, u32[]{:S(2)}, u32[]{:S(2)}) async-start(bf16[4,192,128]{2,1,0:T(8,128)(2,1)} %copy-done.15), calls=%async_computation | async-start | bytes 393216 | tf_op jit(solution)/shard_map/all_to_all | solution.py:658
  57.3 114.0 %reduce-scatter.5.cloned.1.call-start = ((), (), s32[]{:S(2)}) async-start(), calls=%async_computation.5 | async-start | bytes 4202496 | tf_op jit(solution)/shard_map/reduce_scatter | solution.py:1272
  68.2 7.9 %collective-permute-start.11 = (bf16[128,768]{1,0:T(8,128)(2,1)S(1)}, bf16[128,768]{1,0:T(8,128)(2,1)S(1)}, u32[]{:S(2)}, u32[]{:S(2)}) collective-permute-start(bf16[128,768]{1,0:T(8,128)(2,1)S(1)} %get-tuple-element.89.refs_0_), channel_id=1, source_target_pairs={{0,8},{8,0},{16,24},{24,16},{1,9},{9,1},{17,25},{25,17},{2,10},{10... | collective-permute-start | bytes 589832 | tf_op jit(solution)/shard_map/ppermute | solution.py:609
  69.7 10.4 %collective-permute-start.12 = (bf16[128,768]{1,0:T(8,128)(2,1)S(1)}, bf16[128,768]{1,0:T(8,128)(2,1)S(1)}, u32[]{:S(2)}, u32[]{:S(2)}) collective-permute-start(bf16[128,768]{1,0:T(8,128)(2,1)S(1)} %get-tuple-element.89.refs_0_), channel_id=1, source_target_pairs={{0,16},{8,24},{16,0},{24,8},{1,17},{9,25},{17,1},{25,9},{2,18},{10... | collective-permute-start | bytes 589832 | tf_op jit(solution)/shard_map/ppermute | solution.py:609
  71.2 9.6 %collective-permute-start.13 = (bf16[128,768]{1,0:T(8,128)(2,1)S(1)}, bf16[128,768]{1,0:T(8,128)(2,1)}, u32[]{:S(2)}, u32[]{:S(2)}) collective-permute-start(bf16[128,768]{1,0:T(8,128)(2,1)S(1)} %get-tuple-element.89.refs_0_), channel_id=1, source_target_pairs={{0,24},{8,16},{16,8},{24,0},{1,25},{9,17},{17,9},{25,1},{2,26},{10... | collective-permute-start | bytes 589832 | tf_op jit(solution)/shard_map/ppermute | solution.py:609
  86.0 7.1 %collective-permute-start.14 = (bf16[128,768]{1,0:T(8,128)(2,1)S(1)}, bf16[128,768]{1,0:T(8,128)(2,1)S(1)}, u32[]{:S(2)}, u32[]{:S(2)}) collective-permute-start(bf16[128,768]{1,0:T(8,128)(2,1)S(1)} %get-tuple-element.91), channel_id=1, source_target_pairs={{0,8},{8,0},{16,24},{24,16},{1,9},{9,1},{17,25},{25,17},{2,10},{10... | collective-permute-start | bytes 589832 | tf_op jit(solution)/shard_map/ppermute | solution.py:609
  86.7 9.5 %collective-permute-start.15 = (bf16[128,768]{1,0:T(8,128)(2,1)S(1)}, bf16[128,768]{1,0:T(8,128)(2,1)S(1)}, u32[]{:S(2)}, u32[]{:S(2)}) collective-permute-start(bf16[128,768]{1,0:T(8,128)(2,1)S(1)} %get-tuple-element.92), channel_id=1, source_target_pairs={{0,16},{8,24},{16,0},{24,8},{1,17},{9,25},{17,1},{25,9},{2,18},{10... | collective-permute-start | bytes 589832 | tf_op jit(solution)/shard_map/ppermute | solution.py:609
  88.1 8.1 %collective-permute-start.16 = (bf16[128,768]{1,0:T(8,128)(2,1)S(1)}, bf16[128,768]{1,0:T(8,128)(2,1)S(1)}, u32[]{:S(2)}, u32[]{:S(2)}) collective-permute-start(bf16[128,768]{1,0:T(8,128)(2,1)S(1)} %get-tuple-element.93), channel_id=1, source_target_pairs={{0,24},{8,16},{16,8},{24,0},{1,25},{9,17},{17,9},{25,1},{2,26},{10... | collective-permute-start | bytes 589832 | tf_op jit(solution)/shard_map/ppermute | solution.py:609
  97.8 7.1 %collective-permute-start.18 = (bf16[128,768]{1,0:T(8,128)(2,1)S(1)}, bf16[128,768]{1,0:T(8,128)(2,1)S(1)}, u32[]{:S(2)}, u32[]{:S(2)}) collective-permute-start(bf16[128,768]{1,0:T(8,128)(2,1)S(1)} %get-tuple-element.99.refs_0_.refs_4_), channel_id=1, source_target_pairs={{0,16},{8,24},{16,0},{24,8},{1,17},{9,25},{17,1},{25,9},{2,18},{10... | collective-permute-start | bytes 589832 | tf_op jit(solution)/shard_map/ppermute | solution.py:609
  99.6 6.6 %collective-permute-start.19 = (bf16[128,768]{1,0:T(8,128)(2,1)S(1)}, bf16[128,768]{1,0:T(8,128)(2,1)S(1)}, u32[]{:S(2)}, u32[]{:S(2)}) collective-permute-start(bf16[128,768]{1,0:T(8,128)(2,1)S(1)} %get-tuple-element.99.refs_0_.refs_4_), channel_id=1, source_target_pairs={{0,24},{8,16},{16,8},{24,0},{1,25},{9,17},{17,9},{25,1},{2,26},{10... | collective-permute-start | bytes 589832 | tf_op jit(solution)/shard_map/ppermute | solution.py:609
  108.3 5.9 %collective-permute-start.20 = (bf16[128,768]{1,0:T(8,128)(2,1)S(1)}, bf16[128,768]{1,0:T(8,128)(2,1)S(1)}, u32[]{:S(2)}, u32[]{:S(2)}) collective-permute-start(bf16[128,768]{1,0:T(8,128)(2,1)S(1)} %get-tuple-element.105), channel_id=1, source_target_pairs={{0,8},{8,0},{16,24},{24,16},{1,9},{9,1},{17,25},{25,17},{2,10},{10... | collective-permute-start | bytes 589832 | tf_op jit(solution)/shard_map/ppermute | solution.py:609
  109.2 7.8 %collective-permute-start.21 = (bf16[128,768]{1,0:T(8,128)(2,1)S(1)}, bf16[128,768]{1,0:T(8,128)(2,1)S(1)}, u32[]{:S(2)}, u32[]{:S(2)}) collective-permute-start(bf16[128,768]{1,0:T(8,128)(2,1)S(1)} %get-tuple-element.106), channel_id=1, source_target_pairs={{0,16},{8,24},{16,0},{24,8},{1,17},{9,25},{17,1},{25,9},{2,18},{10... | collective-permute-start | bytes 589832 | tf_op jit(solution)/shard_map/ppermute | solution.py:609
  110.1 6.9 %collective-permute-start.22 = (bf16[128,768]{1,0:T(8,128)(2,1)S(1)}, bf16[128,768]{1,0:T(8,128)(2,1)S(1)}, u32[]{:S(2)}, u32[]{:S(2)}) collective-permute-start(bf16[128,768]{1,0:T(8,128)(2,1)S(1)} %get-tuple-element.107), channel_id=1, source_target_pairs={{0,24},{8,16},{16,8},{24,0},{1,25},{9,17},{17,9},{25,1},{2,26},{10... | collective-permute-start | bytes 589832 | tf_op jit(solution)/shard_map/ppermute | solution.py:609
  120.2 72.1 %reduce-scatter.3.cloned.1.call-start = ((), (), s32[]{:S(2)}) async-start(), calls=%async_computation.4 | async-start | bytes 983040 | tf_op jit(solution)/shard_map/reduce_scatter | solution.py:891
  139.4 11.5 %collective-permute-start.30 = (bf16[4,128,384]{2,1,0:T(8,128)(2,1)S(1)}, bf16[4,128,384]{2,1,0:T(8,128)(2,1)S(1)}, u32[]{:S(2)}, u32[]{:S(2)}) collective-permute-start(bf16[4,128,384]{2,1,0:T(8,128)(2,1)S(1)} %get-tuple-element.127), channel_id=1, source_target_pairs={{0,1},{1,0},{2,3},{3,2},{4,5},{5,4},{6,7},{7,6},{8,9},{9,8},{10,11... | collective-permute-start | bytes 1179656 | tf_op jit(solution)/shard_map/ppermute | solution.py:622
  141.5 6.4 %collective-permute-start.27 = (bf16[104,576]{1,0:T(8,128)(2,1)S(1)}, bf16[104,576]{1,0:T(8,128)(2,1)S(1)}, u32[]{:S(2)}, u32[]{:S(2)}) collective-permute-start(bf16[104,576]{1,0:T(8,128)(2,1)S(1)} %get-tuple-element.121), channel_id=1, source_target_pairs={{0,8},{8,0},{16,24},{24,16},{1,9},{9,1},{17,25},{25,17},{2,10},{10... | collective-permute-start | bytes 359432 | tf_op jit(solution)/shard_map/ppermute | solution.py:609
  142.7 8.2 %collective-permute-start.28 = (bf16[104,576]{1,0:T(8,128)(2,1)S(1)}, bf16[104,576]{1,0:T(8,128)(2,1)S(1)}, u32[]{:S(2)}, u32[]{:S(2)}) collective-permute-start(bf16[104,576]{1,0:T(8,128)(2,1)S(1)} %get-tuple-element.122), channel_id=1, source_target_pairs={{0,16},{8,24},{16,0},{24,8},{1,17},{9,25},{17,1},{25,9},{2,18},{10... | collective-permute-start | bytes 359432 | tf_op jit(solution)/shard_map/ppermute | solution.py:609
  144.0 6.9 %collective-permute-start.29 = (bf16[104,576]{1,0:T(8,128)(2,1)S(1)}, bf16[104,576]{1,0:T(8,128)(2,1)S(1)}, u32[]{:S(2)}, u32[]{:S(2)}) collective-permute-start(bf16[104,576]{1,0:T(8,128)(2,1)S(1)} %get-tuple-element.123), channel_id=1, source_target_pairs={{0,24},{8,16},{16,8},{24,0},{1,25},{9,17},{17,9},{25,1},{2,26},{10... | collective-permute-start | bytes 359432 | tf_op jit(solution)/shard_map/ppermute | solution.py:609
  153.3 6.5 %collective-permute-start.31 = (bf16[24,576]{1,0:T(8,128)(2,1)S(1)}, bf16[24,576]{1,0:T(8,128)(2,1)S(1)}, u32[]{:S(2)}, u32[]{:S(2)}) collective-permute-start(bf16[24,576]{1,0:T(8,128)(2,1)S(1)} %get-tuple-element.128), channel_id=1, source_target_pairs={{0,2},{1,3},{2,0},{3,1},{4,6},{5,7},{6,4},{7,5},{8,10},{9,11},{10,... | collective-permute-start | bytes 82952 | tf_op jit(solution)/shard_map/ppermute | solution.py:627
  165.6 5.8 %collective-permute-start.36 = (bf16[4,24,576]{2,1,0:T(8,128)(2,1)S(1)}, bf16[4,24,576]{2,1,0:T(8,128)(2,1)S(1)}, u32[]{:S(2)}, u32[]{:S(2)}) collective-permute-start(bf16[4,24,576]{2,1,0:T(8,128)(2,1)S(1)} %stack.31.refs_0_), channel_id=1, source_target_pairs={{0,24},{8,16},{16,8},{24,0},{1,25},{9,17},{17,9},{25,1},{2,26},{10... | collective-permute-start | bytes 331784 | tf_op jit(solution)/shard_map/ppermute | solution.py:609
  171.4 22.7 %collective-permute-start.37 = (bf16[304,768]{1,0:T(8,128)(2,1)}, bf16[304,768]{1,0:T(8,128)(2,1)S(1)}, u32[]{:S(2)}, u32[]{:S(2)}) collective-permute-start(bf16[304,768]{1,0:T(8,128)(2,1)} %bitcast.52), channel_id=1, source_target_pairs={{0,8},{8,0},{16,24},{24,16},{1,9},{9,1},{17,25},{25,17},{2,10},{10... | collective-permute-start | bytes 1400840 | tf_op jit(solution)/shard_map/ppermute | solution.py:609
  172.7 21.4 %collective-permute-start.38 = (bf16[304,768]{1,0:T(8,128)(2,1)}, bf16[304,768]{1,0:T(8,128)(2,1)S(1)}, u32[]{:S(2)}, u32[]{:S(2)}) collective-permute-start(bf16[304,768]{1,0:T(8,128)(2,1)} %bitcast.53), channel_id=1, source_target_pairs={{0,16},{8,24},{16,0},{24,8},{1,17},{9,25},{17,1},{25,9},{2,18},{10... | collective-permute-start | bytes 1400840 | tf_op jit(solution)/shard_map/ppermute | solution.py:609
  173.1 21.0 %collective-permute-start.39 = (bf16[304,768]{1,0:T(8,128)(2,1)}, bf16[304,768]{1,0:T(8,128)(2,1)S(1)}, u32[]{:S(2)}, u32[]{:S(2)}) collective-permute-start(bf16[304,768]{1,0:T(8,128)(2,1)} %bitcast.54), channel_id=1, source_target_pairs={{0,24},{8,16},{16,8},{24,0},{1,25},{9,17},{17,9},{25,1},{2,26},{10... | collective-permute-start | bytes 1400840 | tf_op jit(solution)/shard_map/ppermute | solution.py:609
  (57 other events, 561.6 us)
Sparse Core Ops, SparseCore 0:
  9.8 29.8 all-gather.3
  42.3 33.7 all-gather.5
  120.4 45.7 reduce-scatter.4
  168.9 23.4 reduce-scatter.2

commit v6 on v5

--- a/solution.py
+++ b/solution.py
@@ -89,11 +89,9 @@
     return jnp.where(same, jnp.concatenate(rows, 0), bn)
 
 
-def place(ids, mine, other, out):
-    for k in range(out.shape[0] // 2):
-        chip = ids[1] ^ k
-        out[2 * chip + ids[0]] = mine[k]
-        out[2 * chip + 1 - ids[0]] = other[k]
+def here():
+    position = lax.axis_index("seq")
+    return lax.rem(position, 2), lax.div(position, 2), lax.axis_index("dp")
 
 
 def concat_kernel(*refs):
@@ -110,7 +108,8 @@
         refs[-1][k] = r[...]
 
 
-def cut_kernel(ids, wq, wk, wv, *refs):
+def cut_kernel(wq, wk, wv, *refs):
+    ids = here()
     outs = refs[:-3]
     raw, scratch, sems = refs[-3:]
     _, half, _ = raw.shape
@@ -133,7 +132,8 @@
         out[...] = scratch[ids[1] ^ k]
 
 
-def assemble_kernel(ids, mine, other, out):
+def assemble_kernel(mine, other, out):
+    ids = here()
     core = ids[0]
     own = lax.rem(ids[2], 2)
     _, chips, _, _ = mine.shape
@@ -144,10 +144,11 @@
             out[2 * chip + 1 - core, own ^ h] = other[h, k]
 
 
-def cut_output_kernel(ids, wo, vec, out):
+def cut_output_kernel(wo, vec, out):
+    ids = here()
     half = wo.shape[0] // 2
     count, rows = vec.shape
-    start = pl.multiple_of(lax.rem(ids[2] // 2, 2) * half, half)
+    start = pl.multiple_of(lax.rem(lax.div(ids[2], 2), 2) * half, half)
     tall, model = out.shape
     each = model // rows
     out[:half, :] = wo[pl.ds(start, half), :]
@@ -160,7 +161,8 @@
     out[half:, :] = jnp.concatenate(lines + [fill], 0)
 
 
-def cut_inner_kernel(ids, w1, w2, out, scratch):
+def cut_inner_kernel(w1, w2, out, scratch):
+    ids = here()
     groups, rows, model = scratch.shape
     units = w2.shape[0] // groups
     pieces = model // units
@@ -176,11 +178,12 @@
     out[rows:, :] = w2[pl.ds(pl.multiple_of(ids[2] * units, units), units), :]
 
 
-def assemble_output_kernel(ids, mine, other, out, vec, scratch):
+def assemble_output_kernel(mine, other, out, vec, scratch):
+    ids = here()
     core = ids[0]
     pieces, _, half, _ = out.shape
     chips = pieces // 2
-    own = lax.rem(ids[2] // 2, 2)
+    own = lax.rem(lax.div(ids[2], 2), 2)
     for k in range(chips):
         chip = ids[1] ^ k
         scratch[2 * chip + core] = mine[0, k, half:, :]
@@ -198,7 +201,8 @@
         )
 
 
-def attend_kernel(ids, w, be, bn, sk, sq, ours, theirs, hid_raw, *refs):
+def attend_kernel(w, be, bn, sk, sq, ours, theirs, hid_raw, *refs):
+    ids = here()
     att = refs[0]
     kept = refs[1:5]
     hid, qo, ko, vo, lse, qs, s_all, p_all, sems = refs[5:]
@@ -270,7 +274,8 @@
         copy.wait()
 
 
-def attend_back_kernel(ids, hid_raw, q_raw, k_raw, v_raw, lse_raw, be, bn, sk, sq, *refs):
+def attend_back_kernel(hid_raw, q_raw, k_raw, v_raw, lse_raw, be, bn, sk, sq, *refs):
+    ids = here()
     chips, piece_len, width = q_raw.shape
     ga_raw = refs[:chips]
     dq, mine, other, dw_mine, dw_other = refs[chips : chips + 5]
@@ -355,7 +360,8 @@
         dw_other[j, chips * rows :] = total.astype(bf16)
 
 
-def input_grad_kernel(ids, dq, mine, recv, w, out, scratch):
+def input_grad_kernel(dq, mine, recv, w, out, scratch):
+    ids = here()
     chips, piece_len, width = dq.shape
     dkv = (mine[...].astype(f32) + recv[...].astype(f32)).astype(bf16)
     grads = jnp.concatenate([dq[...], dkv], 2).reshape(chips * piece_len, 3 * width)
@@ -418,7 +424,7 @@
     return first, both[:, half:, :].reshape(pieces * half, model)
 
 
-def forward_kernel(ids, vec, both_raw, *refs, parts):
+def forward_kernel(vec, both_raw, *refs, parts):
     raw = refs[:parts]
     outs = refs[parts : 2 * parts]
     inner_ref, act_ref, both, x, sems = refs[2 * parts :]
@@ -433,7 +439,7 @@
         copy.wait()
     _, rows, model = x.shape
     weight1 = both[:, :half, :].reshape(-1, model)
-    inner = matmul(x[...].reshape(parts * rows, model), weight1) + vec[pl.ds(8 + ids[2], 1), :]
+    inner = matmul(x[...].reshape(parts * rows, model), weight1) + vec[pl.ds(8 + lax.axis_index("dp"), 1), :]
     act = (0.5 * inner * (1.0 + gelu_parts(inner))).astype(bf16)
     inner_ref[...] = inner
     act_ref[...] = act
@@ -500,7 +506,8 @@
         put_vectors(out, piece, piece, 2 * units, vectors, units)
 
 
-def residual_kernel(ids, mix, normed, inverse, vec, wo, att, above, *refs, parts):
+def residual_kernel(mix, normed, inverse, vec, wo, att, above, *refs, parts, lined):
+    ids = here() if lined else (0, 0, 0)
     recv = refs[:parts]
     res_raw, stacked = refs[parts : parts + 2]
     back_raw = refs[parts + 2 : -4]
@@ -511,8 +518,8 @@
         copies.append(pltpu.make_async_copy(here, there, sems.at[len(copies)]))
         copies[-1].start()
 
-    tall = above.shape[1]
-    send(above, stacked.at[:, pl.ds(0, tall), :])
+    tall = above.shape[1] - 8
+    send(above.at[:, pl.ds(0, tall), :], stacked.at[:, pl.ds(0, tall), :])
     first = mix[...]
     for r in recv:
         first = first + r[...].astype(f32)
@@ -524,7 +531,7 @@
         send(back.at[k], raw)
     res[...] = grad
     send(res, res_raw)
-    vectors = [
+    vectors = [jnp.zeros((1, wo.shape[2]), f32)] * 4 + [
         jnp.sum(first * n1, 0, keepdims=True),
         jnp.sum(first, 0, keepdims=True),
         jnp.sum(rounded.astype(f32), 0, keepdims=True),
@@ -535,8 +542,9 @@
         part = matmul(att[chip], rounded).astype(bf16)
         for i in range(each):
             piece = each * chip + i
-            out[piece, :rows] = part[i * rows : (i + 1) * rows]
-            put_vectors(out, piece, piece, rows, vectors, rows)
+            out[piece, 8:] = part[i * rows : (i + 1) * rows]
+            put_vectors(out, piece, piece, 0, vectors, rows)
+            out[piece, :8] = out[piece, :8] + above[piece, tall:]
     send(out, stacked.at[:, pl.ds(tall, rows + 8), :])
     for copy in copies:
         copy.wait()
@@ -554,7 +562,8 @@
         scratch[ids[2] ^ k] = r[...]
 
 
-def finish_inner_kernel(ids, *refs, parts):
+def finish_inner_kernel(*refs, parts):
+    ids = here()
     inner, outer, output, vectors, scratch = refs[parts:]
     ordered(ids, refs[:parts], scratch)
     rows = inner.shape[0]
@@ -580,11 +589,11 @@
         last = scratch[0, at + 8 :, :].astype(f32)
         for g in range(1, parts):
             last = last + scratch[g, at + 8 :, :].astype(f32)
-        output[...] = last[:rows]
-        vectors[parts + 1 : parts + 2, :] = last[rows : rows + 1]
-
-
-def finish_kernel(ids, *refs):
+        output[...] = last
+
+
+def finish_kernel(*refs):
+    ids = here()
     parts = len(refs) - 4
     gq, gk, gv, scratch = refs[parts:]
     quarters, chips, rows, wide = scratch.shape
@@ -668,12 +677,7 @@
     return run_kernel(concat_kernel, "concat", [(shape, bf16)], arrays)[0]
 
 
-def device_ids():
-    position = lax.axis_index("seq")
-    return jnp.stack([position % 2, position // 2, lax.axis_index("dp")]).astype(jnp.int32)
-
-
-def finish_inner(ids, shares, rows):
+def finish_inner(shares, rows):
     groups = len(shares)
     share = shares[0]
     model = share.shape[1]
@@ -686,9 +690,8 @@
             ((rows, model), f32),
             ((8, model), f32),
         ],
-        (ids, *shares),
+        tuple(shares),
         scratch=[pltpu.VMEM((groups,) + share.shape, bf16)],
-        scalars=1,
     )
 
 
@@ -700,7 +703,6 @@
         core = position % 2
         chip = position // 2
         group = lax.axis_index("dp")
-        self.ids = device_ids()
         self.packed = lax.all_gather(hidden, "seq")
         piece_len, model = hidden.shape
         rows = model // splits
@@ -711,14 +713,13 @@
             cut_kernel,
             "cut",
             [((half, 3 * width), bf16)] * chips,
-            (self.ids, *weights),
+            tuple(weights),
             scratch=[
                 pltpu.VMEM((3, half, model), bf16),
                 pltpu.VMEM((chips, half, 3 * width), bf16),
                 pltpu.SemaphoreType.DMA((3,)),
             ],
-            scalars=1,
-            raw=range(1, 4),
+            raw=range(3),
         )
         cut = stack(*line_parts(cut))
         cut_next = exchange(cut, 1)
@@ -726,16 +727,14 @@
             cut_output_kernel,
             "cut_output",
             [((half + 8, model), bf16)],
-            (self.ids, output_weight, vec_local),
-            scalars=1,
+            (output_weight, vec_local),
         )
         cut = stack(cut, cut_next)
         (weight,) = run_kernel(
             assemble_kernel,
             "assemble",
             [((splits, 2, half, 3 * width), bf16)],
-            (self.ids, cut, swap_cores(cut)),
-            scalars=1,
+            (cut, swap_cores(cut)),
         )
         self.out_half = stack(*line_all(tied(out_half, cut_next)))
         self.out_next = exchange(self.out_half, 2)
@@ -780,9 +779,8 @@
             cut_inner_kernel,
             "cut_inner",
             [((rows + units, self.model), bf16)],
-            (self.ids, inner_weight, outer_weight),
+            (inner_weight, outer_weight),
             scratch=[pltpu.VMEM((groups, rows, self.model), bf16)],
-            scalars=1,
         )
         self.pair = jnp.stack(self.biases, 0)
         self.pair_other = swap_cores(self.pair)
@@ -802,7 +800,7 @@
             attend_kernel,
             "attend",
             [((chips, width, piece_len), bf16)] + kept,
-            (self.ids, self.weight, *self.masks(), self.pair, self.pair_other, self.packed),
+            (self.weight, *self.masks(), self.pair, self.pair_other, self.packed),
             scratch=[pltpu.VMEM(self.packed.shape, bf16)]
             + [pltpu.VMEM(*spec) for spec in kept]
             + [
@@ -811,8 +809,7 @@
                 pltpu.VMEM((chips * piece_len, tokens), bf16),
                 pltpu.SemaphoreType.DMA((len(kept) + 2,)),
             ],
-            scalars=1,
-            raw=(8,),
+            raw=(7,),
             raw_outs=range(1, 1 + len(kept)),
             flops=6 * tokens * model * width + 2 * tokens * tokens * width,
             powers=tokens * tokens * 3 // 2,
@@ -824,9 +821,8 @@
             assemble_output_kernel,
             "assemble_output",
             [((self.splits, 2, half, model), bf16), ((16, model), f32)],
-            (self.ids, out_half, swap_cores(out_half)),
+            (out_half, swap_cores(out_half)),
             scratch=[pltpu.VMEM((self.splits, 8, model), bf16)],
-            scalars=1,
         )
         self.output_weight = weight.reshape(chips, width, model)
         att = along_line(att)
@@ -848,7 +844,7 @@
             attend_back_kernel,
             "attend_back",
             [(one, bf16), (two, bf16), (two, bf16), (wide[0], f32), wide],
-            (self.ids,) + keep + self.masks() + tuple(grads),
+            keep + self.masks() + tuple(grads),
             scratch=[pltpu.VMEM(a.shape, a.dtype) for a in keep]
             + [
                 pltpu.VMEM((chips,) + grads[0].shape, bf16),
@@ -860,8 +856,7 @@
                 pltpu.VMEM((splits, groups) + quarter, f32),
                 pltpu.SemaphoreType.DMA((len(keep) + chips,)),
             ],
-            scalars=1,
-            raw=(*range(1, 6), *range(10, 10 + chips)),
+            raw=(*range(5), *range(9, 9 + chips)),
             flops=5 * tokens * tokens * width + 6 * tokens * model * width,
             powers=tokens * tokens * 3 // 2,
             grant=24 << 20,
@@ -876,9 +871,8 @@
             input_grad_kernel,
             "input_grad",
             [((chips,) + full, bf16)],
-            (self.ids, dq, mine, recv, self.weight),
+            (dq, mine, recv, self.weight),
             scratch=[pltpu.VMEM((chips,) + full, bf16)],
-            scalars=1,
             flops=3 * tokens * model * width,
         )
         dws = line_parts(dws)
@@ -895,9 +889,8 @@
             finish_kernel,
             "finish",
             [((rows, model), f32)] * 3,
-            (self.ids, *every),
+            tuple(every),
             scratch=[pltpu.VMEM((groups,) + part, bf16)],
-            scalars=1,
         )
         (input_grad,) = run_kernel(
             sum_rows_kernel, "sum_rows", [(full, f32)], (grad_res, partial)
@@ -932,7 +925,6 @@
     def __init__(self, hidden, weights, biases, segments, random_blocks, output_weight, vec_local):
         self.splits = splits = lax.axis_size("seq")
         self.position = position = lax.axis_index("seq")
-        self.ids = device_ids() * jnp.array([1, 0, 1], jnp.int32)
         self.hidden = hidden
         self.segments = segments
         self.random_blocks = random_blocks
@@ -1195,7 +1187,6 @@
     attention.inner_weights(inner_weight, outer_weight)
     attended = attention.forward()
     vec = attention.vec
-    ids = attention.ids
     w_out = attention.output_weight
     full = (row_count, model)
     wide = (groups * row_count, splits * units)
@@ -1213,14 +1204,13 @@
         functools.partial(forward_kernel, parts=groups),
         "forward",
         [(full, f32)] + [(full, bf16)] * (groups - 1) + [(wide, f32), (wide, bf16)],
-        (ids, vec, both, *lows),
+        (vec, both, *lows),
         scratch=[
             pltpu.VMEM(both.shape, bf16),
             pltpu.VMEM((groups,) + full, bf16),
             pltpu.SemaphoreType.DMA((groups + 2,)),
         ],
-        scalars=1,
-        raw=range(2, 3 + groups),
+        raw=range(1, 2 + groups),
         flops=2 * work,
         powers=wide[0] * wide[1],
         grant=10 << 20,
@@ -1253,18 +1243,17 @@
     slots = attended.shape[0]
     below = rows + 8
     grad_res, stacked, *grad_att = run_kernel(
-        functools.partial(residual_kernel, parts=groups),
+        functools.partial(residual_kernel, parts=groups, lined=by_heads),
         "residual",
-        [(full, f32), ((splits, 3 * rows + 16, model), bf16)]
+        [(full, f32), ((splits, 3 * rows + 8, model), bf16)]
         + [(attended.shape[1:], bf16)] * slots,
-        (ids, grad_mix, normed, inverse, vec, w_out, attended, above, *recv),
+        (grad_mix, normed, inverse, vec, w_out, attended, above, *recv),
         scratch=[
             pltpu.VMEM(full, f32),
             pltpu.VMEM(attended.shape, bf16),
             pltpu.VMEM((splits, below, model), bf16),
             pltpu.SemaphoreType.DMA((slots + 3,)),
         ],
-        scalars=1,
         raw_outs=range(2 + slots),
         flops=4 * row_count * model * model,
         grant=2 * VMEM_BYTES,
@@ -1273,9 +1262,8 @@
     if by_heads:
         grad_att = line_parts(grad_att)
     input_grad, gq, bias_q, gk, gv, bias_v = attention.backward(grad_att, grad_res, share)
-    d_inner, d_outer, d_output, vectors = finish_inner(ids, attention.shares, rows)
-    first_sums = vectors[groups + 1]
-    second_sums = vectors[groups]
+    d_inner, d_outer, d_output, vectors = finish_inner(attention.shares, rows)
+    norm_sums = vectors[groups]
 
     def cut(line, i):
         return line[i * rows : (i + 1) * rows]
@@ -1289,15 +1277,15 @@
         gv,
         bias_v,
         d_output,
-        cut(first_sums, 2),
-        cut(first_sums, 0),
-        cut(first_sums, 1),
+        cut(norm_sums, 6),
+        cut(norm_sums, 4),
+        cut(norm_sums, 5),
         d_inner,
         vectors[:groups, 3 * rows : 3 * rows + units].reshape(-1),
         d_outer,
-        cut(second_sums, 2),
-        cut(second_sums, 0),
-        cut(second_sums, 1),
+        cut(norm_sums, 2),
+        cut(norm_sums, 0),
+        cut(norm_sums, 1),
     )
 
 

time: 208 us -> 206 us (level)
  Pallas kernels: 43.2 us -> 36.5 us
  starting transfers between devices: 49.7 us -> 53.3 us
  waiting for transfers between devices: 87.7 us -> 90.2 us
    pallas_call x24, Pallas kernels: 43.2 us -> 36.5 us  [run_kernel(): pl.pallas_call(kernel, name=name, out_shape=out_shape, in_specs=specs, ou...]
    ppermute x12, starting transfers between devices: 17 us -> 19.3 us  [line_exchange(): return lax.ppermute(array, 'seq', [(i, i ^ 2 * k) for i in range(count)])]
    unnamed x89 -> x81, local copies, waits for them, and re-layouts: 6.16 us -> 4.85 us
  transfers between devices with their start and end apart: 45 -> 45, of which waited for: 30 -> 28; matrix products, arithmetic and copies ran while one was open for 1% -> 1% of each run, Pallas kernels for 15% -> 12%
where the time goes in v6:
time: 206 us; the launch traced here: 203 us
  waiting for transfers between devices  90.2 us (44%)
  starting transfers between devices  53.3 us (26%)
  Pallas kernels  36.5 us (18%)
  between operations  14.4 us (7%)
  local copies, waits for them, and re-layouts  7.85 us (4%)
    ppermute x23, waiting for transfers between devices, exchange(): return lax.ppermute(array, 'dp', [(i, i ^ k) for i in range(count)])  39.8 us
    pallas_call x24, Pallas kernels, run_kernel(): pl.pallas_call(kernel, name=name, out_shape=out_shape, in_specs=specs, ou...  36.5 us
    ppermute x23, starting transfers between devices, exchange(): return lax.ppermute(array, 'dp', [(i, i ^ k) for i in range(count)])  27.8 us
    ppermute x12, waiting for transfers between devices, line_exchange(): return lax.ppermute(array, 'seq', [(i, i ^ 2 * k) for i in range(count)])  25.2 us
    ppermute x12, starting transfers between devices, line_exchange(): return lax.ppermute(array, 'seq', [(i, i ^ 2 * k) for i in range(count)])  19.3 us
    reduce_scatter x1, waiting for transfers between devices, backward(): lax.psum_scatter(partial, 'seq', scatter_dimension=0, axis_index_groups=l...  14.9 us
    all_to_all x1, waiting for transfers between devices, along_line(): lax.all_to_all(array, 'seq', 0, 0, tiled=True, axis_index_groups=lines)  8.21 us
    all_to_all x1, starting transfers between devices, along_line(): lax.all_to_all(array, 'seq', 0, 0, tiled=True, axis_index_groups=lines)  5.05 us
  transfers between devices with their start and end apart: 45, of which 28 were waited for; matrix products, arithmetic and copies ran while one was open for 1% of the time, Pallas kernels for 12%

profile of v6, /device:TPU:8, one launch (start us, length us, event | category | flops | bytes accessed | tf_op | source)
XLA Modules:
  0.0 202.6 jit_solution(8993704156982153489)
XLA Ops:
  9.3 3.0 %collective-permute-start.1 = (bf16[48,576]{1,0:T(8,128)(2,1)S(1)}, bf16[48,576]{1,0:T(8,128)(2,1)S(1)}, u32[]{:S(2)}, u32[]{:S(2)}) collective-permute-start(bf16[48,576]{1,0:T(8,128)(2,1)S(1)} %get-tuple-element.81), channel_id=1, source_target_pairs={{0,4},{1,5},{2,6},{3,7},{4,0},{5,1},{6,2},{7,3},{8,12},{9,13},{10,... | collective-permute-start | bytes 165896 | tf_op jit(solution)/shard_map/ppermute | solution.py:636
  13.5 3.1 %collective-permute-done.1.refs_2_ = bf16[48,576]{1,0:T(8,128)(2,1)S(1)} collective-permute-done((bf16[48,576]{1,0:T(8,128)(2,1)S(1)}, bf16[48,576]{1,0:T(8,128)(2,1)S(1)}, u32[]{:S(2)}, u32[]{:S(2)}) %collective-permute-start.1) | collective-permute-done | bytes 55328 | tf_op jit(solution)/shard_map/ppermute | solution.py:636
  19.1 4.7 %collective-permute-done.3.refs_1_ = bf16[4,48,576]{2,1,0:T(8,128)(2,1)S(1)} collective-permute-done((bf16[4,48,576]{2,1,0:T(8,128)(2,1)S(1)}, bf16[4,48,576]{2,1,0:T(8,128)(2,1)S(1)}, u32[]{:S(2)}, u32[]{:S(2)}) %collective-permute-start.3) | collective-permute-done | bytes 221216 | tf_op jit(solution)/shard_map/ppermute | solution.py:618
  24.2 2.5 %collective-permute-start.4 = (bf16[56,768]{1,0:T(8,128)(2,1)S(1)}, bf16[56,768]{1,0:T(8,128)(2,1)S(1)}, u32[]{:S(2)}, u32[]{:S(2)}) collective-permute-start(bf16[56,768]{1,0:T(8,128)(2,1)S(1)} %cut_output.1.refs_0_), channel_id=1, source_target_pairs={{0,2},{1,3},{2,0},{3,1},{4,6},{5,7},{6,4},{7,5},{8,10},{9,11},{10,... | collective-permute-start | bytes 258056 | tf_op jit(solution)/shard_map/ppermute | solution.py:636
  29.3 5.4 %collective-permute-done.4.refs_1_ = bf16[56,768]{1,0:T(8,128)(2,1)S(1)} collective-permute-done((bf16[56,768]{1,0:T(8,128)(2,1)S(1)}, bf16[56,768]{1,0:T(8,128)(2,1)S(1)}, u32[]{:S(2)}, u32[]{:S(2)}) %collective-permute-start.4) | collective-permute-done | bytes 86048 | tf_op jit(solution)/shard_map/ppermute | solution.py:636
  34.8 2.9 %collective-permute-done.5.refs_2_ = bf16[56,768]{1,0:T(8,128)(2,1)S(1)} collective-permute-done((bf16[56,768]{1,0:T(8,128)(2,1)S(1)}, bf16[56,768]{1,0:T(8,128)(2,1)S(1)}, u32[]{:S(2)}, u32[]{:S(2)}) %collective-permute-start.5) | collective-permute-done | bytes 86048 | tf_op jit(solution)/shard_map/ppermute | solution.py:636
  37.7 3.7 %collective-permute-done.6.refs_3_ = bf16[56,768]{1,0:T(8,128)(2,1)S(1)} collective-permute-done((bf16[56,768]{1,0:T(8,128)(2,1)S(1)}, bf16[56,768]{1,0:T(8,128)(2,1)S(1)}, u32[]{:S(2)}, u32[]{:S(2)}) %collective-permute-start.6) | collective-permute-done | bytes 86048 | tf_op jit(solution)/shard_map/ppermute | solution.py:636
  44.7 6.5 %attend.1 = (bf16[4,192,128]{2,1,0:T(8,128)(2,1)S(1)}, bf16[4,128,192]{2,1,0:T(8,128)(2,1)}, bf16[1024,192]{1,0:T(8,128)(2,1)}, bf16[1024,192]{1,0:T(8,128)(2,1)}, f32[4,128,128]{2,1,0:T(8,128)}) custom-call(bf16[768,576]{1,0:T(8,128)(2,1)S(1)} %bitcast.44, f32[12,2,1024]{2,1,0:T(2,128)S(1)} %reshape_reshape.3.be, f32[1,1024]{1,0:T(1,128)S(1)} %broadcast_in_dim.37.bn, ...), custom_call_target="tpu_custom_call" | custom-call | flops 1308622848 | bytes 4008704 | tf_op jit(solution)/shard_map/attend/pallas_call | solution.py:48
  53.1 5.0 %all-to-all-start = ((bf16[4,192,128]{2,1,0:T(8,128)(2,1)}), bf16[4,192,128]{2,1,0:T(8,128)(2,1)S(1)}, u32[]{:S(2)}, u32[]{:S(2)}) async-start(bf16[4,192,128]{2,1,0:T(8,128)(2,1)} %copy-done.15), calls=%async_computation | async-start | bytes 393216 | tf_op jit(solution)/shard_map/all_to_all | solution.py:667
  60.4 8.2 %all-to-all-done.att = bf16[4,192,128]{2,1,0:T(8,128)(2,1)S(1)} async-done(((bf16[4,192,128]{2,1,0:T(8,128)(2,1)}), bf16[4,192,128]{2,1,0:T(8,128)(2,1)S(1)}, u32[]{:S(2)}, u32[]{:S(2)}) %all-to-all-start) | async-done | bytes 196640 | tf_op jit(solution)/shard_map/all_to_all | solution.py:667
  72.8 4.3 %collective-permute-done.11.refs_1_ = bf16[128,768]{1,0:T(8,128)(2,1)S(1)} collective-permute-done((bf16[128,768]{1,0:T(8,128)(2,1)S(1)}, bf16[128,768]{1,0:T(8,128)(2,1)S(1)}, u32[]{:S(2)}, u32[]{:S(2)}) %collective-permute-start.11) | collective-permute-done | bytes 196640 | tf_op jit(solution)/shard_map/ppermute | solution.py:618
  77.1 4.0 %collective-permute-done.12.refs_2_ = bf16[128,768]{1,0:T(8,128)(2,1)S(1)} collective-permute-done((bf16[128,768]{1,0:T(8,128)(2,1)S(1)}, bf16[128,768]{1,0:T(8,128)(2,1)S(1)}, u32[]{:S(2)}, u32[]{:S(2)}) %collective-permute-start.12) | collective-permute-done | bytes 196640 | tf_op jit(solution)/shard_map/ppermute | solution.py:618
  81.8 3.9 %forward.1 = (f32[128,768]{1,0:T(8,128)S(1)}, bf16[128,768]{1,0:T(8,128)(2,1)S(1)}, bf16[128,768]{1,0:T(8,128)(2,1)S(1)}, bf16[128,768]{1,0:T(8,128)(2,1)S(1)}, ...) custom-call(f32[16,768]{1,0:T(8,128)S(1)} %get-tuple-element.86.vec.refs_6_, bf16[8,192,768]{2,1,0:T(8,128)(2,1)} %bitcast.46, ...), custom_call_target="tpu_custom_call" | custom-call | flops 1207959552 | bytes 6537216 | tf_op jit(solution)/shard_map/forward/pallas_call | solution.py:48
  89.2 3.5 %collective-permute-done.14.refs_1_ = bf16[128,768]{1,0:T(8,128)(2,1)S(1)} collective-permute-done((bf16[128,768]{1,0:T(8,128)(2,1)S(1)}, bf16[128,768]{1,0:T(8,128)(2,1)S(1)}, u32[]{:S(2)}, u32[]{:S(2)}) %collective-permute-start.14) | collective-permute-done | bytes 196640 | tf_op jit(solution)/shard_map/ppermute | solution.py:618
  92.7 3.0 %collective-permute-done.15.refs_2_ = bf16[128,768]{1,0:T(8,128)(2,1)S(1)} collective-permute-done((bf16[128,768]{1,0:T(8,128)(2,1)S(1)}, bf16[128,768]{1,0:T(8,128)(2,1)S(1)}, u32[]{:S(2)}, u32[]{:S(2)}) %collective-permute-start.15) | collective-permute-done | bytes 196640 | tf_op jit(solution)/shard_map/ppermute | solution.py:618
  100.3 2.2 %collective-permute-done.17.refs_1_.refs_5_ = bf16[128,768]{1,0:T(8,128)(2,1)S(1)} collective-permute-done((bf16[128,768]{1,0:T(8,128)(2,1)S(1)}, bf16[128,768]{1,0:T(8,128)(2,1)S(1)}, u32[]{:S(2)}, u32[]{:S(2)}) %collective-permute-start.17) | collective-permute-done | bytes 196640 | tf_op jit(solution)/shard_map/ppermute | solution.py:618
  102.5 2.1 %collective-permute-done.18.refs_2_.refs_6_ = bf16[128,768]{1,0:T(8,128)(2,1)S(1)} collective-permute-done((bf16[128,768]{1,0:T(8,128)(2,1)S(1)}, bf16[128,768]{1,0:T(8,128)(2,1)S(1)}, u32[]{:S(2)}, u32[]{:S(2)}) %collective-permute-start.18) | collective-permute-done | bytes 196640 | tf_op jit(solution)/shard_map/ppermute | solution.py:618
  105.8 2.1 %backward.1 = (f32[128,768]{1,0:T(8,128)S(1)}, bf16[128,768]{1,0:T(8,128)(2,1)S(1)}, bf16[128,768]{1,0:T(8,128)(2,1)S(1)}, bf16[128,768]{1,0:T(8,128)(2,1)S(1)},...) custom-call(bf16[8,192,768]{2,1,0:T(8,128)(2,1)S(1)} %bitcast.47, f32[512,768]{1,0:T(8,128)S(1)} %get-tuple-element.98.inner_ref, ...), custom_call_target="tpu_custom_call" | custom-call | flops 1207959552 | bytes 6491136 | tf_op jit(solution)/shard_map/backward/pallas_call | solution.py:48
  109.6 1.8 collective-permute-start.22
  111.5 2.3 %inner_outer.1.above = bf16[8,200,768]{2,1,0:T(8,128)(2,1)S(1)} custom-call(bf16[512,768]{1,0:T(8,128)(2,1)S(1)} %get-tuple-element.100.gi, bf16[512,768]{1,0:T(8,128)(2,1)S(1)} %get-tuple-element.101.act, f32[8,768]{1,0:T(8,128)S(1)} %get-tuple-element.102.sums, f32[1,768]{1,0:T(1,128)S(1)} %get-tuple-element.103.total, bf16[128,768]{1,0:T(8,128)(2,1)S(1)} %copy-done.9, ...), custom_call_target="tpu_custom_call" | custom-call | flops 1207959552 | bytes 5630976 | tf_op jit(solution)/shard_map/inner_outer/pallas_call | solution.py:48
  113.8 2.7 %collective-permute-done.21.refs_2_ = bf16[128,768]{1,0:T(8,128)(2,1)S(1)} collective-permute-done((bf16[128,768]{1,0:T(8,128)(2,1)S(1)}, bf16[128,768]{1,0:T(8,128)(2,1)S(1)}, u32[]{:S(2)}, u32[]{:S(2)}) %collective-permute-start.21) | collective-permute-done | bytes 196640 | tf_op jit(solution)/shard_map/ppermute | solution.py:618
  116.6 2.5 %residual.1 = (f32[128,768]{1,0:T(8,128)}, bf16[8,296,768]{2,1,0:T(8,128)(2,1)}, bf16[192,128]{1,0:T(8,128)(2,1)}, bf16[192,128]{1,0:T(8,128)(2,1)}, bf16[192,128]{1,0:T(8,128)(2,1)}, /*index=5*/bf16[192,128]{1,0:T(8,128)(2,1)}) custom-call(f32[128,768]{1,0:T(8,128)S(1)} %get-tuple-element.96.mix, f32[128,768]{1,0:T(8,128)S(1)} %get-tuple-element.94.refs_4_.normed, ...), custom_call_target="tpu_custom_call" | custom-call | flops 301989888 | bytes 9945088 | tf_op jit(solution)/shard_map/residual/pallas_call | solution.py:48
  119.9 4.7 %collective-permute-start.23 = (bf16[192,128]{1,0:T(8,128)(2,1)S(1)}, bf16[192,128]{1,0:T(8,128)(2,1)S(1)}, u32[]{:S(2)}, u32[]{:S(2)}) collective-permute-start(bf16[192,128]{1,0:T(8,128)(2,1)S(1)} %copy-done.36), channel_id=1, source_target_pairs={{0,2},{1,3},{2,0},{3,1},{4,6},{5,7},{6,4},{7,5},{8,10},{9,11},{10,... | collective-permute-start | bytes 147464 | tf_op jit(solution)/shard_map/ppermute | solution.py:636
  126.7 2.9 %collective-permute-done.24.refs_2_ = bf16[192,128]{1,0:T(8,128)(2,1)S(1)} collective-permute-done((bf16[192,128]{1,0:T(8,128)(2,1)S(1)}, bf16[192,128]{1,0:T(8,128)(2,1)S(1)}, u32[]{:S(2)}, u32[]{:S(2)}) %collective-permute-start.24) | collective-permute-done | bytes 49184 | tf_op jit(solution)/shard_map/ppermute | solution.py:636
  130.2 9.0 %attend_back.1 = (bf16[4,128,192]{2,1,0:T(8,128)(2,1)S(1)}, bf16[4,128,384]{2,1,0:T(8,128)(2,1)S(1)}, bf16[4,128,384]{2,1,0:T(8,128)(2,1)S(1)}, f32[4,104,576]{2,1,0:T(8,128)S(1)}, bf16[4,104,576]{2,1,0:T(8,128)(2,1)S(1)}) custom-call(bf16[8,128,768]{2,1,0:T(8,128)(2,1)} %all-gather.4.cloned.1.call-done.hid_raw, ...), custom_call_target="tpu_custom_call" | custom-call | flops 1912602624 | bytes 5543936 | tf_op jit(solution)/shard_map/attend_back/pallas_call | solution.py:48
  144.9 2.9 %collective-permute-done.27.refs_1_ = bf16[104,576]{1,0:T(8,128)(2,1)S(1)} collective-permute-done((bf16[104,576]{1,0:T(8,128)(2,1)S(1)}, bf16[104,576]{1,0:T(8,128)(2,1)S(1)}, u32[]{:S(2)}, u32[]{:S(2)}) %collective-permute-start.27) | collective-permute-done | bytes 119840 | tf_op jit(solution)/shard_map/ppermute | solution.py:618
  147.8 2.9 %collective-permute-done.28.refs_2_ = bf16[104,576]{1,0:T(8,128)(2,1)S(1)} collective-permute-done((bf16[104,576]{1,0:T(8,128)(2,1)S(1)}, bf16[104,576]{1,0:T(8,128)(2,1)S(1)}, u32[]{:S(2)}, u32[]{:S(2)}) %collective-permute-start.28) | collective-permute-done | bytes 119840 | tf_op jit(solution)/shard_map/ppermute | solution.py:618
  152.5 2.3 %collective-permute-start.31 = (bf16[24,576]{1,0:T(8,128)(2,1)S(1)}, bf16[24,576]{1,0:T(8,128)(2,1)S(1)}, u32[]{:S(2)}, u32[]{:S(2)}) collective-permute-start(bf16[24,576]{1,0:T(8,128)(2,1)S(1)} %get-tuple-element.128), channel_id=1, source_target_pairs={{0,2},{1,3},{2,0},{3,1},{4,6},{5,7},{6,4},{7,5},{8,10},{9,11},{10,... | collective-permute-start | bytes 82952 | tf_op jit(solution)/shard_map/ppermute | solution.py:636
  154.8 2.7 %collective-permute-start.32 = (bf16[24,576]{1,0:T(8,128)(2,1)S(1)}, bf16[24,576]{1,0:T(8,128)(2,1)S(1)}, u32[]{:S(2)}, u32[]{:S(2)}) collective-permute-start(bf16[24,576]{1,0:T(8,128)(2,1)S(1)} %get-tuple-element.129), channel_id=1, source_target_pairs={{0,4},{1,5},{2,6},{3,7},{4,0},{5,1},{6,2},{7,3},{8,12},{9,13},{10,... | collective-permute-start | bytes 82952 | tf_op jit(solution)/shard_map/ppermute | solution.py:636
  158.0 3.3 %collective-permute-done.32.refs_2_ = bf16[24,576]{1,0:T(8,128)(2,1)S(1)} collective-permute-done((bf16[24,576]{1,0:T(8,128)(2,1)S(1)}, bf16[24,576]{1,0:T(8,128)(2,1)S(1)}, u32[]{:S(2)}, u32[]{:S(2)}) %collective-permute-start.32) | collective-permute-done | bytes 27680 | tf_op jit(solution)/shard_map/ppermute | solution.py:636
  176.1 14.9 %reduce-scatter.3.cloned.1.call-done.parts = bf16[1,128,768]{2,1,0:T(8,128)(2,1)} async-done(((bf16[4,128,768]{2,1,0:T(8,128)(2,1)}), bf16[1,128,768]{2,1,0:T(8,128)(2,1)}) %reduce-scatter.3.cloned.1.call-update) | async-done | bytes 196624 | tf_op jit(solution)/shard_map/reduce_scatter | solution.py:885
  192.7 2.0 finish_inner.1
  (192 shorter events, 61.0 us)
Async XLA Ops:
  7.3 34.3 %all-gather.4.cloned.1.call-start = ((), (), s32[]{:S(2)}) async-start(), calls=%async_computation.3 | async-start | bytes 1769472 | tf_op jit(solution)/shard_map/all_gather | solution.py:706
  8.0 73.7 %all-gather.6.cloned.1.call-start = ((), (), s32[]{:S(2)}) async-start(), calls=%async_computation.6 | async-start | bytes 2654208 | tf_op jit(solution)/shard_map/all_gather | solution.py:787
  9.3 7.3 %collective-permute-start.1 = (bf16[48,576]{1,0:T(8,128)(2,1)S(1)}, bf16[48,576]{1,0:T(8,128)(2,1)S(1)}, u32[]{:S(2)}, u32[]{:S(2)}) collective-permute-start(bf16[48,576]{1,0:T(8,128)(2,1)S(1)} %get-tuple-element.81), channel_id=1, source_target_pairs={{0,4},{1,5},{2,6},{3,7},{4,0},{5,1},{6,2},{7,3},{8,12},{9,13},{10,... | collective-permute-start | bytes 165896 | tf_op jit(solution)/shard_map/ppermute | solution.py:636
  17.5 6.3 %collective-permute-start.3 = (bf16[4,48,576]{2,1,0:T(8,128)(2,1)S(1)}, bf16[4,48,576]{2,1,0:T(8,128)(2,1)S(1)}, u32[]{:S(2)}, u32[]{:S(2)}) collective-permute-start(bf16[4,48,576]{2,1,0:T(8,128)(2,1)S(1)} %stack.11.refs_0_), channel_id=1, source_target_pairs={{0,8},{8,0},{16,24},{24,16},{1,9},{9,1},{17,25},{25,17},{2,10},{10... | collective-permute-start | bytes 663560 | tf_op jit(solution)/shard_map/ppermute | solution.py:618
  23.9 17.6 %collective-permute-start.7 = (bf16[2,4,48,576]{3,2,1,0:T(8,128)(2,1)S(1)}, bf16[2,4,48,576]{3,2,1,0:T(8,128)(2,1)S(1)}, u32[]{:S(2)}, u32[]{:S(2)}) collective-permute-start(bf16[2,4,48,576]{3,2,1,0:T(8,128)(2,1)S(1)} %stack.13.mine), channel_id=1, source_target_pairs={{0,1},{1,0},{2,3},{3,2},{4,5},{5,4},{6,7},{7,6},{8,9},{9,8},{10,11... | collective-permute-start | bytes 1327112 | tf_op jit(solution)/shard_map/ppermute | solution.py:631
  24.2 10.5 %collective-permute-start.4 = (bf16[56,768]{1,0:T(8,128)(2,1)S(1)}, bf16[56,768]{1,0:T(8,128)(2,1)S(1)}, u32[]{:S(2)}, u32[]{:S(2)}) collective-permute-start(bf16[56,768]{1,0:T(8,128)(2,1)S(1)} %cut_output.1.refs_0_), channel_id=1, source_target_pairs={{0,2},{1,3},{2,0},{3,1},{4,6},{5,7},{6,4},{7,5},{8,10},{9,11},{10,... | collective-permute-start | bytes 258056 | tf_op jit(solution)/shard_map/ppermute | solution.py:636
  26.7 11.0 %collective-permute-start.5 = (bf16[56,768]{1,0:T(8,128)(2,1)S(1)}, bf16[56,768]{1,0:T(8,128)(2,1)S(1)}, u32[]{:S(2)}, u32[]{:S(2)}) collective-permute-start(bf16[56,768]{1,0:T(8,128)(2,1)S(1)} %cut_output.1.refs_0_), channel_id=1, source_target_pairs={{0,4},{1,5},{2,6},{3,7},{4,0},{5,1},{6,2},{7,3},{8,12},{9,13},{10,... | collective-permute-start | bytes 258056 | tf_op jit(solution)/shard_map/ppermute | solution.py:636
  28.3 13.1 %collective-permute-start.6 = (bf16[56,768]{1,0:T(8,128)(2,1)S(1)}, bf16[56,768]{1,0:T(8,128)(2,1)S(1)}, u32[]{:S(2)}, u32[]{:S(2)}) collective-permute-start(bf16[56,768]{1,0:T(8,128)(2,1)S(1)} %cut_output.1.refs_0_), channel_id=1, source_target_pairs={{0,6},{1,7},{2,4},{3,5},{4,2},{5,3},{6,0},{7,1},{8,14},{9,15},{10,... | collective-permute-start | bytes 258056 | tf_op jit(solution)/shard_map/ppermute | solution.py:636
  42.5 10.5 %collective-permute-start.9 = (bf16[4,56,768]{2,1,0:T(8,128)(2,1)S(1)}, bf16[4,56,768]{2,1,0:T(8,128)(2,1)S(1)}, u32[]{:S(2)}, u32[]{:S(2)}) collective-permute-start(bf16[4,56,768]{2,1,0:T(8,128)(2,1)S(1)} %stack.12.refs_0_), channel_id=1, source_target_pairs={{0,16},{8,24},{16,0},{24,8},{1,17},{9,25},{17,1},{25,9},{2,18},{10... | collective-permute-start | bytes 1032200 | tf_op jit(solution)/shard_map/ppermute | solution.py:618
  53.1 15.4 %all-to-all-start = ((bf16[4,192,128]{2,1,0:T(8,128)(2,1)}), bf16[4,192,128]{2,1,0:T(8,128)(2,1)S(1)}, u32[]{:S(2)}, u32[]{:S(2)}) async-start(bf16[4,192,128]{2,1,0:T(8,128)(2,1)} %copy-done.15), calls=%async_computation | async-start | bytes 393216 | tf_op jit(solution)/shard_map/all_to_all | solution.py:667
  58.2 112.7 %reduce-scatter.5.cloned.1.call-start = ((), (), s32[]{:S(2)}) async-start(), calls=%async_computation.5 | async-start | bytes 4091904 | tf_op jit(solution)/shard_map/reduce_scatter | solution.py:1261
  69.2 7.9 %collective-permute-start.11 = (bf16[128,768]{1,0:T(8,128)(2,1)S(1)}, bf16[128,768]{1,0:T(8,128)(2,1)S(1)}, u32[]{:S(2)}, u32[]{:S(2)}) collective-permute-start(bf16[128,768]{1,0:T(8,128)(2,1)S(1)} %get-tuple-element.89.refs_0_), channel_id=1, source_target_pairs={{0,8},{8,0},{16,24},{24,16},{1,9},{9,1},{17,25},{25,17},{2,10},{10... | collective-permute-start | bytes 589832 | tf_op jit(solution)/shard_map/ppermute | solution.py:618
  70.7 10.3 %collective-permute-start.12 = (bf16[128,768]{1,0:T(8,128)(2,1)S(1)}, bf16[128,768]{1,0:T(8,128)(2,1)S(1)}, u32[]{:S(2)}, u32[]{:S(2)}) collective-permute-start(bf16[128,768]{1,0:T(8,128)(2,1)S(1)} %get-tuple-element.89.refs_0_), channel_id=1, source_target_pairs={{0,16},{8,24},{16,0},{24,8},{1,17},{9,25},{17,1},{25,9},{2,18},{10... | collective-permute-start | bytes 589832 | tf_op jit(solution)/shard_map/ppermute | solution.py:618
  72.2 9.6 %collective-permute-start.13 = (bf16[128,768]{1,0:T(8,128)(2,1)S(1)}, bf16[128,768]{1,0:T(8,128)(2,1)}, u32[]{:S(2)}, u32[]{:S(2)}) collective-permute-start(bf16[128,768]{1,0:T(8,128)(2,1)S(1)} %get-tuple-element.89.refs_0_), channel_id=1, source_target_pairs={{0,24},{8,16},{16,8},{24,0},{1,25},{9,17},{17,9},{25,1},{2,26},{10... | collective-permute-start | bytes 589832 | tf_op jit(solution)/shard_map/ppermute | solution.py:618
  85.6 7.1 %collective-permute-start.14 = (bf16[128,768]{1,0:T(8,128)(2,1)S(1)}, bf16[128,768]{1,0:T(8,128)(2,1)S(1)}, u32[]{:S(2)}, u32[]{:S(2)}) collective-permute-start(bf16[128,768]{1,0:T(8,128)(2,1)S(1)} %get-tuple-element.91), channel_id=1, source_target_pairs={{0,8},{8,0},{16,24},{24,16},{1,9},{9,1},{17,25},{25,17},{2,10},{10... | collective-permute-start | bytes 589832 | tf_op jit(solution)/shard_map/ppermute | solution.py:618
  86.3 9.4 %collective-permute-start.15 = (bf16[128,768]{1,0:T(8,128)(2,1)S(1)}, bf16[128,768]{1,0:T(8,128)(2,1)S(1)}, u32[]{:S(2)}, u32[]{:S(2)}) collective-permute-start(bf16[128,768]{1,0:T(8,128)(2,1)S(1)} %get-tuple-element.92), channel_id=1, source_target_pairs={{0,16},{8,24},{16,0},{24,8},{1,17},{9,25},{17,1},{25,9},{2,18},{10... | collective-permute-start | bytes 589832 | tf_op jit(solution)/shard_map/ppermute | solution.py:618
  87.7 8.0 %collective-permute-start.16 = (bf16[128,768]{1,0:T(8,128)(2,1)S(1)}, bf16[128,768]{1,0:T(8,128)(2,1)S(1)}, u32[]{:S(2)}, u32[]{:S(2)}) collective-permute-start(bf16[128,768]{1,0:T(8,128)(2,1)S(1)} %get-tuple-element.93), channel_id=1, source_target_pairs={{0,24},{8,16},{16,8},{24,0},{1,25},{9,17},{17,9},{25,1},{2,26},{10... | collective-permute-start | bytes 589832 | tf_op jit(solution)/shard_map/ppermute | solution.py:618
  97.4 7.1 %collective-permute-start.18 = (bf16[128,768]{1,0:T(8,128)(2,1)S(1)}, bf16[128,768]{1,0:T(8,128)(2,1)S(1)}, u32[]{:S(2)}, u32[]{:S(2)}) collective-permute-start(bf16[128,768]{1,0:T(8,128)(2,1)S(1)} %get-tuple-element.99.refs_0_.refs_4_), channel_id=1, source_target_pairs={{0,16},{8,24},{16,0},{24,8},{1,17},{9,25},{17,1},{25,9},{2,18},{10... | collective-permute-start | bytes 589832 | tf_op jit(solution)/shard_map/ppermute | solution.py:618
  99.2 6.6 %collective-permute-start.19 = (bf16[128,768]{1,0:T(8,128)(2,1)S(1)}, bf16[128,768]{1,0:T(8,128)(2,1)S(1)}, u32[]{:S(2)}, u32[]{:S(2)}) collective-permute-start(bf16[128,768]{1,0:T(8,128)(2,1)S(1)} %get-tuple-element.99.refs_0_.refs_4_), channel_id=1, source_target_pairs={{0,24},{8,16},{16,8},{24,0},{1,25},{9,17},{17,9},{25,1},{2,26},{10... | collective-permute-start | bytes 589832 | tf_op jit(solution)/shard_map/ppermute | solution.py:618
  107.9 5.9 %collective-permute-start.20 = (bf16[128,768]{1,0:T(8,128)(2,1)S(1)}, bf16[128,768]{1,0:T(8,128)(2,1)S(1)}, u32[]{:S(2)}, u32[]{:S(2)}) collective-permute-start(bf16[128,768]{1,0:T(8,128)(2,1)S(1)} %get-tuple-element.105), channel_id=1, source_target_pairs={{0,8},{8,0},{16,24},{24,16},{1,9},{9,1},{17,25},{25,17},{2,10},{10... | collective-permute-start | bytes 589832 | tf_op jit(solution)/shard_map/ppermute | solution.py:618
  108.8 7.8 %collective-permute-start.21 = (bf16[128,768]{1,0:T(8,128)(2,1)S(1)}, bf16[128,768]{1,0:T(8,128)(2,1)S(1)}, u32[]{:S(2)}, u32[]{:S(2)}) collective-permute-start(bf16[128,768]{1,0:T(8,128)(2,1)S(1)} %get-tuple-element.106), channel_id=1, source_target_pairs={{0,16},{8,24},{16,0},{24,8},{1,17},{9,25},{17,1},{25,9},{2,18},{10... | collective-permute-start | bytes 589832 | tf_op jit(solution)/shard_map/ppermute | solution.py:618
  109.6 7.0 %collective-permute-start.22 = (bf16[128,768]{1,0:T(8,128)(2,1)S(1)}, bf16[128,768]{1,0:T(8,128)(2,1)S(1)}, u32[]{:S(2)}, u32[]{:S(2)}) collective-permute-start(bf16[128,768]{1,0:T(8,128)(2,1)S(1)} %get-tuple-element.107), channel_id=1, source_target_pairs={{0,24},{8,16},{16,8},{24,0},{1,25},{9,17},{17,9},{25,1},{2,26},{10... | collective-permute-start | bytes 589832 | tf_op jit(solution)/shard_map/ppermute | solution.py:618
  119.2 71.8 %reduce-scatter.3.cloned.1.call-start = ((), (), s32[]{:S(2)}) async-start(), calls=%async_computation.4 | async-start | bytes 983040 | tf_op jit(solution)/shard_map/reduce_scatter | solution.py:885
  119.9 6.8 %collective-permute-start.23 = (bf16[192,128]{1,0:T(8,128)(2,1)S(1)}, bf16[192,128]{1,0:T(8,128)(2,1)S(1)}, u32[]{:S(2)}, u32[]{:S(2)}) collective-permute-start(bf16[192,128]{1,0:T(8,128)(2,1)S(1)} %copy-done.36), channel_id=1, source_target_pairs={{0,2},{1,3},{2,0},{3,1},{4,6},{5,7},{6,4},{7,5},{8,10},{9,11},{10,... | collective-permute-start | bytes 147464 | tf_op jit(solution)/shard_map/ppermute | solution.py:636
  139.3 11.4 %collective-permute-start.30 = (bf16[4,128,384]{2,1,0:T(8,128)(2,1)S(1)}, bf16[4,128,384]{2,1,0:T(8,128)(2,1)S(1)}, u32[]{:S(2)}, u32[]{:S(2)}) collective-permute-start(bf16[4,128,384]{2,1,0:T(8,128)(2,1)S(1)} %get-tuple-element.127), channel_id=1, source_target_pairs={{0,1},{1,0},{2,3},{3,2},{4,5},{5,4},{6,7},{7,6},{8,9},{9,8},{10,11... | collective-permute-start | bytes 1179656 | tf_op jit(solution)/shard_map/ppermute | solution.py:631
  141.3 6.4 %collective-permute-start.27 = (bf16[104,576]{1,0:T(8,128)(2,1)S(1)}, bf16[104,576]{1,0:T(8,128)(2,1)S(1)}, u32[]{:S(2)}, u32[]{:S(2)}) collective-permute-start(bf16[104,576]{1,0:T(8,128)(2,1)S(1)} %get-tuple-element.121), channel_id=1, source_target_pairs={{0,8},{8,0},{16,24},{24,16},{1,9},{9,1},{17,25},{25,17},{2,10},{10... | collective-permute-start | bytes 359432 | tf_op jit(solution)/shard_map/ppermute | solution.py:618
  142.5 8.2 %collective-permute-start.28 = (bf16[104,576]{1,0:T(8,128)(2,1)S(1)}, bf16[104,576]{1,0:T(8,128)(2,1)S(1)}, u32[]{:S(2)}, u32[]{:S(2)}) collective-permute-start(bf16[104,576]{1,0:T(8,128)(2,1)S(1)} %get-tuple-element.122), channel_id=1, source_target_pairs={{0,16},{8,24},{16,0},{24,8},{1,17},{9,25},{17,1},{25,9},{2,18},{10... | collective-permute-start | bytes 359432 | tf_op jit(solution)/shard_map/ppermute | solution.py:618
  143.7 6.9 %collective-permute-start.29 = (bf16[104,576]{1,0:T(8,128)(2,1)S(1)}, bf16[104,576]{1,0:T(8,128)(2,1)S(1)}, u32[]{:S(2)}, u32[]{:S(2)}) collective-permute-start(bf16[104,576]{1,0:T(8,128)(2,1)S(1)} %get-tuple-element.123), channel_id=1, source_target_pairs={{0,24},{8,16},{16,8},{24,0},{1,25},{9,17},{17,9},{25,1},{2,26},{10... | collective-permute-start | bytes 359432 | tf_op jit(solution)/shard_map/ppermute | solution.py:618
  154.8 6.5 %collective-permute-start.32 = (bf16[24,576]{1,0:T(8,128)(2,1)S(1)}, bf16[24,576]{1,0:T(8,128)(2,1)S(1)}, u32[]{:S(2)}, u32[]{:S(2)}) collective-permute-start(bf16[24,576]{1,0:T(8,128)(2,1)S(1)} %get-tuple-element.129), channel_id=1, source_target_pairs={{0,4},{1,5},{2,6},{3,7},{4,0},{5,1},{6,2},{7,3},{8,12},{9,13},{10,... | collective-permute-start | bytes 82952 | tf_op jit(solution)/shard_map/ppermute | solution.py:636
  170.9 21.8 %collective-permute-start.37 = (bf16[296,768]{1,0:T(8,128)(2,1)}, bf16[296,768]{1,0:T(8,128)(2,1)S(1)}, u32[]{:S(2)}, u32[]{:S(2)}) collective-permute-start(bf16[296,768]{1,0:T(8,128)(2,1)} %bitcast.49), channel_id=1, source_target_pairs={{0,8},{8,0},{16,24},{24,16},{1,9},{9,1},{17,25},{25,17},{2,10},{10... | collective-permute-start | bytes 1363976 | tf_op jit(solution)/shard_map/ppermute | solution.py:618
  172.0 20.7 %collective-permute-start.38 = (bf16[296,768]{1,0:T(8,128)(2,1)}, bf16[296,768]{1,0:T(8,128)(2,1)S(1)}, u32[]{:S(2)}, u32[]{:S(2)}) collective-permute-start(bf16[296,768]{1,0:T(8,128)(2,1)} %bitcast.50), channel_id=1, source_target_pairs={{0,16},{8,24},{16,0},{24,8},{1,17},{9,25},{17,1},{25,9},{2,18},{10... | collective-permute-start | bytes 1363976 | tf_op jit(solution)/shard_map/ppermute | solution.py:618
  172.8 19.9 %collective-permute-start.39 = (bf16[296,768]{1,0:T(8,128)(2,1)}, bf16[296,768]{1,0:T(8,128)(2,1)S(1)}, u32[]{:S(2)}, u32[]{:S(2)}) collective-permute-start(bf16[296,768]{1,0:T(8,128)(2,1)} %bitcast.51), channel_id=1, source_target_pairs={{0,24},{8,16},{16,8},{24,0},{1,25},{9,17},{17,9},{25,1},{2,26},{10... | collective-permute-start | bytes 1363976 | tf_op jit(solution)/shard_map/ppermute | solution.py:618
  (53 other events, 519.3 us)
Sparse Core Ops, SparseCore 0:
  9.8 31.0 all-gather.3
  43.1 34.7 all-gather.5
  119.3 45.3 reduce-scatter.4
  167.4 23.5 reduce-scatter.2

commit v7 on v6

--- a/solution.py
+++ b/solution.py
@@ -375,13 +375,6 @@
     out[...] = (left[...].astype(f32) + right[...].astype(f32)).astype(out.dtype)
 
 
-def sum_rows_kernel(first, parts, out):
-    total = first[...]
-    for i in range(parts.shape[0]):
-        total = total + parts[i].astype(f32)
-    out[...] = total
-
-
 def add_split_kernel(left, right, *outs):
     for k, out in enumerate(outs):
         out[...] = (left[k].astype(f32) + right[k].astype(f32)).astype(out.dtype)
@@ -557,15 +550,24 @@
     out[at, row : row + 8, :] = jnp.broadcast_to(line, (8, out.shape[2])).astype(bf16)
 
 
-def ordered(ids, refs, scratch):
-    for k, r in enumerate(refs):
-        scratch[ids[2] ^ k] = r[...]
-
-
-def finish_inner_kernel(*refs, parts):
+def finish_inner_kernel(*refs, parts, summed):
     ids = here()
-    inner, outer, output, vectors, scratch = refs[parts:]
-    ordered(ids, refs[:parts], scratch)
+    if summed:
+        raws = refs[parts : parts + 2]
+        inner, outer, output, vectors, total_ref, scratch, res, part, sems = refs[parts + 2 :]
+        copies = [
+            pltpu.make_async_copy(raw, held, sems.at[1 + i])
+            for i, (raw, held) in enumerate(zip(raws, (res, part)))
+        ]
+        for copy in copies:
+            copy.start()
+    else:
+        inner, outer, output, vectors, scratch, sems = refs[parts:]
+    own = pltpu.make_async_copy(refs[0], scratch.at[ids[2]], sems.at[0])
+    own.start()
+    for k in range(1, parts):
+        scratch[ids[2] ^ k] = refs[k][...]
+    own.wait()
     rows = inner.shape[0]
     units = outer.shape[0] // parts
     pieces = scratch.shape[2] // units
@@ -590,6 +592,10 @@
         for g in range(1, parts):
             last = last + scratch[g, at + 8 :, :].astype(f32)
         output[...] = last
+    if summed:
+        for copy in copies:
+            copy.wait()
+        total_ref[...] = res[...] + part[...].astype(f32)
 
 
 def finish_kernel(*refs):
@@ -677,21 +683,28 @@
     return run_kernel(concat_kernel, "concat", [(shape, bf16)], arrays)[0]
 
 
-def finish_inner(shares, rows):
+def finish_inner(shares, rows, terms=()):
     groups = len(shares)
     share = shares[0]
     model = share.shape[1]
+    outs = [
+        ((rows, groups * model), f32),
+        ((groups * rows, model), f32),
+        ((rows, model), f32),
+        ((8, model), f32),
+    ]
+    scratch = [pltpu.VMEM((groups,) + share.shape, bf16)]
+    if terms:
+        outs.append((terms[0].shape, f32))
+        scratch += [pltpu.VMEM(t.shape, t.dtype) for t in terms]
     return run_kernel(
-        functools.partial(finish_inner_kernel, parts=groups),
+        functools.partial(finish_inner_kernel, parts=groups, summed=bool(terms)),
         "finish_inner",
-        [
-            ((rows, groups * model), f32),
-            ((groups * rows, model), f32),
-            ((rows, model), f32),
-            ((8, model), f32),
-        ],
-        tuple(shares),
-        scratch=[pltpu.VMEM((groups,) + share.shape, bf16)],
+        outs,
+        (*shares, *terms),
+        scratch=scratch + [pltpu.SemaphoreType.DMA((1 + len(terms),))],
+        raw=(0, *range(groups, groups + len(terms))),
+        grant=2 * VMEM_BYTES,
     )
 
 
@@ -884,7 +897,7 @@
         lines = [[2 * i + c for i in range(count // 2)] for c in range(2)]
         partial = lax.psum_scatter(
             partial, "seq", scatter_dimension=0, axis_index_groups=lines, tiled=False
-        )[None]
+        )
         gq, gk, gv = run_kernel(
             finish_kernel,
             "finish",
@@ -892,9 +905,7 @@
             tuple(every),
             scratch=[pltpu.VMEM((groups,) + part, bf16)],
         )
-        (input_grad,) = run_kernel(
-            sum_rows_kernel, "sum_rows", [(full, f32)], (grad_res, partial)
-        )
+        *self.finished, input_grad = finish_inner(self.shares, rows, (grad_res, partial))
         core = self.position % 2
         bias_q = lax.dynamic_slice_in_dim(sums[0], core * rows, rows)
         bias_v = lax.dynamic_slice_in_dim(sums[0], 2 * width + core * rows, rows)
@@ -1049,7 +1060,7 @@
     def backward(self, grads, grad_res, share):
         hidden = self.hidden
         grad = grads[0].T
-        self.shares = exchange_all(share)
+        self.finished = finish_inner(exchange_all(share), hidden.shape[1] // self.splits)
         splits, position = self.splits, self.position
         seq_count, per, _, _, size = self.query.shape
         row_count, model = hidden.shape
@@ -1262,7 +1273,7 @@
     if by_heads:
         grad_att = line_parts(grad_att)
     input_grad, gq, bias_q, gk, gv, bias_v = attention.backward(grad_att, grad_res, share)
-    d_inner, d_outer, d_output, vectors = finish_inner(attention.shares, rows)
+    d_inner, d_outer, d_output, vectors = attention.finished
     norm_sums = vectors[groups]
 
     def cut(line, i):

time: 206 us -> 206 us (level)
    unnamed x81 -> x75, local copies, waits for them, and re-layouts: 4.85 us -> 3.92 us
    pallas_call x24 -> x23, Pallas kernels: 36.5 us -> 37.1 us  [run_kernel(): pl.pallas_call(kernel, name=name, out_shape=out_shape, in_specs=specs, ou...]
  transfers between devices with their start and end apart: 45 -> 45, of which waited for: 28 -> 29; matrix products, arithmetic and copies ran while one was open for 1% -> 1% of each run, Pallas kernels for 12% -> 12%
where the time goes in v7:
time: 206 us; the launch traced here: 203 us
  waiting for transfers between devices  90.8 us (44%)
  starting transfers between devices  53.3 us (26%)
  Pallas kernels  37.1 us (18%)
  between operations  14.4 us (7%)
  local copies, waits for them, and re-layouts  6.92 us (3%)
    ppermute x23, waiting for transfers between devices, exchange(): return lax.ppermute(array, 'dp', [(i, i ^ k) for i in range(count)])  40.2 us
    pallas_call x23, Pallas kernels, run_kernel(): pl.pallas_call(kernel, name=name, out_shape=out_shape, in_specs=specs, ou...  37.1 us
    ppermute x23, starting transfers between devices, exchange(): return lax.ppermute(array, 'dp', [(i, i ^ k) for i in range(count)])  27.8 us
    ppermute x12, waiting for transfers between devices, line_exchange(): return lax.ppermute(array, 'seq', [(i, i ^ 2 * k) for i in range(count)])  25.2 us
    ppermute x12, starting transfers between devices, line_exchange(): return lax.ppermute(array, 'seq', [(i, i ^ 2 * k) for i in range(count)])  19.2 us
    reduce_scatter x1, waiting for transfers between devices, backward(): lax.psum_scatter(partial, 'seq', scatter_dimension=0, axis_index_groups=l...  15 us
    all_to_all x1, waiting for transfers between devices, along_line(): lax.all_to_all(array, 'seq', 0, 0, tiled=True, axis_index_groups=lines)  8.21 us
    all_to_all x1, starting transfers between devices, along_line(): lax.all_to_all(array, 'seq', 0, 0, tiled=True, axis_index_groups=lines)  5.05 us
  transfers between devices with their start and end apart: 45, of which 29 were waited for; matrix products, arithmetic and copies ran while one was open for 1% of the time, Pallas kernels for 12%

profile of v7, /device:TPU:8, one launch (start us, length us, event | category | flops | bytes accessed | tf_op | source)
XLA Modules:
  0.0 202.7 jit_solution(251434678017066304)
XLA Ops:
  9.3 3.0 %collective-permute-start.1 = (bf16[48,576]{1,0:T(8,128)(2,1)S(1)}, bf16[48,576]{1,0:T(8,128)(2,1)S(1)}, u32[]{:S(2)}, u32[]{:S(2)}) collective-permute-start(bf16[48,576]{1,0:T(8,128)(2,1)S(1)} %get-tuple-element.82), channel_id=1, source_target_pairs={{0,4},{1,5},{2,6},{3,7},{4,0},{5,1},{6,2},{7,3},{8,12},{9,13},{10,... | collective-permute-start | bytes 165896 | tf_op jit(solution)/shard_map/ppermute | solution.py:642
  13.5 3.1 %collective-permute-done.1.refs_2_ = bf16[48,576]{1,0:T(8,128)(2,1)S(1)} collective-permute-done((bf16[48,576]{1,0:T(8,128)(2,1)S(1)}, bf16[48,576]{1,0:T(8,128)(2,1)S(1)}, u32[]{:S(2)}, u32[]{:S(2)}) %collective-permute-start.1) | collective-permute-done | bytes 55328 | tf_op jit(solution)/shard_map/ppermute | solution.py:642
  19.1 4.7 %collective-permute-done.3.refs_1_ = bf16[4,48,576]{2,1,0:T(8,128)(2,1)S(1)} collective-permute-done((bf16[4,48,576]{2,1,0:T(8,128)(2,1)S(1)}, bf16[4,48,576]{2,1,0:T(8,128)(2,1)S(1)}, u32[]{:S(2)}, u32[]{:S(2)}) %collective-permute-start.3) | collective-permute-done | bytes 221216 | tf_op jit(solution)/shard_map/ppermute | solution.py:624
  24.2 2.5 %collective-permute-start.4 = (bf16[56,768]{1,0:T(8,128)(2,1)S(1)}, bf16[56,768]{1,0:T(8,128)(2,1)S(1)}, u32[]{:S(2)}, u32[]{:S(2)}) collective-permute-start(bf16[56,768]{1,0:T(8,128)(2,1)S(1)} %cut_output.1.refs_0_), channel_id=1, source_target_pairs={{0,2},{1,3},{2,0},{3,1},{4,6},{5,7},{6,4},{7,5},{8,10},{9,11},{10,... | collective-permute-start | bytes 258056 | tf_op jit(solution)/shard_map/ppermute | solution.py:642
  29.3 5.4 %collective-permute-done.4.refs_1_ = bf16[56,768]{1,0:T(8,128)(2,1)S(1)} collective-permute-done((bf16[56,768]{1,0:T(8,128)(2,1)S(1)}, bf16[56,768]{1,0:T(8,128)(2,1)S(1)}, u32[]{:S(2)}, u32[]{:S(2)}) %collective-permute-start.4) | collective-permute-done | bytes 86048 | tf_op jit(solution)/shard_map/ppermute | solution.py:642
  34.8 2.9 %collective-permute-done.5.refs_2_ = bf16[56,768]{1,0:T(8,128)(2,1)S(1)} collective-permute-done((bf16[56,768]{1,0:T(8,128)(2,1)S(1)}, bf16[56,768]{1,0:T(8,128)(2,1)S(1)}, u32[]{:S(2)}, u32[]{:S(2)}) %collective-permute-start.5) | collective-permute-done | bytes 86048 | tf_op jit(solution)/shard_map/ppermute | solution.py:642
  37.7 3.7 %collective-permute-done.6.refs_3_ = bf16[56,768]{1,0:T(8,128)(2,1)S(1)} collective-permute-done((bf16[56,768]{1,0:T(8,128)(2,1)S(1)}, bf16[56,768]{1,0:T(8,128)(2,1)S(1)}, u32[]{:S(2)}, u32[]{:S(2)}) %collective-permute-start.6) | collective-permute-done | bytes 86048 | tf_op jit(solution)/shard_map/ppermute | solution.py:642
  44.7 6.5 %attend.1 = (bf16[4,192,128]{2,1,0:T(8,128)(2,1)S(1)}, bf16[4,128,192]{2,1,0:T(8,128)(2,1)}, bf16[1024,192]{1,0:T(8,128)(2,1)}, bf16[1024,192]{1,0:T(8,128)(2,1)}, f32[4,128,128]{2,1,0:T(8,128)}) custom-call(bf16[768,576]{1,0:T(8,128)(2,1)S(1)} %bitcast.45, f32[12,2,1024]{2,1,0:T(2,128)S(1)} %reshape_reshape.3.be, f32[1,1024]{1,0:T(1,128)S(1)} %broadcast_in_dim.37.bn, ...), custom_call_target="tpu_custom_call" | custom-call | flops 1308622848 | bytes 4008704 | tf_op jit(solution)/shard_map/attend/pallas_call | solution.py:48
  53.1 5.0 %all-to-all-start = ((bf16[4,192,128]{2,1,0:T(8,128)(2,1)}), bf16[4,192,128]{2,1,0:T(8,128)(2,1)S(1)}, u32[]{:S(2)}, u32[]{:S(2)}) async-start(bf16[4,192,128]{2,1,0:T(8,128)(2,1)} %copy-done.13), calls=%async_computation | async-start | bytes 393216 | tf_op jit(solution)/shard_map/all_to_all | solution.py:673
  60.4 8.2 %all-to-all-done.att = bf16[4,192,128]{2,1,0:T(8,128)(2,1)S(1)} async-done(((bf16[4,192,128]{2,1,0:T(8,128)(2,1)}), bf16[4,192,128]{2,1,0:T(8,128)(2,1)S(1)}, u32[]{:S(2)}, u32[]{:S(2)}) %all-to-all-start) | async-done | bytes 196640 | tf_op jit(solution)/shard_map/all_to_all | solution.py:673
  72.8 4.3 %collective-permute-done.11.refs_1_ = bf16[128,768]{1,0:T(8,128)(2,1)S(1)} collective-permute-done((bf16[128,768]{1,0:T(8,128)(2,1)S(1)}, bf16[128,768]{1,0:T(8,128)(2,1)S(1)}, u32[]{:S(2)}, u32[]{:S(2)}) %collective-permute-start.11) | collective-permute-done | bytes 196640 | tf_op jit(solution)/shard_map/ppermute | solution.py:624
  77.1 4.0 %collective-permute-done.12.refs_2_ = bf16[128,768]{1,0:T(8,128)(2,1)S(1)} collective-permute-done((bf16[128,768]{1,0:T(8,128)(2,1)S(1)}, bf16[128,768]{1,0:T(8,128)(2,1)S(1)}, u32[]{:S(2)}, u32[]{:S(2)}) %collective-permute-start.12) | collective-permute-done | bytes 196640 | tf_op jit(solution)/shard_map/ppermute | solution.py:624
  81.8 3.9 %forward.1 = (f32[128,768]{1,0:T(8,128)S(1)}, bf16[128,768]{1,0:T(8,128)(2,1)S(1)}, bf16[128,768]{1,0:T(8,128)(2,1)S(1)}, bf16[128,768]{1,0:T(8,128)(2,1)S(1)}, ...) custom-call(f32[16,768]{1,0:T(8,128)S(1)} %get-tuple-element.87.vec.refs_6_, bf16[8,192,768]{2,1,0:T(8,128)(2,1)} %bitcast.47, ...), custom_call_target="tpu_custom_call" | custom-call | flops 1207959552 | bytes 6537216 | tf_op jit(solution)/shard_map/forward/pallas_call | solution.py:48
  89.2 3.5 %collective-permute-done.14.refs_1_ = bf16[128,768]{1,0:T(8,128)(2,1)S(1)} collective-permute-done((bf16[128,768]{1,0:T(8,128)(2,1)S(1)}, bf16[128,768]{1,0:T(8,128)(2,1)S(1)}, u32[]{:S(2)}, u32[]{:S(2)}) %collective-permute-start.14) | collective-permute-done | bytes 196640 | tf_op jit(solution)/shard_map/ppermute | solution.py:624
  92.7 3.0 %collective-permute-done.15.refs_2_ = bf16[128,768]{1,0:T(8,128)(2,1)S(1)} collective-permute-done((bf16[128,768]{1,0:T(8,128)(2,1)S(1)}, bf16[128,768]{1,0:T(8,128)(2,1)S(1)}, u32[]{:S(2)}, u32[]{:S(2)}) %collective-permute-start.15) | collective-permute-done | bytes 196640 | tf_op jit(solution)/shard_map/ppermute | solution.py:624
  100.3 2.2 %collective-permute-done.17.refs_1_.refs_5_ = bf16[128,768]{1,0:T(8,128)(2,1)S(1)} collective-permute-done((bf16[128,768]{1,0:T(8,128)(2,1)S(1)}, bf16[128,768]{1,0:T(8,128)(2,1)S(1)}, u32[]{:S(2)}, u32[]{:S(2)}) %collective-permute-start.17) | collective-permute-done | bytes 196640 | tf_op jit(solution)/shard_map/ppermute | solution.py:624
  102.5 2.1 %collective-permute-done.18.refs_2_.refs_6_ = bf16[128,768]{1,0:T(8,128)(2,1)S(1)} collective-permute-done((bf16[128,768]{1,0:T(8,128)(2,1)S(1)}, bf16[128,768]{1,0:T(8,128)(2,1)S(1)}, u32[]{:S(2)}, u32[]{:S(2)}) %collective-permute-start.18) | collective-permute-done | bytes 196640 | tf_op jit(solution)/shard_map/ppermute | solution.py:624
  105.8 2.1 %backward.1 = (f32[128,768]{1,0:T(8,128)S(1)}, bf16[128,768]{1,0:T(8,128)(2,1)S(1)}, bf16[128,768]{1,0:T(8,128)(2,1)S(1)}, bf16[128,768]{1,0:T(8,128)(2,1)S(1)},...) custom-call(bf16[8,192,768]{2,1,0:T(8,128)(2,1)S(1)} %bitcast.48, f32[512,768]{1,0:T(8,128)S(1)} %get-tuple-element.99.inner_ref, ...), custom_call_target="tpu_custom_call" | custom-call | flops 1207959552 | bytes 6491136 | tf_op jit(solution)/shard_map/backward/pallas_call | solution.py:48
  109.6 1.8 collective-permute-start.22
  111.5 2.3 %inner_outer.1.above = bf16[8,200,768]{2,1,0:T(8,128)(2,1)S(1)} custom-call(bf16[512,768]{1,0:T(8,128)(2,1)S(1)} %get-tuple-element.101.gi, bf16[512,768]{1,0:T(8,128)(2,1)S(1)} %get-tuple-element.102.act, f32[8,768]{1,0:T(8,128)S(1)} %get-tuple-element.103.sums, f32[1,768]{1,0:T(1,128)S(1)} %get-tuple-element.104.total, bf16[128,768]{1,0:T(8,128)(2,1)S(1)} %copy-done.7, ...), custom_call_target="tpu_custom_call" | custom-call | flops 1207959552 | bytes 5630976 | tf_op jit(solution)/shard_map/inner_outer/pallas_call | solution.py:48
  113.8 2.7 %collective-permute-done.21.refs_2_ = bf16[128,768]{1,0:T(8,128)(2,1)S(1)} collective-permute-done((bf16[128,768]{1,0:T(8,128)(2,1)S(1)}, bf16[128,768]{1,0:T(8,128)(2,1)S(1)}, u32[]{:S(2)}, u32[]{:S(2)}) %collective-permute-start.21) | collective-permute-done | bytes 196640 | tf_op jit(solution)/shard_map/ppermute | solution.py:624
  116.6 2.5 %residual.1 = (f32[128,768]{1,0:T(8,128)}, bf16[8,296,768]{2,1,0:T(8,128)(2,1)}, bf16[192,128]{1,0:T(8,128)(2,1)}, bf16[192,128]{1,0:T(8,128)(2,1)}, bf16[192,128]{1,0:T(8,128)(2,1)}, /*index=5*/bf16[192,128]{1,0:T(8,128)(2,1)}) custom-call(f32[128,768]{1,0:T(8,128)S(1)} %get-tuple-element.97.mix, f32[128,768]{1,0:T(8,128)S(1)} %get-tuple-element.95.refs_4_.normed, ...), custom_call_target="tpu_custom_call" | custom-call | flops 301989888 | bytes 9945088 | tf_op jit(solution)/shard_map/residual/pallas_call | solution.py:48
  119.9 4.7 %collective-permute-start.23 = (bf16[192,128]{1,0:T(8,128)(2,1)S(1)}, bf16[192,128]{1,0:T(8,128)(2,1)S(1)}, u32[]{:S(2)}, u32[]{:S(2)}) collective-permute-start(bf16[192,128]{1,0:T(8,128)(2,1)S(1)} %copy-done.33), channel_id=1, source_target_pairs={{0,2},{1,3},{2,0},{3,1},{4,6},{5,7},{6,4},{7,5},{8,10},{9,11},{10,... | collective-permute-start | bytes 147464 | tf_op jit(solution)/shard_map/ppermute | solution.py:642
  126.7 2.9 %collective-permute-done.24.refs_2_ = bf16[192,128]{1,0:T(8,128)(2,1)S(1)} collective-permute-done((bf16[192,128]{1,0:T(8,128)(2,1)S(1)}, bf16[192,128]{1,0:T(8,128)(2,1)S(1)}, u32[]{:S(2)}, u32[]{:S(2)}) %collective-permute-start.24) | collective-permute-done | bytes 49184 | tf_op jit(solution)/shard_map/ppermute | solution.py:642
  130.2 9.0 %attend_back.1 = (bf16[4,128,192]{2,1,0:T(8,128)(2,1)S(1)}, bf16[4,128,384]{2,1,0:T(8,128)(2,1)S(1)}, bf16[4,128,384]{2,1,0:T(8,128)(2,1)S(1)}, f32[4,104,576]{2,1,0:T(8,128)S(1)}, bf16[4,104,576]{2,1,0:T(8,128)(2,1)S(1)}) custom-call(bf16[8,128,768]{2,1,0:T(8,128)(2,1)} %all-gather.4.cloned.1.call-done.hid_raw, ...), custom_call_target="tpu_custom_call" | custom-call | flops 1912602624 | bytes 5543936 | tf_op jit(solution)/shard_map/attend_back/pallas_call | solution.py:48
  144.8 2.9 %collective-permute-done.27.refs_1_ = bf16[104,576]{1,0:T(8,128)(2,1)S(1)} collective-permute-done((bf16[104,576]{1,0:T(8,128)(2,1)S(1)}, bf16[104,576]{1,0:T(8,128)(2,1)S(1)}, u32[]{:S(2)}, u32[]{:S(2)}) %collective-permute-start.27) | collective-permute-done | bytes 119840 | tf_op jit(solution)/shard_map/ppermute | solution.py:624
  147.7 2.9 %collective-permute-done.28.refs_2_ = bf16[104,576]{1,0:T(8,128)(2,1)S(1)} collective-permute-done((bf16[104,576]{1,0:T(8,128)(2,1)S(1)}, bf16[104,576]{1,0:T(8,128)(2,1)S(1)}, u32[]{:S(2)}, u32[]{:S(2)}) %collective-permute-start.28) | collective-permute-done | bytes 119840 | tf_op jit(solution)/shard_map/ppermute | solution.py:624
  152.5 2.3 %collective-permute-start.30 = (bf16[24,576]{1,0:T(8,128)(2,1)S(1)}, bf16[24,576]{1,0:T(8,128)(2,1)S(1)}, u32[]{:S(2)}, u32[]{:S(2)}) collective-permute-start(bf16[24,576]{1,0:T(8,128)(2,1)S(1)} %get-tuple-element.125), channel_id=1, source_target_pairs={{0,2},{1,3},{2,0},{3,1},{4,6},{5,7},{6,4},{7,5},{8,10},{9,11},{10,... | collective-permute-start | bytes 82952 | tf_op jit(solution)/shard_map/ppermute | solution.py:642
  154.8 2.7 %collective-permute-start.31 = (bf16[24,576]{1,0:T(8,128)(2,1)S(1)}, bf16[24,576]{1,0:T(8,128)(2,1)S(1)}, u32[]{:S(2)}, u32[]{:S(2)}) collective-permute-start(bf16[24,576]{1,0:T(8,128)(2,1)S(1)} %get-tuple-element.126), channel_id=1, source_target_pairs={{0,4},{1,5},{2,6},{3,7},{4,0},{5,1},{6,2},{7,3},{8,12},{9,13},{10,... | collective-permute-start | bytes 82952 | tf_op jit(solution)/shard_map/ppermute | solution.py:642
  158.0 3.3 %collective-permute-done.31.refs_2_ = bf16[24,576]{1,0:T(8,128)(2,1)S(1)} collective-permute-done((bf16[24,576]{1,0:T(8,128)(2,1)S(1)}, bf16[24,576]{1,0:T(8,128)(2,1)S(1)}, u32[]{:S(2)}, u32[]{:S(2)}) %collective-permute-start.31) | collective-permute-done | bytes 27680 | tf_op jit(solution)/shard_map/ppermute | solution.py:642
  176.0 15.0 %reduce-scatter.5.cloned.1.call-done = bf16[1,128,768]{2,1,0:T(8,128)(2,1)} async-done(((bf16[4,128,768]{2,1,0:T(8,128)(2,1)}), bf16[1,128,768]{2,1,0:T(8,128)(2,1)}) %reduce-scatter.5.cloned.1.call-update) | async-done | bytes 196624 | tf_op jit(solution)/shard_map/reduce_scatter | solution.py:898
  191.4 3.4 %finish_inner.1 = (f32[96,3072]{1,0:T(8,128)}, f32[384,768]{1,0:T(8,128)}, f32[96,768]{1,0:T(8,128)}, f32[8,768]{1,0:T(8,128)S(1)}, f32[128,768]{1,0:T(8,128)}) custom-call(bf16[296,768]{1,0:T(8,128)(2,1)} %bitcast.55, bf16[296,768]{1,0:T(8,128)(2,1)S(1)} %collective-permute-done.36.refs_1_, bf16[296,768]{1,0:T(8,128)(2,1)S(1)} %collective-permute-done.37.refs_2_, ...), custom_call_target="tpu_custom_call" | custom-call | bytes 5480448 | tf_op jit(solution)/shard_map/finish_inner/pallas_call | solution.py:48
  (185 shorter events, 59.7 us)
Async XLA Ops:
  7.3 34.3 %all-gather.4.cloned.1.call-start = ((), (), s32[]{:S(2)}) async-start(), calls=%async_computation.3 | async-start | bytes 1769472 | tf_op jit(solution)/shard_map/all_gather | solution.py:719
  8.0 73.7 %all-gather.6.cloned.1.call-start = ((), (), s32[]{:S(2)}) async-start(), calls=%async_computation.6 | async-start | bytes 2654208 | tf_op jit(solution)/shard_map/all_gather | solution.py:800
  9.3 7.3 %collective-permute-start.1 = (bf16[48,576]{1,0:T(8,128)(2,1)S(1)}, bf16[48,576]{1,0:T(8,128)(2,1)S(1)}, u32[]{:S(2)}, u32[]{:S(2)}) collective-permute-start(bf16[48,576]{1,0:T(8,128)(2,1)S(1)} %get-tuple-element.82), channel_id=1, source_target_pairs={{0,4},{1,5},{2,6},{3,7},{4,0},{5,1},{6,2},{7,3},{8,12},{9,13},{10,... | collective-permute-start | bytes 165896 | tf_op jit(solution)/shard_map/ppermute | solution.py:642
  17.5 6.3 %collective-permute-start.3 = (bf16[4,48,576]{2,1,0:T(8,128)(2,1)S(1)}, bf16[4,48,576]{2,1,0:T(8,128)(2,1)S(1)}, u32[]{:S(2)}, u32[]{:S(2)}) collective-permute-start(bf16[4,48,576]{2,1,0:T(8,128)(2,1)S(1)} %stack.11.refs_0_), channel_id=1, source_target_pairs={{0,8},{8,0},{16,24},{24,16},{1,9},{9,1},{17,25},{25,17},{2,10},{10... | collective-permute-start | bytes 663560 | tf_op jit(solution)/shard_map/ppermute | solution.py:624
  23.9 17.6 %collective-permute-start.7 = (bf16[2,4,48,576]{3,2,1,0:T(8,128)(2,1)S(1)}, bf16[2,4,48,576]{3,2,1,0:T(8,128)(2,1)S(1)}, u32[]{:S(2)}, u32[]{:S(2)}) collective-permute-start(bf16[2,4,48,576]{3,2,1,0:T(8,128)(2,1)S(1)} %stack.13.mine), channel_id=1, source_target_pairs={{0,1},{1,0},{2,3},{3,2},{4,5},{5,4},{6,7},{7,6},{8,9},{9,8},{10,11... | collective-permute-start | bytes 1327112 | tf_op jit(solution)/shard_map/ppermute | solution.py:637
  24.2 10.5 %collective-permute-start.4 = (bf16[56,768]{1,0:T(8,128)(2,1)S(1)}, bf16[56,768]{1,0:T(8,128)(2,1)S(1)}, u32[]{:S(2)}, u32[]{:S(2)}) collective-permute-start(bf16[56,768]{1,0:T(8,128)(2,1)S(1)} %cut_output.1.refs_0_), channel_id=1, source_target_pairs={{0,2},{1,3},{2,0},{3,1},{4,6},{5,7},{6,4},{7,5},{8,10},{9,11},{10,... | collective-permute-start | bytes 258056 | tf_op jit(solution)/shard_map/ppermute | solution.py:642
  26.7 11.0 %collective-permute-start.5 = (bf16[56,768]{1,0:T(8,128)(2,1)S(1)}, bf16[56,768]{1,0:T(8,128)(2,1)S(1)}, u32[]{:S(2)}, u32[]{:S(2)}) collective-permute-start(bf16[56,768]{1,0:T(8,128)(2,1)S(1)} %cut_output.1.refs_0_), channel_id=1, source_target_pairs={{0,4},{1,5},{2,6},{3,7},{4,0},{5,1},{6,2},{7,3},{8,12},{9,13},{10,... | collective-permute-start | bytes 258056 | tf_op jit(solution)/shard_map/ppermute | solution.py:642
  28.3 13.1 %collective-permute-start.6 = (bf16[56,768]{1,0:T(8,128)(2,1)S(1)}, bf16[56,768]{1,0:T(8,128)(2,1)S(1)}, u32[]{:S(2)}, u32[]{:S(2)}) collective-permute-start(bf16[56,768]{1,0:T(8,128)(2,1)S(1)} %cut_output.1.refs_0_), channel_id=1, source_target_pairs={{0,6},{1,7},{2,4},{3,5},{4,2},{5,3},{6,0},{7,1},{8,14},{9,15},{10,... | collective-permute-start | bytes 258056 | tf_op jit(solution)/shard_map/ppermute | solution.py:642
  42.5 10.5 %collective-permute-start.9 = (bf16[4,56,768]{2,1,0:T(8,128)(2,1)S(1)}, bf16[4,56,768]{2,1,0:T(8,128)(2,1)S(1)}, u32[]{:S(2)}, u32[]{:S(2)}) collective-permute-start(bf16[4,56,768]{2,1,0:T(8,128)(2,1)S(1)} %stack.12.refs_0_), channel_id=1, source_target_pairs={{0,16},{8,24},{16,0},{24,8},{1,17},{9,25},{17,1},{25,9},{2,18},{10... | collective-permute-start | bytes 1032200 | tf_op jit(solution)/shard_map/ppermute | solution.py:624
  53.1 15.4 %all-to-all-start = ((bf16[4,192,128]{2,1,0:T(8,128)(2,1)}), bf16[4,192,128]{2,1,0:T(8,128)(2,1)S(1)}, u32[]{:S(2)}, u32[]{:S(2)}) async-start(bf16[4,192,128]{2,1,0:T(8,128)(2,1)} %copy-done.13), calls=%async_computation | async-start | bytes 393216 | tf_op jit(solution)/shard_map/all_to_all | solution.py:673
  58.2 112.7 %reduce-scatter.3.cloned.1.call-start = ((), (), s32[]{:S(2)}) async-start(), calls=%async_computation.4 | async-start | bytes 4091904 | tf_op jit(solution)/shard_map/reduce_scatter | solution.py:1272
  69.2 7.9 %collective-permute-start.11 = (bf16[128,768]{1,0:T(8,128)(2,1)S(1)}, bf16[128,768]{1,0:T(8,128)(2,1)S(1)}, u32[]{:S(2)}, u32[]{:S(2)}) collective-permute-start(bf16[128,768]{1,0:T(8,128)(2,1)S(1)} %get-tuple-element.90.refs_0_), channel_id=1, source_target_pairs={{0,8},{8,0},{16,24},{24,16},{1,9},{9,1},{17,25},{25,17},{2,10},{10... | collective-permute-start | bytes 589832 | tf_op jit(solution)/shard_map/ppermute | solution.py:624
  70.7 10.3 %collective-permute-start.12 = (bf16[128,768]{1,0:T(8,128)(2,1)S(1)}, bf16[128,768]{1,0:T(8,128)(2,1)S(1)}, u32[]{:S(2)}, u32[]{:S(2)}) collective-permute-start(bf16[128,768]{1,0:T(8,128)(2,1)S(1)} %get-tuple-element.90.refs_0_), channel_id=1, source_target_pairs={{0,16},{8,24},{16,0},{24,8},{1,17},{9,25},{17,1},{25,9},{2,18},{10... | collective-permute-start | bytes 589832 | tf_op jit(solution)/shard_map/ppermute | solution.py:624
  72.2 9.6 %collective-permute-start.13 = (bf16[128,768]{1,0:T(8,128)(2,1)S(1)}, bf16[128,768]{1,0:T(8,128)(2,1)}, u32[]{:S(2)}, u32[]{:S(2)}) collective-permute-start(bf16[128,768]{1,0:T(8,128)(2,1)S(1)} %get-tuple-element.90.refs_0_), channel_id=1, source_target_pairs={{0,24},{8,16},{16,8},{24,0},{1,25},{9,17},{17,9},{25,1},{2,26},{10... | collective-permute-start | bytes 589832 | tf_op jit(solution)/shard_map/ppermute | solution.py:624
  85.6 7.1 %collective-permute-start.14 = (bf16[128,768]{1,0:T(8,128)(2,1)S(1)}, bf16[128,768]{1,0:T(8,128)(2,1)S(1)}, u32[]{:S(2)}, u32[]{:S(2)}) collective-permute-start(bf16[128,768]{1,0:T(8,128)(2,1)S(1)} %get-tuple-element.92), channel_id=1, source_target_pairs={{0,8},{8,0},{16,24},{24,16},{1,9},{9,1},{17,25},{25,17},{2,10},{10... | collective-permute-start | bytes 589832 | tf_op jit(solution)/shard_map/ppermute | solution.py:624
  86.3 9.4 %collective-permute-start.15 = (bf16[128,768]{1,0:T(8,128)(2,1)S(1)}, bf16[128,768]{1,0:T(8,128)(2,1)S(1)}, u32[]{:S(2)}, u32[]{:S(2)}) collective-permute-start(bf16[128,768]{1,0:T(8,128)(2,1)S(1)} %get-tuple-element.93), channel_id=1, source_target_pairs={{0,16},{8,24},{16,0},{24,8},{1,17},{9,25},{17,1},{25,9},{2,18},{10... | collective-permute-start | bytes 589832 | tf_op jit(solution)/shard_map/ppermute | solution.py:624
  87.7 8.0 %collective-permute-start.16 = (bf16[128,768]{1,0:T(8,128)(2,1)S(1)}, bf16[128,768]{1,0:T(8,128)(2,1)S(1)}, u32[]{:S(2)}, u32[]{:S(2)}) collective-permute-start(bf16[128,768]{1,0:T(8,128)(2,1)S(1)} %get-tuple-element.94), channel_id=1, source_target_pairs={{0,24},{8,16},{16,8},{24,0},{1,25},{9,17},{17,9},{25,1},{2,26},{10... | collective-permute-start | bytes 589832 | tf_op jit(solution)/shard_map/ppermute | solution.py:624
  97.4 7.1 %collective-permute-start.18 = (bf16[128,768]{1,0:T(8,128)(2,1)S(1)}, bf16[128,768]{1,0:T(8,128)(2,1)S(1)}, u32[]{:S(2)}, u32[]{:S(2)}) collective-permute-start(bf16[128,768]{1,0:T(8,128)(2,1)S(1)} %get-tuple-element.100.refs_0_.refs_4_), channel_id=1, source_target_pairs={{0,16},{8,24},{16,0},{24,8},{1,17},{9,25},{17,1},{25,9},{2,18},{10... | collective-permute-start | bytes 589832 | tf_op jit(solution)/shard_map/ppermute | solution.py:624
  99.2 6.6 %collective-permute-start.19 = (bf16[128,768]{1,0:T(8,128)(2,1)S(1)}, bf16[128,768]{1,0:T(8,128)(2,1)S(1)}, u32[]{:S(2)}, u32[]{:S(2)}) collective-permute-start(bf16[128,768]{1,0:T(8,128)(2,1)S(1)} %get-tuple-element.100.refs_0_.refs_4_), channel_id=1, source_target_pairs={{0,24},{8,16},{16,8},{24,0},{1,25},{9,17},{17,9},{25,1},{2,26},{10... | collective-permute-start | bytes 589832 | tf_op jit(solution)/shard_map/ppermute | solution.py:624
  107.9 5.9 %collective-permute-start.20 = (bf16[128,768]{1,0:T(8,128)(2,1)S(1)}, bf16[128,768]{1,0:T(8,128)(2,1)S(1)}, u32[]{:S(2)}, u32[]{:S(2)}) collective-permute-start(bf16[128,768]{1,0:T(8,128)(2,1)S(1)} %get-tuple-element.106), channel_id=1, source_target_pairs={{0,8},{8,0},{16,24},{24,16},{1,9},{9,1},{17,25},{25,17},{2,10},{10... | collective-permute-start | bytes 589832 | tf_op jit(solution)/shard_map/ppermute | solution.py:624
  108.8 7.8 %collective-permute-start.21 = (bf16[128,768]{1,0:T(8,128)(2,1)S(1)}, bf16[128,768]{1,0:T(8,128)(2,1)S(1)}, u32[]{:S(2)}, u32[]{:S(2)}) collective-permute-start(bf16[128,768]{1,0:T(8,128)(2,1)S(1)} %get-tuple-element.107), channel_id=1, source_target_pairs={{0,16},{8,24},{16,0},{24,8},{1,17},{9,25},{17,1},{25,9},{2,18},{10... | collective-permute-start | bytes 589832 | tf_op jit(solution)/shard_map/ppermute | solution.py:624
  109.6 7.0 %collective-permute-start.22 = (bf16[128,768]{1,0:T(8,128)(2,1)S(1)}, bf16[128,768]{1,0:T(8,128)(2,1)S(1)}, u32[]{:S(2)}, u32[]{:S(2)}) collective-permute-start(bf16[128,768]{1,0:T(8,128)(2,1)S(1)} %get-tuple-element.108), channel_id=1, source_target_pairs={{0,24},{8,16},{16,8},{24,0},{1,25},{9,17},{17,9},{25,1},{2,26},{10... | collective-permute-start | bytes 589832 | tf_op jit(solution)/shard_map/ppermute | solution.py:624
  119.2 71.9 %reduce-scatter.5.cloned.1.call-start = ((), (), s32[]{:S(2)}) async-start(), calls=%async_computation.5 | async-start | bytes 983040 | tf_op jit(solution)/shard_map/reduce_scatter | solution.py:898
  119.9 6.8 %collective-permute-start.23 = (bf16[192,128]{1,0:T(8,128)(2,1)S(1)}, bf16[192,128]{1,0:T(8,128)(2,1)S(1)}, u32[]{:S(2)}, u32[]{:S(2)}) collective-permute-start(bf16[192,128]{1,0:T(8,128)(2,1)S(1)} %copy-done.33), channel_id=1, source_target_pairs={{0,2},{1,3},{2,0},{3,1},{4,6},{5,7},{6,4},{7,5},{8,10},{9,11},{10,... | collective-permute-start | bytes 147464 | tf_op jit(solution)/shard_map/ppermute | solution.py:642
  139.3 11.4 %collective-permute-start.39 = (bf16[4,128,384]{2,1,0:T(8,128)(2,1)S(1)}, bf16[4,128,384]{2,1,0:T(8,128)(2,1)S(1)}, u32[]{:S(2)}, u32[]{:S(2)}) collective-permute-start(bf16[4,128,384]{2,1,0:T(8,128)(2,1)S(1)} %get-tuple-element.133), channel_id=1, source_target_pairs={{0,1},{1,0},{2,3},{3,2},{4,5},{5,4},{6,7},{7,6},{8,9},{9,8},{10,11... | collective-permute-start | bytes 1179656 | tf_op jit(solution)/shard_map/ppermute | solution.py:637
  141.3 6.4 %collective-permute-start.27 = (bf16[104,576]{1,0:T(8,128)(2,1)S(1)}, bf16[104,576]{1,0:T(8,128)(2,1)S(1)}, u32[]{:S(2)}, u32[]{:S(2)}) collective-permute-start(bf16[104,576]{1,0:T(8,128)(2,1)S(1)} %get-tuple-element.121), channel_id=1, source_target_pairs={{0,8},{8,0},{16,24},{24,16},{1,9},{9,1},{17,25},{25,17},{2,10},{10... | collective-permute-start | bytes 359432 | tf_op jit(solution)/shard_map/ppermute | solution.py:624
  142.4 8.2 %collective-permute-start.28 = (bf16[104,576]{1,0:T(8,128)(2,1)S(1)}, bf16[104,576]{1,0:T(8,128)(2,1)S(1)}, u32[]{:S(2)}, u32[]{:S(2)}) collective-permute-start(bf16[104,576]{1,0:T(8,128)(2,1)S(1)} %get-tuple-element.122), channel_id=1, source_target_pairs={{0,16},{8,24},{16,0},{24,8},{1,17},{9,25},{17,1},{25,9},{2,18},{10... | collective-permute-start | bytes 359432 | tf_op jit(solution)/shard_map/ppermute | solution.py:624
  143.7 7.0 %collective-permute-start.29 = (bf16[104,576]{1,0:T(8,128)(2,1)S(1)}, bf16[104,576]{1,0:T(8,128)(2,1)S(1)}, u32[]{:S(2)}, u32[]{:S(2)}) collective-permute-start(bf16[104,576]{1,0:T(8,128)(2,1)S(1)} %get-tuple-element.123), channel_id=1, source_target_pairs={{0,24},{8,16},{16,8},{24,0},{1,25},{9,17},{17,9},{25,1},{2,26},{10... | collective-permute-start | bytes 359432 | tf_op jit(solution)/shard_map/ppermute | solution.py:624
  154.8 6.5 %collective-permute-start.31 = (bf16[24,576]{1,0:T(8,128)(2,1)S(1)}, bf16[24,576]{1,0:T(8,128)(2,1)S(1)}, u32[]{:S(2)}, u32[]{:S(2)}) collective-permute-start(bf16[24,576]{1,0:T(8,128)(2,1)S(1)} %get-tuple-element.126), channel_id=1, source_target_pairs={{0,4},{1,5},{2,6},{3,7},{4,0},{5,1},{6,2},{7,3},{8,12},{9,13},{10,... | collective-permute-start | bytes 82952 | tf_op jit(solution)/shard_map/ppermute | solution.py:642
  170.9 20.2 %collective-permute-start.36 = (bf16[296,768]{1,0:T(8,128)(2,1)}, bf16[296,768]{1,0:T(8,128)(2,1)S(1)}, u32[]{:S(2)}, u32[]{:S(2)}) collective-permute-start(bf16[296,768]{1,0:T(8,128)(2,1)} %bitcast.52), channel_id=1, source_target_pairs={{0,8},{8,0},{16,24},{24,16},{1,9},{9,1},{17,25},{25,17},{2,10},{10... | collective-permute-start | bytes 1363976 | tf_op jit(solution)/shard_map/ppermute | solution.py:624
  172.0 19.4 %collective-permute-start.37 = (bf16[296,768]{1,0:T(8,128)(2,1)}, bf16[296,768]{1,0:T(8,128)(2,1)S(1)}, u32[]{:S(2)}, u32[]{:S(2)}) collective-permute-start(bf16[296,768]{1,0:T(8,128)(2,1)} %bitcast.53), channel_id=1, source_target_pairs={{0,16},{8,24},{16,0},{24,8},{1,17},{9,25},{17,1},{25,9},{2,18},{10... | collective-permute-start | bytes 1363976 | tf_op jit(solution)/shard_map/ppermute | solution.py:624
  172.8 18.7 %collective-permute-start.38 = (bf16[296,768]{1,0:T(8,128)(2,1)}, bf16[296,768]{1,0:T(8,128)(2,1)S(1)}, u32[]{:S(2)}, u32[]{:S(2)}) collective-permute-start(bf16[296,768]{1,0:T(8,128)(2,1)} %bitcast.54), channel_id=1, source_target_pairs={{0,24},{8,16},{16,8},{24,0},{1,25},{9,17},{17,9},{25,1},{2,26},{10... | collective-permute-start | bytes 1363976 | tf_op jit(solution)/shard_map/ppermute | solution.py:624
  (50 other events, 456.3 us)
Sparse Core Ops, SparseCore 0:
  9.8 31.0 all-gather.3
  43.1 34.7 all-gather.5
  119.3 45.3 reduce-scatter.2
  167.4 23.6 reduce-scatter.4

commit v8 on v6

--- a/solution.py
+++ b/solution.py
@@ -585,6 +585,9 @@
         vectors[g : g + 1, :] = line
         total = total + line
     vectors[parts : parts + 1, :] = total
+    bias = [vectors[g : g + 1, 3 * rows : 4 * rows] for g in range(parts)]
+    fill = jnp.zeros((1, scratch.shape[2] - parts * rows), f32)
+    vectors[parts + 1 : parts + 2, :] = jnp.concatenate(bias + [fill], 1)
     if scratch.shape[1] > at + 8:
         last = scratch[0, at + 8 :, :].astype(f32)
         for g in range(1, parts):
@@ -1281,7 +1284,7 @@
         cut(norm_sums, 4),
         cut(norm_sums, 5),
         d_inner,
-        vectors[:groups, 3 * rows : 3 * rows + units].reshape(-1),
+        vectors[groups + 1, : groups * units],
         d_outer,
         cut(norm_sums, 2),
         cut(norm_sums, 0),

time: 206 us -> 206 us (level)
  no operation moved by 1% of the time
where the time goes in v8:
time: 206 us; the launch traced here: 202 us
  waiting for transfers between devices  90.2 us (44%)
  starting transfers between devices  53.3 us (26%)
  Pallas kernels  36.5 us (18%)
  between operations  14.4 us (7%)
  local copies, waits for them, and re-layouts  7.71 us (4%)
    ppermute x23, waiting for transfers between devices, exchange(): return lax.ppermute(array, 'dp', [(i, i ^ k) for i in range(count)])  39.8 us
    pallas_call x24, Pallas kernels, run_kernel(): pl.pallas_call(kernel, name=name, out_shape=out_shape, in_specs=specs, ou...  36.5 us
    ppermute x23, starting transfers between devices, exchange(): return lax.ppermute(array, 'dp', [(i, i ^ k) for i in range(count)])  27.8 us
    ppermute x12, waiting for transfers between devices, line_exchange(): return lax.ppermute(array, 'seq', [(i, i ^ 2 * k) for i in range(count)])  25.2 us
    ppermute x12, starting transfers between devices, line_exchange(): return lax.ppermute(array, 'seq', [(i, i ^ 2 * k) for i in range(count)])  19.3 us
    reduce_scatter x1, waiting for transfers between devices, backward(): lax.psum_scatter(partial, 'seq', scatter_dimension=0, axis_index_groups=l...  14.9 us
    all_to_all x1, waiting for transfers between devices, along_line(): lax.all_to_all(array, 'seq', 0, 0, tiled=True, axis_index_groups=lines)  8.21 us
    all_to_all x1, starting transfers between devices, along_line(): lax.all_to_all(array, 'seq', 0, 0, tiled=True, axis_index_groups=lines)  5.05 us
  transfers between devices with their start and end apart: 45, of which 28 were waited for; matrix products, arithmetic and copies ran while one was open for 1% of the time, Pallas kernels for 12%

profile of v8, /device:TPU:8, one launch (start us, length us, event | category | flops | bytes accessed | tf_op | source)
XLA Modules:
  0.0 202.4 jit_solution(13044739600644636186)
XLA Ops:
  9.3 3.0 %collective-permute-start.1 = (bf16[48,576]{1,0:T(8,128)(2,1)S(1)}, bf16[48,576]{1,0:T(8,128)(2,1)S(1)}, u32[]{:S(2)}, u32[]{:S(2)}) collective-permute-start(bf16[48,576]{1,0:T(8,128)(2,1)S(1)} %get-tuple-element.81), channel_id=1, source_target_pairs={{0,4},{1,5},{2,6},{3,7},{4,0},{5,1},{6,2},{7,3},{8,12},{9,13},{10,... | collective-permute-start | bytes 165896 | tf_op jit(solution)/shard_map/ppermute | solution.py:639
  13.5 3.1 %collective-permute-done.1.refs_2_ = bf16[48,576]{1,0:T(8,128)(2,1)S(1)} collective-permute-done((bf16[48,576]{1,0:T(8,128)(2,1)S(1)}, bf16[48,576]{1,0:T(8,128)(2,1)S(1)}, u32[]{:S(2)}, u32[]{:S(2)}) %collective-permute-start.1) | collective-permute-done | bytes 55328 | tf_op jit(solution)/shard_map/ppermute | solution.py:639
  19.1 4.7 %collective-permute-done.3.refs_1_ = bf16[4,48,576]{2,1,0:T(8,128)(2,1)S(1)} collective-permute-done((bf16[4,48,576]{2,1,0:T(8,128)(2,1)S(1)}, bf16[4,48,576]{2,1,0:T(8,128)(2,1)S(1)}, u32[]{:S(2)}, u32[]{:S(2)}) %collective-permute-start.3) | collective-permute-done | bytes 221216 | tf_op jit(solution)/shard_map/ppermute | solution.py:621
  24.2 2.5 %collective-permute-start.4 = (bf16[56,768]{1,0:T(8,128)(2,1)S(1)}, bf16[56,768]{1,0:T(8,128)(2,1)S(1)}, u32[]{:S(2)}, u32[]{:S(2)}) collective-permute-start(bf16[56,768]{1,0:T(8,128)(2,1)S(1)} %cut_output.1.refs_0_), channel_id=1, source_target_pairs={{0,2},{1,3},{2,0},{3,1},{4,6},{5,7},{6,4},{7,5},{8,10},{9,11},{10,... | collective-permute-start | bytes 258056 | tf_op jit(solution)/shard_map/ppermute | solution.py:639
  29.3 5.4 %collective-permute-done.4.refs_1_ = bf16[56,768]{1,0:T(8,128)(2,1)S(1)} collective-permute-done((bf16[56,768]{1,0:T(8,128)(2,1)S(1)}, bf16[56,768]{1,0:T(8,128)(2,1)S(1)}, u32[]{:S(2)}, u32[]{:S(2)}) %collective-permute-start.4) | collective-permute-done | bytes 86048 | tf_op jit(solution)/shard_map/ppermute | solution.py:639
  34.8 2.9 %collective-permute-done.5.refs_2_ = bf16[56,768]{1,0:T(8,128)(2,1)S(1)} collective-permute-done((bf16[56,768]{1,0:T(8,128)(2,1)S(1)}, bf16[56,768]{1,0:T(8,128)(2,1)S(1)}, u32[]{:S(2)}, u32[]{:S(2)}) %collective-permute-start.5) | collective-permute-done | bytes 86048 | tf_op jit(solution)/shard_map/ppermute | solution.py:639
  37.7 3.7 %collective-permute-done.6.refs_3_ = bf16[56,768]{1,0:T(8,128)(2,1)S(1)} collective-permute-done((bf16[56,768]{1,0:T(8,128)(2,1)S(1)}, bf16[56,768]{1,0:T(8,128)(2,1)S(1)}, u32[]{:S(2)}, u32[]{:S(2)}) %collective-permute-start.6) | collective-permute-done | bytes 86048 | tf_op jit(solution)/shard_map/ppermute | solution.py:639
  44.7 6.5 %attend.1 = (bf16[4,192,128]{2,1,0:T(8,128)(2,1)S(1)}, bf16[4,128,192]{2,1,0:T(8,128)(2,1)}, bf16[1024,192]{1,0:T(8,128)(2,1)}, bf16[1024,192]{1,0:T(8,128)(2,1)}, f32[4,128,128]{2,1,0:T(8,128)}) custom-call(bf16[768,576]{1,0:T(8,128)(2,1)S(1)} %bitcast.44, f32[12,2,1024]{2,1,0:T(2,128)S(1)} %reshape_reshape.3.be, f32[1,1024]{1,0:T(1,128)S(1)} %broadcast_in_dim.37.bn, ...), custom_call_target="tpu_custom_call" | custom-call | flops 1308622848 | bytes 4008704 | tf_op jit(solution)/shard_map/attend/pallas_call | solution.py:48
  53.1 5.0 %all-to-all-start = ((bf16[4,192,128]{2,1,0:T(8,128)(2,1)}), bf16[4,192,128]{2,1,0:T(8,128)(2,1)S(1)}, u32[]{:S(2)}, u32[]{:S(2)}) async-start(bf16[4,192,128]{2,1,0:T(8,128)(2,1)} %copy-done.15), calls=%async_computation | async-start | bytes 393216 | tf_op jit(solution)/shard_map/all_to_all | solution.py:670
  60.4 8.2 %all-to-all-done.att = bf16[4,192,128]{2,1,0:T(8,128)(2,1)S(1)} async-done(((bf16[4,192,128]{2,1,0:T(8,128)(2,1)}), bf16[4,192,128]{2,1,0:T(8,128)(2,1)S(1)}, u32[]{:S(2)}, u32[]{:S(2)}) %all-to-all-start) | async-done | bytes 196640 | tf_op jit(solution)/shard_map/all_to_all | solution.py:670
  72.8 4.3 %collective-permute-done.11.refs_1_ = bf16[128,768]{1,0:T(8,128)(2,1)S(1)} collective-permute-done((bf16[128,768]{1,0:T(8,128)(2,1)S(1)}, bf16[128,768]{1,0:T(8,128)(2,1)S(1)}, u32[]{:S(2)}, u32[]{:S(2)}) %collective-permute-start.11) | collective-permute-done | bytes 196640 | tf_op jit(solution)/shard_map/ppermute | solution.py:621
  77.1 4.0 %collective-permute-done.12.refs_2_ = bf16[128,768]{1,0:T(8,128)(2,1)S(1)} collective-permute-done((bf16[128,768]{1,0:T(8,128)(2,1)S(1)}, bf16[128,768]{1,0:T(8,128)(2,1)S(1)}, u32[]{:S(2)}, u32[]{:S(2)}) %collective-permute-start.12) | collective-permute-done | bytes 196640 | tf_op jit(solution)/shard_map/ppermute | solution.py:621
  81.8 3.9 %forward.1 = (f32[128,768]{1,0:T(8,128)S(1)}, bf16[128,768]{1,0:T(8,128)(2,1)S(1)}, bf16[128,768]{1,0:T(8,128)(2,1)S(1)}, bf16[128,768]{1,0:T(8,128)(2,1)S(1)}, ...) custom-call(f32[16,768]{1,0:T(8,128)S(1)} %get-tuple-element.86.vec.refs_6_, bf16[8,192,768]{2,1,0:T(8,128)(2,1)} %bitcast.46, ...), custom_call_target="tpu_custom_call" | custom-call | flops 1207959552 | bytes 6537216 | tf_op jit(solution)/shard_map/forward/pallas_call | solution.py:48
  89.2 3.5 %collective-permute-done.14.refs_1_ = bf16[128,768]{1,0:T(8,128)(2,1)S(1)} collective-permute-done((bf16[128,768]{1,0:T(8,128)(2,1)S(1)}, bf16[128,768]{1,0:T(8,128)(2,1)S(1)}, u32[]{:S(2)}, u32[]{:S(2)}) %collective-permute-start.14) | collective-permute-done | bytes 196640 | tf_op jit(solution)/shard_map/ppermute | solution.py:621
  92.7 3.0 %collective-permute-done.15.refs_2_ = bf16[128,768]{1,0:T(8,128)(2,1)S(1)} collective-permute-done((bf16[128,768]{1,0:T(8,128)(2,1)S(1)}, bf16[128,768]{1,0:T(8,128)(2,1)S(1)}, u32[]{:S(2)}, u32[]{:S(2)}) %collective-permute-start.15) | collective-permute-done | bytes 196640 | tf_op jit(solution)/shard_map/ppermute | solution.py:621
  100.3 2.2 %collective-permute-done.17.refs_1_.refs_5_ = bf16[128,768]{1,0:T(8,128)(2,1)S(1)} collective-permute-done((bf16[128,768]{1,0:T(8,128)(2,1)S(1)}, bf16[128,768]{1,0:T(8,128)(2,1)S(1)}, u32[]{:S(2)}, u32[]{:S(2)}) %collective-permute-start.17) | collective-permute-done | bytes 196640 | tf_op jit(solution)/shard_map/ppermute | solution.py:621
  102.5 2.1 %collective-permute-done.18.refs_2_.refs_6_ = bf16[128,768]{1,0:T(8,128)(2,1)S(1)} collective-permute-done((bf16[128,768]{1,0:T(8,128)(2,1)S(1)}, bf16[128,768]{1,0:T(8,128)(2,1)S(1)}, u32[]{:S(2)}, u32[]{:S(2)}) %collective-permute-start.18) | collective-permute-done | bytes 196640 | tf_op jit(solution)/shard_map/ppermute | solution.py:621
  105.8 2.1 %backward.1 = (f32[128,768]{1,0:T(8,128)S(1)}, bf16[128,768]{1,0:T(8,128)(2,1)S(1)}, bf16[128,768]{1,0:T(8,128)(2,1)S(1)}, bf16[128,768]{1,0:T(8,128)(2,1)S(1)},...) custom-call(bf16[8,192,768]{2,1,0:T(8,128)(2,1)S(1)} %bitcast.47, f32[512,768]{1,0:T(8,128)S(1)} %get-tuple-element.98.inner_ref, ...), custom_call_target="tpu_custom_call" | custom-call | flops 1207959552 | bytes 6491136 | tf_op jit(solution)/shard_map/backward/pallas_call | solution.py:48
  109.6 1.8 collective-permute-start.22
  111.5 2.3 %inner_outer.1.above = bf16[8,200,768]{2,1,0:T(8,128)(2,1)S(1)} custom-call(bf16[512,768]{1,0:T(8,128)(2,1)S(1)} %get-tuple-element.100.gi, bf16[512,768]{1,0:T(8,128)(2,1)S(1)} %get-tuple-element.101.act, f32[8,768]{1,0:T(8,128)S(1)} %get-tuple-element.102.sums, f32[1,768]{1,0:T(1,128)S(1)} %get-tuple-element.103.total, bf16[128,768]{1,0:T(8,128)(2,1)S(1)} %copy-done.9, ...), custom_call_target="tpu_custom_call" | custom-call | flops 1207959552 | bytes 5630976 | tf_op jit(solution)/shard_map/inner_outer/pallas_call | solution.py:48
  113.8 2.7 %collective-permute-done.21.refs_2_ = bf16[128,768]{1,0:T(8,128)(2,1)S(1)} collective-permute-done((bf16[128,768]{1,0:T(8,128)(2,1)S(1)}, bf16[128,768]{1,0:T(8,128)(2,1)S(1)}, u32[]{:S(2)}, u32[]{:S(2)}) %collective-permute-start.21) | collective-permute-done | bytes 196640 | tf_op jit(solution)/shard_map/ppermute | solution.py:621
  116.6 2.5 %residual.1 = (f32[128,768]{1,0:T(8,128)}, bf16[8,296,768]{2,1,0:T(8,128)(2,1)}, bf16[192,128]{1,0:T(8,128)(2,1)}, bf16[192,128]{1,0:T(8,128)(2,1)}, bf16[192,128]{1,0:T(8,128)(2,1)}, /*index=5*/bf16[192,128]{1,0:T(8,128)(2,1)}) custom-call(f32[128,768]{1,0:T(8,128)S(1)} %get-tuple-element.96.mix, f32[128,768]{1,0:T(8,128)S(1)} %get-tuple-element.94.refs_4_.normed, ...), custom_call_target="tpu_custom_call" | custom-call | flops 301989888 | bytes 9945088 | tf_op jit(solution)/shard_map/residual/pallas_call | solution.py:48
  119.9 4.7 %collective-permute-start.23 = (bf16[192,128]{1,0:T(8,128)(2,1)S(1)}, bf16[192,128]{1,0:T(8,128)(2,1)S(1)}, u32[]{:S(2)}, u32[]{:S(2)}) collective-permute-start(bf16[192,128]{1,0:T(8,128)(2,1)S(1)} %copy-done.36), channel_id=1, source_target_pairs={{0,2},{1,3},{2,0},{3,1},{4,6},{5,7},{6,4},{7,5},{8,10},{9,11},{10,... | collective-permute-start | bytes 147464 | tf_op jit(solution)/shard_map/ppermute | solution.py:639
  126.7 2.9 %collective-permute-done.24.refs_2_ = bf16[192,128]{1,0:T(8,128)(2,1)S(1)} collective-permute-done((bf16[192,128]{1,0:T(8,128)(2,1)S(1)}, bf16[192,128]{1,0:T(8,128)(2,1)S(1)}, u32[]{:S(2)}, u32[]{:S(2)}) %collective-permute-start.24) | collective-permute-done | bytes 49184 | tf_op jit(solution)/shard_map/ppermute | solution.py:639
  130.2 9.0 %attend_back.1 = (bf16[4,128,192]{2,1,0:T(8,128)(2,1)S(1)}, bf16[4,128,384]{2,1,0:T(8,128)(2,1)S(1)}, bf16[4,128,384]{2,1,0:T(8,128)(2,1)S(1)}, f32[4,104,576]{2,1,0:T(8,128)S(1)}, bf16[4,104,576]{2,1,0:T(8,128)(2,1)S(1)}) custom-call(bf16[8,128,768]{2,1,0:T(8,128)(2,1)} %all-gather.4.cloned.1.call-done.hid_raw, ...), custom_call_target="tpu_custom_call" | custom-call | flops 1912602624 | bytes 5543936 | tf_op jit(solution)/shard_map/attend_back/pallas_call | solution.py:48
  144.8 2.9 %collective-permute-done.27.refs_1_ = bf16[104,576]{1,0:T(8,128)(2,1)S(1)} collective-permute-done((bf16[104,576]{1,0:T(8,128)(2,1)S(1)}, bf16[104,576]{1,0:T(8,128)(2,1)S(1)}, u32[]{:S(2)}, u32[]{:S(2)}) %collective-permute-start.27) | collective-permute-done | bytes 119840 | tf_op jit(solution)/shard_map/ppermute | solution.py:621
  147.7 2.9 %collective-permute-done.28.refs_2_ = bf16[104,576]{1,0:T(8,128)(2,1)S(1)} collective-permute-done((bf16[104,576]{1,0:T(8,128)(2,1)S(1)}, bf16[104,576]{1,0:T(8,128)(2,1)S(1)}, u32[]{:S(2)}, u32[]{:S(2)}) %collective-permute-start.28) | collective-permute-done | bytes 119840 | tf_op jit(solution)/shard_map/ppermute | solution.py:621
  152.5 2.3 %collective-permute-start.31 = (bf16[24,576]{1,0:T(8,128)(2,1)S(1)}, bf16[24,576]{1,0:T(8,128)(2,1)S(1)}, u32[]{:S(2)}, u32[]{:S(2)}) collective-permute-start(bf16[24,576]{1,0:T(8,128)(2,1)S(1)} %get-tuple-element.128), channel_id=1, source_target_pairs={{0,2},{1,3},{2,0},{3,1},{4,6},{5,7},{6,4},{7,5},{8,10},{9,11},{10,... | collective-permute-start | bytes 82952 | tf_op jit(solution)/shard_map/ppermute | solution.py:639
  154.8 2.7 %collective-permute-start.32 = (bf16[24,576]{1,0:T(8,128)(2,1)S(1)}, bf16[24,576]{1,0:T(8,128)(2,1)S(1)}, u32[]{:S(2)}, u32[]{:S(2)}) collective-permute-start(bf16[24,576]{1,0:T(8,128)(2,1)S(1)} %get-tuple-element.129), channel_id=1, source_target_pairs={{0,4},{1,5},{2,6},{3,7},{4,0},{5,1},{6,2},{7,3},{8,12},{9,13},{10,... | collective-permute-start | bytes 82952 | tf_op jit(solution)/shard_map/ppermute | solution.py:639
  158.0 3.3 %collective-permute-done.32.refs_2_ = bf16[24,576]{1,0:T(8,128)(2,1)S(1)} collective-permute-done((bf16[24,576]{1,0:T(8,128)(2,1)S(1)}, bf16[24,576]{1,0:T(8,128)(2,1)S(1)}, u32[]{:S(2)}, u32[]{:S(2)}) %collective-permute-start.32) | collective-permute-done | bytes 27680 | tf_op jit(solution)/shard_map/ppermute | solution.py:639
  176.1 14.9 %reduce-scatter.3.cloned.1.call-done.parts = bf16[1,128,768]{2,1,0:T(8,128)(2,1)} async-done(((bf16[4,128,768]{2,1,0:T(8,128)(2,1)}), bf16[1,128,768]{2,1,0:T(8,128)(2,1)}) %reduce-scatter.3.cloned.1.call-update) | async-done | bytes 196624 | tf_op jit(solution)/shard_map/reduce_scatter | solution.py:888
  192.7 2.0 finish_inner.1
  (191 shorter events, 60.9 us)
Async XLA Ops:
  7.3 34.3 %all-gather.4.cloned.1.call-start = ((), (), s32[]{:S(2)}) async-start(), calls=%async_computation.3 | async-start | bytes 1769472 | tf_op jit(solution)/shard_map/all_gather | solution.py:709
  8.0 73.7 %all-gather.6.cloned.1.call-start = ((), (), s32[]{:S(2)}) async-start(), calls=%async_computation.6 | async-start | bytes 2654208 | tf_op jit(solution)/shard_map/all_gather | solution.py:790
  9.3 7.3 %collective-permute-start.1 = (bf16[48,576]{1,0:T(8,128)(2,1)S(1)}, bf16[48,576]{1,0:T(8,128)(2,1)S(1)}, u32[]{:S(2)}, u32[]{:S(2)}) collective-permute-start(bf16[48,576]{1,0:T(8,128)(2,1)S(1)} %get-tuple-element.81), channel_id=1, source_target_pairs={{0,4},{1,5},{2,6},{3,7},{4,0},{5,1},{6,2},{7,3},{8,12},{9,13},{10,... | collective-permute-start | bytes 165896 | tf_op jit(solution)/shard_map/ppermute | solution.py:639
  17.5 6.3 %collective-permute-start.3 = (bf16[4,48,576]{2,1,0:T(8,128)(2,1)S(1)}, bf16[4,48,576]{2,1,0:T(8,128)(2,1)S(1)}, u32[]{:S(2)}, u32[]{:S(2)}) collective-permute-start(bf16[4,48,576]{2,1,0:T(8,128)(2,1)S(1)} %stack.11.refs_0_), channel_id=1, source_target_pairs={{0,8},{8,0},{16,24},{24,16},{1,9},{9,1},{17,25},{25,17},{2,10},{10... | collective-permute-start | bytes 663560 | tf_op jit(solution)/shard_map/ppermute | solution.py:621
  23.9 17.6 %collective-permute-start.7 = (bf16[2,4,48,576]{3,2,1,0:T(8,128)(2,1)S(1)}, bf16[2,4,48,576]{3,2,1,0:T(8,128)(2,1)S(1)}, u32[]{:S(2)}, u32[]{:S(2)}) collective-permute-start(bf16[2,4,48,576]{3,2,1,0:T(8,128)(2,1)S(1)} %stack.13.mine), channel_id=1, source_target_pairs={{0,1},{1,0},{2,3},{3,2},{4,5},{5,4},{6,7},{7,6},{8,9},{9,8},{10,11... | collective-permute-start | bytes 1327112 | tf_op jit(solution)/shard_map/ppermute | solution.py:634
  24.2 10.5 %collective-permute-start.4 = (bf16[56,768]{1,0:T(8,128)(2,1)S(1)}, bf16[56,768]{1,0:T(8,128)(2,1)S(1)}, u32[]{:S(2)}, u32[]{:S(2)}) collective-permute-start(bf16[56,768]{1,0:T(8,128)(2,1)S(1)} %cut_output.1.refs_0_), channel_id=1, source_target_pairs={{0,2},{1,3},{2,0},{3,1},{4,6},{5,7},{6,4},{7,5},{8,10},{9,11},{10,... | collective-permute-start | bytes 258056 | tf_op jit(solution)/shard_map/ppermute | solution.py:639
  26.7 11.0 %collective-permute-start.5 = (bf16[56,768]{1,0:T(8,128)(2,1)S(1)}, bf16[56,768]{1,0:T(8,128)(2,1)S(1)}, u32[]{:S(2)}, u32[]{:S(2)}) collective-permute-start(bf16[56,768]{1,0:T(8,128)(2,1)S(1)} %cut_output.1.refs_0_), channel_id=1, source_target_pairs={{0,4},{1,5},{2,6},{3,7},{4,0},{5,1},{6,2},{7,3},{8,12},{9,13},{10,... | collective-permute-start | bytes 258056 | tf_op jit(solution)/shard_map/ppermute | solution.py:639
  28.3 13.1 %collective-permute-start.6 = (bf16[56,768]{1,0:T(8,128)(2,1)S(1)}, bf16[56,768]{1,0:T(8,128)(2,1)S(1)}, u32[]{:S(2)}, u32[]{:S(2)}) collective-permute-start(bf16[56,768]{1,0:T(8,128)(2,1)S(1)} %cut_output.1.refs_0_), channel_id=1, source_target_pairs={{0,6},{1,7},{2,4},{3,5},{4,2},{5,3},{6,0},{7,1},{8,14},{9,15},{10,... | collective-permute-start | bytes 258056 | tf_op jit(solution)/shard_map/ppermute | solution.py:639
  42.5 10.5 %collective-permute-start.9 = (bf16[4,56,768]{2,1,0:T(8,128)(2,1)S(1)}, bf16[4,56,768]{2,1,0:T(8,128)(2,1)S(1)}, u32[]{:S(2)}, u32[]{:S(2)}) collective-permute-start(bf16[4,56,768]{2,1,0:T(8,128)(2,1)S(1)} %stack.12.refs_0_), channel_id=1, source_target_pairs={{0,16},{8,24},{16,0},{24,8},{1,17},{9,25},{17,1},{25,9},{2,18},{10... | collective-permute-start | bytes 1032200 | tf_op jit(solution)/shard_map/ppermute | solution.py:621
  53.1 15.4 %all-to-all-start = ((bf16[4,192,128]{2,1,0:T(8,128)(2,1)}), bf16[4,192,128]{2,1,0:T(8,128)(2,1)S(1)}, u32[]{:S(2)}, u32[]{:S(2)}) async-start(bf16[4,192,128]{2,1,0:T(8,128)(2,1)} %copy-done.15), calls=%async_computation | async-start | bytes 393216 | tf_op jit(solution)/shard_map/all_to_all | solution.py:670
  58.2 112.7 %reduce-scatter.5.cloned.1.call-start = ((), (), s32[]{:S(2)}) async-start(), calls=%async_computation.5 | async-start | bytes 4091904 | tf_op jit(solution)/shard_map/reduce_scatter | solution.py:1264
  69.2 7.9 %collective-permute-start.11 = (bf16[128,768]{1,0:T(8,128)(2,1)S(1)}, bf16[128,768]{1,0:T(8,128)(2,1)S(1)}, u32[]{:S(2)}, u32[]{:S(2)}) collective-permute-start(bf16[128,768]{1,0:T(8,128)(2,1)S(1)} %get-tuple-element.89.refs_0_), channel_id=1, source_target_pairs={{0,8},{8,0},{16,24},{24,16},{1,9},{9,1},{17,25},{25,17},{2,10},{10... | collective-permute-start | bytes 589832 | tf_op jit(solution)/shard_map/ppermute | solution.py:621
  70.7 10.3 %collective-permute-start.12 = (bf16[128,768]{1,0:T(8,128)(2,1)S(1)}, bf16[128,768]{1,0:T(8,128)(2,1)S(1)}, u32[]{:S(2)}, u32[]{:S(2)}) collective-permute-start(bf16[128,768]{1,0:T(8,128)(2,1)S(1)} %get-tuple-element.89.refs_0_), channel_id=1, source_target_pairs={{0,16},{8,24},{16,0},{24,8},{1,17},{9,25},{17,1},{25,9},{2,18},{10... | collective-permute-start | bytes 589832 | tf_op jit(solution)/shard_map/ppermute | solution.py:621
  72.2 9.6 %collective-permute-start.13 = (bf16[128,768]{1,0:T(8,128)(2,1)S(1)}, bf16[128,768]{1,0:T(8,128)(2,1)}, u32[]{:S(2)}, u32[]{:S(2)}) collective-permute-start(bf16[128,768]{1,0:T(8,128)(2,1)S(1)} %get-tuple-element.89.refs_0_), channel_id=1, source_target_pairs={{0,24},{8,16},{16,8},{24,0},{1,25},{9,17},{17,9},{25,1},{2,26},{10... | collective-permute-start | bytes 589832 | tf_op jit(solution)/shard_map/ppermute | solution.py:621
  85.6 7.1 %collective-permute-start.14 = (bf16[128,768]{1,0:T(8,128)(2,1)S(1)}, bf16[128,768]{1,0:T(8,128)(2,1)S(1)}, u32[]{:S(2)}, u32[]{:S(2)}) collective-permute-start(bf16[128,768]{1,0:T(8,128)(2,1)S(1)} %get-tuple-element.91), channel_id=1, source_target_pairs={{0,8},{8,0},{16,24},{24,16},{1,9},{9,1},{17,25},{25,17},{2,10},{10... | collective-permute-start | bytes 589832 | tf_op jit(solution)/shard_map/ppermute | solution.py:621
  86.3 9.4 %collective-permute-start.15 = (bf16[128,768]{1,0:T(8,128)(2,1)S(1)}, bf16[128,768]{1,0:T(8,128)(2,1)S(1)}, u32[]{:S(2)}, u32[]{:S(2)}) collective-permute-start(bf16[128,768]{1,0:T(8,128)(2,1)S(1)} %get-tuple-element.92), channel_id=1, source_target_pairs={{0,16},{8,24},{16,0},{24,8},{1,17},{9,25},{17,1},{25,9},{2,18},{10... | collective-permute-start | bytes 589832 | tf_op jit(solution)/shard_map/ppermute | solution.py:621
  87.7 8.0 %collective-permute-start.16 = (bf16[128,768]{1,0:T(8,128)(2,1)S(1)}, bf16[128,768]{1,0:T(8,128)(2,1)S(1)}, u32[]{:S(2)}, u32[]{:S(2)}) collective-permute-start(bf16[128,768]{1,0:T(8,128)(2,1)S(1)} %get-tuple-element.93), channel_id=1, source_target_pairs={{0,24},{8,16},{16,8},{24,0},{1,25},{9,17},{17,9},{25,1},{2,26},{10... | collective-permute-start | bytes 589832 | tf_op jit(solution)/shard_map/ppermute | solution.py:621
  97.4 7.1 %collective-permute-start.18 = (bf16[128,768]{1,0:T(8,128)(2,1)S(1)}, bf16[128,768]{1,0:T(8,128)(2,1)S(1)}, u32[]{:S(2)}, u32[]{:S(2)}) collective-permute-start(bf16[128,768]{1,0:T(8,128)(2,1)S(1)} %get-tuple-element.99.refs_0_.refs_4_), channel_id=1, source_target_pairs={{0,16},{8,24},{16,0},{24,8},{1,17},{9,25},{17,1},{25,9},{2,18},{10... | collective-permute-start | bytes 589832 | tf_op jit(solution)/shard_map/ppermute | solution.py:621
  99.2 6.6 %collective-permute-start.19 = (bf16[128,768]{1,0:T(8,128)(2,1)S(1)}, bf16[128,768]{1,0:T(8,128)(2,1)S(1)}, u32[]{:S(2)}, u32[]{:S(2)}) collective-permute-start(bf16[128,768]{1,0:T(8,128)(2,1)S(1)} %get-tuple-element.99.refs_0_.refs_4_), channel_id=1, source_target_pairs={{0,24},{8,16},{16,8},{24,0},{1,25},{9,17},{17,9},{25,1},{2,26},{10... | collective-permute-start | bytes 589832 | tf_op jit(solution)/shard_map/ppermute | solution.py:621
  107.9 5.9 %collective-permute-start.20 = (bf16[128,768]{1,0:T(8,128)(2,1)S(1)}, bf16[128,768]{1,0:T(8,128)(2,1)S(1)}, u32[]{:S(2)}, u32[]{:S(2)}) collective-permute-start(bf16[128,768]{1,0:T(8,128)(2,1)S(1)} %get-tuple-element.105), channel_id=1, source_target_pairs={{0,8},{8,0},{16,24},{24,16},{1,9},{9,1},{17,25},{25,17},{2,10},{10... | collective-permute-start | bytes 589832 | tf_op jit(solution)/shard_map/ppermute | solution.py:621
  108.8 7.8 %collective-permute-start.21 = (bf16[128,768]{1,0:T(8,128)(2,1)S(1)}, bf16[128,768]{1,0:T(8,128)(2,1)S(1)}, u32[]{:S(2)}, u32[]{:S(2)}) collective-permute-start(bf16[128,768]{1,0:T(8,128)(2,1)S(1)} %get-tuple-element.106), channel_id=1, source_target_pairs={{0,16},{8,24},{16,0},{24,8},{1,17},{9,25},{17,1},{25,9},{2,18},{10... | collective-permute-start | bytes 589832 | tf_op jit(solution)/shard_map/ppermute | solution.py:621
  109.6 7.0 %collective-permute-start.22 = (bf16[128,768]{1,0:T(8,128)(2,1)S(1)}, bf16[128,768]{1,0:T(8,128)(2,1)S(1)}, u32[]{:S(2)}, u32[]{:S(2)}) collective-permute-start(bf16[128,768]{1,0:T(8,128)(2,1)S(1)} %get-tuple-element.107), channel_id=1, source_target_pairs={{0,24},{8,16},{16,8},{24,0},{1,25},{9,17},{17,9},{25,1},{2,26},{10... | collective-permute-start | bytes 589832 | tf_op jit(solution)/shard_map/ppermute | solution.py:621
  119.2 71.8 %reduce-scatter.3.cloned.1.call-start = ((), (), s32[]{:S(2)}) async-start(), calls=%async_computation.4 | async-start | bytes 983040 | tf_op jit(solution)/shard_map/reduce_scatter | solution.py:888
  119.9 6.8 %collective-permute-start.23 = (bf16[192,128]{1,0:T(8,128)(2,1)S(1)}, bf16[192,128]{1,0:T(8,128)(2,1)S(1)}, u32[]{:S(2)}, u32[]{:S(2)}) collective-permute-start(bf16[192,128]{1,0:T(8,128)(2,1)S(1)} %copy-done.36), channel_id=1, source_target_pairs={{0,2},{1,3},{2,0},{3,1},{4,6},{5,7},{6,4},{7,5},{8,10},{9,11},{10,... | collective-permute-start | bytes 147464 | tf_op jit(solution)/shard_map/ppermute | solution.py:639
  139.3 11.4 %collective-permute-start.30 = (bf16[4,128,384]{2,1,0:T(8,128)(2,1)S(1)}, bf16[4,128,384]{2,1,0:T(8,128)(2,1)S(1)}, u32[]{:S(2)}, u32[]{:S(2)}) collective-permute-start(bf16[4,128,384]{2,1,0:T(8,128)(2,1)S(1)} %get-tuple-element.127), channel_id=1, source_target_pairs={{0,1},{1,0},{2,3},{3,2},{4,5},{5,4},{6,7},{7,6},{8,9},{9,8},{10,11... | collective-permute-start | bytes 1179656 | tf_op jit(solution)/shard_map/ppermute | solution.py:634
  141.3 6.4 %collective-permute-start.27 = (bf16[104,576]{1,0:T(8,128)(2,1)S(1)}, bf16[104,576]{1,0:T(8,128)(2,1)S(1)}, u32[]{:S(2)}, u32[]{:S(2)}) collective-permute-start(bf16[104,576]{1,0:T(8,128)(2,1)S(1)} %get-tuple-element.121), channel_id=1, source_target_pairs={{0,8},{8,0},{16,24},{24,16},{1,9},{9,1},{17,25},{25,17},{2,10},{10... | collective-permute-start | bytes 359432 | tf_op jit(solution)/shard_map/ppermute | solution.py:621
  142.4 8.2 %collective-permute-start.28 = (bf16[104,576]{1,0:T(8,128)(2,1)S(1)}, bf16[104,576]{1,0:T(8,128)(2,1)S(1)}, u32[]{:S(2)}, u32[]{:S(2)}) collective-permute-start(bf16[104,576]{1,0:T(8,128)(2,1)S(1)} %get-tuple-element.122), channel_id=1, source_target_pairs={{0,16},{8,24},{16,0},{24,8},{1,17},{9,25},{17,1},{25,9},{2,18},{10... | collective-permute-start | bytes 359432 | tf_op jit(solution)/shard_map/ppermute | solution.py:621
  143.6 6.9 %collective-permute-start.29 = (bf16[104,576]{1,0:T(8,128)(2,1)S(1)}, bf16[104,576]{1,0:T(8,128)(2,1)S(1)}, u32[]{:S(2)}, u32[]{:S(2)}) collective-permute-start(bf16[104,576]{1,0:T(8,128)(2,1)S(1)} %get-tuple-element.123), channel_id=1, source_target_pairs={{0,24},{8,16},{16,8},{24,0},{1,25},{9,17},{17,9},{25,1},{2,26},{10... | collective-permute-start | bytes 359432 | tf_op jit(solution)/shard_map/ppermute | solution.py:621
  154.8 6.5 %collective-permute-start.32 = (bf16[24,576]{1,0:T(8,128)(2,1)S(1)}, bf16[24,576]{1,0:T(8,128)(2,1)S(1)}, u32[]{:S(2)}, u32[]{:S(2)}) collective-permute-start(bf16[24,576]{1,0:T(8,128)(2,1)S(1)} %get-tuple-element.129), channel_id=1, source_target_pairs={{0,4},{1,5},{2,6},{3,7},{4,0},{5,1},{6,2},{7,3},{8,12},{9,13},{10,... | collective-permute-start | bytes 82952 | tf_op jit(solution)/shard_map/ppermute | solution.py:639
  170.9 21.8 %collective-permute-start.37 = (bf16[296,768]{1,0:T(8,128)(2,1)}, bf16[296,768]{1,0:T(8,128)(2,1)S(1)}, u32[]{:S(2)}, u32[]{:S(2)}) collective-permute-start(bf16[296,768]{1,0:T(8,128)(2,1)} %bitcast.49), channel_id=1, source_target_pairs={{0,8},{8,0},{16,24},{24,16},{1,9},{9,1},{17,25},{25,17},{2,10},{10... | collective-permute-start | bytes 1363976 | tf_op jit(solution)/shard_map/ppermute | solution.py:621
  172.0 20.7 %collective-permute-start.38 = (bf16[296,768]{1,0:T(8,128)(2,1)}, bf16[296,768]{1,0:T(8,128)(2,1)S(1)}, u32[]{:S(2)}, u32[]{:S(2)}) collective-permute-start(bf16[296,768]{1,0:T(8,128)(2,1)} %bitcast.50), channel_id=1, source_target_pairs={{0,16},{8,24},{16,0},{24,8},{1,17},{9,25},{17,1},{25,9},{2,18},{10... | collective-permute-start | bytes 1363976 | tf_op jit(solution)/shard_map/ppermute | solution.py:621
  172.8 19.9 %collective-permute-start.39 = (bf16[296,768]{1,0:T(8,128)(2,1)}, bf16[296,768]{1,0:T(8,128)(2,1)S(1)}, u32[]{:S(2)}, u32[]{:S(2)}) collective-permute-start(bf16[296,768]{1,0:T(8,128)(2,1)} %bitcast.51), channel_id=1, source_target_pairs={{0,24},{8,16},{16,8},{24,0},{1,25},{9,17},{17,9},{25,1},{2,26},{10... | collective-permute-start | bytes 1363976 | tf_op jit(solution)/shard_map/ppermute | solution.py:621
  (53 other events, 519.3 us)
Sparse Core Ops, SparseCore 0:
  9.8 31.0 all-gather.3
  43.1 34.7 all-gather.5
  119.3 45.3 reduce-scatter.4
  167.4 23.5 reduce-scatter.2
